TPU v7x, 32 devices: a whole 2x2x4 slice. The times are simulated.
32 devices in a mesh: dp: 8 (over y, x, core), tensor: 4 (over z).
Axes of the slice: x: 2, y: 2, z: 4, core: 2. Of those that a mesh axis runs over, the one named last changes fastest.
Arguments:
- block_input: bfloat16 [8, 3072, 768], P('dp', 'tensor'), may hold values from -6 to 6
- attention_gain: float32 [768], replicated, may hold values from 0.5 to 1.5
- qkv_weight: bfloat16 [3, 768, 768], P(None, None, 'tensor'), may hold values from -0.21875 to 0.21875
- proj_weight: bfloat16 [768, 768], P('tensor'), may hold values from -3.5 to 3.5
- moe_gain: float32 [768], replicated, may hold values from 0.5 to 1.5
- centroids: bfloat16 [4, 768], replicated, may hold values from -0.15625 to 0.15625
- expert_up: bfloat16 [4, 768, 3072], P(None, None, 'tensor'), may hold values from -0.21875 to 0.21875
- expert_down: bfloat16 [4, 3072, 768], P(None, 'tensor'), may hold values from -0.21875 to 0.21875
- out_grad: bfloat16 [8, 3072, 768], P('dp', 'tensor'), may hold values from -6 to 6
- routes: int32 [8, 3072, 1], P('dp'), may hold values from 0 to 3
- priority: int32 [8, 3072], P('dp'), may hold values from 0 to 3071, each once within a row
- segments: int32 [8, 3072], P('dp'), may hold values from 0 to 8, as said below
Outputs:
- block_output: bfloat16 [8, 3072, 768], P('dp', 'tensor')
- input_grad: bfloat16 [8, 3072, 768], P('dp', 'tensor')
- attention_gain_grad: float32 [768], P(('dp', 'tensor'))
- moe_gain_grad: float32 [768], P(('dp', 'tensor'))
- centroid_grad: float32 [4, 768], P(None, ('dp', 'tensor'))
- qkv_grad: float32 [3, 768, 768], P(None, 'dp', 'tensor')
- proj_grad: float32 [768, 768], P('tensor', 'dp')
- expert_up_grad: float32 [4, 768, 3072], P(None, 'dp', 'tensor')
- expert_down_grad: float32 [4, 3072, 768], P(None, 'tensor', 'dp')
Inputs may be any that keep to these rules, and one draw needn't show every extreme that they name: `segments`: along each group's row the ids never fall and start at 0; the prompt (id 0) holds 1024 tokens or more, and every continuation id 1 to 8 holds at least one token.
All inputs are finite; a program needn't handle non-finite values.
Results may differ from a plain program's by a relative error of at most 0.023.
Values may be sent and summed in bfloat16 or wider, within the bound.
No kernel may reach another device: no remote copies, remote signals or barrier semaphores. Data moves between devices by JAX's collectives and lax.ppermute only.
A program may use at most 192 MiB of HBM per device.

v0:
```python
import jax
import jax.numpy as jnp
from jax import lax
from jax.sharding import PartitionSpec as P

HEAD_DIM = 64


epsilon = 1e-05
highest = lax.Precision.HIGHEST


def gelu_tanh(values):
    return (
        0.5
        * values
        * (1.0 + jnp.tanh(0.7978845608028654 * (values + 0.044715 * values * values * values)))
    )


def normalize_plain(values):
    centered = values - jnp.mean(values, axis=-1, keepdims=True)
    variance = jnp.mean(centered * centered, axis=-1, keepdims=True)
    inverse = lax.rsqrt(variance + epsilon)
    return (centered * inverse, inverse)


def normalize_back(upstream, unit_rows, inverse, gain_row):
    scaled = upstream * gain_row
    centered = scaled - jnp.mean(scaled, axis=-1, keepdims=True)
    return inverse * (centered - unit_rows * jnp.mean(scaled * unit_rows, axis=-1, keepdims=True))


def route_slots(route_col, priority_row, experts, capacity):
    token_count = route_col.shape[0]
    route_hot = (route_col[:, None] == jnp.arange(experts, dtype=jnp.int32)[None, :]).astype(
        jnp.int32
    )
    inverse = (
        jnp.zeros((token_count,), jnp.int32)
        .at[priority_row]
        .set(jnp.arange(token_count, dtype=jnp.int32))
    )
    ranked = route_hot[inverse]
    before = jnp.cumsum(ranked, axis=0) - ranked
    slot_rank = jnp.sum(before * ranked, axis=1)[priority_row]
    kept_mask = slot_rank < capacity
    target = jnp.where(kept_mask, route_col * capacity + slot_rank, experts * capacity)
    slot_table = (
        jnp.full((experts * capacity + 1,), token_count, jnp.int32)
        .at[target]
        .set(jnp.arange(token_count, dtype=jnp.int32))
    )
    return (route_hot, kept_mask, target, slot_table[: experts * capacity])


def allowed_mask(segment, offset, block_rows):
    query_pos = offset + jnp.arange(block_rows, dtype=jnp.int32)
    key_pos = jnp.arange(segment.shape[0], dtype=jnp.int32)
    query_seg = lax.dynamic_slice_in_dim(segment, offset, block_rows, 0)
    causal = key_pos[None, :] <= query_pos[:, None]
    shared = (segment[None, :] == 0) | (segment[None, :] == query_seg[:, None])
    return causal & shared


def body(
    block_input,
    attention_gain,
    qkv_weight,
    proj_weight,
    moe_gain,
    centroids,
    expert_up,
    expert_down,
    out_grad,
    routes,
    priority,
    segments,
):
    row_count = block_input.shape[1]
    model_width = block_input.shape[2]
    experts = expert_up.shape[0]
    segment = segments[0]
    token_count = segment.shape[0]
    capacity = 9 * token_count // (8 * experts)
    local_width = qkv_weight.shape[2]
    head_count = local_width // HEAD_DIM
    block_rows = min(512, token_count)
    score_scale = HEAD_DIM ** (-0.5)
    own_start = lax.axis_index("tensor") * row_count
    inputs = block_input[0].astype(jnp.float32)
    unit_one, inverse_one = normalize_plain(inputs)
    normed_one_rows = (unit_one * attention_gain).astype(jnp.bfloat16)
    normed_one = lax.all_gather(normed_one_rows, "tensor", axis=0, tiled=True)
    qkv_all = jnp.einsum(
        "td,kdh->kth", normed_one, qkv_weight, preferred_element_type=jnp.float32
    ).astype(jnp.bfloat16)
    queries = qkv_all[0].reshape(token_count, head_count, HEAD_DIM)
    keys_all = qkv_all[1].reshape(token_count, head_count, HEAD_DIM)
    values_all = qkv_all[2].reshape(token_count, head_count, HEAD_DIM)

    def masked_scores(offset):
        query_block = lax.dynamic_slice_in_dim(queries, offset, block_rows, 0)
        scores = (
            jnp.einsum("qhd,khd->hqk", query_block, keys_all, preferred_element_type=jnp.float32)
            * score_scale
        )
        return (
            jnp.where(allowed_mask(segment, offset, block_rows)[None], scores, -1e30),
            query_block,
        )

    def attend(offset):
        scores = masked_scores(offset)[0]
        top_score = jnp.max(scores, axis=-1, keepdims=True)
        weights = jnp.exp(scores - top_score)
        totals = jnp.sum(weights, axis=-1, keepdims=True)
        prob_rows = (weights / totals).astype(jnp.bfloat16)
        context_block = jnp.einsum(
            "hqk,khd->qhd", prob_rows, values_all, preferred_element_type=jnp.float32
        )
        return (context_block.astype(jnp.bfloat16), (top_score + jnp.log(totals))[:, :, 0])

    offsets = jnp.arange(token_count // block_rows, dtype=jnp.int32) * block_rows
    context_blocks, log_totals = lax.map(attend, offsets)
    context = context_blocks.reshape(token_count, local_width)
    attended = lax.psum_scatter(
        jnp.dot(context, proj_weight, preferred_element_type=jnp.float32).astype(jnp.bfloat16),
        "tensor",
        scatter_dimension=0,
        tiled=True,
    ).astype(jnp.float32)
    mixed_one = inputs + attended
    unit_two, inverse_two = normalize_plain(mixed_one)
    normed_two_rows = (unit_two * moe_gain).astype(jnp.bfloat16)
    normed_two = lax.all_gather(normed_two_rows, "tensor", axis=0, tiled=True)
    route_hot, kept_mask, target, slot_table = route_slots(
        routes[0, :, 0], priority[0], experts, capacity
    )
    zero_row = jnp.zeros((1, model_width), jnp.bfloat16)
    zero_float = jnp.zeros((1, model_width), jnp.float32)
    dispatched = jnp.concatenate([normed_two, zero_row], axis=0)[slot_table].reshape(
        experts, capacity, model_width
    )
    upward = jnp.einsum("ecd,edf->ecf", dispatched, expert_up, preferred_element_type=jnp.float32)
    hidden = gelu_tanh(upward).astype(jnp.bfloat16)
    returned = jnp.einsum(
        "ecf,efd->ecd", hidden, expert_down, preferred_element_type=jnp.float32
    ).reshape(experts * capacity, model_width)
    returned = jnp.concatenate([returned, zero_float], axis=0)
    expert_out = lax.psum_scatter(
        returned[target].astype(jnp.bfloat16), "tensor", scatter_dimension=0, tiled=True
    ).astype(jnp.float32)
    hot_rows = lax.dynamic_slice_in_dim(route_hot, own_start, row_count, 0)
    kept_rows = lax.dynamic_slice_in_dim(kept_mask, own_start, row_count, 0)
    centroid_rows = jnp.dot(
        hot_rows.astype(jnp.bfloat16), centroids, preferred_element_type=jnp.float32
    )
    normed_two_float = normed_two_rows.astype(jnp.float32)
    gate_prob = jax.nn.sigmoid(jnp.sum(normed_two_float * centroid_rows, axis=-1))
    gate_used = jnp.where(kept_rows, gate_prob, 0.0)
    mixed_two = mixed_one + gate_used[:, None] * expert_out
    block_output = mixed_two.astype(jnp.bfloat16)[None]
    upstream = out_grad[0].astype(jnp.float32)
    grad_eo_rows = (gate_used[:, None] * upstream).astype(jnp.bfloat16)
    grad_gate = jnp.where(kept_rows, jnp.sum(upstream * expert_out, axis=-1), 0.0)
    grad_score = grad_gate * gate_prob * (1.0 - gate_prob)
    grad_eo = lax.all_gather(grad_eo_rows, "tensor", axis=0, tiled=True)
    grad_dispatched = jnp.concatenate([grad_eo, zero_row], axis=0)[slot_table].reshape(
        experts, capacity, model_width
    )
    grad_hidden = jnp.einsum(
        "ecd,efd->ecf", grad_dispatched, expert_down, preferred_element_type=jnp.float32
    )
    down_part = jnp.einsum(
        "ecf,ecd->efd", hidden, grad_dispatched, preferred_element_type=jnp.float32
    )
    gelu_value, gelu_pull = jax.vjp(gelu_tanh, upward)
    grad_upward = gelu_pull(grad_hidden)[0].astype(jnp.bfloat16)
    up_part = jnp.einsum(
        "ecd,ecf->edf", dispatched, grad_upward, preferred_element_type=jnp.float32
    )
    back_moe = jnp.einsum(
        "ecf,edf->ecd", grad_upward, expert_up, preferred_element_type=jnp.float32
    ).reshape(experts * capacity, model_width)
    back_moe = jnp.concatenate([back_moe, zero_float], axis=0)
    grad_two = (
        lax.psum_scatter(
            back_moe[target].astype(jnp.bfloat16), "tensor", scatter_dimension=0, tiled=True
        ).astype(jnp.float32)
        + grad_score[:, None] * centroid_rows
    )
    centroid_part = jnp.einsum(
        "te,td->ed",
        hot_rows.astype(jnp.float32),
        grad_score[:, None] * normed_two_float,
        precision=highest,
    )
    moe_gain_part = jnp.sum(grad_two * unit_two, axis=0)
    grad_mixed = upstream + normalize_back(grad_two, unit_two, inverse_two, moe_gain)
    grad_att_rows = grad_mixed.astype(jnp.bfloat16)
    grad_att = lax.all_gather(grad_att_rows, "tensor", axis=0, tiled=True)
    proj_part = jnp.einsum("tc,td->cd", context, grad_att, preferred_element_type=jnp.float32)
    grad_context = jnp.einsum(
        "td,cd->tc", grad_att, proj_weight, preferred_element_type=jnp.float32
    ).astype(jnp.bfloat16)
    grad_context = grad_context.reshape(token_count, head_count, HEAD_DIM)

    def back_block(carried, offset_and_log):
        offset, log_block = offset_and_log
        key_grad, value_grad = carried
        scores, query_block = masked_scores(offset)
        prob_rows = jnp.exp(scores - log_block[:, :, None])
        prob_low = prob_rows.astype(jnp.bfloat16)
        grad_block = lax.dynamic_slice_in_dim(grad_context, offset, block_rows, 0)
        grad_probs = jnp.einsum(
            "qhd,khd->hqk", grad_block, values_all, preferred_element_type=jnp.float32
        )
        row_inner = jnp.sum(prob_rows * grad_probs, axis=-1, keepdims=True)
        grad_scores = (prob_rows * (grad_probs - row_inner)).astype(jnp.bfloat16)
        query_grad = (
            jnp.einsum("hqk,khd->qhd", grad_scores, keys_all, preferred_element_type=jnp.float32)
            * score_scale
        ).astype(jnp.bfloat16)
        key_grad = (
            key_grad
            + jnp.einsum(
                "hqk,qhd->khd", grad_scores, query_block, preferred_element_type=jnp.float32
            )
            * score_scale
        )
        value_grad = value_grad + jnp.einsum(
            "hqk,qhd->khd", prob_low, grad_block, preferred_element_type=jnp.float32
        )
        return ((key_grad, value_grad), query_grad)

    zero_keys = jnp.zeros((token_count, head_count, HEAD_DIM), jnp.float32)
    (key_grad, value_grad), query_blocks = lax.scan(
        back_block, (zero_keys, zero_keys), (offsets, log_totals)
    )
    grad_qkv = jnp.stack(
        [
            query_blocks.reshape(token_count, local_width),
            key_grad.astype(jnp.bfloat16).reshape(token_count, local_width),
            value_grad.astype(jnp.bfloat16).reshape(token_count, local_width),
        ]
    )
    qkv_part = jnp.einsum("td,kth->kdh", normed_one, grad_qkv, preferred_element_type=jnp.float32)
    grad_one = lax.psum_scatter(
        jnp.einsum("kth,kdh->td", grad_qkv, qkv_weight, preferred_element_type=jnp.float32).astype(
            jnp.bfloat16
        ),
        "tensor",
        scatter_dimension=0,
        tiled=True,
    ).astype(jnp.float32)
    attention_gain_part = jnp.sum(grad_one * unit_one, axis=0)
    input_grad = (
        grad_mixed + normalize_back(grad_one, unit_one, inverse_one, attention_gain)
    ).astype(jnp.bfloat16)[None]
    gain_one_sum, gain_two_sum, centroid_sum = (
        lax.psum_scatter(attention_gain_part, ("dp", "tensor"), scatter_dimension=0, tiled=True),
        lax.psum_scatter(moe_gain_part, ("dp", "tensor"), scatter_dimension=0, tiled=True),
        lax.psum_scatter(centroid_part, ("dp", "tensor"), scatter_dimension=1, tiled=True),
    )
    qkv_summed, proj_summed, up_summed, down_summed = (
        lax.psum_scatter(qkv_part, "dp", scatter_dimension=1, tiled=True),
        lax.psum_scatter(proj_part, "dp", scatter_dimension=1, tiled=True),
        lax.psum_scatter(up_part, "dp", scatter_dimension=1, tiled=True),
        lax.psum_scatter(down_part, "dp", scatter_dimension=2, tiled=True),
    )
    return (
        block_output,
        input_grad,
        gain_one_sum,
        gain_two_sum,
        centroid_sum,
        qkv_summed,
        proj_summed,
        up_summed,
        down_summed,
    )


def solution(mesh):
    return jax.shard_map(
        body,
        mesh=mesh,
        in_specs=(
            P("dp", "tensor", None),
            P(),
            P(None, None, "tensor"),
            P("tensor", None),
            P(),
            P(),
            P(None, None, "tensor"),
            P(None, "tensor", None),
            P("dp", "tensor", None),
            P("dp", None, None),
            P("dp", None),
            P("dp", None),
        ),
        out_specs=(
            P("dp", "tensor", None),
            P("dp", "tensor", None),
            P(("dp", "tensor")),
            P(("dp", "tensor")),
            P(None, ("dp", "tensor")),
            P(None, "dp", "tensor"),
            P("tensor", "dp"),
            P(None, "dp", "tensor"),
            P(None, "tensor", "dp"),
        ),
        check_vma=False,
    )
```

profile of v0, /device:TPU:0, one launch (start us, length us, event | category | flops | bytes accessed | tf_op | source)
XLA Modules:
  0.0 1640.8 jit_solution(9726711043699947455)
XLA Ops:
  12.8 92.2 %all-gather.5.cloned.1.call-done = bf16[3072,768]{1,0:T(8,128)(2,1)} async-done(((bf16[768,768]{1,0:T(8,128)(2,1)}), bf16[3072,768]{1,0:T(8,128)(2,1)}) %all-gather.5.cloned.1.call-update) | async-done | bytes 4718608 | tf_op jit(solution)/shard_map/all_gather | solution.py:94
  113.2 148.3 %while.27 = (s32[]{:T(128)}, bf16[6,512,3,64]{1,3,2,0:T(8,128)(2,1)}, f32[6,3,512]{2,1,0:T(4,128)}, s32[6]{0:T(128)S(1)}, s32[1,3072]{1,0:T(1,128)S(1)}, /*index...) while((s32[]{:T(128)}, ...), condition=%wide.region_5.6_spmd, body=%wide.region_2.5_spmd.sunk | while | flops 1270974464 | bytes 72050904 | solution.py:125
  129.2 8.0 fusion.152
  153.9 8.0 fusion.152
  178.6 8.0 fusion.152
  203.3 8.0 fusion.152
  228.0 8.0 fusion.152
  271.6 80.9 %reduce-scatter.14.cloned.1.call-done = bf16[768,768]{1,0:T(8,128)(2,1)} async-done(((bf16[3072,768]{1,0:T(8,128)(2,1)}), bf16[768,768]{1,0:T(8,128)(2,1)}) %reduce-scatter.14.cloned.1.call-update) | async-done | bytes 1179664 | tf_op jit(solution)/shard_map/reduce_scatter | solution.py:127
  358.6 11.8 scatter_custom_fusion
  370.4 12.2 gather_fusion
  390.2 17.4 %gather_fusion.1 = s32[3072]{0:T(1024)S(1)} fusion(s32[3072]{0:T(1024)S(1)} %fusion.72, s32[3072]{0:T(1024)S(1)} %broadcast_clamp_fusion.1), kind=kCustom, calls=%fused_computation.1 | custom fusion | bytes 36864 | tf_op jit(solution)/shard_map/gather | solution.py:46
  407.7 11.8 scatter_custom_fusion.1
  419.5 29.0 %all-gather.7.cloned.1.call-done = bf16[3072,768]{1,0:T(8,128)(2,1)} async-done(((bf16[768,768]{1,0:T(8,128)(2,1)}), bf16[3072,768]{1,0:T(8,128)(2,1)}) %all-gather.7.cloned.1.call-update) | async-done | bytes 4718608 | tf_op jit(solution)/shard_map/all_gather | solution.py:136
  453.3 17.2 %gather_fusion.2 = bf16[3456,768]{1,0:T(8,128)(2,1)} fusion(bf16[3073,768]{1,0:T(8,128)(2,1)} %concatenate.12, s32[4096]{0:T(1024)S(1)} %pad_clamp_fusion), kind=kCustom, calls=%fused_computation.2 | custom fusion | bytes 10630656 | tf_op jit(solution)/shard_map/gather | solution.py:142
  478.2 11.1 fusion.93
  492.0 17.7 %gather_fusion.3 = bf16[3072,768]{1,0:T(8,128)(2,1)} fusion(bf16[3457,768]{1,0:T(8,128)(2,1)} %concatenate.13, s32[3072]{0:T(1024)S(1)} %broadcast_clamp_fusion), kind=kCustom, calls=%fused_computation.3 | custom fusion | bytes 9449472 | tf_op jit(solution)/shard_map/gather | solution.py:152
  509.8 83.8 %reduce-scatter.16.cloned.1.call-done = bf16[768,768]{1,0:T(8,128)(2,1)} async-done(((bf16[3072,768]{1,0:T(8,128)(2,1)}), bf16[768,768]{1,0:T(8,128)(2,1)}) %reduce-scatter.16.cloned.1.call-update) | async-done | bytes 1179664 | tf_op jit(solution)/shard_map/reduce_scatter | solution.py:151
  597.2 90.0 %all-gather.9.cloned.1.call-done = bf16[3072,768]{1,0:T(8,128)(2,1)} async-done(((bf16[768,768]{1,0:T(8,128)(2,1)}), bf16[3072,768]{1,0:T(8,128)(2,1)}) %all-gather.9.cloned.1.call-update) | async-done | bytes 4718608 | tf_op jit(solution)/shard_map/all_gather | solution.py:168
  691.9 17.0 %gather_fusion.4 = bf16[3456,768]{1,0:T(8,128)(2,1)} fusion(bf16[3073,768]{1,0:T(8,128)(2,1)} %concatenate.14, s32[4096]{0:T(1024)S(1)} %pad_clamp_fusion), kind=kCustom, calls=%fused_computation.4 | custom fusion | bytes 10630656 | tf_op jit(solution)/shard_map/gather | solution.py:169
  708.9 15.8 fusion.43
  724.8 8.8 fusion.98
  736.3 17.9 %gather_fusion.5 = bf16[3072,768]{1,0:T(8,128)(2,1)} fusion(bf16[3457,768]{1,0:T(8,128)(2,1)} %concatenate.15, s32[3072]{0:T(1024)S(1)} %broadcast_clamp_fusion), kind=kCustom, calls=%fused_computation.5 | custom fusion | bytes 9449472 | tf_op jit(solution)/shard_map/gather | solution.py:189
  754.3 83.8 %reduce-scatter.18.cloned.1.call-done = bf16[768,768]{1,0:T(8,128)(2,1)} async-done(((bf16[3072,768]{1,0:T(8,128)(2,1)}), bf16[768,768]{1,0:T(8,128)(2,1)}) %reduce-scatter.18.cloned.1.call-update) | async-done | bytes 1179664 | tf_op jit(solution)/shard_map/reduce_scatter | solution.py:188
  846.9 90.0 %all-gather.11.cloned.1.call-done = bf16[3072,768]{1,0:T(8,128)(2,1)} async-done(((bf16[768,768]{1,0:T(8,128)(2,1)}), bf16[3072,768]{1,0:T(8,128)(2,1)}) %all-gather.11.cloned.1.call-update) | async-done | bytes 4718608 | tf_op jit(solution)/shard_map/all_gather | solution.py:202
  948.8 374.2 %while.28 = (s32[]{:T(128)}, f32[3072,3,64]{0,2,1:T(8,128)}, f32[3072,3,64]{0,2,1:T(8,128)}, bf16[6,512,3,64]{1,3,2,0:T(8,128)(2,1)}, s32[6]{0:T(128)S(1)}, /*in...) while((s32[]{:T(128)}, f32[3072,3,64]{0,2,1:T(8,128)}, ...), condition=%wide.region_22.23_spmd.clone, body=%wide.region_20.22_spmd.clone.sunk | while | flops 3100116992 | bytes 237390064 | solution.py:238
  973.4 14.8 multiply_reduce_fusion.6
  988.2 13.9 multiply_convert_fusion.7
  1026.3 8.9 fusion.165
  1035.2 14.7 multiply_reduce_fusion.6
  1049.9 13.9 multiply_convert_fusion.7
  1088.9 8.9 fusion.165
  1097.7 14.7 multiply_reduce_fusion.6
  1112.5 13.9 multiply_convert_fusion.7
  1151.5 8.9 fusion.165
  1160.3 14.7 multiply_reduce_fusion.6
  1175.1 13.9 multiply_convert_fusion.7
  1214.0 8.9 fusion.165
  1222.9 14.7 multiply_reduce_fusion.6
  1237.6 13.9 multiply_convert_fusion.7
  1276.6 8.8 fusion.165
  1285.4 14.7 multiply_reduce_fusion.6
  1300.2 13.9 multiply_convert_fusion.7
  1352.2 13.5 fusion.92
  1365.8 11.1 fusion.99
  1385.1 85.6 %reduce-scatter.20.cloned.1.call-done = bf16[768,768]{1,0:T(8,128)(2,1)} async-done(((bf16[3072,768]{1,0:T(8,128)(2,1)}), bf16[768,768]{1,0:T(8,128)(2,1)}) %reduce-scatter.20.cloned.1.call-update) | async-done | bytes 1179664 | tf_op jit(solution)/shard_map/reduce_scatter | solution.py:249
  1473.3 41.3 %all-reduce.7 = (f32[768]{0:T(1024)S(1)}, f32[768]{0:T(1024)S(1)}, f32[4,768]{1,0:T(4,128)S(1)}) all-reduce(f32[768]{0:T(1024)S(1)} %get-tuple-element.195, f32[768]{0:T(1024)S(1)} %copy-done.34, f32[4,768]{1,0:T(4,128)S(1)} %fusion.64), channel_id=6, replica_groups=mesh['dp'=8,'tensor'=4] {'dp','tensor'}, use_global_device_ids=true, to_apply=%region_27.28.clone | all-reduce | flops 4608 | bytes 36864
  1519.6 33.3 %reduce-scatter.24.cloned.1.call-done = f32[4,768,96]{1,2,0:T(8,128)} async-done(((f32[4,768,768]{1,2,0:T(8,128)}), f32[4,768,96]{1,2,0:T(8,128)}) %reduce-scatter.24.cloned.1.call-update) | async-done | bytes 1179664 | tf_op jit(solution)/shard_map/reduce_scatter | solution.py:270
  1552.8 80.8 %reduce-scatter.22.cloned.1.call-done = f32[4,96,768]{2,1,0:T(8,128)} async-done(((f32[4,768,768]{2,1,0:T(8,128)}), f32[4,96,768]{2,1,0:T(8,128)}) %reduce-scatter.22.cloned.1.call-update) | async-done | bytes 1179664 | tf_op jit(solution)/shard_map/reduce_scatter | solution.py:269
  (300 shorter events, 370.7 us)
Async XLA Ops:
  7.2 97.8 %copy-start = (bf16[3,768,192]{1,2,0:T(8,128)(2,1)S(1)}, bf16[3,768,192]{1,2,0:T(8,128)(2,1)}, u32[]{:S(2)}) copy-start(bf16[3,768,192]{1,2,0:T(8,128)(2,1)} %param.18) | copy-start | bytes 2654212
  7.2 4.1 copy-start.3
  7.2 4.1 copy-start.31
  7.2 97.8 %all-gather.5.cloned.1.call-start = ((), (), s32[]{:S(2)}) async-start(), calls=%async_computation.8 | async-start | bytes 5898240 | tf_op jit(solution)/shard_map/all_gather | solution.py:94
  12.8 339.8 %reduce-scatter.14.cloned.1.call-start = ((), (), s32[]{:S(2)}) async-start(), calls=%async_computation.9 | async-start | bytes 5898240 | tf_op jit(solution)/shard_map/reduce_scatter | solution.py:127
  118.5 5.4 copy-start.2
  143.2 5.4 copy-start.2
  167.9 5.4 copy-start.2
  192.6 5.4 copy-start.2
  217.3 5.4 copy-start.2
  242.0 5.3 copy-start.2
  261.5 3.6 copy-start.22
  268.6 83.9 %copy-start.4 = (bf16[1,768,768]{2,1,0:T(8,128)(2,1)S(1)}, bf16[1,768,768]{2,1,0:T(8,128)(2,1)}, u32[]{:S(2)}) copy-start(bf16[1,768,768]{2,1,0:T(8,128)(2,1)} %param.16) | copy-start | bytes 3538948
  268.7 179.9 %all-gather.7.cloned.1.call-start = ((), (), s32[]{:S(2)}) async-start(), calls=%async_computation.10 | async-start | bytes 5898240 | tf_op jit(solution)/shard_map/all_gather | solution.py:136
  271.6 83.3 %copy-start.33 = (f32[768]{0:T(1024)S(1)}, f32[768]{0:T(1024)}, u32[]{:S(2)}) copy-start(f32[768]{0:T(1024)} %param.20) | copy-start | bytes 9220
  271.6 83.3 %copy-start.36 = (bf16[4,768]{1,0:T(4,128)(2,1)S(1)}, bf16[4,768]{1,0:T(4,128)(2,1)}, u32[]{:S(2)}) copy-start(bf16[4,768]{1,0:T(4,128)(2,1)} %param.21) | copy-start | bytes 18436
  354.9 3.6 copy-start.35
  358.5 235.1 %reduce-scatter.16.cloned.1.call-start = ((), (), s32[]{:S(2)}) async-start(), calls=%async_computation.11 | async-start | bytes 5898240 | tf_op jit(solution)/shard_map/reduce_scatter | solution.py:151
  478.2 11.1 copy-start.37
  509.7 177.5 %all-gather.9.cloned.1.call-start = ((), (), s32[]{:S(2)}) async-start(), calls=%async_computation.12 | async-start | bytes 5898240 | tf_op jit(solution)/shard_map/all_gather | solution.py:168
  595.8 246.7 %copy-start.28 = (f32[768]{0:T(1024)}, f32[768]{0:T(1024)S(1)}, u32[]{:S(2)}) copy-start(f32[768]{0:T(1024)S(1)} %get-tuple-element.245) | copy-start | bytes 9220
  597.1 241.0 %reduce-scatter.18.cloned.1.call-start = ((), (), s32[]{:S(2)}) async-start(), calls=%async_computation.13 | async-start | bytes 5898240 | tf_op jit(solution)/shard_map/reduce_scatter | solution.py:188
  724.8 8.8 copy-start.38
  754.2 182.7 %all-gather.11.cloned.1.call-start = ((), (), s32[]{:S(2)}) async-start(), calls=%async_computation.14 | async-start | bytes 5898240 | tf_op jit(solution)/shard_map/all_gather | solution.py:202
  838.1 4.4 copy-start.7
  838.1 4.4 copy-start.8
  838.1 4.4 copy-start.10
  838.1 4.5 copy-start.15
  846.8 533.8 %reduce-scatter.28.cloned.1.call-start = ((), (), s32[]{:S(2)}) async-start(), calls=%async_computation.19 | async-start | bytes 884736
  846.9 95.7 %copy-start.23 = (bf16[192,768]{1,0:T(8,128)(2,1)S(1)}, bf16[192,768]{1,0:T(8,128)(2,1)}, u32[]{:S(2)}) copy-start(bf16[192,768]{1,0:T(8,128)(2,1)} %param.19) | copy-start | bytes 884740
  942.5 440.7 %reduce-scatter.26.cloned.1.call-start = ((), (), s32[]{:S(2)}) async-start(), calls=%async_computation.18 | async-start | bytes 2211840
  959.0 6.5 copy-start.1
  1019.8 6.5 copy-start.1
  1082.4 6.5 copy-start.1
  1145.0 6.5 copy-start.1
  1207.6 6.5 copy-start.1
  1270.1 6.5 copy-start.1
  1339.4 4.9 copy-start.18
  1339.4 4.9 copy-start.20
  1344.3 126.5 %reduce-scatter.20.cloned.1.call-start = ((), (), s32[]{:S(2)}) async-start(), calls=%async_computation.15 | async-start | bytes 5898240 | tf_op jit(solution)/shard_map/reduce_scatter | solution.py:249
  1352.1 200.7 %reduce-scatter.24.cloned.1.call-start = ((), (), s32[]{:S(2)}) async-start(), calls=%async_computation.17 | async-start | bytes 10616832 | tf_op jit(solution)/shard_map/reduce_scatter | solution.py:270
  1365.7 268.0 %reduce-scatter.22.cloned.1.call-start = ((), (), s32[]{:S(2)}) async-start(), calls=%async_computation.16 | async-start | bytes 10616832 | tf_op jit(solution)/shard_map/reduce_scatter | solution.py:269
  1376.9 93.8 %copy-start.5 = (bf16[1,768,768]{2,1,0:T(8,128)(2,1)S(1)}, bf16[1,768,768]{2,1,0:T(8,128)(2,1)}, u32[]{:S(2)}) copy-start(bf16[1,768,768]{2,1,0:T(8,128)(2,1)} %param.16) | copy-start | bytes 3538948
  1376.9 93.8 %copy-start.25 = (f32[768]{0:T(1024)S(1)}, f32[768]{0:T(1024)}, u32[]{:S(2)}) copy-start(f32[768]{0:T(1024)} %copy-done.24) | copy-start | bytes 9220
  1376.9 93.8 %copy-start.27 = (f32[768]{0:T(1024)S(1)}, f32[768]{0:T(1024)}, u32[]{:S(2)}) copy-start(f32[768]{0:T(1024)} %copy-done.26) | copy-start | bytes 9220
  1376.9 93.8 %copy-start.32 = (f32[768]{0:T(1024)S(1)}, f32[768]{0:T(1024)}, u32[]{:S(2)}) copy-start(f32[768]{0:T(1024)} %param.17) | copy-start | bytes 9220
  1378.2 95.1 %copy-start.34 = (f32[768]{0:T(1024)S(1)}, f32[768]{0:T(1024)}, u32[]{:S(2)}) copy-start(f32[768]{0:T(1024)} %get-tuple-element.192) | copy-start | bytes 9220
  1470.7 45.7 %copy-start.14 = (bf16[768,768]{1,0:T(8,128)(2,1)S(1)}, bf16[768,768]{1,0:T(8,128)(2,1)}, u32[]{:S(2)}) copy-start(bf16[768,768]{1,0:T(8,128)(2,1)} %reduce-scatter.20.cloned.1.call-done) | copy-start | bytes 3538948
  (13 other events, 20.2 us)
Sparse Core Ops, SparseCore 0:
  12.9 92.0 all-gather.4
  268.8 83.6 reduce-scatter.13
  358.6 89.9 all-gather.6
  509.9 83.6 reduce-scatter.15
  597.2 89.9 all-gather.8
  754.3 83.6 reduce-scatter.17
  846.9 89.9 all-gather.10
  942.6 33.4 reduce-scatter.27
  1344.4 38.7 reduce-scatter.25
  1385.4 85.2 reduce-scatter.19
  1475.2 77.6 reduce-scatter.23
  1557.2 76.4 reduce-scatter.21
where the time goes:
time: 1650 us; the launch traced here: 1640 us
  waiting for transfers between devices  751 us (46%)
  matrix products  401 us (24%)
  local copies, waits for them, and re-layouts  222 us (13%)
  other arithmetic  185 us (11%)
  blocking collectives  41.3 us (3%)
  loops' own time  24.5 us (1%)
    all_gather x1, waiting for transfers between devices, body(): normed_one = lax.all_gather(normed_one_rows, 'tensor', axis=0, tiled=True)  92.2 us
    all_gather x1, waiting for transfers between devices, body(): grad_eo = lax.all_gather(grad_eo_rows, 'tensor', axis=0, tiled=True)  90 us
    all_gather x1, waiting for transfers between devices, body(): grad_att = lax.all_gather(grad_att_rows, 'tensor', axis=0, tiled=True)  90 us
    dot_general x6, matrix products, back_block(): jnp.einsum('qhd,khd->hqk', grad_block, values_all, preferred_element_type...  88.5 us
    reduce_scatter x1, waiting for transfers between devices, body(): lax.psum_scatter(jnp.einsum('kth,kdh->td', grad_qkv, qkv_weight, preferre...  85.6 us
    reduce_scatter x1, waiting for transfers between devices, body(): lax.psum_scatter(returned[target].astype(jnp.bfloat16), 'tensor', scatter...  83.8 us
    reduce_scatter x1, waiting for transfers between devices, body(): lax.psum_scatter(back_moe[target].astype(jnp.bfloat16), 'tensor', scatter...  83.8 us
    convert_element_type x6, other arithmetic, back_block(): grad_scores = (prob_rows * (grad_probs - row_inner)).astype(jnp.bfloat16)  83.2 us
  transfers between devices with their start and end apart: 12, of which 11 were waited for; matrix products, arithmetic and copies ran while one was open for 28% of the time, Pallas kernels for 0%

commit v1 on v0

--- a/solution.py
+++ b/solution.py
@@ -1,6 +1,7 @@
 import jax
 import jax.numpy as jnp
 from jax import lax
+from jax.sharding import Mesh
 from jax.sharding import PartitionSpec as P
 
 HEAD_DIM = 64
@@ -61,6 +62,63 @@
     causal = key_pos[None, :] <= query_pos[:, None]
     shared = (segment[None, :] == 0) | (segment[None, :] == query_seg[:, None])
     return causal & shared
+
+
+def swap_roles(value):
+    moves = [(2 * c + h, 2 * h + c) for c in range(2) for h in range(2)]
+    return lax.ppermute(value, ("c", "zh"), moves)
+
+
+def flip(value, axis):
+    return lax.ppermute(value, axis, [(0, 1), (1, 0)])
+
+
+def gather_rows(rows):
+    count, width = rows.shape
+    core, near = lax.axis_index("c"), lax.axis_index("zl")
+    across = flip(rows, "zl")
+    beside = flip(rows, "c")
+    corner = flip(across, "c")
+    whole = jnp.zeros((4 * count, width), rows.dtype)
+    for block, c, z in (
+        (rows, core, near),
+        (beside, 1 - core, near),
+        (across, core, 1 - near),
+        (corner, 1 - core, 1 - near),
+    ):
+        whole = lax.dynamic_update_slice_in_dim(whole, block, (2 * c + z) * count, 0)
+    return whole
+
+
+def scatter_rows(partial):
+    count = partial.shape[0] // 4
+    core, near = lax.axis_index("c"), lax.axis_index("zl")
+
+    def block(c, z):
+        return lax.dynamic_slice_in_dim(partial, (2 * c + z) * count, count, 0)
+
+    far = flip(block(1 - core, 1 - near), "c").astype(jnp.float32)
+    far = (far + block(core, 1 - near).astype(jnp.float32)).astype(partial.dtype)
+    far = flip(far, "zl").astype(jnp.float32)
+    beside = flip(block(1 - core, near), "c").astype(jnp.float32)
+    return block(core, near).astype(jnp.float32) + beside + far
+
+
+def other_quarter(weight, after=None):
+    users = lax.axis_size("u") * lax.axis_size("c")
+    flat = weight.reshape(-1, weight.shape[-1])
+    part = flat.shape[0] // users
+    mine = lax.axis_index("u") * 2 + lax.axis_index("c")
+    piece = lax.dynamic_slice_in_dim(flat, mine * part, part, 0)
+    if after is not None:
+        piece, after = lax.optimization_barrier((piece, after))
+    piece = flip(piece, "zh")
+    return lax.all_gather(piece, ("u", "c"), axis=0, tiled=True).reshape(weight.shape)
+
+
+def pick_quarter(weight, after=None):
+    keep = lax.axis_index("c") == lax.axis_index("zh")
+    return jnp.where(keep, weight, other_quarter(weight, after))
 
 
 def body(
@@ -80,18 +138,25 @@
     row_count = block_input.shape[1]
     model_width = block_input.shape[2]
     experts = expert_up.shape[0]
-    segment = segments[0]
-    token_count = segment.shape[0]
+    token_count = segments.shape[1]
     capacity = 9 * token_count // (8 * experts)
     local_width = qkv_weight.shape[2]
     head_count = local_width // HEAD_DIM
     block_rows = min(512, token_count)
     score_scale = HEAD_DIM ** (-0.5)
-    own_start = lax.axis_index("tensor") * row_count
-    inputs = block_input[0].astype(jnp.float32)
+    own_start = (2 * lax.axis_index("c") + lax.axis_index("zl")) * row_count
+    held = swap_roles(block_input[0])
+    indices = swap_roles(jnp.stack([routes[0, :, 0], priority[0], segments[0]]))
+    segment = indices[2]
+    qkv_weight = pick_quarter(qkv_weight)
+    proj_weight = pick_quarter(proj_weight)
+    out_grad = swap_roles(out_grad[0])
+    expert_up = pick_quarter(expert_up, held)
+    expert_down = pick_quarter(expert_down, held)
+    inputs = held.astype(jnp.float32)
     unit_one, inverse_one = normalize_plain(inputs)
     normed_one_rows = (unit_one * attention_gain).astype(jnp.bfloat16)
-    normed_one = lax.all_gather(normed_one_rows, "tensor", axis=0, tiled=True)
+    normed_one = gather_rows(normed_one_rows)
     qkv_all = jnp.einsum(
         "td,kdh->kth", normed_one, qkv_weight, preferred_element_type=jnp.float32
     ).astype(jnp.bfloat16)
@@ -124,18 +189,13 @@
     offsets = jnp.arange(token_count // block_rows, dtype=jnp.int32) * block_rows
     context_blocks, log_totals = lax.map(attend, offsets)
     context = context_blocks.reshape(token_count, local_width)
-    attended = lax.psum_scatter(
-        jnp.dot(context, proj_weight, preferred_element_type=jnp.float32).astype(jnp.bfloat16),
-        "tensor",
-        scatter_dimension=0,
-        tiled=True,
-    ).astype(jnp.float32)
+    attended = scatter_rows(jnp.dot(context, proj_weight, preferred_element_type=jnp.float32).astype(jnp.bfloat16))
     mixed_one = inputs + attended
     unit_two, inverse_two = normalize_plain(mixed_one)
     normed_two_rows = (unit_two * moe_gain).astype(jnp.bfloat16)
-    normed_two = lax.all_gather(normed_two_rows, "tensor", axis=0, tiled=True)
+    normed_two = gather_rows(normed_two_rows)
     route_hot, kept_mask, target, slot_table = route_slots(
-        routes[0, :, 0], priority[0], experts, capacity
+        indices[0], indices[1], experts, capacity
     )
     zero_row = jnp.zeros((1, model_width), jnp.bfloat16)
     zero_float = jnp.zeros((1, model_width), jnp.float32)
@@ -148,9 +208,7 @@
         "ecf,efd->ecd", hidden, expert_down, preferred_element_type=jnp.float32
     ).reshape(experts * capacity, model_width)
     returned = jnp.concatenate([returned, zero_float], axis=0)
-    expert_out = lax.psum_scatter(
-        returned[target].astype(jnp.bfloat16), "tensor", scatter_dimension=0, tiled=True
-    ).astype(jnp.float32)
+    expert_out = scatter_rows(returned[target].astype(jnp.bfloat16))
     hot_rows = lax.dynamic_slice_in_dim(route_hot, own_start, row_count, 0)
     kept_rows = lax.dynamic_slice_in_dim(kept_mask, own_start, row_count, 0)
     centroid_rows = jnp.dot(
@@ -160,12 +218,12 @@
     gate_prob = jax.nn.sigmoid(jnp.sum(normed_two_float * centroid_rows, axis=-1))
     gate_used = jnp.where(kept_rows, gate_prob, 0.0)
     mixed_two = mixed_one + gate_used[:, None] * expert_out
-    block_output = mixed_two.astype(jnp.bfloat16)[None]
-    upstream = out_grad[0].astype(jnp.float32)
+    block_output = swap_roles(mixed_two.astype(jnp.bfloat16))[None]
+    upstream = out_grad.astype(jnp.float32)
     grad_eo_rows = (gate_used[:, None] * upstream).astype(jnp.bfloat16)
     grad_gate = jnp.where(kept_rows, jnp.sum(upstream * expert_out, axis=-1), 0.0)
     grad_score = grad_gate * gate_prob * (1.0 - gate_prob)
-    grad_eo = lax.all_gather(grad_eo_rows, "tensor", axis=0, tiled=True)
+    grad_eo = gather_rows(grad_eo_rows)
     grad_dispatched = jnp.concatenate([grad_eo, zero_row], axis=0)[slot_table].reshape(
         experts, capacity, model_width
     )
@@ -185,9 +243,7 @@
     ).reshape(experts * capacity, model_width)
     back_moe = jnp.concatenate([back_moe, zero_float], axis=0)
     grad_two = (
-        lax.psum_scatter(
-            back_moe[target].astype(jnp.bfloat16), "tensor", scatter_dimension=0, tiled=True
-        ).astype(jnp.float32)
+        scatter_rows(back_moe[target].astype(jnp.bfloat16))
         + grad_score[:, None] * centroid_rows
     )
     centroid_part = jnp.einsum(
@@ -199,7 +255,7 @@
     moe_gain_part = jnp.sum(grad_two * unit_two, axis=0)
     grad_mixed = upstream + normalize_back(grad_two, unit_two, inverse_two, moe_gain)
     grad_att_rows = grad_mixed.astype(jnp.bfloat16)
-    grad_att = lax.all_gather(grad_att_rows, "tensor", axis=0, tiled=True)
+    grad_att = gather_rows(grad_att_rows)
     proj_part = jnp.einsum("tc,td->cd", context, grad_att, preferred_element_type=jnp.float32)
     grad_context = jnp.einsum(
         "td,cd->tc", grad_att, proj_weight, preferred_element_type=jnp.float32
@@ -246,28 +302,33 @@
         ]
     )
     qkv_part = jnp.einsum("td,kth->kdh", normed_one, grad_qkv, preferred_element_type=jnp.float32)
-    grad_one = lax.psum_scatter(
-        jnp.einsum("kth,kdh->td", grad_qkv, qkv_weight, preferred_element_type=jnp.float32).astype(
+    grad_one = scatter_rows(jnp.einsum("kth,kdh->td", grad_qkv, qkv_weight, preferred_element_type=jnp.float32).astype(
             jnp.bfloat16
-        ),
-        "tensor",
-        scatter_dimension=0,
-        tiled=True,
-    ).astype(jnp.float32)
+        ))
     attention_gain_part = jnp.sum(grad_one * unit_one, axis=0)
-    input_grad = (
-        grad_mixed + normalize_back(grad_one, unit_one, inverse_one, attention_gain)
-    ).astype(jnp.bfloat16)[None]
+    input_grad = swap_roles(
+        (grad_mixed + normalize_back(grad_one, unit_one, inverse_one, attention_gain)).astype(
+            jnp.bfloat16
+        )
+    )[None]
+    everyone = ("u", "c", "zh", "zl")
     gain_one_sum, gain_two_sum, centroid_sum = (
-        lax.psum_scatter(attention_gain_part, ("dp", "tensor"), scatter_dimension=0, tiled=True),
-        lax.psum_scatter(moe_gain_part, ("dp", "tensor"), scatter_dimension=0, tiled=True),
-        lax.psum_scatter(centroid_part, ("dp", "tensor"), scatter_dimension=1, tiled=True),
-    )
+        lax.psum_scatter(attention_gain_part, everyone, scatter_dimension=0, tiled=True),
+        lax.psum_scatter(moe_gain_part, everyone, scatter_dimension=0, tiled=True),
+        lax.psum_scatter(centroid_part, everyone, scatter_dimension=1, tiled=True),
+    )
+
+    def summed(part, dimension):
+        part = lax.psum_scatter(
+            part.astype(jnp.bfloat16), ("u", "zh"), scatter_dimension=dimension, tiled=True
+        )
+        return swap_roles(part).astype(jnp.float32)
+
     qkv_summed, proj_summed, up_summed, down_summed = (
-        lax.psum_scatter(qkv_part, "dp", scatter_dimension=1, tiled=True),
-        lax.psum_scatter(proj_part, "dp", scatter_dimension=1, tiled=True),
-        lax.psum_scatter(up_part, "dp", scatter_dimension=1, tiled=True),
-        lax.psum_scatter(down_part, "dp", scatter_dimension=2, tiled=True),
+        summed(qkv_part, 1),
+        summed(proj_part, 1),
+        summed(up_part, 1),
+        summed(down_part, 2),
     )
     return (
         block_output,
@@ -283,33 +344,37 @@
 
 
 def solution(mesh):
+    shape = mesh.devices.shape
+    bits = (shape[0] // 2, 2, shape[1] // 2, 2)
+    dp, tensor = ("u", "c"), ("zh", "zl")
+    mesh = Mesh(mesh.devices.reshape(bits), dp + tensor)
     return jax.shard_map(
         body,
         mesh=mesh,
         in_specs=(
-            P("dp", "tensor", None),
+            P(dp, tensor, None),
             P(),
-            P(None, None, "tensor"),
-            P("tensor", None),
+            P(None, None, tensor),
+            P(tensor, None),
             P(),
             P(),
-            P(None, None, "tensor"),
-            P(None, "tensor", None),
-            P("dp", "tensor", None),
-            P("dp", None, None),
-            P("dp", None),
-            P("dp", None),
+            P(None, None, tensor),
+            P(None, tensor, None),
+            P(dp, tensor, None),
+            P(dp, None, None),
+            P(dp, None),
+            P(dp, None),
         ),
         out_specs=(
-            P("dp", "tensor", None),
-            P("dp", "tensor", None),
-            P(("dp", "tensor")),
-            P(("dp", "tensor")),
-            P(None, ("dp", "tensor")),
-            P(None, "dp", "tensor"),
-            P("tensor", "dp"),
-            P(None, "dp", "tensor"),
-            P(None, "tensor", "dp"),
+            P(dp, tensor, None),
+            P(dp, tensor, None),
+            P(dp + tensor),
+            P(dp + tensor),
+            P(None, dp + tensor),
+            P(None, dp, tensor),
+            P(tensor, dp),
+            P(None, dp, tensor),
+            P(None, tensor, dp),
         ),
         check_vma=False,
     )

time: 1650 us -> 1280 us (0.78)
  waiting for transfers between devices: 751 us -> 254 us
  starting transfers between devices: 0.5 us -> 84.9 us
  blocking collectives: 41.3 us -> 64.2 us
  local copies, waits for them, and re-layouts: 222 us -> 244 us
    reduce_scatter x6 -> x2, waiting for transfers between devices: 448 us -> 0.02 us  [summed(): lax.psum_scatter(part.astype(jnp.bfloat16), ('u', 'zh'), scatter_dimensio...]
    all_gather x4 -> x2, waiting for transfers between devices: 301 us -> 0.01 us  [other_quarter(): lax.all_gather(piece, ('u', 'c'), axis=0, tiled=True).reshape(weight.shape)]
    ppermute x0 -> x37, waiting for transfers between devices: none -> 195 us  [the longest x28 195 us: flip(): return lax.ppermute(value, axis, [(0, 1), (1, 0)])]
    ppermute x0 -> x37, starting transfers between devices: none -> 83.8 us  [the longest x28 59.7 us: flip(): return lax.ppermute(value, axis, [(0, 1), (1, 0)])]
    unnamed x14 -> x8, waiting for transfers between devices: 1.16 us -> 58.9 us
    all_gather x0 -> x2, blocking collectives: none -> 22.3 us  [other_quarter(): lax.all_gather(piece, ('u', 'c'), axis=0, tiled=True).reshape(weight.shape)]
    while x24 -> x12, local copies, waits for them, and re-layouts: 38.8 us -> 39 us
  transfers between devices with their start and end apart: 12 -> 43, of which waited for: 11 -> 11; matrix products, arithmetic and copies ran while one was open for 28% -> 56% of each run, Pallas kernels for 0% -> 0%
where the time goes in v1:
time: 1280 us; the launch traced here: 1270 us
  matrix products  396 us (31%)
  waiting for transfers between devices  254 us (20%)
  local copies, waits for them, and re-layouts  244 us (19%)
  other arithmetic  187 us (15%)
  starting transfers between devices  84.9 us (7%)
  blocking collectives  64.2 us (5%)
  loops' own time  24.1 us (2%)
  between operations  15.6 us (1%)
    ppermute x28, waiting for transfers between devices, flip(): return lax.ppermute(value, axis, [(0, 1), (1, 0)])  195 us
    dot_general x6, matrix products, back_block(): jnp.einsum('qhd,khd->hqk', grad_block, values_all, preferred_element_type...  88.5 us
    convert_element_type x6, other arithmetic, back_block(): grad_scores = (prob_rows * (grad_probs - row_inner)).astype(jnp.bfloat16)  83.2 us
    ppermute x28, starting transfers between devices, flip(): return lax.ppermute(value, axis, [(0, 1), (1, 0)])  59.7 us
    unnamed x8, waiting for transfers between devices  58.9 us
    dot_general x12, matrix products, masked_scores(): jnp.einsum('qhd,khd->hqk', query_block, keys_all, preferred_element_type=...  56.8 us
    dot_general x6, matrix products, back_block(): jnp.einsum('hqk,qhd->khd', prob_low, grad_block, preferred_element_type=j...  52.5 us
    dot_general x6, matrix products, attend(): jnp.einsum('hqk,khd->qhd', prob_rows, values_all, preferred_element_type=...  44.9 us
  transfers between devices with their start and end apart: 43, of which 11 were waited for; matrix products, arithmetic and copies ran while one was open for 56% of the time, Pallas kernels for 0%

profile of v1, /device:TPU:0, one launch (start us, length us, event | category | flops | bytes accessed | tf_op | source)
XLA Modules:
  0.0 1268.4 jit_solution(12411178366212257825)
XLA Ops:
  18.0 31.9 %collective-permute-start.6 = (bf16[24,768]{1,0:T(8,128)(2,1)S(1)}, bf16[24,768]{1,0:T(8,128)(2,1)S(1)}, u32[]{:S(2)}, u32[]{:S(2)}) collective-permute-start(bf16[24,768]{1,0:T(8,128)(2,1)S(1)} %constant_dynamic-slice_fusion.10), channel_id=1, source_target_pairs={{0,2},{2,0},{1,3},{3,1},{4,6},{6,4},{5,7},{7,5},{8,10},{10,8},{9,1... | collective-permute-start | bytes 110600 | tf_op jit(solution)/shard_map/ppermute | solution.py:73
  54.4 10.7 collective-permute-start.13
  65.8 10.5 all_gather.13
  76.4 11.8 all_gather.12
  109.7 146.5 %while.27 = (s32[]{:T(128)}, bf16[6,512,3,64]{1,3,2,0:T(8,128)(2,1)}, f32[6,3,512]{2,1,0:T(4,128)}, s32[6]{0:T(128)S(1)}, s32[1,3072]{1,0:T(1,128)S(1)}, /*index...) while((s32[]{:T(128)}, ...), condition=%wide.region_5.6_spmd, body=%wide.region_2.5_spmd.sunk | while | flops 1270974464 | bytes 65759424 | solution.py:190
  174.9 7.5 fusion.149
  270.1 25.8 %collective-permute-done.9 = bf16[768,768]{1,0:T(8,128)(2,1)S(1)} collective-permute-done((bf16[768,768]{1,0:T(8,128)(2,1)S(1)}, bf16[768,768]{1,0:T(8,128)(2,1)S(1)}, u32[]{:S(2)}, u32[]{:S(2)}) %collective-permute-start.9) | collective-permute-done | bytes 1179680 | tf_op jit(solution)/shard_map/ppermute | solution.py:73
  302.8 11.8 scatter_custom_fusion
  314.6 8.1 gather_fusion
  328.6 17.4 %gather_fusion.1 = s32[3072]{0:T(1024)S(1)} fusion(s32[3072]{0:T(1024)S(1)} %fusion.78, s32[3072]{0:T(1024)S(1)} %broadcast_clamp_fusion.1), kind=kCustom, calls=%fused_computation.1 | custom fusion | bytes 36864 | tf_op jit(solution)/shard_map/gather | solution.py:47
  346.6 12.3 scatter_custom_fusion.1
  364.8 16.8 %gather_fusion.2 = bf16[3456,768]{1,0:T(8,128)(2,1)} fusion(bf16[3073,768]{1,0:T(8,128)(2,1)} %concatenate.12, s32[4096]{0:T(1024)S(1)} %pad_clamp_fusion), kind=kCustom, calls=%fused_computation.2 | custom fusion | bytes 10630656 | tf_op jit(solution)/shard_map/gather | solution.py:202
  381.6 12.3 fusion.75
  393.9 9.5 fusion.77
  406.1 17.9 %gather_fusion.3 = bf16[3072,768]{1,0:T(8,128)(2,1)} fusion(bf16[3457,768]{1,0:T(8,128)(2,1)} %concatenate.13, s32[3072]{0:T(1024)S(1)} %broadcast_clamp_fusion), kind=kCustom, calls=%fused_computation.3 | custom fusion | bytes 9449472 | tf_op jit(solution)/shard_map/gather | solution.py:211
  431.4 38.5 %collective-permute-done.17 = bf16[768,768]{1,0:T(8,128)(2,1)S(1)} collective-permute-done((bf16[768,768]{1,0:T(8,128)(2,1)S(1)}, bf16[768,768]{1,0:T(8,128)(2,1)S(1)}, u32[]{:S(2)}, u32[]{:S(2)}) %collective-permute-start.17) | collective-permute-done | bytes 1179680 | tf_op jit(solution)/shard_map/ppermute | solution.py:73
  472.4 27.0 %collective-permute-done.21 = bf16[768,768]{1,0:T(8,128)(2,1)S(1)} collective-permute-done((bf16[768,768]{1,0:T(8,128)(2,1)S(1)}, bf16[768,768]{1,0:T(8,128)(2,1)S(1)}, u32[]{:S(2)}, u32[]{:S(2)}) %collective-permute-start.21) | collective-permute-done | bytes 1179680 | tf_op jit(solution)/shard_map/ppermute | solution.py:73
  504.9 16.8 %gather_fusion.4 = bf16[3456,768]{1,0:T(8,128)(2,1)} fusion(bf16[3073,768]{1,0:T(8,128)(2,1)} %concatenate.14, s32[4096]{0:T(1024)S(1)} %pad_clamp_fusion), kind=kCustom, calls=%fused_computation.4 | custom fusion | bytes 10630656 | tf_op jit(solution)/shard_map/gather | solution.py:227
  521.7 12.5 convolution_convert_fusion.2
  534.6 18.7 %fusion.43 = bf16[4,864,768]{2,1,0:T(8,128)(2,1)} fusion(f32[4,864,768]{2,1,0:T(8,128)} %fusion.75, bf16[4,864,768]{2,1,0:T(8,128)(2,1)} %bitcast.175, bf16[4,768,768]{2,1,0:T(8,128)(2,1)} %param.23, bf16[4,768,768]{2,1,0:T(8,128)(2,1)} %bitcast.203, pred[]{:T(512)S(6)} %eq.75), kind=kOutput, calls=%fused_computation.66 | convolution fusion | flops 4142923776 | bytes 30670848 | tf_op jit(solution)/shard_map/ecd,efd->ecf/dot_general | solution.py:230
  553.3 8.2 fusion.74
  564.3 18.8 %gather_fusion.5 = bf16[3072,768]{1,0:T(8,128)(2,1)} fusion(bf16[3457,768]{1,0:T(8,128)(2,1)} %concatenate.15, s32[3072]{0:T(1024)} %copy-done.33), kind=kCustom, calls=%fused_computation.5 | custom fusion | bytes 9449472 | tf_op jit(solution)/shard_map/gather | solution.py:246
  589.7 38.6 %collective-permute-done.25 = bf16[768,768]{1,0:T(8,128)(2,1)S(1)} collective-permute-done((bf16[768,768]{1,0:T(8,128)(2,1)S(1)}, bf16[768,768]{1,0:T(8,128)(2,1)S(1)}, u32[]{:S(2)}, u32[]{:S(2)}) %collective-permute-start.25) | collective-permute-done | bytes 1179680 | tf_op jit(solution)/shard_map/ppermute | solution.py:73
  638.0 27.4 %collective-permute-done.27 = bf16[768,768]{1,0:T(8,128)(2,1)S(1)} collective-permute-done((bf16[768,768]{1,0:T(8,128)(2,1)S(1)}, bf16[768,768]{1,0:T(8,128)(2,1)S(1)}, u32[]{:S(2)}, u32[]{:S(2)}) %collective-permute-start.27) | collective-permute-done | bytes 1179680 | tf_op jit(solution)/shard_map/ppermute | solution.py:73
  665.4 10.0 convolution_convert_fusion.3
  686.7 374.1 %while.28 = (s32[]{:T(128)}, f32[3072,3,64]{0,2,1:T(8,128)}, f32[3072,3,64]{0,2,1:T(8,128)}, bf16[6,512,3,64]{1,3,2,0:T(8,128)(2,1)}, s32[6]{0:T(128)S(1)}, /*in...) while((s32[]{:T(128)}, f32[3072,3,64]{0,2,1:T(8,128)}, ...), condition=%wide.region_19.20_spmd.clone, body=%wide.region_17.19_spmd.clone.sunk | while | flops 3100116992 | bytes 237390064 | solution.py:294
  703.4 8.0 fusion.162
  711.4 15.0 %multiply_reduce_fusion.7 = (f32[3,512]{1,0:T(4,128)S(1)}, f32[3,512,3072]{2,1,0:T(8,128)}) fusion(f32[3,512,3072]{2,1,0:T(8,128)} %copy-done.2, f32[3,512]{1,0:T(4,128)S(1)} %dynamic-slice_bitcast_fusion.2, pred[512,3072]{1,0:T(8,128)(4,1)S(1)} %fusion.160, bf16[3072,3,64]{0,2,1:T(8,128)(2,1)} %get-tuple-element.495, ...), kind=kOutput, calls=%fused_computation.28.clone.1 | convolution fusion | flops 627571200 | bytes 40710148 | tf_op jit(solution)/shard_map/while/body/eval_jaxpr/qhd,khd->hqk/dot_general | solution.py:272
  726.4 13.9 %multiply_convert_fusion.7 = bf16[3,512,3072]{2,1,0:T(8,128)(2,1)S(1)} fusion(f32[3,512,3072]{2,1,0:T(8,128)} %get-tuple-element.416, f32[3,512,3072]{2,1,0:T(8,128)} %copy-done.2, f32[3,512]{1,0:T(4,128)S(1)} %get-tuple-element.417, f32[3,512]{1,0:T(4,128)S(1)} %dynamic-slice_bitcast_fusion.2, pred[512,3072]{1,0:T(8,128)(4,1)S(1)} %fusion.160), kind=kLoop, calls=%fused_computation.27.clone.1 | loop fusion | flops 28311552 | bytes 48771072 | tf_op jit(solution)/shard_map/while/body/eval_jaxpr/convert_element_type | solution.py:276
  764.4 8.9 fusion.162
  773.3 14.7 %multiply_reduce_fusion.7 = (f32[3,512]{1,0:T(4,128)S(1)}, f32[3,512,3072]{2,1,0:T(8,128)}) fusion(f32[3,512,3072]{2,1,0:T(8,128)} %copy-done.2, f32[3,512]{1,0:T(4,128)S(1)} %dynamic-slice_bitcast_fusion.2, pred[512,3072]{1,0:T(8,128)(4,1)S(1)} %fusion.160, bf16[3072,3,64]{0,2,1:T(8,128)(2,1)} %get-tuple-element.495, ...), kind=kOutput, calls=%fused_computation.28.clone.1 | convolution fusion | flops 627571200 | bytes 40710148 | tf_op jit(solution)/shard_map/while/body/eval_jaxpr/qhd,khd->hqk/dot_general | solution.py:272
  788.0 13.9 %multiply_convert_fusion.7 = bf16[3,512,3072]{2,1,0:T(8,128)(2,1)S(1)} fusion(f32[3,512,3072]{2,1,0:T(8,128)} %get-tuple-element.416, f32[3,512,3072]{2,1,0:T(8,128)} %copy-done.2, f32[3,512]{1,0:T(4,128)S(1)} %get-tuple-element.417, f32[3,512]{1,0:T(4,128)S(1)} %dynamic-slice_bitcast_fusion.2, pred[512,3072]{1,0:T(8,128)(4,1)S(1)} %fusion.160), kind=kLoop, calls=%fused_computation.27.clone.1 | loop fusion | flops 28311552 | bytes 48771072 | tf_op jit(solution)/shard_map/while/body/eval_jaxpr/convert_element_type | solution.py:276
  826.9 8.9 fusion.162
  835.8 14.7 %multiply_reduce_fusion.7 = (f32[3,512]{1,0:T(4,128)S(1)}, f32[3,512,3072]{2,1,0:T(8,128)}) fusion(f32[3,512,3072]{2,1,0:T(8,128)} %copy-done.2, f32[3,512]{1,0:T(4,128)S(1)} %dynamic-slice_bitcast_fusion.2, pred[512,3072]{1,0:T(8,128)(4,1)S(1)} %fusion.160, bf16[3072,3,64]{0,2,1:T(8,128)(2,1)} %get-tuple-element.495, ...), kind=kOutput, calls=%fused_computation.28.clone.1 | convolution fusion | flops 627571200 | bytes 40710148 | tf_op jit(solution)/shard_map/while/body/eval_jaxpr/qhd,khd->hqk/dot_general | solution.py:272
  850.5 13.9 %multiply_convert_fusion.7 = bf16[3,512,3072]{2,1,0:T(8,128)(2,1)S(1)} fusion(f32[3,512,3072]{2,1,0:T(8,128)} %get-tuple-element.416, f32[3,512,3072]{2,1,0:T(8,128)} %copy-done.2, f32[3,512]{1,0:T(4,128)S(1)} %get-tuple-element.417, f32[3,512]{1,0:T(4,128)S(1)} %dynamic-slice_bitcast_fusion.2, pred[512,3072]{1,0:T(8,128)(4,1)S(1)} %fusion.160), kind=kLoop, calls=%fused_computation.27.clone.1 | loop fusion | flops 28311552 | bytes 48771072 | tf_op jit(solution)/shard_map/while/body/eval_jaxpr/convert_element_type | solution.py:276
  889.4 8.9 fusion.162
  898.3 14.7 %multiply_reduce_fusion.7 = (f32[3,512]{1,0:T(4,128)S(1)}, f32[3,512,3072]{2,1,0:T(8,128)}) fusion(f32[3,512,3072]{2,1,0:T(8,128)} %copy-done.2, f32[3,512]{1,0:T(4,128)S(1)} %dynamic-slice_bitcast_fusion.2, pred[512,3072]{1,0:T(8,128)(4,1)S(1)} %fusion.160, bf16[3072,3,64]{0,2,1:T(8,128)(2,1)} %get-tuple-element.495, ...), kind=kOutput, calls=%fused_computation.28.clone.1 | convolution fusion | flops 627571200 | bytes 40710148 | tf_op jit(solution)/shard_map/while/body/eval_jaxpr/qhd,khd->hqk/dot_general | solution.py:272
  913.0 13.9 %multiply_convert_fusion.7 = bf16[3,512,3072]{2,1,0:T(8,128)(2,1)S(1)} fusion(f32[3,512,3072]{2,1,0:T(8,128)} %get-tuple-element.416, f32[3,512,3072]{2,1,0:T(8,128)} %copy-done.2, f32[3,512]{1,0:T(4,128)S(1)} %get-tuple-element.417, f32[3,512]{1,0:T(4,128)S(1)} %dynamic-slice_bitcast_fusion.2, pred[512,3072]{1,0:T(8,128)(4,1)S(1)} %fusion.160), kind=kLoop, calls=%fused_computation.27.clone.1 | loop fusion | flops 28311552 | bytes 48771072 | tf_op jit(solution)/shard_map/while/body/eval_jaxpr/convert_element_type | solution.py:276
  951.9 8.9 fusion.162
  960.8 14.7 %multiply_reduce_fusion.7 = (f32[3,512]{1,0:T(4,128)S(1)}, f32[3,512,3072]{2,1,0:T(8,128)}) fusion(f32[3,512,3072]{2,1,0:T(8,128)} %copy-done.2, f32[3,512]{1,0:T(4,128)S(1)} %dynamic-slice_bitcast_fusion.2, pred[512,3072]{1,0:T(8,128)(4,1)S(1)} %fusion.160, bf16[3072,3,64]{0,2,1:T(8,128)(2,1)} %get-tuple-element.495, ...), kind=kOutput, calls=%fused_computation.28.clone.1 | convolution fusion | flops 627571200 | bytes 40710148 | tf_op jit(solution)/shard_map/while/body/eval_jaxpr/qhd,khd->hqk/dot_general | solution.py:272
  975.5 13.9 %multiply_convert_fusion.7 = bf16[3,512,3072]{2,1,0:T(8,128)(2,1)S(1)} fusion(f32[3,512,3072]{2,1,0:T(8,128)} %get-tuple-element.416, f32[3,512,3072]{2,1,0:T(8,128)} %copy-done.2, f32[3,512]{1,0:T(4,128)S(1)} %get-tuple-element.417, f32[3,512]{1,0:T(4,128)S(1)} %dynamic-slice_bitcast_fusion.2, pred[512,3072]{1,0:T(8,128)(4,1)S(1)} %fusion.160), kind=kLoop, calls=%fused_computation.27.clone.1 | loop fusion | flops 28311552 | bytes 48771072 | tf_op jit(solution)/shard_map/while/body/eval_jaxpr/convert_element_type | solution.py:276
  1014.4 8.9 fusion.162
  1023.3 14.7 %multiply_reduce_fusion.7 = (f32[3,512]{1,0:T(4,128)S(1)}, f32[3,512,3072]{2,1,0:T(8,128)}) fusion(f32[3,512,3072]{2,1,0:T(8,128)} %copy-done.2, f32[3,512]{1,0:T(4,128)S(1)} %dynamic-slice_bitcast_fusion.2, pred[512,3072]{1,0:T(8,128)(4,1)S(1)} %fusion.160, bf16[3072,3,64]{0,2,1:T(8,128)(2,1)} %get-tuple-element.495, ...), kind=kOutput, calls=%fused_computation.28.clone.1 | convolution fusion | flops 627571200 | bytes 40710148 | tf_op jit(solution)/shard_map/while/body/eval_jaxpr/qhd,khd->hqk/dot_general | solution.py:272
  1038.0 13.9 %multiply_convert_fusion.7 = bf16[3,512,3072]{2,1,0:T(8,128)(2,1)S(1)} fusion(f32[3,512,3072]{2,1,0:T(8,128)} %get-tuple-element.416, f32[3,512,3072]{2,1,0:T(8,128)} %copy-done.2, f32[3,512]{1,0:T(4,128)S(1)} %get-tuple-element.417, f32[3,512]{1,0:T(4,128)S(1)} %dynamic-slice_bitcast_fusion.2, pred[512,3072]{1,0:T(8,128)(4,1)S(1)} %fusion.160), kind=kLoop, calls=%fused_computation.27.clone.1 | loop fusion | flops 28311552 | bytes 48771072 | tf_op jit(solution)/shard_map/while/body/eval_jaxpr/convert_element_type | solution.py:276
  1073.8 10.5 collective-permute-start.18
  1100.6 28.4 %collective-permute-done.31 = bf16[768,768]{1,0:T(8,128)(2,1)} collective-permute-done((bf16[768,768]{1,0:T(8,128)(2,1)}, bf16[768,768]{1,0:T(8,128)(2,1)}, u32[]{:S(2)}, u32[]{:S(2)}) %collective-permute-start.31) | collective-permute-done | bytes 1179680 | tf_op jit(solution)/shard_map/ppermute | solution.py:73
  1145.3 58.8 %reduce-scatter.14.cloned.1.call-done = bf16[96,576]{1,0:T(8,128)(2,1)} async-done(((bf16[768,576]{1,0:T(8,128)(2,1)}), bf16[96,576]{1,0:T(8,128)(2,1)}) %reduce-scatter.14.cloned.1.call-update) | async-done | bytes 110608
  1210.7 41.9 %all-reduce.7 = (f32[768]{0:T(1024)S(1)}, f32[768]{0:T(1024)S(1)}, f32[4,768]{1,0:T(4,128)S(1)}) all-reduce(f32[768]{0:T(1024)S(1)} %get-tuple-element.196, f32[768]{0:T(1024)S(1)} %copy-done.50, f32[4,768]{1,0:T(4,128)S(1)} %fusion.71), channel_id=2, replica_groups=mesh['u'=4,'c'=2,'zh'=2,'zl'=2] {'u','c','zh','zl'}, use_global_device_ids=true, to_apply=%region_23.24.clone | all-reduce | flops 4608 | bytes 36864
  (430 shorter events, 444.0 us)
Async XLA Ops:
  7.2 291.1 %copy-start = (bf16[4,768]{1,0:T(4,128)(2,1)S(1)}, bf16[4,768]{1,0:T(4,128)(2,1)}, u32[]{:S(2)}) copy-start(bf16[4,768]{1,0:T(4,128)(2,1)} %param.21) | copy-start | bytes 18436
  7.2 374.4 %all-gather.3.cloned.1.call-start = ((), (), s32[]{:S(2)}) async-start(), calls=%async_computation.4 | async-start | bytes 5308416 | tf_op jit(solution)/shard_map/all_gather | solution.py:116
  7.2 1.9 collective-permute-start
  14.2 51.0 %collective-permute-start.4 = (bf16[768,768]{1,0:T(8,128)(2,1)}, bf16[768,768]{1,0:T(8,128)(2,1)}, u32[]{:S(2)}, u32[]{:S(2)}) collective-permute-start(bf16[768,768]{1,0:T(8,128)(2,1)} %get-tuple-element.260), channel_id=1, source_target_pairs={{0,1},{1,0},{2,3},{3,2},{4,5},{5,4},{6,7},{7,6},{8,9},{9,8},{10,11... | collective-permute-start | bytes 3538952 | tf_op jit(solution)/shard_map/ppermute | solution.py:73
  18.0 47.8 %collective-permute-start.6 = (bf16[24,768]{1,0:T(8,128)(2,1)S(1)}, bf16[24,768]{1,0:T(8,128)(2,1)S(1)}, u32[]{:S(2)}, u32[]{:S(2)}) collective-permute-start(bf16[24,768]{1,0:T(8,128)(2,1)S(1)} %constant_dynamic-slice_fusion.10), channel_id=1, source_target_pairs={{0,2},{2,0},{1,3},{3,1},{4,6},{6,4},{5,7},{7,5},{8,10},{10,8},{9,1... | collective-permute-start | bytes 110600 | tf_op jit(solution)/shard_map/ppermute | solution.py:73
  49.9 4.5 collective-permute-start.1
  50.8 25.5 %collective-permute-start.2 = (bf16[288,192]{0,1:T(8,128)(2,1)S(1)}, bf16[288,192]{0,1:T(8,128)(2,1)S(1)}, u32[]{:S(2)}, u32[]{:S(2)}) collective-permute-start(bf16[288,192]{0,1:T(8,128)(2,1)S(1)} %constant_dynamic-slice_fusion.11), channel_id=1, source_target_pairs={{0,2},{2,0},{1,3},{3,1},{4,6},{6,4},{5,7},{7,5},{8,10},{10,8},{9,1... | collective-permute-start | bytes 331784 | tf_op jit(solution)/shard_map/ppermute | solution.py:73
  54.3 39.5 %collective-permute-start.3 = (bf16[768,768]{1,0:T(8,128)(2,1)}, bf16[768,768]{1,0:T(8,128)(2,1)}, u32[]{:S(2)}, u32[]{:S(2)}) collective-permute-start(bf16[768,768]{1,0:T(8,128)(2,1)} %get-tuple-element.260), channel_id=1, source_target_pairs={{0,4},{4,0},{1,5},{5,1},{2,6},{6,2},{3,7},{7,3},{8,12},{12,8},{9,1... | collective-permute-start | bytes 3538952 | tf_op jit(solution)/shard_map/ppermute | solution.py:73
  54.4 39.1 %collective-permute-start.13 = (bf16[384,768]{1,0:T(8,128)(2,1)S(1)}, bf16[384,768]{1,0:T(8,128)(2,1)}, u32[]{:S(2)}, u32[]{:S(2)}) collective-permute-start(bf16[384,768]{1,0:T(8,128)(2,1)S(1)} %get-tuple-element.124), channel_id=1, source_target_pairs={{0,2},{2,0},{1,3},{3,1},{4,6},{6,4},{5,7},{7,5},{8,10},{10,8},{9,1... | collective-permute-start | bytes 1769480 | tf_op jit(solution)/shard_map/ppermute | solution.py:73
  65.2 33.4 %collective-permute-start.5 = (bf16[768,768]{1,0:T(8,128)(2,1)}, bf16[768,768]{1,0:T(8,128)(2,1)}, u32[]{:S(2)}, u32[]{:S(2)}) collective-permute-start(bf16[768,768]{1,0:T(8,128)(2,1)} %collective-permute-done.4), channel_id=1, source_target_pairs={{0,4},{4,0},{1,5},{5,1},{2,6},{6,2},{3,7},{7,3},{8,12},{12,8},{9,1... | collective-permute-start | bytes 3538952 | tf_op jit(solution)/shard_map/ppermute | solution.py:73
  91.5 171.0 %collective-permute-start.14 = (bf16[384,768]{1,0:T(8,128)(2,1)}, bf16[384,768]{1,0:T(8,128)(2,1)}, u32[]{:S(2)}, u32[]{:S(2)}) collective-permute-start(bf16[384,768]{1,0:T(8,128)(2,1)} %get-tuple-element.125), channel_id=1, source_target_pairs={{0,2},{2,0},{1,3},{3,1},{4,6},{6,4},{5,7},{7,5},{8,10},{10,8},{9,1... | collective-permute-start | bytes 1769480 | tf_op jit(solution)/shard_map/ppermute | solution.py:73
  93.5 300.3 %all-gather.5.cloned.1.call-start = ((), (), s32[]{:S(2)}) async-start(), calls=%async_computation.5 | async-start | bytes 5308416 | tf_op jit(solution)/shard_map/all_gather | solution.py:116
  262.3 3.0 collective-permute-start.8
  262.4 873.6 %reduce-scatter.12.cloned.1.call-start = ((), (), s32[]{:S(2)}) async-start(), calls=%async_computation.7 | async-start | bytes 5308416 | tf_op jit(solution)/shard_map/reduce_scatter | solution.py:322
  262.8 7.3 collective-permute-start.7
  267.2 28.7 %collective-permute-start.9 = (bf16[768,768]{1,0:T(8,128)(2,1)S(1)}, bf16[768,768]{1,0:T(8,128)(2,1)S(1)}, u32[]{:S(2)}, u32[]{:S(2)}) collective-permute-start(bf16[768,768]{1,0:T(8,128)(2,1)S(1)} %add_convert_fusion.4), channel_id=1, source_target_pairs={{0,1},{1,0},{2,3},{3,2},{4,5},{5,4},{6,7},{7,6},{8,9},{9,8},{10,11... | collective-permute-start | bytes 3538952 | tf_op jit(solution)/shard_map/ppermute | solution.py:73
  300.9 45.1 %collective-permute-start.11 = (bf16[768,768]{1,0:T(8,128)(2,1)}, bf16[768,768]{1,0:T(8,128)(2,1)}, u32[]{:S(2)}, u32[]{:S(2)}) collective-permute-start(bf16[768,768]{1,0:T(8,128)(2,1)} %get-tuple-element.256), channel_id=1, source_target_pairs={{0,1},{1,0},{2,3},{3,2},{4,5},{5,4},{6,7},{7,6},{8,9},{9,8},{10,11... | collective-permute-start | bytes 3538952 | tf_op jit(solution)/shard_map/ppermute | solution.py:73
  346.0 14.6 %collective-permute-start.10 = (bf16[768,768]{1,0:T(8,128)(2,1)}, bf16[768,768]{1,0:T(8,128)(2,1)S(1)}, u32[]{:S(2)}, u32[]{:S(2)}) collective-permute-start(bf16[768,768]{1,0:T(8,128)(2,1)} %get-tuple-element.256), channel_id=1, source_target_pairs={{0,4},{4,0},{1,5},{5,1},{2,6},{6,2},{3,7},{7,3},{8,12},{12,8},{9,1... | collective-permute-start | bytes 3538952 | tf_op jit(solution)/shard_map/ppermute | solution.py:73
  346.1 16.1 %collective-permute-start.12 = (bf16[768,768]{1,0:T(8,128)(2,1)}, bf16[768,768]{1,0:T(8,128)(2,1)S(1)}, u32[]{:S(2)}, u32[]{:S(2)}) collective-permute-start(bf16[768,768]{1,0:T(8,128)(2,1)} %collective-permute-done.11), channel_id=1, source_target_pairs={{0,4},{4,0},{1,5},{5,1},{2,6},{6,2},{3,7},{7,3},{8,12},{12,8},{9,1... | collective-permute-start | bytes 3538952 | tf_op jit(solution)/shard_map/ppermute | solution.py:73
  425.9 3.0 collective-permute-start.16
  426.1 3.6 collective-permute-start.19
  427.1 4.3 collective-permute-start.15
  429.3 40.6 %collective-permute-start.17 = (bf16[768,768]{1,0:T(8,128)(2,1)S(1)}, bf16[768,768]{1,0:T(8,128)(2,1)S(1)}, u32[]{:S(2)}, u32[]{:S(2)}) collective-permute-start(bf16[768,768]{1,0:T(8,128)(2,1)S(1)} %add_convert_fusion.3), channel_id=1, source_target_pairs={{0,1},{1,0},{2,3},{3,2},{4,5},{5,4},{6,7},{7,6},{8,9},{9,8},{10,11... | collective-permute-start | bytes 3538952 | tf_op jit(solution)/shard_map/ppermute | solution.py:73
  472.3 27.2 %collective-permute-start.21 = (bf16[768,768]{1,0:T(8,128)(2,1)S(1)}, bf16[768,768]{1,0:T(8,128)(2,1)S(1)}, u32[]{:S(2)}, u32[]{:S(2)}) collective-permute-start(bf16[768,768]{1,0:T(8,128)(2,1)S(1)} %get-tuple-element.254), channel_id=1, source_target_pairs={{0,1},{1,0},{2,3},{3,2},{4,5},{5,4},{6,7},{7,6},{8,9},{9,8},{10,11... | collective-permute-start | bytes 3538952 | tf_op jit(solution)/shard_map/ppermute | solution.py:73
  472.4 27.1 %collective-permute-start.20 = (bf16[768,768]{1,0:T(8,128)(2,1)S(1)}, bf16[768,768]{1,0:T(8,128)(2,1)S(1)}, u32[]{:S(2)}, u32[]{:S(2)}) collective-permute-start(bf16[768,768]{1,0:T(8,128)(2,1)S(1)} %get-tuple-element.254), channel_id=1, source_target_pairs={{0,4},{4,0},{1,5},{5,1},{2,6},{6,2},{3,7},{7,3},{8,12},{12,8},{9,1... | collective-permute-start | bytes 3538952 | tf_op jit(solution)/shard_map/ppermute | solution.py:73
  499.4 2.8 collective-permute-start.22
  534.2 603.6 %reduce-scatter.10.cloned.1.call-start = ((), (), s32[]{:S(2)}) async-start(), calls=%async_computation.6 | async-start | bytes 5308416 | tf_op jit(solution)/shard_map/reduce_scatter | solution.py:322
  564.3 64.0 %copy-start.14 = (f32[768,768]{1,0:T(8,128)S(1)}, f32[768,768]{1,0:T(8,128)}, u32[]{:S(2)}) copy-start(f32[768,768]{1,0:T(8,128)} %get-tuple-element.279) | copy-start | bytes 7077892
  564.3 64.0 %copy-start.46 = (f32[768]{0:T(1024)S(1)}, f32[768]{0:T(1024)}, u32[]{:S(2)}) copy-start(f32[768]{0:T(1024)} %param.20) | copy-start | bytes 9220
  585.0 2.9 collective-permute-start.24
  585.5 4.2 collective-permute-start.23
  588.3 39.9 %collective-permute-start.25 = (bf16[768,768]{1,0:T(8,128)(2,1)S(1)}, bf16[768,768]{1,0:T(8,128)(2,1)S(1)}, u32[]{:S(2)}, u32[]{:S(2)}) collective-permute-start(bf16[768,768]{1,0:T(8,128)(2,1)S(1)} %add_convert_fusion.1), channel_id=1, source_target_pairs={{0,1},{1,0},{2,3},{3,2},{4,5},{5,4},{6,7},{7,6},{8,9},{9,8},{10,11... | collective-permute-start | bytes 3538952 | tf_op jit(solution)/shard_map/ppermute | solution.py:73
  637.9 27.4 %collective-permute-start.27 = (bf16[768,768]{1,0:T(8,128)(2,1)S(1)}, bf16[768,768]{1,0:T(8,128)(2,1)S(1)}, u32[]{:S(2)}, u32[]{:S(2)}) collective-permute-start(bf16[768,768]{1,0:T(8,128)(2,1)S(1)} %get-tuple-element.248), channel_id=1, source_target_pairs={{0,1},{1,0},{2,3},{3,2},{4,5},{5,4},{6,7},{7,6},{8,9},{9,8},{10,11... | collective-permute-start | bytes 3538952 | tf_op jit(solution)/shard_map/ppermute | solution.py:73
  637.9 37.6 %collective-permute-start.26 = (bf16[768,768]{1,0:T(8,128)(2,1)S(1)}, bf16[768,768]{1,0:T(8,128)(2,1)S(1)}, u32[]{:S(2)}, u32[]{:S(2)}) collective-permute-start(bf16[768,768]{1,0:T(8,128)(2,1)S(1)} %get-tuple-element.248), channel_id=1, source_target_pairs={{0,4},{4,0},{1,5},{5,1},{2,6},{6,2},{3,7},{7,3},{8,12},{12,8},{9,1... | collective-permute-start | bytes 3538952 | tf_op jit(solution)/shard_map/ppermute | solution.py:73
  665.4 12.4 collective-permute-start.28
  675.4 468.3 %reduce-scatter.16.cloned.1.call-start = ((), (), s32[]{:S(2)}) async-start(), calls=%async_computation.9 | async-start | bytes 442368
  1073.1 11.2 collective-permute-start.30
  1073.8 131.6 %collective-permute-start.18 = (bf16[768,768]{1,0:T(8,128)(2,1)}, bf16[768,768]{1,0:T(8,128)(2,1)}, u32[]{:S(2)}, u32[]{:S(2)}) collective-permute-start(bf16[768,768]{1,0:T(8,128)(2,1)} %get-tuple-element.276), channel_id=1, source_target_pairs={{0,0},{2,4},{4,2},{6,6},{1,1},{3,5},{5,3},{7,7},{8,8},{10,12},{12,... | collective-permute-start | bytes 3538952 | tf_op jit(solution)/shard_map/ppermute | solution.py:69
  1084.3 16.3 %collective-permute-start.29 = (bf16[768,768]{1,0:T(8,128)(2,1)}, bf16[768,768]{1,0:T(8,128)(2,1)}, u32[]{:S(2)}, u32[]{:S(2)}) collective-permute-start(bf16[768,768]{1,0:T(8,128)(2,1)} %get-tuple-element.265), channel_id=1, source_target_pairs={{0,4},{4,0},{1,5},{5,1},{2,6},{6,2},{3,7},{7,3},{8,12},{12,8},{9,1... | collective-permute-start | bytes 3538952 | tf_op jit(solution)/shard_map/ppermute | solution.py:73
  1085.7 43.3 %collective-permute-start.31 = (bf16[768,768]{1,0:T(8,128)(2,1)}, bf16[768,768]{1,0:T(8,128)(2,1)}, u32[]{:S(2)}, u32[]{:S(2)}) collective-permute-start(bf16[768,768]{1,0:T(8,128)(2,1)} %add_convert_fusion), channel_id=1, source_target_pairs={{0,1},{1,0},{2,3},{3,2},{4,5},{5,4},{6,7},{7,6},{8,9},{9,8},{10,11... | collective-permute-start | bytes 3538952 | tf_op jit(solution)/shard_map/ppermute | solution.py:73
  1089.5 114.7 %reduce-scatter.14.cloned.1.call-start = ((), (), s32[]{:S(2)}) async-start(), calls=%async_computation.8 | async-start | bytes 1105920
  1132.4 73.9 %copy-start.49 = (f32[768]{0:T(1024)S(1)}, f32[768]{0:T(1024)}, u32[]{:S(2)}) copy-start(f32[768]{0:T(1024)} %get-tuple-element.251) | copy-start | bytes 9220
  1135.3 75.4 %copy-start.50 = (f32[768]{0:T(1024)S(1)}, f32[768]{0:T(1024)}, u32[]{:S(2)}) copy-start(f32[768]{0:T(1024)} %get-tuple-element.199) | copy-start | bytes 9220
  1135.3 119.1 %collective-permute-start.32 = (bf16[768,768]{1,0:T(8,128)(2,1)S(1)}, bf16[768,768]{1,0:T(8,128)(2,1)S(1)}, u32[]{:S(2)}, u32[]{:S(2)}) collective-permute-start(bf16[768,768]{1,0:T(8,128)(2,1)S(1)} %fusion.67), channel_id=1, source_target_pairs={{0,0},{2,4},{4,2},{6,6},{1,1},{3,5},{5,3},{7,7},{8,8},{10,12},{12,... | collective-permute-start | bytes 3538952 | tf_op jit(solution)/shard_map/ppermute | solution.py:69
  1136.1 118.3 %collective-permute-start.36 = (bf16[4,768,96]{1,2,0:T(8,128)(2,1)}, bf16[4,768,96]{1,2,0:T(8,128)(2,1)S(1)}, u32[]{:S(2)}, u32[]{:S(2)}) collective-permute-start(bf16[4,768,96]{1,2,0:T(8,128)(2,1)} %reduce-scatter.12.cloned.1.call-done), channel_id=1, source_target_pairs={{0,0},{2,4},{4,2},{6,6},{1,1},{3,5},{5,3},{7,7},{8,8},{10,12},{12,... | collective-permute-start | bytes 1769480 | tf_op jit(solution)/shard_map/ppermute | solution.py:69
  1137.8 117.7 %collective-permute-start.35 = (bf16[4,96,768]{2,1,0:T(8,128)(2,1)}, bf16[4,96,768]{2,1,0:T(8,128)(2,1)}, u32[]{:S(2)}, u32[]{:S(2)}) collective-permute-start(bf16[4,96,768]{2,1,0:T(8,128)(2,1)} %reduce-scatter.10.cloned.1.call-done), channel_id=1, source_target_pairs={{0,0},{2,4},{4,2},{6,6},{1,1},{3,5},{5,3},{7,7},{8,8},{10,12},{12,... | collective-permute-start | bytes 1769480 | tf_op jit(solution)/shard_map/ppermute | solution.py:69
  1144.7 64.5 %collective-permute-start.34 = (bf16[192,96]{1,0:T(8,128)(2,1)S(1)}, bf16[192,96]{1,0:T(8,128)(2,1)S(1)}, u32[]{:S(2)}, u32[]{:S(2)}) collective-permute-start(bf16[192,96]{1,0:T(8,128)(2,1)S(1)} %copy.64), channel_id=1, source_target_pairs={{0,0},{2,4},{4,2},{6,6},{1,1},{3,5},{5,3},{7,7},{8,8},{10,12},{12,... | collective-permute-start | bytes 110600 | tf_op jit(solution)/shard_map/ppermute | solution.py:69
  1205.4 4.4 collective-permute-start.33
  (59 other events, 903.6 us)
Sparse Core Ops, SparseCore 0:
  93.7 38.1 all-gather.2
  262.6 38.3 all-gather.4
  534.3 85.6 reduce-scatter.11
  675.6 87.4 reduce-scatter.9
  1089.6 44.7 reduce-scatter.15
  1138.9 65.2 reduce-scatter.13

commit v2 on v1

v2 whole, which is shorter than its diff:
```python
import jax
import jax.numpy as jnp
from jax import lax
from jax.experimental import pallas as pl
from jax.experimental.pallas import tpu as pltpu
from jax.sharding import Mesh
from jax.sharding import PartitionSpec as P

HEAD_DIM = 64
QUERY_BLOCK = 512
BLOCK = 256
LOG2E = 1.4426950408889634
NEGATIVE = -1e30
TILE = 256
ALIGN = 16
HBM = pl.BlockSpec(memory_space=pl.ANY)

epsilon = 1e-05
highest = lax.Precision.HIGHEST


def normalize_plain(values):
    centered = values - jnp.mean(values, axis=-1, keepdims=True)
    variance = jnp.mean(centered * centered, axis=-1, keepdims=True)
    inverse = lax.rsqrt(variance + epsilon)
    return (centered * inverse, inverse)


def normalize_back(upstream, unit_rows, inverse, gain_row):
    scaled = upstream * gain_row
    centered = scaled - jnp.mean(scaled, axis=-1, keepdims=True)
    return inverse * (centered - unit_rows * jnp.mean(scaled * unit_rows, axis=-1, keepdims=True))


def matmul(a, b, dims=((1,), (0,))):
    return lax.dot_general(a, b, (dims, ((), ())), preferred_element_type=jnp.float32)


def key_ranges(segment, block):
    token_count = segment.shape[0]
    position = jnp.arange(token_count, dtype=jnp.int32)
    prompt = jnp.sum((segment == 0).astype(jnp.int32))
    fresh = jnp.concatenate([jnp.ones((1,), jnp.bool_), segment[1:] != segment[:-1]])
    start = lax.cummax(jnp.where(fresh, position, 0), axis=0)
    first = jnp.arange(token_count // block, dtype=jnp.int32) * block
    whole = jnp.minimum(prompt, first) // block
    shared = (jnp.minimum(prompt, first + block) + block - 1) // block
    own = jnp.maximum(shared, start[first] // block)
    last = first // block + 1
    return (jnp.stack([whole, shared, own, last, jnp.full_like(whole, prompt)]), start[None, :])


def copies(pairs, semaphores):
    moved = [
        pltpu.make_async_copy(source, target, semaphores.at[place])
        for place, (source, target) in enumerate(pairs)
    ]
    for copy in moved:
        copy.start()
    for copy in moved:
        copy.wait()


def rank_rows(ref, rank, like):
    count = like.shape[0]
    return ref.at[pl.ds(pl.multiple_of(rank * count, count), count)]


def send_ranks(ref, targets, ranks, semaphores, edge, block, down):
    count = targets[0].shape[0]
    for rank in range(4):
        if down:
            first = rank * count
            due = (edge <= first) & (edge + block > first)
        else:
            last = (rank + 1) * count
            due = (edge >= last) & (edge - block < last)

        @pl.when(due)
        def _(rank=rank):
            for b, target in enumerate(targets):

                @pl.when(ranks[b] == rank)
                def _(b=b, target=target):
                    source = ref.at[rank * count : (rank + 1) * count]
                    pltpu.make_async_copy(source, target, semaphores.at[b]).start()


def await_ranks(ref, targets, ranks, semaphores):
    for b, target in enumerate(targets):
        pltpu.make_async_copy(rank_rows(ref, ranks[b], target), target, semaphores.at[b]).wait()


def forward_kernel(
    ranges, ranks, x0, x1, x2, x3, w_ref, proj_ref, start_ref,
    p0, p1, p2, p3, q_ref, qt_ref, k_ref, kt_ref, v_ref, ctx_ref, lse_ref,
    x_ref, part_ref, vt_ref, score_ref, top_ref, sum_ref, arrived, left,
):
    step = pl.program_id(0)
    heads = q_ref.shape[0]
    block = q_ref.shape[1]
    rows = pl.ds(pl.multiple_of(step * block, block), block)

    @pl.when(step == 0)
    def _():
        copies(
            [(x, rank_rows(x_ref, ranks[b], x)) for b, x in enumerate((x0, x1, x2, x3))], arrived
        )

    x = x_ref[rows, :]
    kinds = []
    for kind in range(3):
        made = matmul(x, w_ref[kind])
        kinds.append((made.astype(jnp.bfloat16), made.T.astype(jnp.bfloat16)))
    for head in range(heads):
        part = slice(head * HEAD_DIM, (head + 1) * HEAD_DIM)
        q_ref[head] = kinds[0][0][:, part]
        k_ref[head, rows, :] = kinds[1][0][:, part]
        v_ref[head, rows, :] = kinds[2][0][:, part]
        qt_ref[head] = kinds[0][1][part]
        for piece in range(kt_ref.shape[0]):
            columns = slice(piece * kt_ref.shape[3], (piece + 1) * kt_ref.shape[3])
            kt_ref[piece, head] = kinds[1][1][part, columns]
        vt_ref[step, head, :HEAD_DIM] = kinds[2][1][part]
        vt_ref[step, head, HEAD_DIM:] = jnp.ones((16, block), jnp.bfloat16)
    top_ref[...] = jnp.full_like(top_ref, NEGATIVE)
    sum_ref[...] = jnp.zeros_like(sum_ref)
    prompt = ranges[4, step]
    scale = LOG2E * HEAD_DIM ** (-0.5)

    def visit(key, masked):
        place = pl.ds(pl.multiple_of(key * block, block), block)
        if masked:
            key_at = key * block + lax.broadcasted_iota(jnp.int32, (block, block), 0)
            query_at = step * block + lax.broadcasted_iota(jnp.int32, (block, block), 1)
            seen = (key_at <= query_at) & ((key_at < prompt) | (key_at >= start_ref[...]))
        for head in range(heads):
            scores = matmul(k_ref[head, place, :], qt_ref[head])
            if masked:
                scores = jnp.where(seen, scores, NEGATIVE)
            score_ref[key, head] = scores
            top_ref[head] = jnp.maximum(
                top_ref[head], jnp.max(scores.reshape(block // 8, 8, block), axis=0)
            )

    def plain(key, carry):
        visit(key, False)
        return carry

    def edge(key, carry):
        visit(key, True)
        return carry

    lax.fori_loop(0, ranges[0, step], plain, 0)
    lax.fori_loop(ranges[0, step], ranges[1, step], edge, 0)
    lax.fori_loop(ranges[2, step], ranges[3, step], edge, 0)
    for head in range(heads):
        top_ref[head, :1] = jnp.max(top_ref[head], axis=0, keepdims=True) * scale

    def add(key, carry):
        for head in range(heads):
            weights = jnp.exp2(score_ref[key, head] * scale - top_ref[head, :1])
            sum_ref[head] += matmul(vt_ref[key, head], weights.astype(jnp.bfloat16))
        return carry

    lax.fori_loop(0, ranges[1, step], add, 0)
    lax.fori_loop(ranges[2, step], ranges[3, step], add, 0)
    for head in range(heads):
        total = sum_ref[head, HEAD_DIM : HEAD_DIM + 1]
        context = sum_ref[head, :HEAD_DIM] / total
        ctx_ref[head * HEAD_DIM : (head + 1) * HEAD_DIM] = context.astype(jnp.bfloat16)
        lse_ref[head] = top_ref[head, :1] + jnp.log(total) * LOG2E
    part_ref[rows, :] = matmul(ctx_ref[...], proj_ref[...], ((0,), (0,))).astype(jnp.bfloat16)
    send_ranks(part_ref, (p0, p1, p2, p3), ranks, left, (step + 1) * block, block, False)

    @pl.when(step == pl.num_programs(0) - 1)
    def _():
        await_ranks(part_ref, (p0, p1, p2, p3), ranks, left)


def attention_forward(ranges, start, ranks, x, w, proj):
    tokens, width = start.shape[1], x[0].shape[1]
    local = w.shape[2]
    heads = local // HEAD_DIM
    block = QUERY_BLOCK
    fine = BLOCK
    count = tokens // block
    low = jnp.bfloat16
    head_rows = pl.BlockSpec((heads, tokens, HEAD_DIM), lambda i, r, n: (0, 0, 0))
    flops = 2 * tokens * width * local * 4 + tokens * tokens * local * 2
    return pl.pallas_call(
        forward_kernel,
        grid_spec=pltpu.PrefetchScalarGridSpec(
            num_scalar_prefetch=2,
            grid=(count,),
            in_specs=[
                *[HBM] * 4,
                pl.BlockSpec((3, width, local), lambda i, r, n: (0, 0, 0)),
                pl.BlockSpec((local, width), lambda i, r, n: (0, 0)),
                pl.BlockSpec((1, block), lambda i, r, n: (0, i)),
            ],
            out_specs=[
                *[HBM] * 4,
                pl.BlockSpec((heads, block, HEAD_DIM), lambda i, r, n: (0, i, 0)),
                pl.BlockSpec((heads, HEAD_DIM, block), lambda i, r, n: (0, 0, i)),
                head_rows,
                pl.BlockSpec((block // fine, heads, HEAD_DIM, fine), lambda i, r, n: (i, 0, 0, 0)),
                head_rows,
                pl.BlockSpec((local, block), lambda i, r, n: (0, i)),
                pl.BlockSpec((heads, 1, block), lambda i, r, n: (0, 0, i)),
            ],
            scratch_shapes=[
                pltpu.VMEM((tokens, width), low),
                pltpu.VMEM((tokens, width), low),
                pltpu.VMEM((count, heads, HEAD_DIM + 16, block), low),
                pltpu.VMEM((count, heads, block, block), jnp.float32),
                pltpu.VMEM((heads, 8, block), jnp.float32),
                pltpu.VMEM((heads, HEAD_DIM + 16, block), jnp.float32),
                pltpu.SemaphoreType.DMA((4,)),
                pltpu.SemaphoreType.DMA((4,)),
            ],
        ),
        out_shape=[
            *[jax.ShapeDtypeStruct(x[0].shape, low)] * 4,
            jax.ShapeDtypeStruct((heads, tokens, HEAD_DIM), low),
            jax.ShapeDtypeStruct((heads, HEAD_DIM, tokens), low),
            jax.ShapeDtypeStruct((heads, tokens, HEAD_DIM), low),
            jax.ShapeDtypeStruct((tokens // fine, heads, HEAD_DIM, fine), low),
            jax.ShapeDtypeStruct((heads, tokens, HEAD_DIM), low),
            jax.ShapeDtypeStruct((local, tokens), low),
            jax.ShapeDtypeStruct((heads, 1, tokens), jnp.float32),
        ],
        compiler_params=pltpu.CompilerParams(vmem_limit_bytes=56 << 20),
        cost_estimate=pl.CostEstimate(
            flops=4 * flops, transcendentals=tokens * tokens * heads // 2, bytes_accessed=40 << 20
        ),
        name="attention_forward",
    )(ranges, ranks, *x, w, proj, start)


def backward_kernel(
    ranges, ranks, g0, g1, g2, g3, x0, x1, x2, x3,
    ctx_ref, lse_ref, q_ref, qt_ref, start_ref, k_ref, kt_ref, v_ref, w_ref, proj_ref,
    p0, p1, p2, p3, weights_ref,
    g_ref, x_ref, part_ref, wgrad_ref, pgrad_ref,
    dk_ref, dv_ref, dqt_ref, out_ref, outt_ref, inner_ref, arrived, left,
):
    number = pl.program_id(0)
    step = pl.num_programs(0) - 1 - number
    heads = q_ref.shape[0]
    block = q_ref.shape[1]
    rows = pl.ds(pl.multiple_of(step * block, block), block)

    @pl.when(number == 0)
    def _():
        copies(
            [(g, rank_rows(g_ref, ranks[b], g)) for b, g in enumerate((g0, g1, g2, g3))]
            + [(x, rank_rows(x_ref, ranks[b], x)) for b, x in enumerate((x0, x1, x2, x3))],
            arrived,
        )
        dk_ref[...] = jnp.zeros_like(dk_ref)
        dv_ref[...] = jnp.zeros_like(dv_ref)
        wgrad_ref[...] = jnp.zeros_like(wgrad_ref)
        pgrad_ref[...] = jnp.zeros_like(pgrad_ref)

    upstream = g_ref[rows, :]
    outer = matmul(upstream, proj_ref[...], ((1,), (1,)))
    low = outer.astype(jnp.bfloat16)
    turned = outer.T.astype(jnp.bfloat16)
    for head in range(heads):
        part = slice(head * HEAD_DIM, (head + 1) * HEAD_DIM)
        out_ref[head] = low[:, part]
        outt_ref[head] = turned[part]
        inner_ref[head] = jnp.sum(
            turned[part].astype(jnp.float32) * ctx_ref[part].astype(jnp.float32),
            axis=0,
            keepdims=True,
        )
    pgrad_ref[...] += matmul(ctx_ref[...], upstream)
    dqt_ref[...] = jnp.zeros_like(dqt_ref)
    prompt = ranges[4, step]
    scale = LOG2E * HEAD_DIM ** (-0.5)

    def visit(key, masked):
        place = pl.ds(pl.multiple_of(key * block, block), block)
        if masked:
            key_at = key * block + lax.broadcasted_iota(jnp.int32, (block, block), 0)
            query_at = step * block + lax.broadcasted_iota(jnp.int32, (block, block), 1)
            seen = (key_at <= query_at) & ((key_at < prompt) | (key_at >= start_ref[...]))
        made = [
            (
                matmul(k_ref[head, place, :], qt_ref[head]),
                matmul(v_ref[head, place, :], outt_ref[head]),
            )
            for head in range(heads)
        ]
        for head in range(heads):
            scores, dprob = made[head]
            scores = scores * scale
            if masked:
                scores = jnp.where(seen, scores, NEGATIVE)
            prob = jnp.exp2(scores - lse_ref[head])
            dscore = (prob * (dprob - inner_ref[head])).astype(jnp.bfloat16)
            made[head] = prob.astype(jnp.bfloat16), dscore
        for head in range(heads):
            prob, dscore = made[head]
            dv_ref[head, place, :] += matmul(prob, out_ref[head])
            dk_ref[head, place, :] += matmul(dscore, q_ref[head])
            dqt_ref[head] += matmul(kt_ref[key, head], dscore)

    def plain(key, carry):
        visit(key, False)
        return carry

    def edge(key, carry):
        visit(key, True)
        return carry

    lax.fori_loop(0, ranges[0, step], plain, 0)
    lax.fori_loop(ranges[0, step], ranges[1, step], edge, 0)
    lax.fori_loop(ranges[2, step], ranges[3, step], edge, 0)
    small = HEAD_DIM ** (-0.5)
    x = x_ref[rows, :]
    total = None
    for kind in range(3):
        if kind == 0:
            grad = jnp.concatenate([dqt_ref[head] for head in range(heads)], axis=0).T * small
        elif kind == 1:
            grad = jnp.concatenate([dk_ref[head, rows, :] for head in range(heads)], axis=1) * small
        else:
            grad = jnp.concatenate([dv_ref[head, rows, :] for head in range(heads)], axis=1)
        grad = grad.astype(jnp.bfloat16)
        wgrad_ref[kind] += matmul(x, grad, ((0,), (0,)))
        term = matmul(grad, w_ref[kind], ((1,), (1,)))
        total = term if total is None else total + term
    part_ref[rows, :] = total.astype(jnp.bfloat16)
    send_ranks(part_ref, (p0, p1, p2, p3), ranks, left, step * block, block, True)

    @pl.when(step == 0)
    def _():
        weights_ref[:3] = wgrad_ref[...].astype(jnp.bfloat16)
        weights_ref[3] = pgrad_ref[...].T.astype(jnp.bfloat16)
        await_ranks(part_ref, (p0, p1, p2, p3), ranks, left)


def attention_backward(ranges, start, ranks, upstream, x, saved, w, proj):
    q, qt, k, kt, v, ctx, lse = saved
    tokens, width = start.shape[1], x[0].shape[1]
    local = w.shape[2]
    heads = local // HEAD_DIM
    block = BLOCK
    count = tokens // block
    low = jnp.bfloat16

    def at(i):
        return count - 1 - i

    head_rows = pl.BlockSpec((heads, tokens, HEAD_DIM), lambda i, r, n: (0, 0, 0))
    flops = 2 * tokens * width * local * 8 + tokens * tokens * local * 5
    return pl.pallas_call(
        backward_kernel,
        grid_spec=pltpu.PrefetchScalarGridSpec(
            num_scalar_prefetch=2,
            grid=(count,),
            in_specs=[
                *[HBM] * 8,
                pl.BlockSpec((local, block), lambda i, r, n: (0, at(i))),
                pl.BlockSpec((heads, 1, block), lambda i, r, n: (0, 0, at(i))),
                pl.BlockSpec((heads, block, HEAD_DIM), lambda i, r, n: (0, at(i), 0)),
                pl.BlockSpec((heads, HEAD_DIM, block), lambda i, r, n: (0, 0, at(i))),
                pl.BlockSpec((1, block), lambda i, r, n: (0, at(i))),
                head_rows,
                pl.BlockSpec((count, heads, HEAD_DIM, block), lambda i, r, n: (0, 0, 0, 0)),
                head_rows,
                pl.BlockSpec((3, width, local), lambda i, r, n: (0, 0, 0)),
                pl.BlockSpec((local, width), lambda i, r, n: (0, 0)),
            ],
            out_specs=[
                *[HBM] * 4,
                pl.BlockSpec((4, width, local), lambda i, r, n: (0, 0, 0)),
            ],
            scratch_shapes=[
                pltpu.VMEM((tokens, width), low),
                pltpu.VMEM((tokens, width), low),
                pltpu.VMEM((tokens, width), low),
                pltpu.VMEM((3, width, local), jnp.float32),
                pltpu.VMEM((local, width), jnp.float32),
                pltpu.VMEM((heads, tokens, HEAD_DIM), jnp.float32),
                pltpu.VMEM((heads, tokens, HEAD_DIM), jnp.float32),
                pltpu.VMEM((heads, HEAD_DIM, block), jnp.float32),
                pltpu.VMEM((heads, block, HEAD_DIM), low),
                pltpu.VMEM((heads, HEAD_DIM, block), low),
                pltpu.VMEM((heads, 1, block), jnp.float32),
                pltpu.SemaphoreType.DMA((8,)),
                pltpu.SemaphoreType.DMA((4,)),
            ],
        ),
        out_shape=[
            *[jax.ShapeDtypeStruct(x[0].shape, low)] * 4,
            jax.ShapeDtypeStruct((4, width, local), low),
        ],
        compiler_params=pltpu.CompilerParams(vmem_limit_bytes=56 << 20),
        cost_estimate=pl.CostEstimate(
            flops=4 * flops, transcendentals=tokens * tokens * heads // 2, bytes_accessed=40 << 20
        ),
        name="attention_backward",
    )(ranges, ranks, *upstream, *x, ctx, lse, q, qt, start, k, kt, v, w, proj)


def route_rows(route, priority, experts, capacity, row_count, ranks):
    own_start = ranks[0] * row_count
    own_route = lax.dynamic_slice_in_dim(route, own_start, row_count, 0)
    own_priority = lax.dynamic_slice_in_dim(priority, own_start, row_count, 0)
    ahead = (route[None, :] == own_route[:, None]) & (priority[None, :] < own_priority[:, None])
    kept = jnp.sum(ahead.astype(jnp.int32), axis=1) < capacity
    kinds = jnp.arange(experts, dtype=jnp.int32)
    block_hot = (route.reshape(-1, row_count)[:, :, None] == kinds).astype(jnp.int32)
    lengths = (jnp.sum(block_hot, axis=1) + ALIGN - 1) // ALIGN * ALIGN
    starts = jnp.cumsum(lengths, axis=1) - lengths
    own_hot = (own_route[:, None] == kinds).astype(jnp.int32)
    index = jnp.arange(row_count, dtype=jnp.int32)
    before = (own_route[None, :] == own_route[:, None]) & (index[None, :] < index[:, None])
    own_starts = lax.dynamic_slice_in_dim(starts, ranks[0], 1, 0)
    place = jnp.sum(before.astype(jnp.int32), axis=1) + jnp.sum(own_hot * own_starts, axis=1)
    slots = jnp.arange(row_count + experts * ALIGN, dtype=jnp.int32)
    order = (slots[:, None] == place[None, :]).astype(jnp.bfloat16)
    picked = [
        lax.dynamic_slice_in_dim(array, ranks[b], 1, 0)[0]
        for array in (starts, lengths)
        for b in range(4)
    ]
    home = at_home().astype(jnp.int32)[None]
    return (kept, order, jnp.concatenate([*picked, home]), own_hot)


def sort_rows(order, rows):
    return jnp.dot(order, rows, preferred_element_type=jnp.float32).astype(jnp.bfloat16)


def unsort_rows(order, rows):
    return matmul(order, rows.astype(jnp.bfloat16), ((0,), (0,)))


def each_tile(table, expert, experts, visit):
    for block in range(4):
        start = table[block * experts + expert]
        length = table[(4 + block) * experts + expert]

        def tile(number, carry, block=block, start=start, length=length):
            place = pl.ds(pl.multiple_of(start + number * TILE, ALIGN), TILE)
            visit(block, place, length - number * TILE)
            return carry

        lax.fori_loop(0, (length + TILE - 1) // TILE, tile, 0)


def fetch_weights(choice, kept, given, targets, semaphores):
    for place, target in enumerate(targets):
        for expert in range(target.shape[0]):
            ready = semaphores.at[place, expert]

            @pl.when(choice == 1)
            def _(place=place, target=target, expert=expert, ready=ready):
                pltpu.make_async_copy(kept[place].at[expert], target.at[expert], ready).start()

            @pl.when(choice == 0)
            def _(place=place, target=target, expert=expert, ready=ready):
                pltpu.make_async_copy(given[place].at[expert], target.at[expert], ready).start()


def await_weights(kept, targets, expert, semaphores):
    for place, target in enumerate(targets):
        pltpu.make_async_copy(
            kept[place].at[expert], target.at[expert], semaphores.at[place, expert]
        ).wait()


def within(rows, left):
    return jnp.where(lax.broadcasted_iota(jnp.int32, rows.shape, 0) < left, rows, 0)


def moe_forward_kernel(
    table, x0, x1, x2, x3, own_up, own_down, new_up, new_down,
    y0, y1, y2, y3, hidden_out, slope_out,
    x_ref, y_ref, hidden_ref, slope_ref, up_ref, down_ref, semaphores, ready,
):
    expert = pl.program_id(0)
    experts = pl.num_programs(0)
    count = x0.shape[0]
    kept, given, held = (own_up, own_down), (new_up, new_down), (up_ref, down_ref)

    @pl.when(expert == 0)
    def _():
        fetch_weights(table[8 * experts], kept, given, held, ready)
        for ref in (hidden_ref, slope_ref, y_ref):
            ref[...] = jnp.zeros_like(ref)
        x_ref[:, count:, :] = jnp.zeros((4, TILE, x_ref.shape[2]), jnp.bfloat16)
        copies([(x, x_ref.at[b, :count]) for b, x in enumerate((x0, x1, x2, x3))], semaphores)

    await_weights(kept, held, expert, ready)

    def visit(block, place, left):
        u = matmul(x_ref[block, place, :], up_ref[expert])
        bend = jnp.tanh(0.7978845608028654 * (u + 0.044715 * u * u * u))
        hidden = (0.5 * u * (1.0 + bend)).astype(jnp.bfloat16)
        slope = 0.5 * (1.0 + bend) + 0.5 * u * (1.0 - bend * bend) * (
            0.7978845608028654 * (1.0 + 3.0 * 0.044715 * u * u)
        )
        hidden_ref[block, place, :] = hidden
        slope_ref[block, place, :] = slope.astype(jnp.bfloat16)
        y_ref[block, place, :] = matmul(hidden, down_ref[expert]).astype(jnp.bfloat16)

    each_tile(table, expert, experts, visit)

    @pl.when(expert == experts - 1)
    def _():
        copies(
            [(y_ref.at[b, :count], y) for b, y in enumerate((y0, y1, y2, y3))]
            + [(hidden_ref, hidden_out), (slope_ref, slope_out)],
            semaphores,
        )


def moe_backward_kernel(
    table, d0, d1, d2, d3, slope_in, own_up, own_down, new_up, new_down,
    y0, y1, y2, y3, grad_out,
    d_ref, slope_ref, y_ref, grad_ref, up_ref, down_ref, semaphores, ready,
):
    expert = pl.program_id(0)
    experts = pl.num_programs(0)
    count = d0.shape[0]
    kept, given, held = (own_up, own_down), (new_up, new_down), (up_ref, down_ref)

    @pl.when(expert == 0)
    def _():
        fetch_weights(table[8 * experts], kept, given, held, ready)
        for ref in (grad_ref, y_ref):
            ref[...] = jnp.zeros_like(ref)
        d_ref[:, count:, :] = jnp.zeros((4, TILE, d_ref.shape[2]), jnp.bfloat16)
        copies(
            [(d, d_ref.at[b, :count]) for b, d in enumerate((d0, d1, d2, d3))]
            + [(slope_in, slope_ref)],
            semaphores,
        )

    await_weights(kept, held, expert, ready)

    def visit(block, place, left):
        upstream = within(d_ref[block, place, :], left)
        slope = slope_ref[block, place, :].astype(jnp.float32)
        grad = (matmul(upstream, down_ref[expert], ((1,), (1,))) * slope).astype(jnp.bfloat16)
        grad_ref[block, place, :] = grad
        y_ref[block, place, :] = matmul(grad, up_ref[expert], ((1,), (1,))).astype(jnp.bfloat16)

    each_tile(table, expert, experts, visit)

    @pl.when(expert == experts - 1)
    def _():
        copies(
            [(y_ref.at[b, :count], y) for b, y in enumerate((y0, y1, y2, y3))]
            + [(grad_ref, grad_out)],
            semaphores,
        )


def moe_weights_kernel(
    table, x0, x1, x2, x3, d0, d1, d2, d3, hidden_in, grad_in,
    out_ref,
    x_ref, d_ref, hidden_ref, grad_ref, up_sum, down_sum, semaphores,
):
    expert = pl.program_id(0)
    experts = pl.num_programs(0)
    count = x0.shape[0]

    @pl.when(expert == 0)
    def _():
        for ref in (x_ref, d_ref):
            ref[:, count:, :] = jnp.zeros((4, TILE, ref.shape[2]), jnp.bfloat16)
        copies(
            [(x, x_ref.at[b, :count]) for b, x in enumerate((x0, x1, x2, x3))]
            + [(d, d_ref.at[b, :count]) for b, d in enumerate((d0, d1, d2, d3))]
            + [(hidden_in, hidden_ref), (grad_in, grad_ref)],
            semaphores,
        )

    up_sum[...] = jnp.zeros_like(up_sum)
    down_sum[...] = jnp.zeros_like(down_sum)

    def visit(block, place, left):
        up_sum[...] += matmul(
            x_ref[block, place, :], within(grad_ref[block, place, :], left), ((0,), (0,))
        )
        down_sum[...] += matmul(
            within(d_ref[block, place, :], left), hidden_ref[block, place, :], ((0,), (0,))
        )

    each_tile(table, expert, experts, visit)
    out_ref[0, 0] = up_sum[...].astype(jnp.bfloat16)
    out_ref[1, 0] = down_sum[...].astype(jnp.bfloat16)


def moe_call(kernel, name, table, arrays, outs, scratch, sums, experts, cost):
    low = jnp.bfloat16
    specs = [HBM] * len(outs)
    ready = [pltpu.SemaphoreType.DMA((2, experts))]
    if sums:
        specs = [pl.BlockSpec((2, 1) + outs[0][2:], lambda e, t: (0, e, 0, 0))]
        ready = []
    return pl.pallas_call(
        kernel,
        grid_spec=pltpu.PrefetchScalarGridSpec(
            num_scalar_prefetch=1,
            grid=(experts,),
            in_specs=[HBM] * len(arrays),
            out_specs=specs,
            scratch_shapes=[
                *[pltpu.VMEM(shape, low) for shape in scratch],
                *[pltpu.VMEM(shape, jnp.float32) for shape in sums],
                pltpu.SemaphoreType.DMA((10,)),
                *ready,
            ],
        ),
        out_shape=[jax.ShapeDtypeStruct(shape, low) for shape in outs],
        compiler_params=pltpu.CompilerParams(vmem_limit_bytes=58 << 20),
        cost_estimate=pl.CostEstimate(flops=cost, transcendentals=0, bytes_accessed=40 << 20),
        name=name,
    )(table, *arrays)


def moe_forward(table, x, own, new):
    count, width = x[0].shape
    experts, _, hidden = own[0].shape
    wide, tall = (4, count + TILE, width), (4, count + TILE, hidden)
    *y, hid, slope = moe_call(
        moe_forward_kernel, "moe_forward", table, [*x, *own, *new],
        [(count, width)] * 4 + [tall, tall],
        [wide, wide, tall, tall, own[0].shape, own[1].shape], [], experts,
        20 * count * width * hidden,
    )
    return (y, hid, slope)


def moe_backward(table, d, slope, own, new):
    count, width = d[0].shape
    experts, _, hidden = own[0].shape
    wide, tall = (4, count + TILE, width), (4, count + TILE, hidden)
    *y, grad = moe_call(
        moe_backward_kernel, "moe_backward", table, [*d, slope, *own, *new],
        [(count, width)] * 4 + [tall],
        [wide, tall, wide, tall, own[0].shape, own[1].shape], [], experts,
        20 * count * width * hidden,
    )
    return (y, grad)


def moe_weights(table, x, d, hid, grad, experts):
    count, width = x[0].shape
    hidden = hid.shape[2]
    wide, tall = (4, count + TILE, width), (4, count + TILE, hidden)
    return moe_call(
        moe_weights_kernel, "moe_weights", table, [*x, *d, hid, grad],
        [(2, experts, width, hidden)], [wide, wide, tall, tall], [(width, hidden)] * 2, experts,
        20 * count * width * hidden,
    )[0]


def at_home():
    return lax.axis_index("c") == lax.axis_index("zh")


def swap_roles(value):
    moved = lax.ppermute(value, ("c", "zh"), [(1, 2), (2, 1)])
    return jnp.where(at_home(), value, moved)


def flip(value, axis):
    return lax.ppermute(value, axis, [(0, 1), (1, 0)])


def gather_blocks(rows):
    across = flip(rows, "zl")
    return [rows, flip(rows, "c"), across, flip(across, "c")]


def scatter_blocks(blocks):
    own, beside, across, corner = blocks
    far = flip(corner, "c").astype(jnp.float32)
    far = flip((far + across.astype(jnp.float32)).astype(own.dtype), "zl").astype(jnp.float32)
    return own.astype(jnp.float32) + flip(beside, "c").astype(jnp.float32) + far


def halve(value, axis, dimension):
    count = value.shape[dimension] // 2
    side = lax.axis_index(axis)
    kept = lax.dynamic_slice_in_dim(value, side * count, count, dimension)
    sent = lax.dynamic_slice_in_dim(value, (1 - side) * count, count, dimension)
    total = kept.astype(jnp.float32) + flip(sent, axis).astype(jnp.float32)
    return total.astype(value.dtype)


def sum_home(value, dimension):
    count = value.shape[dimension] // 2
    high = lax.axis_index("zh")
    straight = lax.dynamic_slice_in_dim(value, high * count, count, dimension)
    turned = lax.dynamic_slice_in_dim(value, (1 - high) * count, count, dimension)
    turned = lax.ppermute(turned, ("c", "zh"), [(0, 2), (1, 0), (2, 3), (3, 1)])
    return swap_roles(straight).astype(jnp.float32) + turned.astype(jnp.float32)


def other_quarter(weight, users):
    flat = weight.reshape(-1, weight.shape[-1])
    part = flat.shape[0] // lax.axis_size(users)
    piece = lax.dynamic_slice_in_dim(flat, lax.axis_index(users) * part, part, 0)
    piece = flip(piece, "zh")
    return lax.all_gather(piece, users, axis=0, tiled=True).reshape(weight.shape)


def body(
    high_bits,
    block_input,
    attention_gain,
    qkv_weight,
    proj_weight,
    moe_gain,
    centroids,
    expert_up,
    expert_down,
    out_grad,
    routes,
    priority,
    segments,
):
    row_count = block_input.shape[1]
    model_width = block_input.shape[2]
    experts = expert_up.shape[0]
    token_count = segments.shape[1]
    capacity = 9 * token_count // (8 * experts)
    local_width = qkv_weight.shape[2]
    users = (*high_bits, "c")
    core, near = lax.axis_index("c"), lax.axis_index("zl")
    ranks = jnp.stack(
        [2 * core + near, 2 * (1 - core) + near, 2 * core + 1 - near, 3 - 2 * core - near]
    )
    indices = jnp.stack([routes[0, :, 0], priority[0], segments[0]])
    indices = jnp.where(at_home(), indices, flip(indices, "c"))
    segment = indices[2]
    held = swap_roles(block_input[0])
    small = jnp.concatenate([qkv_weight, proj_weight.reshape(1, model_width, local_width)], axis=0)
    small = jnp.where(at_home(), small, other_quarter(small, users))
    qkv_used, proj_used = small[:3], small[3].reshape(local_width, model_width)
    own_experts = (expert_up, expert_down)
    expert_up, expert_down, held = lax.optimization_barrier((expert_up, expert_down, held))
    new_experts = [other_quarter(weight, users) for weight in (expert_up, expert_down)]
    inputs = held.astype(jnp.float32)
    unit_one, inverse_one = normalize_plain(inputs)
    normed_one_rows = (unit_one * attention_gain).astype(jnp.bfloat16)
    normed_one = gather_blocks(normed_one_rows)
    *attended, q, qt, k, kt, v, ctx, lse = attention_forward(
        *key_ranges(segment, QUERY_BLOCK), ranks, normed_one, qkv_used, proj_used
    )
    saved = (q, qt, k, kt, v, ctx, lse)
    upstream = swap_roles(out_grad[0]).astype(jnp.float32)
    kept_rows, order, table, hot_rows = route_rows(
        indices[0], indices[1], experts, capacity, row_count, ranks
    )
    attended = scatter_blocks(attended)
    mixed_one = inputs + attended
    unit_two, inverse_two = normalize_plain(mixed_one)
    normed_two_rows = (unit_two * moe_gain).astype(jnp.bfloat16)
    centroid_rows = jnp.dot(
        hot_rows.astype(jnp.bfloat16), centroids, preferred_element_type=jnp.float32
    )
    normed_two_float = normed_two_rows.astype(jnp.float32)
    gate_prob = jax.nn.sigmoid(jnp.sum(normed_two_float * centroid_rows, axis=-1))
    gate_used = jnp.where(kept_rows, gate_prob, 0.0)
    grad_eo_rows = (gate_used[:, None] * upstream).astype(jnp.bfloat16)
    dispatched = gather_blocks(sort_rows(order, normed_two_rows))
    grad_sorted = sort_rows(order, grad_eo_rows)
    grad_sorted, *dispatched = lax.optimization_barrier((grad_sorted, *dispatched))
    grad_dispatched = gather_blocks(grad_sorted)
    returned, hidden, slope = moe_forward(table, dispatched, own_experts, new_experts)
    expert_out = unsort_rows(order, scatter_blocks(returned))
    mixed_two = mixed_one + gate_used[:, None] * expert_out
    block_output = swap_roles(mixed_two.astype(jnp.bfloat16))[None]
    grad_gate = jnp.where(kept_rows, jnp.sum(upstream * expert_out, axis=-1), 0.0)
    grad_score = grad_gate * gate_prob * (1.0 - gate_prob)
    back_moe, grad_upward = moe_backward(table, grad_dispatched, slope, own_experts, new_experts)
    expert_part = moe_weights(table, dispatched, grad_dispatched, hidden, grad_upward, experts)
    grad_two = unsort_rows(order, scatter_blocks(back_moe)) + grad_score[:, None] * centroid_rows
    centroid_part = jnp.einsum(
        "te,td->ed",
        hot_rows.astype(jnp.float32),
        grad_score[:, None] * normed_two_float,
        precision=highest,
    )
    moe_gain_part = jnp.sum(grad_two * unit_two, axis=0)
    grad_mixed = upstream + normalize_back(grad_two, unit_two, inverse_two, moe_gain)
    grad_att = gather_blocks(grad_mixed.astype(jnp.bfloat16))
    *grad_one, weights_part = attention_backward(
        *key_ranges(segment, BLOCK), ranks, grad_att, normed_one, saved, qkv_used, proj_used
    )
    grad_one = scatter_blocks(grad_one)
    input_grad = swap_roles(
        (grad_mixed + normalize_back(grad_one, unit_one, inverse_one, attention_gain)).astype(
            jnp.bfloat16
        )
    )[None]

    expert_part = lax.psum_scatter(expert_part, high_bits, scatter_dimension=2, tiled=True)
    expert_summed = sum_home(expert_part, 2)
    up_summed, down_summed = expert_summed[0], jnp.swapaxes(expert_summed[1], 1, 2)
    for bit in high_bits:
        weights_part = halve(weights_part, bit, 1)
    weights_part = sum_home(weights_part, 1)
    qkv_summed, proj_summed = weights_part[:3], weights_part[3].T
    early = jnp.concatenate([moe_gain_part[None], centroid_part], axis=0)
    for bit in (*users, "zh", "zl"):
        early = halve(early, bit, 1)
    gain_two_sum, centroid_sum = early[0], early[1:]
    slice_rows = qkv_summed.shape[1]
    own_rows = lax.dynamic_slice_in_dim(
        qkv_weight, lax.axis_index(users) * slice_rows, slice_rows, 1
    )
    gain_one = jnp.sum(own_rows.astype(jnp.float32) * qkv_summed, axis=(0, 2))
    for bit in ("zh", "zl"):
        gain_one = halve(gain_one, bit, 0)
    share = gain_one.shape[0]
    own_gain = lax.axis_index((*users, "zh", "zl")) * share
    gain_one_sum = gain_one / lax.dynamic_slice_in_dim(attention_gain, own_gain, share, 0)
    return (
        block_output,
        input_grad,
        gain_one_sum,
        gain_two_sum,
        centroid_sum,
        qkv_summed,
        proj_summed,
        up_summed,
        down_summed,
    )


def solution(mesh):
    shape = mesh.devices.shape
    high_bits = tuple(f"u{place}" for place in range((shape[0] // 2).bit_length() - 1))
    dp, tensor = (*high_bits, "c"), ("zh", "zl")
    mesh = Mesh(mesh.devices.reshape((2,) * len(dp + tensor)), dp + tensor)

    def program(*arguments):
        return body(high_bits, *arguments)

    return jax.shard_map(
        program,
        mesh=mesh,
        in_specs=(
            P(dp, tensor, None),
            P(),
            P(None, None, tensor),
            P(tensor, None),
            P(),
            P(),
            P(None, None, tensor),
            P(None, tensor, None),
            P(dp, tensor, None),
            P(dp, None, None),
            P(dp, None),
            P(dp, None),
        ),
        out_specs=(
            P(dp, tensor, None),
            P(dp, tensor, None),
            P(dp + tensor),
            P(dp + tensor),
            P(None, dp + tensor),
            P(None, dp, tensor),
            P(tensor, dp),
            P(None, dp, tensor),
            P(None, tensor, dp),
        ),
        check_vma=False,
    )
```

time: 1280 us -> 724 us (0.57)
  matrix products: 396 us -> 11.9 us
  local copies, waits for them, and re-layouts: 244 us -> 30.9 us
  Pallas kernels: 0 us -> 203 us
  other arithmetic: 187 us -> 38.7 us
  waiting for transfers between devices: 254 us -> 357 us
  blocking collectives: 64.2 us -> 0 us
  starting transfers between devices: 84.9 us -> 60 us
  loops' own time: 24.1 us -> 0 us
    dot_general x54 -> x4, matrix products: 390 us -> 8.29 us  [the longest x2 4.57 us: matmul(): lax.dot_general(a, b, (dims, ((), ())), preferred_element_type=jnp.float32)]
    pallas_call x0 -> x5, Pallas kernels: none -> 203 us  [the longest x3 85.9 us: moe_call(): pl.pallas_call(kernel, grid_spec=pltpu.PrefetchScalarGridSpec(num_scalar_...]
    ppermute x28 -> x37, waiting for transfers between devices: 195 us -> 357 us  [flip(): return lax.ppermute(value, axis, [(0, 1), (1, 0)])]
    gather x6 -> x2, local copies, waits for them, and re-layouts: 95.9 us -> 1.29 us  [key_ranges(): own = jnp.maximum(shared, start[first] // block)]
    convert_element_type x16 -> x8, other arithmetic: 93.7 us -> 12.3 us  [the longest x4 6.46 us: scatter_blocks(): (far + across.astype(jnp.float32)).astype(own.dtype)]
    unnamed x8 -> x4, waiting for transfers between devices: 58.9 us -> 0.07 us
    while x14 -> x0, local copies, waits for them, and re-layouts: 42.9 us -> none
    unnamed x1 -> x0, blocking collectives: 41.9 us -> none
  transfers between devices with their start and end apart: 43 -> 49, of which waited for: 11 -> 19; matrix products, arithmetic and copies ran while one was open for 56% -> 10% of each run, Pallas kernels for 0% -> 21%
where the time goes in v2:
time: 724 us; the launch traced here: 717 us
  waiting for transfers between devices  357 us (49%)
  Pallas kernels  203 us (28%)
  starting transfers between devices  60 us (8%)
  other arithmetic  38.7 us (5%)
  local copies, waits for them, and re-layouts  30.9 us (4%)
  between operations  14.9 us (2%)
  matrix products  11.9 us (2%)
    ppermute x37, waiting for transfers between devices, flip(): return lax.ppermute(value, axis, [(0, 1), (1, 0)])  357 us
    pallas_call x3, Pallas kernels, moe_call(): pl.pallas_call(kernel, grid_spec=pltpu.PrefetchScalarGridSpec(num_scalar_...  85.9 us
    pallas_call x1, Pallas kernels, attention_backward(): pl.pallas_call(backward_kernel, grid_spec=pltpu.PrefetchScalarGridSpec(nu...  73.4 us
    ppermute x37, starting transfers between devices, flip(): return lax.ppermute(value, axis, [(0, 1), (1, 0)])  50.3 us
    pallas_call x1, Pallas kernels, attention_forward(): pl.pallas_call(forward_kernel, grid_spec=pltpu.PrefetchScalarGridSpec(num...  44.1 us
  transfers between devices with their start and end apart: 49, of which 19 were waited for; matrix products, arithmetic and copies ran while one was open for 10% of the time, Pallas kernels for 21%

profile of v2, /device:TPU:0, one launch (start us, length us, event | category | flops | bytes accessed | tf_op | source)
XLA Modules:
  0.0 717.0 jit_solution(15639133692887752325)
XLA Ops:
  10.6 4.1 collective-permute-start.5
  16.4 20.1 %collective-permute-done.5 = bf16[384,192]{1,0:T(8,128)(2,1)S(1)} collective-permute-done((bf16[384,192]{1,0:T(8,128)(2,1)S(1)}, bf16[384,192]{1,0:T(8,128)(2,1)S(1)}, u32[]{:S(2)}, u32[]{:S(2)}) %collective-permute-start.5) | collective-permute-done | bytes 147488 | tf_op jit(solution)/shard_map/ppermute | solution.py:677
  39.8 11.8 %collective-permute-start.13 = (bf16[384,768]{1,0:T(8,128)(2,1)S(1)}, bf16[384,768]{1,0:T(8,128)(2,1)S(1)}, u32[]{:S(2)}, u32[]{:S(2)}) collective-permute-start(bf16[384,768]{1,0:T(8,128)(2,1)S(1)} %constant_dynamic-slice_fusion.15), channel_id=1, source_target_pairs={{0,2},{2,0},{1,3},{3,1},{4,6},{6,4},{5,7},{7,5},{8,10},{10,8},{9,1... | collective-permute-start | bytes 1769480 | tf_op jit(solution)/shard_map/ppermute | solution.py:677
  51.6 24.5 %collective-permute-done.13 = bf16[384,768]{1,0:T(8,128)(2,1)S(1)} collective-permute-done((bf16[384,768]{1,0:T(8,128)(2,1)S(1)}, bf16[384,768]{1,0:T(8,128)(2,1)S(1)}, u32[]{:S(2)}, u32[]{:S(2)}) %collective-permute-start.13) | collective-permute-done | bytes 589856 | tf_op jit(solution)/shard_map/ppermute | solution.py:677
  77.1 2.2 collective-permute-start.1
  84.3 26.2 %collective-permute-done.3.x2 = bf16[768,768]{1,0:T(8,128)(2,1)} collective-permute-done((bf16[768,768]{1,0:T(8,128)(2,1)}, bf16[768,768]{1,0:T(8,128)(2,1)}, u32[]{:S(2)}, u32[]{:S(2)}) %collective-permute-start.3) | collective-permute-done | bytes 1179680 | tf_op jit(solution)/shard_map/ppermute | solution.py:677
  114.4 1.9 constant_dynamic-slice_fusion.14
  116.3 2.4 collective-permute-start.14
  121.3 44.1 %attention_forward.1 = (bf16[768,768]{1,0:T(8,128)(2,1)}, bf16[768,768]{1,0:T(8,128)(2,1)}, bf16[768,768]{1,0:T(8,128)(2,1)}, bf16[768,768]{1,0:T(8,128)(2,1)}, ...) custom-call(s32[5,6]{1,0:T(8,128)} %stack.33.ranges, ...), custom_call_target="tpu_custom_call" | custom-call | flops 28991029248 | bytes 41943040 | tf_op jit(solution)/shard_map/attention_forward/pallas_call | solution.py:191
  170.7 1.9 add_convert_fusion.6
  172.6 1.9 collective-permute-start.8
  175.4 25.7 %collective-permute-done.8 = bf16[768,768]{1,0:T(8,128)(2,1)} collective-permute-done((bf16[768,768]{1,0:T(8,128)(2,1)S(1)}, bf16[768,768]{1,0:T(8,128)(2,1)}, u32[]{:S(2)}, u32[]{:S(2)}) %collective-permute-start.8) | collective-permute-done | bytes 1179680 | tf_op jit(solution)/shard_map/ppermute | solution.py:677
  201.1 2.8 fusion.62
  204.7 2.2 fusion.16
  208.2 1.8 collective-permute-start.11
  212.0 38.4 %collective-permute-done.11.x2 = bf16[832,768]{1,0:T(8,128)(2,1)S(1)} collective-permute-done((bf16[832,768]{1,0:T(8,128)(2,1)S(1)}, bf16[832,768]{1,0:T(8,128)(2,1)S(1)}, u32[]{:S(2)}, u32[]{:S(2)}) %collective-permute-start.11) | collective-permute-done | bytes 1277984 | tf_op jit(solution)/shard_map/ppermute | solution.py:677
  250.4 1.9 convert_reduce_fusion
  252.5 2.5 fusion.21.d0
  257.6 29.3 %collective-permute-done.20.d2 = bf16[832,768]{1,0:T(8,128)(2,1)} collective-permute-done((bf16[832,768]{1,0:T(8,128)(2,1)}, bf16[832,768]{1,0:T(8,128)(2,1)}, u32[]{:S(2)}, u32[]{:S(2)}) %collective-permute-start.20) | collective-permute-done | bytes 1277984 | tf_op jit(solution)/shard_map/ppermute | solution.py:677
  287.4 31.7 %moe_forward.1 = (bf16[832,768]{1,0:T(8,128)(2,1)}, bf16[832,768]{1,0:T(8,128)(2,1)}, bf16[832,768]{1,0:T(8,128)(2,1)}, bf16[832,768]{1,0:T(8,128)(2,1)}, bf16[4...) custom-call(s32[33]{0:T(128)} %concatenate.18.table, bf16[832,768]{1,0:T(8,128)(2,1)} %copy-done.29, ...), custom_call_target="tpu_custom_call" | custom-call | flops 9814671360 | bytes 41943040 | tf_op jit(solution)/shard_map/moe_forward/pallas_call | solution.py:609
  319.2 28.1 %moe_backward.1 = (bf16[832,768]{1,0:T(8,128)(2,1)}, bf16[832,768]{1,0:T(8,128)(2,1)}, bf16[832,768]{1,0:T(8,128)(2,1)}, bf16[832,768]{1,0:T(8,128)(2,1)}, bf16[4,1088,768]{2,1,0:T(8,128)(2,1)}) custom-call(s32[33]{0:T(128)} %concatenate.18.table, bf16[832,768]{1,0:T(8,128)(2,1)} %fusion.21.d0, bf16[832,768]{1,0:T(8,128)(2,1)} %collective-permute-done.19.d1, ...), custom_call_target="tpu_custom_call" | custom-call | flops 9814671360 | bytes 41943040 | tf_op jit(solution)/shard_map/moe_backward/pallas_call | solution.py:609
  347.3 26.0 %moe_weights.1 = bf16[2,4,768,768]{3,2,1,0:T(8,128)(2,1)} custom-call(s32[33]{0:T(128)} %concatenate.18.table, bf16[832,768]{1,0:T(8,128)(2,1)} %copy-done.29, bf16[832,768]{1,0:T(8,128)(2,1)} %copy-done.31, bf16[832,768]{1,0:T(8,128)(2,1)} %copy-done.30, bf16[832,768]{1,0:T(8,128)(2,1)} %copy-done.32, bf16[832,768]{1,0:T(8,128)(2,1)} %fusion.21.d0, ...), custom_call_target="tpu_custom_call" | custom-call | flops 9814671360 | bytes 41943040 | tf_op jit(solution)/shard_map/moe_weights/pallas_call | solution.py:609
  374.5 2.3 collective-permute-done.16
  379.3 1.7 collective-permute-start.24
  381.0 28.4 %collective-permute-done.17 = bf16[832,768]{1,0:T(8,128)(2,1)S(1)} collective-permute-done((bf16[832,768]{1,0:T(8,128)(2,1)S(1)}, bf16[832,768]{1,0:T(8,128)(2,1)S(1)}, u32[]{:S(2)}, u32[]{:S(2)}) %collective-permute-start.17) | collective-permute-done | bytes 1277984 | tf_op jit(solution)/shard_map/ppermute | solution.py:677
  409.4 1.9 fusion.19
  411.3 24.9 %collective-permute-done.24 = bf16[832,768]{1,0:T(8,128)(2,1)S(1)} collective-permute-done((bf16[832,768]{1,0:T(8,128)(2,1)S(1)}, bf16[832,768]{1,0:T(8,128)(2,1)S(1)}, u32[]{:S(2)}, u32[]{:S(2)}) %collective-permute-start.24) | collective-permute-done | bytes 1277984 | tf_op jit(solution)/shard_map/ppermute | solution.py:677
  436.3 2.7 multiply_reduce_fusion
  439.0 2.8 fusion.61
  442.1 27.5 %collective-permute-done.26.g2 = bf16[768,768]{1,0:T(8,128)(2,1)} collective-permute-done((bf16[768,768]{1,0:T(8,128)(2,1)}, bf16[768,768]{1,0:T(8,128)(2,1)}, u32[]{:S(2)}, u32[]{:S(2)}) %collective-permute-start.26) | collective-permute-done | bytes 1179680 | tf_op jit(solution)/shard_map/ppermute | solution.py:677
  477.5 73.4 %attention_backward.1 = (bf16[768,768]{1,0:T(8,128)(2,1)}, bf16[768,768]{1,0:T(8,128)(2,1)}, bf16[768,768]{1,0:T(8,128)(2,1)}, bf16[768,768]{1,0:T(8,128)(2,1)}, bf16[4,768,192]{2,1,0:T(8,128)(2,1)}) custom-call(s32[5,12]{1,0:T(8,128)} %stack.39.ranges, s32[4]{0:T(128)} %pad_add_fusion.1.ranks, bf16[768,768]{1,0:T(8,128)(2,1)} %get-tuple-element.124.g0, ...), custom_call_target="tpu_custom_call" | custom-call | flops 65229815808 | bytes 41943040 | tf_op jit(solution)/shard_map/attention_backward/pallas_call | solution.py:360
  551.6 2.2 collective-permute-done.40
  555.6 2.8 collective-permute-done.41
  562.9 10.2 %collective-permute-start.28 = (bf16[768,768]{1,0:T(8,128)(2,1)}, bf16[768,768]{1,0:T(8,128)(2,1)S(1)}, u32[]{:S(2)}, u32[]{:S(2)}) collective-permute-start(bf16[768,768]{1,0:T(8,128)(2,1)} %get-tuple-element.73), channel_id=1, source_target_pairs={{0,4},{4,0},{1,5},{5,1},{2,6},{6,2},{3,7},{7,3},{8,12},{12,8},{9,1... | collective-permute-start | bytes 3538952 | tf_op jit(solution)/shard_map/ppermute | solution.py:677
  573.0 2.6 add_convert_fusion.4
  575.7 2.5 collective-permute-start.30
  578.7 2.2 copy.55
  582.7 2.5 select_bitcast_fusion.1
  585.2 8.2 %collective-permute-done.33 = bf16[4,192,192]{2,1,0:T(8,128)(2,1)S(1)} collective-permute-done((bf16[4,192,192]{2,1,0:T(8,128)(2,1)S(1)}, bf16[4,192,192]{2,1,0:T(8,128)(2,1)S(1)}, u32[]{:S(2)}, u32[]{:S(2)}) %collective-permute-start.33) | collective-permute-done | bytes 294944 | tf_op jit(solution)/shard_map/ppermute | solution.py:677
  594.3 20.7 %collective-permute-done.30 = bf16[768,768]{1,0:T(8,128)(2,1)S(1)} collective-permute-done((bf16[768,768]{1,0:T(8,128)(2,1)}, bf16[768,768]{1,0:T(8,128)(2,1)S(1)}, u32[]{:S(2)}, u32[]{:S(2)}) %collective-permute-start.30) | collective-permute-done | bytes 1179680 | tf_op jit(solution)/shard_map/ppermute | solution.py:677
  617.1 2.5 fusion.14
  619.6 1.7 collective-permute-start.31
  621.4 2.8 constant_dynamic-slice_fusion.1
  626.8 1.8 multiply_reduce_fusion.4
  628.6 2.8 collective-permute-start.36
  631.4 69.8 %collective-permute-done.36 = f32[48]{0:T(128)S(1)} collective-permute-done((f32[48]{0:T(128)S(1)}, f32[48]{0:T(128)S(1)}, u32[]{:S(2)}, u32[]{:S(2)}) %collective-permute-start.36) | collective-permute-done | bytes 224 | tf_op jit(solution)/shard_map/ppermute | solution.py:677
  702.2 2.8 collective-permute-done.37
  706.8 1.8 convert_add_fusion.2
  (243 shorter events, 65.2 us)
Async XLA Ops:
  7.2 111.5 %all-gather.4.cloned.1.call-start = ((), (), s32[]{:S(2)}) async-start(), calls=%async_computation.1 | async-start | bytes 1769472 | tf_op jit(solution)/shard_map/all_gather | solution.py:715
  10.6 25.9 %collective-permute-start.5 = (bf16[384,192]{1,0:T(8,128)(2,1)S(1)}, bf16[384,192]{1,0:T(8,128)(2,1)S(1)}, u32[]{:S(2)}, u32[]{:S(2)}) collective-permute-start(bf16[384,192]{1,0:T(8,128)(2,1)S(1)} %constant_dynamic-slice_fusion.26), channel_id=1, source_target_pairs={{0,2},{2,0},{1,3},{3,1},{4,6},{6,4},{5,7},{7,5},{8,10},{10,8},{9,1... | collective-permute-start | bytes 442376 | tf_op jit(solution)/shard_map/ppermute | solution.py:677
  14.7 22.6 %collective-permute-start = (bf16[768,768]{1,0:T(8,128)(2,1)S(1)}, bf16[768,768]{1,0:T(8,128)(2,1)}, u32[]{:S(2)}, u32[]{:S(2)}) collective-permute-start(bf16[768,768]{1,0:T(8,128)(2,1)S(1)} %bitcast.85), channel_id=1, source_target_pairs={{2,4},{4,2},{3,5},{5,3},{10,12},{12,10},{11,13},{13,11},{18,20},{2... | collective-permute-start | bytes 3538952 | tf_op jit(solution)/shard_map/ppermute | solution.py:672
  37.1 250.3 %all-gather.6.cloned.1.call-start = ((), (), s32[]{:S(2)}) async-start(), calls=%async_computation.2 | async-start | bytes 5308416 | tf_op jit(solution)/shard_map/all_gather | solution.py:715
  39.8 36.3 %collective-permute-start.13 = (bf16[384,768]{1,0:T(8,128)(2,1)S(1)}, bf16[384,768]{1,0:T(8,128)(2,1)S(1)}, u32[]{:S(2)}, u32[]{:S(2)}) collective-permute-start(bf16[384,768]{1,0:T(8,128)(2,1)S(1)} %constant_dynamic-slice_fusion.15), channel_id=1, source_target_pairs={{0,2},{2,0},{1,3},{3,1},{4,6},{6,4},{5,7},{7,5},{8,10},{10,8},{9,1... | collective-permute-start | bytes 1769480 | tf_op jit(solution)/shard_map/ppermute | solution.py:677
  77.0 210.5 %all-gather.8.cloned.1.call-start = ((), (), s32[]{:S(2)}) async-start(), calls=%async_computation.3 | async-start | bytes 5308416 | tf_op jit(solution)/shard_map/all_gather | solution.py:715
  77.1 5.4 collective-permute-start.1
  82.2 28.2 %collective-permute-start.3 = (bf16[768,768]{1,0:T(8,128)(2,1)}, bf16[768,768]{1,0:T(8,128)(2,1)}, u32[]{:S(2)}, u32[]{:S(2)}) collective-permute-start(bf16[768,768]{1,0:T(8,128)(2,1)} %fusion.9.x0), channel_id=1, source_target_pairs={{0,1},{1,0},{2,3},{3,2},{4,5},{5,4},{6,7},{7,6},{8,9},{9,8},{10,11... | collective-permute-start | bytes 3538952 | tf_op jit(solution)/shard_map/ppermute | solution.py:677
  84.0 37.3 %collective-permute-start.2 = (bf16[768,768]{1,0:T(8,128)(2,1)}, bf16[768,768]{1,0:T(8,128)(2,1)}, u32[]{:S(2)}, u32[]{:S(2)}) collective-permute-start(bf16[768,768]{1,0:T(8,128)(2,1)} %fusion.9.x0), channel_id=1, source_target_pairs={{0,4},{4,0},{1,5},{5,1},{2,6},{6,2},{3,7},{7,3},{8,12},{12,8},{9,1... | collective-permute-start | bytes 3538952 | tf_op jit(solution)/shard_map/ppermute | solution.py:677
  110.4 10.9 %collective-permute-start.4 = (bf16[768,768]{1,0:T(8,128)(2,1)}, bf16[768,768]{1,0:T(8,128)(2,1)}, u32[]{:S(2)}, u32[]{:S(2)}) collective-permute-start(bf16[768,768]{1,0:T(8,128)(2,1)} %collective-permute-done.3.x2), channel_id=1, source_target_pairs={{0,4},{4,0},{1,5},{5,1},{2,6},{6,2},{3,7},{7,3},{8,12},{12,8},{9,1... | collective-permute-start | bytes 3538952 | tf_op jit(solution)/shard_map/ppermute | solution.py:677
  116.3 50.7 %collective-permute-start.14 = (bf16[384,768]{1,0:T(8,128)(2,1)}, bf16[384,768]{1,0:T(8,128)(2,1)S(1)}, u32[]{:S(2)}, u32[]{:S(2)}) collective-permute-start(bf16[384,768]{1,0:T(8,128)(2,1)} %constant_dynamic-slice_fusion.14), channel_id=1, source_target_pairs={{0,2},{2,0},{1,3},{3,1},{4,6},{6,4},{5,7},{7,5},{8,10},{10,8},{9,1... | collective-permute-start | bytes 1769480 | tf_op jit(solution)/shard_map/ppermute | solution.py:677
  165.4 4.4 collective-permute-start.7
  167.9 453.5 %reduce-scatter.2.cloned.1.call-start = ((), (), s32[]{:S(2)}) async-start(), calls=%async_computation.4 | async-start | bytes 11796480 | tf_op jit(solution)/shard_map/reduce_scatter | solution.py:809
  168.4 7.0 collective-permute-start.6
  172.6 28.4 %collective-permute-start.8 = (bf16[768,768]{1,0:T(8,128)(2,1)S(1)}, bf16[768,768]{1,0:T(8,128)(2,1)}, u32[]{:S(2)}, u32[]{:S(2)}) collective-permute-start(bf16[768,768]{1,0:T(8,128)(2,1)S(1)} %add_convert_fusion.6), channel_id=1, source_target_pairs={{0,1},{1,0},{2,3},{3,2},{4,5},{5,4},{6,7},{7,6},{8,9},{9,8},{10,11... | collective-permute-start | bytes 3538952 | tf_op jit(solution)/shard_map/ppermute | solution.py:677
  208.2 42.3 %collective-permute-start.11 = (bf16[832,768]{1,0:T(8,128)(2,1)S(1)}, bf16[832,768]{1,0:T(8,128)(2,1)S(1)}, u32[]{:S(2)}, u32[]{:S(2)}) collective-permute-start(bf16[832,768]{1,0:T(8,128)(2,1)S(1)} %fusion.22.x0), channel_id=1, source_target_pairs={{0,1},{1,0},{2,3},{3,2},{4,5},{5,4},{6,7},{7,6},{8,9},{9,8},{10,11... | collective-permute-start | bytes 3833864 | tf_op jit(solution)/shard_map/ppermute | solution.py:677
  210.0 42.3 %collective-permute-start.9 = (bf16[768,768]{1,0:T(8,128)(2,1)S(1)}, bf16[768,768]{1,0:T(8,128)(2,1)S(1)}, u32[]{:S(2)}, u32[]{:S(2)}) collective-permute-start(bf16[768,768]{1,0:T(8,128)(2,1)S(1)} %bitcast.86), channel_id=1, source_target_pairs={{2,4},{4,2},{3,5},{5,3},{10,12},{12,10},{11,13},{13,11},{18,20},{2... | collective-permute-start | bytes 3538952 | tf_op jit(solution)/shard_map/ppermute | solution.py:672
  210.7 44.2 %collective-permute-start.10 = (bf16[832,768]{1,0:T(8,128)(2,1)S(1)}, bf16[832,768]{1,0:T(8,128)(2,1)S(1)}, u32[]{:S(2)}, u32[]{:S(2)}) collective-permute-start(bf16[832,768]{1,0:T(8,128)(2,1)S(1)} %fusion.22.x0), channel_id=1, source_target_pairs={{0,4},{4,0},{1,5},{5,1},{2,6},{6,2},{3,7},{7,3},{8,12},{12,8},{9,1... | collective-permute-start | bytes 3833864 | tf_op jit(solution)/shard_map/ppermute | solution.py:677
  250.4 4.5 collective-permute-start.12
  256.0 30.8 %collective-permute-start.20 = (bf16[832,768]{1,0:T(8,128)(2,1)}, bf16[832,768]{1,0:T(8,128)(2,1)}, u32[]{:S(2)}, u32[]{:S(2)}) collective-permute-start(bf16[832,768]{1,0:T(8,128)(2,1)} %fusion.21.d0), channel_id=1, source_target_pairs={{0,1},{1,0},{2,3},{3,2},{4,5},{5,4},{6,7},{7,6},{8,9},{9,8},{10,11... | collective-permute-start | bytes 3833864 | tf_op jit(solution)/shard_map/ppermute | solution.py:677
  257.0 62.1 %collective-permute-start.19 = (bf16[832,768]{1,0:T(8,128)(2,1)}, bf16[832,768]{1,0:T(8,128)(2,1)}, u32[]{:S(2)}, u32[]{:S(2)}) collective-permute-start(bf16[832,768]{1,0:T(8,128)(2,1)} %fusion.21.d0), channel_id=1, source_target_pairs={{0,4},{4,0},{1,5},{5,1},{2,6},{6,2},{3,7},{7,3},{8,12},{12,8},{9,1... | collective-permute-start | bytes 3833864 | tf_op jit(solution)/shard_map/ppermute | solution.py:677
  286.8 32.4 %collective-permute-start.21 = (bf16[832,768]{1,0:T(8,128)(2,1)}, bf16[832,768]{1,0:T(8,128)(2,1)}, u32[]{:S(2)}, u32[]{:S(2)}) collective-permute-start(bf16[832,768]{1,0:T(8,128)(2,1)} %collective-permute-done.20.d2), channel_id=1, source_target_pairs={{0,4},{4,0},{1,5},{5,1},{2,6},{6,2},{3,7},{7,3},{8,12},{12,8},{9,1... | collective-permute-start | bytes 3833864 | tf_op jit(solution)/shard_map/ppermute | solution.py:677
  373.4 3.4 collective-permute-start.16
  374.0 5.0 collective-permute-start.23
  374.1 7.0 collective-permute-start.15
  378.4 31.0 %collective-permute-start.17 = (bf16[832,768]{1,0:T(8,128)(2,1)S(1)}, bf16[832,768]{1,0:T(8,128)(2,1)S(1)}, u32[]{:S(2)}, u32[]{:S(2)}) collective-permute-start(bf16[832,768]{1,0:T(8,128)(2,1)S(1)} %add_convert_fusion.3), channel_id=1, source_target_pairs={{0,1},{1,0},{2,3},{3,2},{4,5},{5,4},{6,7},{7,6},{8,9},{9,8},{10,11... | collective-permute-start | bytes 3833864 | tf_op jit(solution)/shard_map/ppermute | solution.py:677
  378.8 32.5 %collective-permute-start.22 = (bf16[832,768]{1,0:T(8,128)(2,1)S(1)}, bf16[832,768]{1,0:T(8,128)(2,1)S(1)}, u32[]{:S(2)}, u32[]{:S(2)}) collective-permute-start(bf16[832,768]{1,0:T(8,128)(2,1)S(1)} %copy-done.33), channel_id=1, source_target_pairs={{0,4},{4,0},{1,5},{5,1},{2,6},{6,2},{3,7},{7,3},{8,12},{12,8},{9,1... | collective-permute-start | bytes 3833864 | tf_op jit(solution)/shard_map/ppermute | solution.py:677
  379.3 57.0 %collective-permute-start.24 = (bf16[832,768]{1,0:T(8,128)(2,1)S(1)}, bf16[832,768]{1,0:T(8,128)(2,1)S(1)}, u32[]{:S(2)}, u32[]{:S(2)}) collective-permute-start(bf16[832,768]{1,0:T(8,128)(2,1)S(1)} %add_convert_fusion.1), channel_id=1, source_target_pairs={{0,1},{1,0},{2,3},{3,2},{4,5},{5,4},{6,7},{7,6},{8,9},{9,8},{10,11... | collective-permute-start | bytes 3833864 | tf_op jit(solution)/shard_map/ppermute | solution.py:677
  441.8 27.7 %collective-permute-start.26 = (bf16[768,768]{1,0:T(8,128)(2,1)}, bf16[768,768]{1,0:T(8,128)(2,1)}, u32[]{:S(2)}, u32[]{:S(2)}) collective-permute-start(bf16[768,768]{1,0:T(8,128)(2,1)} %get-tuple-element.124.g0), channel_id=1, source_target_pairs={{0,1},{1,0},{2,3},{3,2},{4,5},{5,4},{6,7},{7,6},{8,9},{9,8},{10,11... | collective-permute-start | bytes 3538952 | tf_op jit(solution)/shard_map/ppermute | solution.py:677
  442.1 35.4 %collective-permute-start.25 = (bf16[768,768]{1,0:T(8,128)(2,1)}, bf16[768,768]{1,0:T(8,128)(2,1)}, u32[]{:S(2)}, u32[]{:S(2)}) collective-permute-start(bf16[768,768]{1,0:T(8,128)(2,1)} %get-tuple-element.124.g0), channel_id=1, source_target_pairs={{0,4},{4,0},{1,5},{5,1},{2,6},{6,2},{3,7},{7,3},{8,12},{12,8},{9,1... | collective-permute-start | bytes 3538952 | tf_op jit(solution)/shard_map/ppermute | solution.py:677
  469.5 8.0 %collective-permute-start.27 = (bf16[768,768]{1,0:T(8,128)(2,1)}, bf16[768,768]{1,0:T(8,128)(2,1)}, u32[]{:S(2)}, u32[]{:S(2)}) collective-permute-start(bf16[768,768]{1,0:T(8,128)(2,1)} %collective-permute-done.26.g2), channel_id=1, source_target_pairs={{0,4},{4,0},{1,5},{5,1},{2,6},{6,2},{3,7},{7,3},{8,12},{12,8},{9,1... | collective-permute-start | bytes 3538952 | tf_op jit(solution)/shard_map/ppermute | solution.py:677
  472.4 3.7 collective-permute-start.38
  476.2 74.7 %collective-permute-start.39 = (f32[5,192]{1,0:T(8,128)S(1)}, f32[5,192]{1,0:T(8,128)S(1)}, u32[]{:S(2)}, u32[]{:S(2)}) collective-permute-start(f32[5,192]{1,0:T(8,128)S(1)} %constant_dynamic-slice_fusion.8), channel_id=1, source_target_pairs={{0,8},{8,0},{1,9},{9,1},{2,10},{10,2},{3,11},{11,3},{4,12},{12,4},... | collective-permute-start | bytes 11528 | tf_op jit(solution)/shard_map/ppermute | solution.py:677
  550.9 22.2 %collective-permute-start.29 = (bf16[768,768]{1,0:T(8,128)(2,1)}, bf16[768,768]{1,0:T(8,128)(2,1)}, u32[]{:S(2)}, u32[]{:S(2)}) collective-permute-start(bf16[768,768]{1,0:T(8,128)(2,1)} %get-tuple-element.74), channel_id=1, source_target_pairs={{0,4},{4,0},{1,5},{5,1},{2,6},{6,2},{3,7},{7,3},{8,12},{12,8},{9,1... | collective-permute-start | bytes 3538952 | tf_op jit(solution)/shard_map/ppermute | solution.py:677
  553.9 4.5 collective-permute-start.41
  553.9 28.7 %collective-permute-start.18 = (bf16[768,768]{1,0:T(8,128)(2,1)}, bf16[768,768]{1,0:T(8,128)(2,1)}, u32[]{:S(2)}, u32[]{:S(2)}) collective-permute-start(bf16[768,768]{1,0:T(8,128)(2,1)} %get-tuple-element.136), channel_id=1, source_target_pairs={{2,4},{4,2},{3,5},{5,3},{10,12},{12,10},{11,13},{13,11},{18,20},{2... | collective-permute-start | bytes 3538952 | tf_op jit(solution)/shard_map/ppermute | solution.py:672
  558.6 3.6 collective-permute-start.42
  561.2 17.5 %collective-permute-start.32 = (bf16[4,384,192]{1,2,0:T(8,128)(2,1)}, bf16[4,384,192]{1,2,0:T(8,128)(2,1)}, u32[]{:S(2)}, u32[]{:S(2)}) collective-permute-start(bf16[4,384,192]{1,2,0:T(8,128)(2,1)} %copy.54), channel_id=1, source_target_pairs={{0,16},{16,0},{1,17},{17,1},{2,18},{18,2},{3,19},{19,3},{4,20},{20... | collective-permute-start | bytes 1769480 | tf_op jit(solution)/shard_map/ppermute | solution.py:677
  562.9 31.4 %collective-permute-start.28 = (bf16[768,768]{1,0:T(8,128)(2,1)}, bf16[768,768]{1,0:T(8,128)(2,1)S(1)}, u32[]{:S(2)}, u32[]{:S(2)}) collective-permute-start(bf16[768,768]{1,0:T(8,128)(2,1)} %get-tuple-element.73), channel_id=1, source_target_pairs={{0,4},{4,0},{1,5},{5,1},{2,6},{6,2},{3,7},{7,3},{8,12},{12,8},{9,1... | collective-permute-start | bytes 3538952 | tf_op jit(solution)/shard_map/ppermute | solution.py:677
  575.7 39.4 %collective-permute-start.30 = (bf16[768,768]{1,0:T(8,128)(2,1)}, bf16[768,768]{1,0:T(8,128)(2,1)S(1)}, u32[]{:S(2)}, u32[]{:S(2)}) collective-permute-start(bf16[768,768]{1,0:T(8,128)(2,1)} %add_convert_fusion.4), channel_id=1, source_target_pairs={{0,1},{1,0},{2,3},{3,2},{4,5},{5,4},{6,7},{7,6},{8,9},{9,8},{10,11... | collective-permute-start | bytes 3538952 | tf_op jit(solution)/shard_map/ppermute | solution.py:677
  582.6 10.8 %collective-permute-start.33 = (bf16[4,192,192]{2,1,0:T(8,128)(2,1)S(1)}, bf16[4,192,192]{2,1,0:T(8,128)(2,1)S(1)}, u32[]{:S(2)}, u32[]{:S(2)}) collective-permute-start(bf16[4,192,192]{2,1,0:T(8,128)(2,1)S(1)} %constant_dynamic-slice_fusion.12), channel_id=1, source_target_pairs={{0,8},{8,0},{1,9},{9,1},{2,10},{10,2},{3,11},{11,3},{4,12},{12,4},... | collective-permute-start | bytes 884744 | tf_op jit(solution)/shard_map/ppermute | solution.py:677
  593.5 27.8 %collective-permute-start.35 = (bf16[4,96,192]{2,1,0:T(8,128)(2,1)S(1)}, bf16[4,96,192]{2,1,0:T(8,128)(2,1)S(1)}, u32[]{:S(2)}, u32[]{:S(2)}) collective-permute-start(bf16[4,96,192]{2,1,0:T(8,128)(2,1)S(1)} %get-tuple-element.138), channel_id=1, source_target_pairs={{0,4},{2,0},{4,6},{6,2},{1,5},{3,1},{5,7},{7,3},{8,12},{10,8},{12,... | collective-permute-start | bytes 442376 | tf_op jit(solution)/shard_map/ppermute | solution.py:706
  593.6 27.7 %collective-permute-start.34 = (bf16[4,96,192]{2,1,0:T(8,128)(2,1)S(1)}, bf16[4,96,192]{2,1,0:T(8,128)(2,1)S(1)}, u32[]{:S(2)}, u32[]{:S(2)}) collective-permute-start(bf16[4,96,192]{2,1,0:T(8,128)(2,1)S(1)} %get-tuple-element.137), channel_id=1, source_target_pairs={{2,4},{4,2},{3,5},{5,3},{10,12},{12,10},{11,13},{13,11},{18,20},{2... | collective-permute-start | bytes 442376 | tf_op jit(solution)/shard_map/ppermute | solution.py:672
  619.6 85.9 %collective-permute-start.31 = (bf16[768,768]{1,0:T(8,128)(2,1)S(1)}, bf16[768,768]{1,0:T(8,128)(2,1)}, u32[]{:S(2)}, u32[]{:S(2)}) collective-permute-start(bf16[768,768]{1,0:T(8,128)(2,1)S(1)} %fusion.14), channel_id=1, source_target_pairs={{2,4},{4,2},{3,5},{5,3},{10,12},{12,10},{11,13},{13,11},{18,20},{2... | collective-permute-start | bytes 3538952 | tf_op jit(solution)/shard_map/ppermute | solution.py:672
  624.2 82.5 %collective-permute-start.44 = (bf16[2,4,96,768]{3,2,1,0:T(8,128)(2,1)}, bf16[2,4,96,768]{3,2,1,0:T(8,128)(2,1)}, u32[]{:S(2)}, u32[]{:S(2)}) collective-permute-start(bf16[2,4,96,768]{3,2,1,0:T(8,128)(2,1)} %get-tuple-element.135), channel_id=1, source_target_pairs={{0,4},{2,0},{4,6},{6,2},{1,5},{3,1},{5,7},{7,3},{8,12},{10,8},{12,... | collective-permute-start | bytes 3538952 | tf_op jit(solution)/shard_map/ppermute | solution.py:706
  625.1 81.6 %collective-permute-start.43 = (bf16[2,4,96,768]{3,2,1,0:T(8,128)(2,1)S(1)}, bf16[2,4,96,768]{3,2,1,0:T(8,128)(2,1)}, u32[]{:S(2)}, u32[]{:S(2)}) collective-permute-start(bf16[2,4,96,768]{3,2,1,0:T(8,128)(2,1)S(1)} %get-tuple-element.134), channel_id=1, source_target_pairs={{2,4},{4,2},{3,5},{5,3},{10,12},{12,10},{11,13},{13,11},{18,20},{2... | collective-permute-start | bytes 3538952 | tf_op jit(solution)/shard_map/ppermute | solution.py:672
  628.6 72.6 %collective-permute-start.36 = (f32[48]{0:T(128)S(1)}, f32[48]{0:T(128)S(1)}, u32[]{:S(2)}, u32[]{:S(2)}) collective-permute-start(f32[48]{0:T(128)S(1)} %dynamic_slice.133), channel_id=1, source_target_pairs={{0,2},{2,0},{1,3},{3,1},{4,6},{6,4},{5,7},{7,5},{8,10},{10,8},{9,1... | collective-permute-start | bytes 584 | tf_op jit(solution)/shard_map/ppermute | solution.py:677
  701.4 3.5 collective-permute-start.37
  (37 other events, 858.7 us)
Sparse Core Ops, SparseCore 0:
  37.3 26.9 all-gather.3
  77.1 41.7 all-gather.5
  168.0 38.3 all-gather.7
  373.5 93.4 reduce-scatter.1

commit v3 on v2

--- a/solution.py
+++ b/solution.py
@@ -13,6 +13,7 @@
 NEGATIVE = -1e30
 TILE = 256
 ALIGN = 16
+CONTINUATIONS = 8
 HBM = pl.BlockSpec(memory_space=pl.ANY)
 
 epsilon = 1e-05
@@ -38,14 +39,14 @@
 
 def key_ranges(segment, block):
     token_count = segment.shape[0]
-    position = jnp.arange(token_count, dtype=jnp.int32)
-    prompt = jnp.sum((segment == 0).astype(jnp.int32))
-    fresh = jnp.concatenate([jnp.ones((1,), jnp.bool_), segment[1:] != segment[:-1]])
-    start = lax.cummax(jnp.where(fresh, position, 0), axis=0)
+    numbers = jnp.arange(1, CONTINUATIONS + 1, dtype=jnp.int32)[:, None]
+    earlier = jnp.sum((segment[None, :] < numbers).astype(jnp.int32), axis=1, keepdims=True)
+    prompt = earlier[0, 0]
+    start = jnp.sum(jnp.where(segment[None, :] == numbers, earlier, 0), axis=0)
     first = jnp.arange(token_count // block, dtype=jnp.int32) * block
     whole = jnp.minimum(prompt, first) // block
     shared = (jnp.minimum(prompt, first + block) + block - 1) // block
-    own = jnp.maximum(shared, start[first] // block)
+    own = jnp.maximum(shared, start.reshape(-1, block)[:, 0] // block)
     last = first // block + 1
     return (jnp.stack([whole, shared, own, last, jnp.full_like(whole, prompt)]), start[None, :])
 
@@ -564,39 +565,29 @@
 
 
 def moe_weights_kernel(
-    table, x0, x1, x2, x3, d0, d1, d2, d3, hidden_in, grad_in,
-    out_ref,
-    x_ref, d_ref, hidden_ref, grad_ref, up_sum, down_sum, semaphores,
+    table, a0, a1, a2, a3, b_in, out_ref, a_ref, b_ref, sum_ref, semaphores
 ):
     expert = pl.program_id(0)
     experts = pl.num_programs(0)
-    count = x0.shape[0]
+    count = a0.shape[0]
 
     @pl.when(expert == 0)
     def _():
-        for ref in (x_ref, d_ref):
-            ref[:, count:, :] = jnp.zeros((4, TILE, ref.shape[2]), jnp.bfloat16)
+        a_ref[:, count:, :] = jnp.zeros((4, TILE, a_ref.shape[2]), jnp.bfloat16)
         copies(
-            [(x, x_ref.at[b, :count]) for b, x in enumerate((x0, x1, x2, x3))]
-            + [(d, d_ref.at[b, :count]) for b, d in enumerate((d0, d1, d2, d3))]
-            + [(hidden_in, hidden_ref), (grad_in, grad_ref)],
+            [(a, a_ref.at[b, :count]) for b, a in enumerate((a0, a1, a2, a3))] + [(b_in, b_ref)],
             semaphores,
         )
 
-    up_sum[...] = jnp.zeros_like(up_sum)
-    down_sum[...] = jnp.zeros_like(down_sum)
+    sum_ref[...] = jnp.zeros_like(sum_ref)
 
     def visit(block, place, left):
-        up_sum[...] += matmul(
-            x_ref[block, place, :], within(grad_ref[block, place, :], left), ((0,), (0,))
+        sum_ref[...] += matmul(
+            within(a_ref[block, place, :], left), b_ref[block, place, :], ((0,), (0,))
         )
-        down_sum[...] += matmul(
-            within(d_ref[block, place, :], left), hidden_ref[block, place, :], ((0,), (0,))
-        )
 
     each_tile(table, expert, experts, visit)
-    out_ref[0, 0] = up_sum[...].astype(jnp.bfloat16)
-    out_ref[1, 0] = down_sum[...].astype(jnp.bfloat16)
+    out_ref[0] = sum_ref[...].astype(jnp.bfloat16)
 
 
 def moe_call(kernel, name, table, arrays, outs, scratch, sums, experts, cost):
@@ -604,7 +595,7 @@
     specs = [HBM] * len(outs)
     ready = [pltpu.SemaphoreType.DMA((2, experts))]
     if sums:
-        specs = [pl.BlockSpec((2, 1) + outs[0][2:], lambda e, t: (0, e, 0, 0))]
+        specs = [pl.BlockSpec((1,) + outs[0][1:], lambda e, t: (e, 0, 0))]
         ready = []
     return pl.pallas_call(
         kernel,
@@ -653,14 +644,13 @@
     return (y, grad)
 
 
-def moe_weights(table, x, d, hid, grad, experts):
-    count, width = x[0].shape
-    hidden = hid.shape[2]
-    wide, tall = (4, count + TILE, width), (4, count + TILE, hidden)
+def moe_weights(table, blocks, tall, experts):
+    count, width = blocks[0].shape
+    hidden = tall.shape[2]
     return moe_call(
-        moe_weights_kernel, "moe_weights", table, [*x, *d, hid, grad],
-        [(2, experts, width, hidden)], [wide, wide, tall, tall], [(width, hidden)] * 2, experts,
-        20 * count * width * hidden,
+        moe_weights_kernel, "moe_weights", table, [*blocks, tall], [(experts, width, hidden)],
+        [(4, count + TILE, width), tall.shape], [(width, hidden)], experts,
+        10 * count * width * hidden,
     )[0]
 
 
@@ -677,16 +667,32 @@
     return lax.ppermute(value, axis, [(0, 1), (1, 0)])
 
 
+def flip_some(value, home):
+    moves = [(0, 1), (1, 0), (6, 7), (7, 6)] if home else [(2, 3), (3, 2), (4, 5), (5, 4)]
+    return lax.ppermute(value, ("c", "zh", "zl"), moves)
+
+
+def tie(*values):
+    return lax.optimization_barrier(values)
+
+
 def gather_blocks(rows):
     across = flip(rows, "zl")
     return [rows, flip(rows, "c"), across, flip(across, "c")]
 
 
+def far_rows(blocks):
+    return (
+        flip(blocks[3], "c").astype(jnp.float32) + blocks[2].astype(jnp.float32)
+    ).astype(blocks[2].dtype)
+
+
+def near_rows(blocks):
+    return blocks[0].astype(jnp.float32) + flip(blocks[1], "c").astype(jnp.float32)
+
+
 def scatter_blocks(blocks):
-    own, beside, across, corner = blocks
-    far = flip(corner, "c").astype(jnp.float32)
-    far = flip((far + across.astype(jnp.float32)).astype(own.dtype), "zl").astype(jnp.float32)
-    return own.astype(jnp.float32) + flip(beside, "c").astype(jnp.float32) + far
+    return near_rows(blocks) + flip(far_rows(blocks), "zl").astype(jnp.float32)
 
 
 def halve(value, axis, dimension):
@@ -698,21 +704,36 @@
     return total.astype(value.dtype)
 
 
-def sum_home(value, dimension):
+def send_home(value, dimension):
     count = value.shape[dimension] // 2
     high = lax.axis_index("zh")
     straight = lax.dynamic_slice_in_dim(value, high * count, count, dimension)
     turned = lax.dynamic_slice_in_dim(value, (1 - high) * count, count, dimension)
     turned = lax.ppermute(turned, ("c", "zh"), [(0, 2), (1, 0), (2, 3), (3, 1)])
-    return swap_roles(straight).astype(jnp.float32) + turned.astype(jnp.float32)
-
-
-def other_quarter(weight, users):
+    return [straight, lax.ppermute(straight, ("c", "zh"), [(1, 2), (2, 1)]), turned]
+
+
+def sum_home(straight, moved, turned):
+    straight = jnp.where(at_home(), straight, moved)
+    return straight.astype(jnp.float32) + turned.astype(jnp.float32)
+
+
+def piece_of(weight, users):
     flat = weight.reshape(-1, weight.shape[-1])
     part = flat.shape[0] // lax.axis_size(users)
-    piece = lax.dynamic_slice_in_dim(flat, lax.axis_index(users) * part, part, 0)
-    piece = flip(piece, "zh")
-    return lax.all_gather(piece, users, axis=0, tiled=True).reshape(weight.shape)
+    return lax.dynamic_slice_in_dim(flat, lax.axis_index(users) * part, part, 0)
+
+
+def share(piece, users, shape):
+    return lax.all_gather(piece, users, axis=0, tiled=True).reshape(shape)
+
+
+def share_small(piece, users, shape):
+    for bit in reversed(users):
+        given = flip(piece, bit)
+        low = lax.axis_index(bit) == 0
+        piece = jnp.concatenate([jnp.where(low, piece, given), jnp.where(low, given, piece)], axis=0)
+    return piece.reshape(shape)
 
 
 def body(
@@ -741,29 +762,57 @@
     ranks = jnp.stack(
         [2 * core + near, 2 * (1 - core) + near, 2 * core + 1 - near, 3 - 2 * core - near]
     )
+    home = at_home()
+    staying = block_input[0]
+    coming = lax.ppermute(staying, ("c", "zh"), [(1, 2), (2, 1)])
+    small = jnp.concatenate([qkv_weight, proj_weight.reshape(1, model_width, local_width)], axis=0)
+    small_piece = flip(piece_of(small, users), "zh")
+
+    def normed(rows):
+        return (normalize_plain(rows.astype(jnp.float32))[0] * attention_gain).astype(jnp.bfloat16)
+
+    normed_staying = normed(staying)
+    home_across = flip_some(normed_staying, True)
     indices = jnp.stack([routes[0, :, 0], priority[0], segments[0]])
-    indices = jnp.where(at_home(), indices, flip(indices, "c"))
+    indices = jnp.where(home, indices, flip(indices, "c"))
     segment = indices[2]
-    held = swap_roles(block_input[0])
-    small = jnp.concatenate([qkv_weight, proj_weight.reshape(1, model_width, local_width)], axis=0)
-    small = jnp.where(at_home(), small, other_quarter(small, users))
+    ranges, start = key_ranges(segment, QUERY_BLOCK)
+    coming, small_piece, home_across, ranges, start = tie(
+        coming, small_piece, home_across, ranges, start
+    )
+    small_other = share(small_piece, users, small.shape)
+    normed_coming = normed(coming)
+    away_across = flip_some(normed_coming, False)
+    across = jnp.where(home, home_across, away_across)
+    across, up_piece, down_piece = tie(
+        across, piece_of(expert_up, users), piece_of(expert_down, users)
+    )
+    up_piece, down_piece = flip(up_piece, "zh"), flip(down_piece, "zh")
+    normed_one = jnp.where(home, normed_staying, normed_coming)
+    normed_one = [normed_one, flip(normed_one, "c"), across, flip(across, "c")]
+    inputs = jnp.where(home, staying, coming).astype(jnp.float32)
+    unit_one, inverse_one = normalize_plain(inputs)
+    small = jnp.where(home, small, small_other)
     qkv_used, proj_used = small[:3], small[3].reshape(local_width, model_width)
-    own_experts = (expert_up, expert_down)
-    expert_up, expert_down, held = lax.optimization_barrier((expert_up, expert_down, held))
-    new_experts = [other_quarter(weight, users) for weight in (expert_up, expert_down)]
-    inputs = held.astype(jnp.float32)
-    unit_one, inverse_one = normalize_plain(inputs)
-    normed_one_rows = (unit_one * attention_gain).astype(jnp.bfloat16)
-    normed_one = gather_blocks(normed_one_rows)
     *attended, q, qt, k, kt, v, ctx, lse = attention_forward(
-        *key_ranges(segment, QUERY_BLOCK), ranks, normed_one, qkv_used, proj_used
+        ranges, start, ranks, normed_one, qkv_used, proj_used
     )
     saved = (q, qt, k, kt, v, ctx, lse)
-    upstream = swap_roles(out_grad[0]).astype(jnp.float32)
+    attended[3], up_piece, down_piece, indices, upstream = tie(
+        attended[3], up_piece, down_piece, indices, out_grad[0]
+    )
+    away_upstream = lax.ppermute(upstream, ("c", "zh"), [(1, 2), (2, 1)])
+    new_experts = [share(piece, users, expert_up.shape) for piece in (up_piece, down_piece)]
+    back_ranges = key_ranges(indices[2], BLOCK)[0]
     kept_rows, order, table, hot_rows = route_rows(
         indices[0], indices[1], experts, capacity, row_count, ranks
     )
-    attended = scatter_blocks(attended)
+    own_experts = (expert_up, expert_down)
+    far, back_ranges, order, table, kept_rows = tie(
+        flip(far_rows(attended), "zl"), back_ranges, order, table, kept_rows
+    )
+    upstream = jnp.where(home, upstream, away_upstream).astype(jnp.float32)
+    attended = near_rows(attended) + far.astype(jnp.float32)
     mixed_one = inputs + attended
     unit_two, inverse_two = normalize_plain(mixed_one)
     normed_two_rows = (unit_two * moe_gain).astype(jnp.bfloat16)
@@ -774,19 +823,32 @@
     gate_prob = jax.nn.sigmoid(jnp.sum(normed_two_float * centroid_rows, axis=-1))
     gate_used = jnp.where(kept_rows, gate_prob, 0.0)
     grad_eo_rows = (gate_used[:, None] * upstream).astype(jnp.bfloat16)
-    dispatched = gather_blocks(sort_rows(order, normed_two_rows))
-    grad_sorted = sort_rows(order, grad_eo_rows)
-    grad_sorted, *dispatched = lax.optimization_barrier((grad_sorted, *dispatched))
-    grad_dispatched = gather_blocks(grad_sorted)
+    sorted_rows = sort_rows(order, normed_two_rows)
+    beside, across = flip(sorted_rows, "c"), flip(sorted_rows, "zl")
+    across, grad_sorted = tie(across, sort_rows(order, grad_eo_rows))
+    grad_beside, grad_across = flip(grad_sorted, "c"), flip(grad_sorted, "zl")
+    dispatched = [sorted_rows, beside, across, flip(across, "c")]
     returned, hidden, slope = moe_forward(table, dispatched, own_experts, new_experts)
-    expert_out = unsort_rows(order, scatter_blocks(returned))
-    mixed_two = mixed_one + gate_used[:, None] * expert_out
-    block_output = swap_roles(mixed_two.astype(jnp.bfloat16))[None]
+    grad_across, *returned = tie(grad_across, *returned)
+    returned_far, grad_corner = tie(far_rows(returned), flip(grad_across, "c"))
+    grad_dispatched = [grad_sorted, grad_beside, grad_across, grad_corner]
+    returned_far = flip(returned_far, "zl")
+    returned_near = near_rows(returned)
+    back_moe, grad_upward = moe_backward(table, grad_dispatched, slope, own_experts, new_experts)
+    returned_far, back_moe[3] = tie(returned_far, back_moe[3])
+    back_far, hidden = tie(far_rows(back_moe), hidden)
+    back_far = flip(back_far, "zl")
+    down_part = moe_weights(table, grad_dispatched, hidden, experts)
+    down_rest = lax.psum_scatter(down_part, high_bits, scatter_dimension=1, tiled=True)
+    expert_out = unsort_rows(order, returned_near + returned_far.astype(jnp.float32))
+    mixed_two = (mixed_one + gate_used[:, None] * expert_out).astype(jnp.bfloat16)
     grad_gate = jnp.where(kept_rows, jnp.sum(upstream * expert_out, axis=-1), 0.0)
     grad_score = grad_gate * gate_prob * (1.0 - gate_prob)
-    back_moe, grad_upward = moe_backward(table, grad_dispatched, slope, own_experts, new_experts)
-    expert_part = moe_weights(table, dispatched, grad_dispatched, hidden, grad_upward, experts)
-    grad_two = unsort_rows(order, scatter_blocks(back_moe)) + grad_score[:, None] * centroid_rows
+    grad_score, grad_upward = tie(grad_score, grad_upward)
+    up_part = moe_weights(table, dispatched, grad_upward, experts)
+    back_far, up_part = tie(back_far, up_part)
+    back_moe = near_rows(back_moe) + back_far.astype(jnp.float32)
+    grad_two = unsort_rows(order, back_moe) + grad_score[:, None] * centroid_rows
     centroid_part = jnp.einsum(
         "te,td->ed",
         hot_rows.astype(jnp.float32),
@@ -796,26 +858,43 @@
     moe_gain_part = jnp.sum(grad_two * unit_two, axis=0)
     grad_mixed = upstream + normalize_back(grad_two, unit_two, inverse_two, moe_gain)
     grad_att = gather_blocks(grad_mixed.astype(jnp.bfloat16))
+    up_rest = lax.psum_scatter(up_part, high_bits, scatter_dimension=1, tiled=True)
+    early = jnp.concatenate([moe_gain_part[None], centroid_part], axis=0)
+    everyone = (*users, "zh", "zl")
+    early = jnp.swapaxes(early.reshape(experts + 1, lax.axis_size(everyone), -1), 0, 1)
+    early = jnp.sum(lax.all_to_all(early, everyone, 0, 0, tiled=True), axis=0)
+    grad_att[2], early = tie(grad_att[2], early)
+    grad_att[3] = flip(grad_att[2], "c")
+    down_rest, mixed_two, grad_att[3] = tie(down_rest, mixed_two, grad_att[3])
+    down_home = send_home(down_rest, 1)
+    away_output = lax.ppermute(mixed_two, ("c", "zh"), [(1, 2), (2, 1)])
     *grad_one, weights_part = attention_backward(
-        *key_ranges(segment, BLOCK), ranks, grad_att, normed_one, saved, qkv_used, proj_used
-    )
-    grad_one = scatter_blocks(grad_one)
-    input_grad = swap_roles(
-        (grad_mixed + normalize_back(grad_one, unit_one, inverse_one, attention_gain)).astype(
-            jnp.bfloat16
+        back_ranges, start, ranks, grad_att, normed_one, saved, qkv_used, proj_used
+    )
+    grad_one[3], away_output, *down_home = tie(grad_one[3], away_output, *down_home)
+    block_output = jnp.where(home, mixed_two, away_output)[None]
+    one_far = far_rows(grad_one)
+    one_near = near_rows(grad_one)
+
+    def finish(far):
+        grad = normalize_back(
+            one_near + far.astype(jnp.float32), unit_one, inverse_one, attention_gain
         )
-    )[None]
-
-    expert_part = lax.psum_scatter(expert_part, high_bits, scatter_dimension=2, tiled=True)
-    expert_summed = sum_home(expert_part, 2)
-    up_summed, down_summed = expert_summed[0], jnp.swapaxes(expert_summed[1], 1, 2)
-    for bit in high_bits:
+        return (grad_mixed + grad).astype(jnp.bfloat16)
+
+    going = flip_some(one_far, False)
+    going, one_far, *up_home = tie(going, one_far, *send_home(up_rest, 1))
+    kept_far = flip_some(one_far, True)
+    weights_part = halve(weights_part, high_bits[0], 1)
+    going, weights_part = tie(finish(going), weights_part)
+    going = lax.ppermute(going, ("c", "zh"), [(1, 2), (2, 1)])
+    input_grad = jnp.where(home, finish(kept_far), going)[None]
+    down_summed = jnp.swapaxes(sum_home(*down_home), 1, 2)
+    up_summed = sum_home(*up_home)
+    for bit in high_bits[1:]:
         weights_part = halve(weights_part, bit, 1)
-    weights_part = sum_home(weights_part, 1)
+    weights_part = sum_home(*send_home(weights_part, 1))
     qkv_summed, proj_summed = weights_part[:3], weights_part[3].T
-    early = jnp.concatenate([moe_gain_part[None], centroid_part], axis=0)
-    for bit in (*users, "zh", "zl"):
-        early = halve(early, bit, 1)
     gain_two_sum, centroid_sum = early[0], early[1:]
     slice_rows = qkv_summed.shape[1]
     own_rows = lax.dynamic_slice_in_dim(
@@ -824,9 +903,9 @@
     gain_one = jnp.sum(own_rows.astype(jnp.float32) * qkv_summed, axis=(0, 2))
     for bit in ("zh", "zl"):
         gain_one = halve(gain_one, bit, 0)
-    share = gain_one.shape[0]
-    own_gain = lax.axis_index((*users, "zh", "zl")) * share
-    gain_one_sum = gain_one / lax.dynamic_slice_in_dim(attention_gain, own_gain, share, 0)
+    entries = gain_one.shape[0]
+    own_gain = lax.axis_index((*users, "zh", "zl")) * entries
+    gain_one_sum = gain_one / lax.dynamic_slice_in_dim(attention_gain, own_gain, entries, 0)
     return (
         block_output,
         input_grad,

time: 724 us -> 604 us (0.83)
  waiting for transfers between devices: 357 us -> 158 us
  blocking collectives: 0 us -> 29.1 us
  other arithmetic: 38.7 us -> 64.8 us
  local copies, waits for them, and re-layouts: 30.9 us -> 42.2 us
    ppermute x37 -> x30, waiting for transfers between devices: 357 us -> 80.5 us  [flip(): return lax.ppermute(value, axis, [(0, 1), (1, 0)])]
    ppermute x8 -> x14, waiting for transfers between devices: 0.02 us -> 70.7 us  [the longest x3 49.8 us: send_home(): turned = lax.ppermute(turned, ('c', 'zh'), [(0, 2), (1, 0), (2, 3), (3, 1)])]
    all_to_all x0 -> x1, blocking collectives: none -> 29.1 us  [body(): early = jnp.sum(lax.all_to_all(early, everyone, 0, 0, tiled=True), axis=0)]
    ppermute x37 -> x30, starting transfers between devices: 50.3 us -> 36.3 us  [flip(): return lax.ppermute(value, axis, [(0, 1), (1, 0)])]
    ppermute x8 -> x14, starting transfers between devices: 9.06 us -> 22.1 us  [the longest x4 7.79 us: flip_some(): return lax.ppermute(value, ('c', 'zh', 'zl'), moves)]
    pallas_call x3 -> x4, Pallas kernels: 85.9 us -> 92.8 us  [moe_call(): pl.pallas_call(kernel, grid_spec=pltpu.PrefetchScalarGridSpec(num_scalar_...]
  transfers between devices with their start and end apart: 49 -> 49, of which waited for: 19 -> 21; matrix products, arithmetic and copies ran while one was open for 10% -> 17% of each run, Pallas kernels for 21% -> 32%
where the time goes in v3:
time: 604 us; the launch traced here: 594 us
  Pallas kernels  208 us (34%)
  waiting for transfers between devices  158 us (26%)
  other arithmetic  64.8 us (11%)
  starting transfers between devices  58.6 us (10%)
  local copies, waits for them, and re-layouts  42.2 us (7%)
  blocking collectives  29.1 us (5%)
  matrix products  18.9 us (3%)
  between operations  15.3 us (3%)
    pallas_call x4, Pallas kernels, moe_call(): pl.pallas_call(kernel, grid_spec=pltpu.PrefetchScalarGridSpec(num_scalar_...  92.8 us
    ppermute x30, waiting for transfers between devices, flip(): return lax.ppermute(value, axis, [(0, 1), (1, 0)])  80.5 us
    pallas_call x1, Pallas kernels, attention_backward(): pl.pallas_call(backward_kernel, grid_spec=pltpu.PrefetchScalarGridSpec(nu...  71.4 us
    ppermute x3, waiting for transfers between devices, send_home(): turned = lax.ppermute(turned, ('c', 'zh'), [(0, 2), (1, 0), (2, 3), (3, 1)])  49.8 us
    pallas_call x1, Pallas kernels, attention_forward(): pl.pallas_call(forward_kernel, grid_spec=pltpu.PrefetchScalarGridSpec(num...  43.4 us
    ppermute x30, starting transfers between devices, flip(): return lax.ppermute(value, axis, [(0, 1), (1, 0)])  36.3 us
    all_to_all x1, blocking collectives, body(): early = jnp.sum(lax.all_to_all(early, everyone, 0, 0, tiled=True), axis=0)  29.1 us
    ppermute x4, waiting for transfers between devices, flip_some(): return lax.ppermute(value, ('c', 'zh', 'zl'), moves)  20.9 us
  transfers between devices with their start and end apart: 49, of which 21 were waited for; matrix products, arithmetic and copies ran while one was open for 17% of the time, Pallas kernels for 32%

profile of v3, /device:TPU:0, one launch (start us, length us, event | category | flops | bytes accessed | tf_op | source)
XLA Modules:
  0.0 594.4 jit_solution(1132731219130105257)
XLA Ops:
  12.1 3.6 collective-permute-start.1
  17.9 3.5 collective-permute-start.2
  35.5 12.9 %collective-permute-done.2 = bf16[768,768]{1,0:T(8,128)(2,1)} collective-permute-done((bf16[768,768]{1,0:T(8,128)(2,1)}, bf16[768,768]{1,0:T(8,128)(2,1)}, u32[]{:S(2)}, u32[]{:S(2)}) %collective-permute-start.2) | collective-permute-done | bytes 1179680 | tf_op jit(solution)/shard_map/ppermute | solution.py:672
  49.5 3.1 convert_reduce_fusion.1
  60.3 3.3 collective-permute-start.4
  63.6 2.4 broadcast_select_fusion.3.x2
  66.0 10.6 %collective-permute-start.6 = (bf16[768,768]{1,0:T(8,128)(2,1)}, bf16[768,768]{1,0:T(8,128)(2,1)}, u32[]{:S(2)}, u32[]{:S(2)}) collective-permute-start(bf16[768,768]{1,0:T(8,128)(2,1)} %broadcast_select_fusion.3.x2), channel_id=1, source_target_pairs={{0,4},{4,0},{1,5},{5,1},{2,6},{6,2},{3,7},{7,3},{8,12},{12,8},{9,1... | collective-permute-start | bytes 3538952 | tf_op jit(solution)/shard_map/ppermute | solution.py:667
  77.2 3.4 collective-permute-start.7
  80.7 6.0 %all-gather.4.cloned.1.call-done = bf16[3072,192]{1,0:T(8,128)(2,1)} async-done(((bf16[384,192]{1,0:T(8,128)(2,1)}), bf16[3072,192]{1,0:T(8,128)(2,1)}) %all-gather.4.cloned.1.call-update) | async-done | bytes 1179664 | tf_op jit(solution)/shard_map/all_gather | solution.py:728
  89.3 43.4 %attention_forward.1 = (bf16[768,768]{1,0:T(8,128)(2,1)}, bf16[768,768]{1,0:T(8,128)(2,1)}, bf16[768,768]{1,0:T(8,128)(2,1)}, bf16[768,768]{1,0:T(8,128)(2,1)}, ...) custom-call(s32[5,6]{1,0:T(8,128)} %stack.33.ranges, ...), custom_call_target="tpu_custom_call" | custom-call | flops 28991029248 | bytes 41943040 | tf_op jit(solution)/shard_map/attention_forward/pallas_call | solution.py:192
  151.9 2.6 convert_reduce_fusion
  155.7 26.3 %collective-permute-done.10 = bf16[768,768]{1,0:T(8,128)(2,1)S(1)} collective-permute-done((bf16[768,768]{1,0:T(8,128)(2,1)S(1)}, bf16[768,768]{1,0:T(8,128)(2,1)S(1)}, u32[]{:S(2)}, u32[]{:S(2)}) %collective-permute-start.10) | collective-permute-done | bytes 1179680 | tf_op jit(solution)/shard_map/ppermute | solution.py:667
  183.1 4.0 fusion.62
  187.8 2.2 fusion.28
  192.9 2.3 convolution_convert_fusion.d0.a0
  195.2 25.6 %collective-permute-done.12.x2.a2 = bf16[832,768]{1,0:T(8,128)(2,1)S(1)} collective-permute-done((bf16[832,768]{1,0:T(8,128)(2,1)S(1)}, bf16[832,768]{1,0:T(8,128)(2,1)S(1)}, u32[]{:S(2)}, u32[]{:S(2)}) %collective-permute-start.12) | collective-permute-done | bytes 1277984 | tf_op jit(solution)/shard_map/ppermute | solution.py:667
  224.0 31.8 %moe_forward.1 = (bf16[832,768]{1,0:T(8,128)(2,1)}, bf16[832,768]{1,0:T(8,128)(2,1)}, bf16[832,768]{1,0:T(8,128)(2,1)}, bf16[832,768]{1,0:T(8,128)(2,1)}, bf16[4...) custom-call(s32[33]{0:T(128)} %concatenate.15.table, bf16[832,768]{1,0:T(8,128)(2,1)} %copy-done.61, ...), custom_call_target="tpu_custom_call" | custom-call | flops 9814671360 | bytes 41943040 | tf_op jit(solution)/shard_map/moe_forward/pallas_call | solution.py:600
  256.5 2.6 collective-permute-done.18
  263.8 27.8 %moe_backward.1 = (bf16[832,768]{1,0:T(8,128)(2,1)}, bf16[832,768]{1,0:T(8,128)(2,1)}, bf16[832,768]{1,0:T(8,128)(2,1)}, bf16[832,768]{1,0:T(8,128)(2,1)}, bf16[4,1088,768]{2,1,0:T(8,128)(2,1)}) custom-call(s32[33]{0:T(128)} %concatenate.15.table, bf16[832,768]{1,0:T(8,128)(2,1)} %convolution_convert_fusion.d0.a0, bf16[832,768]{1,0:T(8,128)(2,1)} %copy-done.66, ...), custom_call_target="tpu_custom_call" | custom-call | flops 9814671360 | bytes 41943040 | tf_op jit(solution)/shard_map/moe_backward/pallas_call | solution.py:600
  291.9 3.0 collective-permute-done.21
  295.0 2.7 add_convert_fusion.2
  297.7 16.2 %moe_weights.2 = bf16[4,768,768]{2,1,0:T(8,128)(2,1)} custom-call(s32[33]{0:T(128)} %concatenate.15.table, bf16[832,768]{1,0:T(8,128)(2,1)} %convolution_convert_fusion.d0.a0, bf16[832,768]{1,0:T(8,128)(2,1)} %copy-done.66, bf16[832,768]{1,0:T(8,128)(2,1)} %collective-permute-done.15.d2.a2, bf16[832,768]{1,0:T(8,128)(2,1)} %copy-done.65, ...), custom_call_target="tpu_custom_call" | custom-call | flops 4907335680 | bytes 41943040 | tf_op jit(solution)/shard_map/moe_weights/pallas_call | solution.py:600
  314.6 2.7 collective-permute-done.22
  317.2 5.3 fusion.31
  323.2 16.8 %moe_weights.3 = bf16[4,768,768]{2,1,0:T(8,128)(2,1)} custom-call(s32[33]{0:T(128)} %concatenate.15.table, bf16[832,768]{1,0:T(8,128)(2,1)} %copy-done.61, bf16[832,768]{1,0:T(8,128)(2,1)} %copy-done.63, bf16[832,768]{1,0:T(8,128)(2,1)} %copy-done.62, bf16[832,768]{1,0:T(8,128)(2,1)} %collective-permute-done.17.x3.a3, ...), custom_call_target="tpu_custom_call" | custom-call | flops 4907335680 | bytes 41943040 | tf_op jit(solution)/shard_map/moe_weights/pallas_call | solution.py:600
  340.0 4.8 collective-permute-done.24
  344.9 6.4 %multiply_reduce_fusion = (f32[768]{0:T(1024)}, f32[768]{0:T(1024)S(1)}, f32[768]{0:T(1024)S(1)}, f32[768,768]{1,0:T(8,128)S(1)}) fusion(f32[768,768]{1,0:T(8,128)S(1)} %get-tuple-element.228, f32[768]{0:T(1024)S(1)} %copy-done.40, f32[768]{0:T(1024)S(1)} %copy-done.38, f32[768]{0:T(1024)} %param.16, f32[768,768]{1,0:T(8,128)} %get-tuple-element.252, ...), kind=kOutput, calls=%fused_computation.54 | convolution fusion | flops 991196928 | bytes 12211200 | tf_op jit(solution)/shard_map/dot_general | solution.py:37
  351.4 2.8 fusion.61
  356.9 29.1 %all_to_all.5 = f32[32,5,24]{2,1,0:T(8,128)S(1)} all-to-all(f32[32,5,24]{2,1,0:T(8,128)S(1)} %copy.62), channel_id=1, replica_groups=mesh['u0'=2,'u1'=2,'c'=2,'zh'=2,'zl'=2] {'u0','u1','c','zh','zl'}, dimensions={0} | all-to-all | bytes 30720 | tf_op jit(solution)/shard_map/all_to_all | solution.py:865
  386.6 3.4 collective-permute-done.26.g3
  392.6 2.2 collective-permute-start.30
  395.5 71.4 %attention_backward.1 = (bf16[768,768]{1,0:T(8,128)(2,1)}, bf16[768,768]{1,0:T(8,128)(2,1)}, bf16[768,768]{1,0:T(8,128)(2,1)}, bf16[768,768]{1,0:T(8,128)(2,1)}, bf16[4,768,192]{2,1,0:T(8,128)(2,1)}) custom-call(s32[5,12]{1,0:T(8,128)} %stack.39.ranges, s32[4]{0:T(128)} %pad_add_fusion.1.ranks, bf16[768,768]{1,0:T(8,128)(2,1)} %get-tuple-element.223.g0, ...), custom_call_target="tpu_custom_call" | custom-call | flops 65229815808 | bytes 41943040 | tf_op jit(solution)/shard_map/attention_backward/pallas_call | solution.py:361
  467.0 3.0 collective-permute-start.32
  470.0 2.7 collective-permute-done.32
  472.7 2.6 add_convert_fusion.4
  476.2 2.4 constant_dynamic-slice_fusion.4
  480.0 3.9 collective-permute-start.35
  487.0 24.7 %collective-permute-done.35 = bf16[4,96,768]{2,1,0:T(8,128)(2,1)} collective-permute-done((bf16[4,96,768]{2,1,0:T(8,128)(2,1)}, bf16[4,96,768]{2,1,0:T(8,128)(2,1)}, u32[]{:S(2)}, u32[]{:S(2)}) %collective-permute-start.35) | collective-permute-done | bytes 589856 | tf_op jit(solution)/shard_map/ppermute | solution.py:712
  514.7 2.2 copy.64
  518.7 2.3 add_bitcast_fusion
  522.2 7.9 %collective-permute-done.36 = bf16[768,768]{1,0:T(8,128)(2,1)} collective-permute-done((bf16[768,768]{1,0:T(8,128)(2,1)}, bf16[768,768]{1,0:T(8,128)(2,1)}, u32[]{:S(2)}, u32[]{:S(2)}) %collective-permute-start.36) | collective-permute-done | bytes 1179680 | tf_op jit(solution)/shard_map/ppermute | solution.py:672
  530.1 3.6 fusion.11
  533.8 2.2 fusion.20
  536.0 3.9 collective-permute-start.39
  539.9 2.4 convert_add_fusion.3
  547.2 25.1 %collective-permute-done.41 = bf16[4,96,192]{2,1,0:T(8,128)(2,1)S(1)} collective-permute-done((bf16[4,96,192]{2,1,0:T(8,128)(2,1)S(1)}, bf16[4,96,192]{2,1,0:T(8,128)(2,1)S(1)}, u32[]{:S(2)}, u32[]{:S(2)}) %collective-permute-start.41) | collective-permute-done | bytes 147488 | tf_op jit(solution)/shard_map/ppermute | solution.py:712
  574.9 3.8 collective-permute-done.42
  583.6 3.9 fusion.36
  (315 shorter events, 98.0 us)
Async XLA Ops:
  7.2 79.5 %all-gather.4.cloned.1.call-start = ((), (), s32[]{:S(2)}) async-start(), calls=%async_computation.3 | async-start | bytes 1769472 | tf_op jit(solution)/shard_map/all_gather | solution.py:728
  8.7 14.5 %collective-permute-start.3 = (s32[3,3072]{1,0:T(4,128)}, s32[3,3072]{1,0:T(4,128)}, u32[]{:S(2)}, u32[]{:S(2)}) collective-permute-start(s32[3,3072]{1,0:T(4,128)} %pad_add_fusion), channel_id=1, source_target_pairs={{0,4},{4,0},{1,5},{5,1},{2,6},{6,2},{3,7},{7,3},{8,12},{12,8},{9,1... | collective-permute-start | bytes 110600 | tf_op jit(solution)/shard_map/ppermute | solution.py:667
  12.1 23.4 %collective-permute-start.1 = (bf16[384,192]{1,0:T(8,128)(2,1)}, bf16[384,192]{1,0:T(8,128)(2,1)}, u32[]{:S(2)}, u32[]{:S(2)}) collective-permute-start(bf16[384,192]{1,0:T(8,128)(2,1)} %constant_dynamic-slice_fusion.20), channel_id=1, source_target_pairs={{0,2},{2,0},{1,3},{3,1},{4,6},{6,4},{5,7},{7,5},{8,10},{10,8},{9,1... | collective-permute-start | bytes 442376 | tf_op jit(solution)/shard_map/ppermute | solution.py:667
  17.9 30.5 %collective-permute-start.2 = (bf16[768,768]{1,0:T(8,128)(2,1)}, bf16[768,768]{1,0:T(8,128)(2,1)}, u32[]{:S(2)}, u32[]{:S(2)}) collective-permute-start(bf16[768,768]{1,0:T(8,128)(2,1)} %fusion.27), channel_id=1, source_target_pairs={{0,1},{1,0},{6,7},{7,6},{8,9},{9,8},{14,15},{15,14},{16,17},{17,16... | collective-permute-start | bytes 3538952 | tf_op jit(solution)/shard_map/ppermute | solution.py:672
  21.4 27.1 %collective-permute-start = (bf16[768,768]{1,0:T(8,128)(2,1)S(1)}, bf16[768,768]{1,0:T(8,128)(2,1)S(1)}, u32[]{:S(2)}, u32[]{:S(2)}) collective-permute-start(bf16[768,768]{1,0:T(8,128)(2,1)S(1)} %bitcast.86), channel_id=1, source_target_pairs={{2,4},{4,2},{3,5},{5,3},{10,12},{12,10},{11,13},{13,11},{18,20},{2... | collective-permute-start | bytes 3538952 | tf_op jit(solution)/shard_map/ppermute | solution.py:767
  54.6 9.0 %collective-permute-start.5 = (bf16[768,768]{1,0:T(8,128)(2,1)}, bf16[768,768]{1,0:T(8,128)(2,1)}, u32[]{:S(2)}, u32[]{:S(2)}) collective-permute-start(bf16[768,768]{1,0:T(8,128)(2,1)} %get-tuple-element.230), channel_id=1, source_target_pairs={{2,3},{3,2},{4,5},{5,4},{10,11},{11,10},{12,13},{13,12},{18,19},{1... | collective-permute-start | bytes 3538952 | tf_op jit(solution)/shard_map/ppermute | solution.py:672
  56.3 167.7 %all-gather.6.cloned.1.call-start = ((), (), s32[]{:S(2)}) async-start(), calls=%async_computation.4 | async-start | bytes 5308416 | tf_op jit(solution)/shard_map/all_gather | solution.py:728
  60.3 29.0 %collective-permute-start.4 = (bf16[768,768]{1,0:T(8,128)(2,1)}, bf16[768,768]{1,0:T(8,128)(2,1)}, u32[]{:S(2)}, u32[]{:S(2)}) collective-permute-start(bf16[768,768]{1,0:T(8,128)(2,1)} %get-tuple-element.229.x0), channel_id=1, source_target_pairs={{0,4},{4,0},{1,5},{5,1},{2,6},{6,2},{3,7},{7,3},{8,12},{12,8},{9,1... | collective-permute-start | bytes 3538952 | tf_op jit(solution)/shard_map/ppermute | solution.py:667
  66.0 23.3 %collective-permute-start.6 = (bf16[768,768]{1,0:T(8,128)(2,1)}, bf16[768,768]{1,0:T(8,128)(2,1)}, u32[]{:S(2)}, u32[]{:S(2)}) collective-permute-start(bf16[768,768]{1,0:T(8,128)(2,1)} %broadcast_select_fusion.3.x2), channel_id=1, source_target_pairs={{0,4},{4,0},{1,5},{5,1},{2,6},{6,2},{3,7},{7,3},{8,12},{12,8},{9,1... | collective-permute-start | bytes 3538952 | tf_op jit(solution)/shard_map/ppermute | solution.py:667
  77.2 55.4 %collective-permute-start.7 = (bf16[384,768]{1,0:T(8,128)(2,1)}, bf16[384,768]{1,0:T(8,128)(2,1)S(1)}, u32[]{:S(2)}, u32[]{:S(2)}) collective-permute-start(bf16[384,768]{1,0:T(8,128)(2,1)} %constant_dynamic-slice_fusion.19), channel_id=1, source_target_pairs={{0,2},{2,0},{1,3},{3,1},{4,6},{6,4},{5,7},{7,5},{8,10},{10,8},{9,1... | collective-permute-start | bytes 1769480 | tf_op jit(solution)/shard_map/ppermute | solution.py:667
  80.6 52.2 %collective-permute-start.8 = (bf16[384,768]{1,0:T(8,128)(2,1)}, bf16[384,768]{1,0:T(8,128)(2,1)}, u32[]{:S(2)}, u32[]{:S(2)}) collective-permute-start(bf16[384,768]{1,0:T(8,128)(2,1)} %constant_dynamic-slice_fusion.18), channel_id=1, source_target_pairs={{0,2},{2,0},{1,3},{3,1},{4,6},{6,4},{5,7},{7,5},{8,10},{10,8},{9,1... | collective-permute-start | bytes 1769480 | tf_op jit(solution)/shard_map/ppermute | solution.py:667
  133.5 90.4 %all-gather.8.cloned.1.call-start = ((), (), s32[]{:S(2)}) async-start(), calls=%async_computation.5 | async-start | bytes 5308416 | tf_op jit(solution)/shard_map/all_gather | solution.py:728
  134.3 255.8 %reduce-scatter.3.cloned.1.call-start = ((), (), s32[]{:S(2)}) async-start(), calls=%async_computation.6 | async-start | bytes 5898240 | tf_op jit(solution)/shard_map/reduce_scatter | solution.py:842
  135.0 4.5 collective-permute-start.9
  137.4 44.6 %collective-permute-start.11 = (bf16[768,768]{1,0:T(8,128)(2,1)}, bf16[768,768]{1,0:T(8,128)(2,1)}, u32[]{:S(2)}, u32[]{:S(2)}) collective-permute-start(bf16[768,768]{1,0:T(8,128)(2,1)} %get-tuple-element.103), channel_id=1, source_target_pairs={{0,4},{4,0},{1,5},{5,1},{2,6},{6,2},{3,7},{7,3},{8,12},{12,8},{9,1... | collective-permute-start | bytes 3538952 | tf_op jit(solution)/shard_map/ppermute | solution.py:667
  141.1 41.0 %collective-permute-start.10 = (bf16[768,768]{1,0:T(8,128)(2,1)S(1)}, bf16[768,768]{1,0:T(8,128)(2,1)S(1)}, u32[]{:S(2)}, u32[]{:S(2)}) collective-permute-start(bf16[768,768]{1,0:T(8,128)(2,1)S(1)} %add_convert_fusion.6), channel_id=1, source_target_pairs={{0,1},{1,0},{2,3},{3,2},{4,5},{5,4},{6,7},{7,6},{8,9},{9,8},{10,11... | collective-permute-start | bytes 3538952 | tf_op jit(solution)/shard_map/ppermute | solution.py:667
  143.2 48.1 %collective-permute-start.13 = (bf16[768,768]{1,0:T(8,128)(2,1)}, bf16[768,768]{1,0:T(8,128)(2,1)}, u32[]{:S(2)}, u32[]{:S(2)}) collective-permute-start(bf16[768,768]{1,0:T(8,128)(2,1)} %bitcast.89), channel_id=1, source_target_pairs={{2,4},{4,2},{3,5},{5,3},{10,12},{12,10},{11,13},{13,11},{18,20},{2... | collective-permute-start | bytes 3538952 | tf_op jit(solution)/shard_map/ppermute | solution.py:804
  191.2 29.6 %collective-permute-start.12 = (bf16[832,768]{1,0:T(8,128)(2,1)S(1)}, bf16[832,768]{1,0:T(8,128)(2,1)S(1)}, u32[]{:S(2)}, u32[]{:S(2)}) collective-permute-start(bf16[832,768]{1,0:T(8,128)(2,1)S(1)} %convolution_convert_fusion.1.x0.a0), channel_id=1, source_target_pairs={{0,1},{1,0},{2,3},{3,2},{4,5},{5,4},{6,7},{7,6},{8,9},{9,8},{10,11... | collective-permute-start | bytes 3833864 | tf_op jit(solution)/shard_map/ppermute | solution.py:667
  192.0 29.2 %collective-permute-start.16 = (bf16[832,768]{1,0:T(8,128)(2,1)S(1)}, bf16[832,768]{1,0:T(8,128)(2,1)S(1)}, u32[]{:S(2)}, u32[]{:S(2)}) collective-permute-start(bf16[832,768]{1,0:T(8,128)(2,1)S(1)} %convolution_convert_fusion.1.x0.a0), channel_id=1, source_target_pairs={{0,4},{4,0},{1,5},{5,1},{2,6},{6,2},{3,7},{7,3},{8,12},{12,8},{9,1... | collective-permute-start | bytes 3833864 | tf_op jit(solution)/shard_map/ppermute | solution.py:667
  220.8 3.1 collective-permute-start.17
  220.8 35.0 %collective-permute-start.15 = (bf16[832,768]{1,0:T(8,128)(2,1)}, bf16[832,768]{1,0:T(8,128)(2,1)}, u32[]{:S(2)}, u32[]{:S(2)}) collective-permute-start(bf16[832,768]{1,0:T(8,128)(2,1)} %convolution_convert_fusion.d0.a0), channel_id=1, source_target_pairs={{0,1},{1,0},{2,3},{3,2},{4,5},{5,4},{6,7},{7,6},{8,9},{9,8},{10,11... | collective-permute-start | bytes 3833864 | tf_op jit(solution)/shard_map/ppermute | solution.py:667
  255.8 3.3 collective-permute-start.18
  256.0 4.9 collective-permute-start.19
  256.4 6.3 %collective-permute-start.14 = (bf16[832,768]{1,0:T(8,128)(2,1)}, bf16[832,768]{1,0:T(8,128)(2,1)S(1)}, u32[]{:S(2)}, u32[]{:S(2)}) collective-permute-start(bf16[832,768]{1,0:T(8,128)(2,1)} %convolution_convert_fusion.d0.a0), channel_id=1, source_target_pairs={{0,4},{4,0},{1,5},{5,1},{2,6},{6,2},{3,7},{7,3},{8,12},{12,8},{9,1... | collective-permute-start | bytes 3833864 | tf_op jit(solution)/shard_map/ppermute | solution.py:667
  260.9 30.8 %collective-permute-start.20 = (bf16[832,768]{1,0:T(8,128)(2,1)S(1)}, bf16[832,768]{1,0:T(8,128)(2,1)S(1)}, u32[]{:S(2)}, u32[]{:S(2)}) collective-permute-start(bf16[832,768]{1,0:T(8,128)(2,1)S(1)} %add_convert_fusion.3), channel_id=1, source_target_pairs={{0,1},{1,0},{2,3},{3,2},{4,5},{5,4},{6,7},{7,6},{8,9},{9,8},{10,11... | collective-permute-start | bytes 3833864 | tf_op jit(solution)/shard_map/ppermute | solution.py:667
  291.7 3.3 collective-permute-start.21
  313.9 162.2 %reduce-scatter.5.cloned.1.call-start = ((), (), s32[]{:S(2)}) async-start(), calls=%async_computation.7 | async-start | bytes 5898240 | tf_op jit(solution)/shard_map/reduce_scatter | solution.py:861
  314.0 3.3 collective-permute-start.22
  314.2 30.7 %collective-permute-start.24 = (bf16[832,768]{1,0:T(8,128)(2,1)}, bf16[832,768]{1,0:T(8,128)(2,1)}, u32[]{:S(2)}, u32[]{:S(2)}) collective-permute-start(bf16[832,768]{1,0:T(8,128)(2,1)} %add_convert_fusion.2), channel_id=1, source_target_pairs={{0,1},{1,0},{2,3},{3,2},{4,5},{5,4},{6,7},{7,6},{8,9},{9,8},{10,11... | collective-permute-start | bytes 3833864 | tf_op jit(solution)/shard_map/ppermute | solution.py:667
  314.5 30.4 %collective-permute-start.23 = (bf16[832,768]{1,0:T(8,128)(2,1)}, bf16[832,768]{1,0:T(8,128)(2,1)}, u32[]{:S(2)}, u32[]{:S(2)}) collective-permute-start(bf16[832,768]{1,0:T(8,128)(2,1)} %get-tuple-element.130), channel_id=1, source_target_pairs={{0,4},{4,0},{1,5},{5,1},{2,6},{6,2},{3,7},{7,3},{8,12},{12,8},{9,1... | collective-permute-start | bytes 3833864 | tf_op jit(solution)/shard_map/ppermute | solution.py:667
  354.2 31.9 %collective-permute-start.25 = (bf16[768,768]{1,0:T(8,128)(2,1)}, bf16[768,768]{1,0:T(8,128)(2,1)}, u32[]{:S(2)}, u32[]{:S(2)}) collective-permute-start(bf16[768,768]{1,0:T(8,128)(2,1)} %get-tuple-element.223.g0), channel_id=1, source_target_pairs={{0,1},{1,0},{2,3},{3,2},{4,5},{5,4},{6,7},{7,6},{8,9},{9,8},{10,11... | collective-permute-start | bytes 3538952 | tf_op jit(solution)/shard_map/ppermute | solution.py:667
  386.1 4.0 collective-permute-start.26
  386.1 9.4 %collective-permute-start.27 = (bf16[768,768]{1,0:T(8,128)(2,1)}, bf16[768,768]{1,0:T(8,128)(2,1)}, u32[]{:S(2)}, u32[]{:S(2)}) collective-permute-start(bf16[768,768]{1,0:T(8,128)(2,1)} %get-tuple-element.223.g0), channel_id=1, source_target_pairs={{0,4},{4,0},{1,5},{5,1},{2,6},{6,2},{3,7},{7,3},{8,12},{12,8},{9,1... | collective-permute-start | bytes 3538952 | tf_op jit(solution)/shard_map/ppermute | solution.py:667
  391.9 75.0 %collective-permute-start.29 = (bf16[4,96,768]{2,1,0:T(8,128)(2,1)S(1)}, bf16[4,96,768]{2,1,0:T(8,128)(2,1)S(1)}, u32[]{:S(2)}, u32[]{:S(2)}) collective-permute-start(bf16[4,96,768]{2,1,0:T(8,128)(2,1)S(1)} %get-tuple-element.164), channel_id=1, source_target_pairs={{2,4},{4,2},{3,5},{5,3},{10,12},{12,10},{11,13},{13,11},{18,20},{2... | collective-permute-start | bytes 1769480 | tf_op jit(solution)/shard_map/ppermute | solution.py:713
  392.6 74.4 %collective-permute-start.30 = (bf16[4,96,768]{2,1,0:T(8,128)(2,1)S(1)}, bf16[4,96,768]{2,1,0:T(8,128)(2,1)S(1)}, u32[]{:S(2)}, u32[]{:S(2)}) collective-permute-start(bf16[4,96,768]{2,1,0:T(8,128)(2,1)S(1)} %get-tuple-element.235), channel_id=1, source_target_pairs={{0,4},{2,0},{4,6},{6,2},{1,5},{3,1},{5,7},{7,3},{8,12},{10,8},{12,... | collective-permute-start | bytes 1769480 | tf_op jit(solution)/shard_map/ppermute | solution.py:712
  394.8 72.2 %collective-permute-start.28 = (bf16[768,768]{1,0:T(8,128)(2,1)S(1)}, bf16[768,768]{1,0:T(8,128)(2,1)S(1)}, u32[]{:S(2)}, u32[]{:S(2)}) collective-permute-start(bf16[768,768]{1,0:T(8,128)(2,1)S(1)} %copy-done.14), channel_id=1, source_target_pairs={{2,4},{4,2},{3,5},{5,3},{10,12},{12,10},{11,13},{13,11},{18,20},{2... | collective-permute-start | bytes 3538952 | tf_op jit(solution)/shard_map/ppermute | solution.py:870
  467.0 5.7 collective-permute-start.32
  475.4 36.3 %collective-permute-start.33 = (bf16[768,768]{1,0:T(8,128)(2,1)}, bf16[768,768]{1,0:T(8,128)(2,1)S(1)}, u32[]{:S(2)}, u32[]{:S(2)}) collective-permute-start(bf16[768,768]{1,0:T(8,128)(2,1)} %add_convert_fusion.4), channel_id=1, source_target_pairs={{2,3},{3,2},{4,5},{5,4},{10,11},{11,10},{12,13},{13,12},{18,19},{1... | collective-permute-start | bytes 3538952 | tf_op jit(solution)/shard_map/ppermute | solution.py:672
  478.5 8.5 %collective-permute-start.34 = (bf16[4,96,768]{2,1,0:T(8,128)(2,1)}, bf16[4,96,768]{2,1,0:T(8,128)(2,1)}, u32[]{:S(2)}, u32[]{:S(2)}) collective-permute-start(bf16[4,96,768]{2,1,0:T(8,128)(2,1)} %get-tuple-element.161), channel_id=1, source_target_pairs={{2,4},{4,2},{3,5},{5,3},{10,12},{12,10},{11,13},{13,11},{18,20},{2... | collective-permute-start | bytes 1769480 | tf_op jit(solution)/shard_map/ppermute | solution.py:713
  480.0 31.7 %collective-permute-start.35 = (bf16[4,96,768]{2,1,0:T(8,128)(2,1)}, bf16[4,96,768]{2,1,0:T(8,128)(2,1)}, u32[]{:S(2)}, u32[]{:S(2)}) collective-permute-start(bf16[4,96,768]{2,1,0:T(8,128)(2,1)} %get-tuple-element.232), channel_id=1, source_target_pairs={{0,4},{2,0},{4,6},{6,2},{1,5},{3,1},{5,7},{7,3},{8,12},{10,8},{12,... | collective-permute-start | bytes 1769480 | tf_op jit(solution)/shard_map/ppermute | solution.py:712
  486.2 28.5 %collective-permute-start.37 = (bf16[4,384,192]{1,2,0:T(8,128)(2,1)}, bf16[4,384,192]{1,2,0:T(8,128)(2,1)}, u32[]{:S(2)}, u32[]{:S(2)}) collective-permute-start(bf16[4,384,192]{1,2,0:T(8,128)(2,1)} %copy.63), channel_id=1, source_target_pairs={{0,16},{16,0},{1,17},{17,1},{2,18},{18,2},{3,19},{19,3},{4,20},{20... | collective-permute-start | bytes 1769480 | tf_op jit(solution)/shard_map/ppermute | solution.py:667
  487.0 35.2 %collective-permute-start.31 = (bf16[768,768]{1,0:T(8,128)(2,1)}, bf16[768,768]{1,0:T(8,128)(2,1)S(1)}, u32[]{:S(2)}, u32[]{:S(2)}) collective-permute-start(bf16[768,768]{1,0:T(8,128)(2,1)} %get-tuple-element.151), channel_id=1, source_target_pairs={{0,4},{4,0},{1,5},{5,1},{2,6},{6,2},{3,7},{7,3},{8,12},{12,8},{9,1... | collective-permute-start | bytes 3538952 | tf_op jit(solution)/shard_map/ppermute | solution.py:667
  511.7 18.4 %collective-permute-start.36 = (bf16[768,768]{1,0:T(8,128)(2,1)}, bf16[768,768]{1,0:T(8,128)(2,1)}, u32[]{:S(2)}, u32[]{:S(2)}) collective-permute-start(bf16[768,768]{1,0:T(8,128)(2,1)} %add_convert_fusion.4), channel_id=1, source_target_pairs={{0,1},{1,0},{6,7},{7,6},{8,9},{9,8},{14,15},{15,14},{16,17},{17,16... | collective-permute-start | bytes 3538952 | tf_op jit(solution)/shard_map/ppermute | solution.py:672
  536.0 9.6 %collective-permute-start.39 = (bf16[4,192,192]{2,1,0:T(8,128)(2,1)S(1)}, bf16[4,192,192]{2,1,0:T(8,128)(2,1)S(1)}, u32[]{:S(2)}, u32[]{:S(2)}) collective-permute-start(bf16[4,192,192]{2,1,0:T(8,128)(2,1)S(1)} %constant_dynamic-slice_fusion.2), channel_id=1, source_target_pairs={{0,8},{8,0},{1,9},{9,1},{2,10},{10,2},{3,11},{11,3},{4,12},{12,4},... | collective-permute-start | bytes 884744 | tf_op jit(solution)/shard_map/ppermute | solution.py:667
  542.3 41.2 %collective-permute-start.38 = (bf16[768,768]{1,0:T(8,128)(2,1)}, bf16[768,768]{1,0:T(8,128)(2,1)}, u32[]{:S(2)}, u32[]{:S(2)}) collective-permute-start(bf16[768,768]{1,0:T(8,128)(2,1)} %fusion.20), channel_id=1, source_target_pairs={{2,4},{4,2},{3,5},{5,3},{10,12},{12,10},{11,13},{13,11},{18,20},{2... | collective-permute-start | bytes 3538952 | tf_op jit(solution)/shard_map/ppermute | solution.py:890
  546.5 25.8 %collective-permute-start.41 = (bf16[4,96,192]{2,1,0:T(8,128)(2,1)S(1)}, bf16[4,96,192]{2,1,0:T(8,128)(2,1)S(1)}, u32[]{:S(2)}, u32[]{:S(2)}) collective-permute-start(bf16[4,96,192]{2,1,0:T(8,128)(2,1)S(1)} %get-tuple-element.239), channel_id=1, source_target_pairs={{0,4},{2,0},{4,6},{6,2},{1,5},{3,1},{5,7},{7,3},{8,12},{10,8},{12,... | collective-permute-start | bytes 442376 | tf_op jit(solution)/shard_map/ppermute | solution.py:712
  574.2 4.4 collective-permute-start.42
  579.3 3.7 collective-permute-start.43
  (69 other events, 930.8 us)
Sparse Core Ops, SparseCore 0:
  56.4 30.2 all-gather.3
  133.6 40.3 all-gather.5
  175.9 38.9 all-gather.7
  314.0 57.3 reduce-scatter.2
  374.3 57.3 reduce-scatter.4

commit v4 on v3

--- a/solution.py
+++ b/solution.py
@@ -12,6 +12,8 @@
 LOG2E = 1.4426950408889634
 NEGATIVE = -1e30
 TILE = 256
+CHUNK = 256
+TOKEN = (16, 128)
 ALIGN = 16
 CONTINUATIONS = 8
 HBM = pl.BlockSpec(memory_space=pl.ANY)
@@ -416,15 +418,14 @@
     kept = jnp.sum(ahead.astype(jnp.int32), axis=1) < capacity
     kinds = jnp.arange(experts, dtype=jnp.int32)
     block_hot = (route.reshape(-1, row_count)[:, :, None] == kinds).astype(jnp.int32)
-    lengths = (jnp.sum(block_hot, axis=1) + ALIGN - 1) // ALIGN * ALIGN
+    lengths = jnp.sum(block_hot, axis=1)
     starts = jnp.cumsum(lengths, axis=1) - lengths
     own_hot = (own_route[:, None] == kinds).astype(jnp.int32)
     index = jnp.arange(row_count, dtype=jnp.int32)
     before = (own_route[None, :] == own_route[:, None]) & (index[None, :] < index[:, None])
     own_starts = lax.dynamic_slice_in_dim(starts, ranks[0], 1, 0)
     place = jnp.sum(before.astype(jnp.int32), axis=1) + jnp.sum(own_hot * own_starts, axis=1)
-    slots = jnp.arange(row_count + experts * ALIGN, dtype=jnp.int32)
-    order = (slots[:, None] == place[None, :]).astype(jnp.bfloat16)
+    order = (index[:, None] == place[None, :]).astype(jnp.bfloat16)
     picked = [
         lax.dynamic_slice_in_dim(array, ranks[b], 1, 0)[0]
         for array in (starts, lengths)
@@ -442,17 +443,25 @@
     return matmul(order, rows.astype(jnp.bfloat16), ((0,), (0,)))
 
 
-def each_tile(table, expert, experts, visit):
-    for block in range(4):
-        start = table[block * experts + expert]
-        length = table[(4 + block) * experts + expert]
-
-        def tile(number, carry, block=block, start=start, length=length):
-            place = pl.ds(pl.multiple_of(start + number * TILE, ALIGN), TILE)
-            visit(block, place, length - number * TILE)
-            return carry
-
-        lax.fori_loop(0, (length + TILE - 1) // TILE, tile, 0)
+def each_tile(table, block, expert, experts, visit):
+    start = table[block * experts + expert]
+    end = start + table[(4 + block) * experts + expert]
+    first = start // ALIGN * ALIGN
+
+    def tile(number, carry):
+        at = first + number * TILE
+        visit(pl.ds(pl.multiple_of(at, ALIGN), TILE), start - at, end - at)
+        return carry
+
+    lax.fori_loop(0, jnp.where(end > start, (end - first + TILE - 1) // TILE, 0), tile, 0)
+
+
+def put_rows(ref, block, place, rows, head):
+    top = pl.ds(place.start, ALIGN)
+    old = ref[block, top, :]
+    index = lax.broadcasted_iota(jnp.int32, old.shape, 0)
+    ref[block, place, :] = rows
+    ref[block, top, :] = jnp.where(index < head, old, rows[:ALIGN])
 
 
 def fetch_weights(choice, kept, given, targets, semaphores):
@@ -476,96 +485,135 @@
         ).wait()
 
 
-def within(rows, left):
-    return jnp.where(lax.broadcasted_iota(jnp.int32, rows.shape, 0) < left, rows, 0)
+def within(rows, head, end):
+    index = lax.broadcasted_iota(jnp.int32, rows.shape, 0)
+    return jnp.where((index >= head) & (index < end), rows, 0)
+
+
+def block_copies(block, pairs, semaphores):
+    for place, (source, targets) in enumerate(pairs):
+        for b in range(4):
+
+            @pl.when(block == b)
+            def _(place=place, source=source, targets=targets, b=b):
+                target = targets[b] if isinstance(targets, tuple) else targets.at[b]
+                rows = source.at[b, : target.shape[0]]
+                pltpu.make_async_copy(rows, target, semaphores.at[place, b]).start()
+
+
+def await_blocks(pairs, semaphores):
+    for place, (source, targets) in enumerate(pairs):
+        for b in range(4):
+            target = targets[b] if isinstance(targets, tuple) else targets.at[b]
+            rows = source.at[b, : target.shape[0]]
+            pltpu.make_async_copy(rows, target, semaphores.at[place, b]).wait()
+
+
+def moe_steps(table, experts, inputs, weights, outputs, tails, visit, semaphores):
+    block = pl.program_id(0)
+    kept, given, held = weights
+    arrived, left, ready = semaphores
+    count = inputs[0][1][0].shape[0]
+
+    @pl.when(block == 0)
+    def _():
+        for place, (target, sources) in enumerate(inputs):
+            for b in range(4):
+                source = sources[b] if isinstance(sources, tuple) else sources.at[b]
+                rows = target.at[b, : source.shape[0]]
+                pltpu.make_async_copy(source, rows, arrived.at[place, b]).start()
+        fetch_weights(table[8 * experts], kept, given, held, ready)
+        for ref in tails:
+            ref[:, count:, :] = jnp.zeros((4, TILE, ref.shape[2]), ref.dtype)
+
+    for place, (target, sources) in enumerate(inputs):
+        source = sources[0] if isinstance(sources, tuple) else sources.at[0]
+        rows = target.at[block, : source.shape[0]]
+        pltpu.make_async_copy(source, rows, arrived.at[place, block]).wait()
+
+    def expert_rows(expert, carry):
+        @pl.when(block == 0)
+        def _():
+            await_weights(kept, held, expert, ready)
+
+        each_tile(
+            table, block, expert, experts,
+            lambda place, head, end: visit(block, expert, place, head, end),
+        )
+        return carry
+
+    lax.fori_loop(0, experts, expert_rows, 0)
+    block_copies(block, outputs, left)
+
+    @pl.when(block == 3)
+    def _():
+        await_blocks(outputs, left)
 
 
 def moe_forward_kernel(
     table, x0, x1, x2, x3, own_up, own_down, new_up, new_down,
     y0, y1, y2, y3, hidden_out, slope_out,
-    x_ref, y_ref, hidden_ref, slope_ref, up_ref, down_ref, semaphores, ready,
+    x_ref, y_ref, hidden_ref, slope_ref, up_ref, down_ref, *semaphores,
 ):
-    expert = pl.program_id(0)
-    experts = pl.num_programs(0)
-    count = x0.shape[0]
-    kept, given, held = (own_up, own_down), (new_up, new_down), (up_ref, down_ref)
-
-    @pl.when(expert == 0)
-    def _():
-        fetch_weights(table[8 * experts], kept, given, held, ready)
-        for ref in (hidden_ref, slope_ref, y_ref):
-            ref[...] = jnp.zeros_like(ref)
-        x_ref[:, count:, :] = jnp.zeros((4, TILE, x_ref.shape[2]), jnp.bfloat16)
-        copies([(x, x_ref.at[b, :count]) for b, x in enumerate((x0, x1, x2, x3))], semaphores)
-
-    await_weights(kept, held, expert, ready)
-
-    def visit(block, place, left):
-        u = matmul(x_ref[block, place, :], up_ref[expert])
-        bend = jnp.tanh(0.7978845608028654 * (u + 0.044715 * u * u * u))
-        hidden = (0.5 * u * (1.0 + bend)).astype(jnp.bfloat16)
-        slope = 0.5 * (1.0 + bend) + 0.5 * u * (1.0 - bend * bend) * (
-            0.7978845608028654 * (1.0 + 3.0 * 0.044715 * u * u)
-        )
-        hidden_ref[block, place, :] = hidden
-        slope_ref[block, place, :] = slope.astype(jnp.bfloat16)
-        y_ref[block, place, :] = matmul(hidden, down_ref[expert]).astype(jnp.bfloat16)
-
-    each_tile(table, expert, experts, visit)
-
-    @pl.when(expert == experts - 1)
-    def _():
-        copies(
-            [(y_ref.at[b, :count], y) for b, y in enumerate((y0, y1, y2, y3))]
-            + [(hidden_ref, hidden_out), (slope_ref, slope_out)],
-            semaphores,
-        )
+    width = up_ref.shape[2]
+
+    def visit(block, expert, place, head, end):
+        x = x_ref[block, place, :]
+        total = None
+        for part in range(0, width, CHUNK):
+            chunk = slice(part, part + CHUNK)
+            u = matmul(x, up_ref[expert, :, chunk])
+            cube = 0.7978845608028654 * u * (1.0 + 0.044715 * u * u)
+            bend = 1.0 + jnp.tanh(cube)
+            half = 0.5 * bend
+            hidden = (u * half).astype(jnp.bfloat16)
+            slope = half + u * (half * (2.0 - bend)) * (
+                0.7978845608028654 * (1.0 + 3.0 * 0.044715 * u * u)
+            )
+            put_rows(hidden_ref.at[:, :, chunk], block, place, hidden, head)
+            put_rows(slope_ref.at[:, :, chunk], block, place, slope.astype(jnp.bfloat16), head)
+            term = matmul(hidden, down_ref[expert, chunk, :])
+            total = term if total is None else total + term
+        put_rows(y_ref, block, place, total.astype(jnp.bfloat16), head)
+
+    moe_steps(
+        table, up_ref.shape[0], [(x_ref, (x0, x1, x2, x3))],
+        ((own_up, own_down), (new_up, new_down), (up_ref, down_ref)),
+        [(y_ref, (y0, y1, y2, y3)), (hidden_ref, hidden_out), (slope_ref, slope_out)],
+        (x_ref, hidden_ref, slope_ref), visit, semaphores,
+    )
 
 
 def moe_backward_kernel(
     table, d0, d1, d2, d3, slope_in, own_up, own_down, new_up, new_down,
     y0, y1, y2, y3, grad_out,
-    d_ref, slope_ref, y_ref, grad_ref, up_ref, down_ref, semaphores, ready,
+    d_ref, slope_ref, y_ref, grad_ref, up_ref, down_ref, *semaphores,
 ):
-    expert = pl.program_id(0)
-    experts = pl.num_programs(0)
-    count = d0.shape[0]
-    kept, given, held = (own_up, own_down), (new_up, new_down), (up_ref, down_ref)
-
-    @pl.when(expert == 0)
-    def _():
-        fetch_weights(table[8 * experts], kept, given, held, ready)
-        for ref in (grad_ref, y_ref):
-            ref[...] = jnp.zeros_like(ref)
-        d_ref[:, count:, :] = jnp.zeros((4, TILE, d_ref.shape[2]), jnp.bfloat16)
-        copies(
-            [(d, d_ref.at[b, :count]) for b, d in enumerate((d0, d1, d2, d3))]
-            + [(slope_in, slope_ref)],
-            semaphores,
-        )
-
-    await_weights(kept, held, expert, ready)
-
-    def visit(block, place, left):
-        upstream = within(d_ref[block, place, :], left)
-        slope = slope_ref[block, place, :].astype(jnp.float32)
-        grad = (matmul(upstream, down_ref[expert], ((1,), (1,))) * slope).astype(jnp.bfloat16)
-        grad_ref[block, place, :] = grad
-        y_ref[block, place, :] = matmul(grad, up_ref[expert], ((1,), (1,))).astype(jnp.bfloat16)
-
-    each_tile(table, expert, experts, visit)
-
-    @pl.when(expert == experts - 1)
-    def _():
-        copies(
-            [(y_ref.at[b, :count], y) for b, y in enumerate((y0, y1, y2, y3))]
-            + [(grad_ref, grad_out)],
-            semaphores,
-        )
+    width = up_ref.shape[2]
+
+    def visit(block, expert, place, head, end):
+        upstream = within(d_ref[block, place, :], head, end)
+        total = None
+        for part in range(0, width, CHUNK):
+            chunk = slice(part, part + CHUNK)
+            slope = slope_ref[block, place, chunk].astype(jnp.float32)
+            grad = matmul(upstream, down_ref[expert, chunk, :], ((1,), (1,))) * slope
+            grad = grad.astype(jnp.bfloat16)
+            put_rows(grad_ref.at[:, :, chunk], block, place, grad, head)
+            term = matmul(grad, up_ref[expert, :, chunk], ((1,), (1,)))
+            total = term if total is None else total + term
+        put_rows(y_ref, block, place, total.astype(jnp.bfloat16), head)
+
+    moe_steps(
+        table, up_ref.shape[0], [(d_ref, (d0, d1, d2, d3)), (slope_ref, slope_in)],
+        ((own_up, own_down), (new_up, new_down), (up_ref, down_ref)),
+        [(y_ref, (y0, y1, y2, y3)), (grad_ref, grad_out)],
+        (d_ref, grad_ref), visit, semaphores,
+    )
 
 
 def moe_weights_kernel(
-    table, a0, a1, a2, a3, b_in, out_ref, a_ref, b_ref, sum_ref, semaphores
+    table, a0, a1, a2, a3, b_in, token_in, out_ref, token_ref, a_ref, b_ref, sum_ref, semaphores
 ):
     expert = pl.program_id(0)
     experts = pl.num_programs(0)
@@ -573,6 +621,7 @@
 
     @pl.when(expert == 0)
     def _():
+        token_ref[...] = jnp.zeros_like(token_ref)
         a_ref[:, count:, :] = jnp.zeros((4, TILE, a_ref.shape[2]), jnp.bfloat16)
         copies(
             [(a, a_ref.at[b, :count]) for b, a in enumerate((a0, a1, a2, a3))] + [(b_in, b_ref)],
@@ -581,37 +630,32 @@
 
     sum_ref[...] = jnp.zeros_like(sum_ref)
 
-    def visit(block, place, left):
-        sum_ref[...] += matmul(
-            within(a_ref[block, place, :], left), b_ref[block, place, :], ((0,), (0,))
-        )
-
-    each_tile(table, expert, experts, visit)
+    def of_block(block, carry):
+        def visit(place, head, end):
+            rows = within(a_ref[block, place, :], head, end)
+            sum_ref[...] += matmul(rows, b_ref[block, place, :], ((0,), (0,)))
+
+        each_tile(table, block, expert, experts, visit)
+        return carry
+
+    lax.fori_loop(0, 4, of_block, 0)
     out_ref[0] = sum_ref[...].astype(jnp.bfloat16)
 
 
-def moe_call(kernel, name, table, arrays, outs, scratch, sums, experts, cost):
-    low = jnp.bfloat16
-    specs = [HBM] * len(outs)
-    ready = [pltpu.SemaphoreType.DMA((2, experts))]
-    if sums:
-        specs = [pl.BlockSpec((1,) + outs[0][1:], lambda e, t: (e, 0, 0))]
-        ready = []
+def moe_call(kernel, name, table, arrays, grid, specs, outs, scratch, semaphores, cost):
     return pl.pallas_call(
         kernel,
         grid_spec=pltpu.PrefetchScalarGridSpec(
             num_scalar_prefetch=1,
-            grid=(experts,),
+            grid=(grid,),
             in_specs=[HBM] * len(arrays),
             out_specs=specs,
             scratch_shapes=[
-                *[pltpu.VMEM(shape, low) for shape in scratch],
-                *[pltpu.VMEM(shape, jnp.float32) for shape in sums],
-                pltpu.SemaphoreType.DMA((10,)),
-                *ready,
+                *[pltpu.VMEM(*shape) for shape in scratch],
+                *[pltpu.SemaphoreType.DMA(shape) for shape in semaphores],
             ],
         ),
-        out_shape=[jax.ShapeDtypeStruct(shape, low) for shape in outs],
+        out_shape=[jax.ShapeDtypeStruct(shape, jnp.bfloat16) for shape in outs],
         compiler_params=pltpu.CompilerParams(vmem_limit_bytes=58 << 20),
         cost_estimate=pl.CostEstimate(flops=cost, transcendentals=0, bytes_accessed=40 << 20),
         name=name,
@@ -621,12 +665,13 @@
 def moe_forward(table, x, own, new):
     count, width = x[0].shape
     experts, _, hidden = own[0].shape
-    wide, tall = (4, count + TILE, width), (4, count + TILE, hidden)
+    low = jnp.bfloat16
+    wide, tall = ((4, count + TILE, width), low), ((4, count + TILE, hidden), low)
     *y, hid, slope = moe_call(
-        moe_forward_kernel, "moe_forward", table, [*x, *own, *new],
-        [(count, width)] * 4 + [tall, tall],
-        [wide, wide, tall, tall, own[0].shape, own[1].shape], [], experts,
-        20 * count * width * hidden,
+        moe_forward_kernel, "moe_forward", table, [*x, *own, *new], 4, [HBM] * 6,
+        [(count, width)] * 4 + [tall[0], tall[0]],
+        [wide, wide, tall, tall, (own[0].shape, low), (own[1].shape, low)],
+        [(1, 4), (3, 4), (2, experts)], 20 * count * width * hidden,
     )
     return (y, hid, slope)
 
@@ -634,24 +679,31 @@
 def moe_backward(table, d, slope, own, new):
     count, width = d[0].shape
     experts, _, hidden = own[0].shape
-    wide, tall = (4, count + TILE, width), (4, count + TILE, hidden)
+    low = jnp.bfloat16
+    wide, tall = ((4, count + TILE, width), low), ((4, count + TILE, hidden), low)
     *y, grad = moe_call(
-        moe_backward_kernel, "moe_backward", table, [*d, slope, *own, *new],
-        [(count, width)] * 4 + [tall],
-        [wide, tall, wide, tall, own[0].shape, own[1].shape], [], experts,
-        20 * count * width * hidden,
+        moe_backward_kernel, "moe_backward", table, [*d, slope, *own, *new], 4, [HBM] * 5,
+        [(count, width)] * 4 + [tall[0]],
+        [wide, tall, wide, tall, (own[0].shape, low), (own[1].shape, low)],
+        [(2, 4), (2, 4), (2, experts)], 20 * count * width * hidden,
     )
     return (y, grad)
 
 
-def moe_weights(table, blocks, tall, experts):
+def moe_weights(table, blocks, tall, token, experts):
     count, width = blocks[0].shape
     hidden = tall.shape[2]
     return moe_call(
-        moe_weights_kernel, "moe_weights", table, [*blocks, tall], [(experts, width, hidden)],
-        [(4, count + TILE, width), tall.shape], [(width, hidden)], experts,
-        10 * count * width * hidden,
-    )[0]
+        moe_weights_kernel, "moe_weights", table, [*blocks, tall, token], experts,
+        [
+            pl.BlockSpec((1, width, hidden), lambda e, t: (e, 0, 0)),
+            pl.BlockSpec(TOKEN, lambda e, t: (0, 0)),
+        ],
+        [(experts, width, hidden), TOKEN],
+        [((4, count + TILE, width), jnp.bfloat16), (tall.shape, jnp.bfloat16),
+         ((width, hidden), jnp.float32)],
+        [(5,)], 10 * count * width * hidden,
+    )
 
 
 def at_home():
@@ -695,13 +747,16 @@
     return near_rows(blocks) + flip(far_rows(blocks), "zl").astype(jnp.float32)
 
 
-def halve(value, axis, dimension):
+def send_half(value, axis, dimension):
     count = value.shape[dimension] // 2
     side = lax.axis_index(axis)
     kept = lax.dynamic_slice_in_dim(value, side * count, count, dimension)
     sent = lax.dynamic_slice_in_dim(value, (1 - side) * count, count, dimension)
-    total = kept.astype(jnp.float32) + flip(sent, axis).astype(jnp.float32)
-    return total.astype(value.dtype)
+    return [kept, flip(sent, axis)]
+
+
+def halve(kept, came):
+    return (kept.astype(jnp.float32) + came.astype(jnp.float32)).astype(kept.dtype)
 
 
 def send_home(value, dimension):
@@ -838,16 +893,15 @@
     returned_far, back_moe[3] = tie(returned_far, back_moe[3])
     back_far, hidden = tie(far_rows(back_moe), hidden)
     back_far = flip(back_far, "zl")
-    down_part = moe_weights(table, grad_dispatched, hidden, experts)
-    down_rest = lax.psum_scatter(down_part, high_bits, scatter_dimension=1, tiled=True)
+    back_near = near_rows(back_moe)
+    down_part, token = moe_weights(table, grad_dispatched, hidden, back_moe[3], experts)
+    back_far, token = tie(back_far, token)
     expert_out = unsort_rows(order, returned_near + returned_far.astype(jnp.float32))
     mixed_two = (mixed_one + gate_used[:, None] * expert_out).astype(jnp.bfloat16)
     grad_gate = jnp.where(kept_rows, jnp.sum(upstream * expert_out, axis=-1), 0.0)
     grad_score = grad_gate * gate_prob * (1.0 - gate_prob)
-    grad_score, grad_upward = tie(grad_score, grad_upward)
-    up_part = moe_weights(table, dispatched, grad_upward, experts)
-    back_far, up_part = tie(back_far, up_part)
-    back_moe = near_rows(back_moe) + back_far.astype(jnp.float32)
+    down_rest = lax.psum_scatter(down_part, high_bits, scatter_dimension=1, tiled=True)
+    back_moe = back_near + back_far.astype(jnp.float32)
     grad_two = unsort_rows(order, back_moe) + grad_score[:, None] * centroid_rows
     centroid_part = jnp.einsum(
         "te,td->ed",
@@ -857,14 +911,16 @@
     )
     moe_gain_part = jnp.sum(grad_two * unit_two, axis=0)
     grad_mixed = upstream + normalize_back(grad_two, unit_two, inverse_two, moe_gain)
+    grad_mixed, grad_upward = tie(grad_mixed, grad_upward)
+    up_part, _ = moe_weights(table, dispatched, grad_upward, token, experts)
     grad_att = gather_blocks(grad_mixed.astype(jnp.bfloat16))
-    up_rest = lax.psum_scatter(up_part, high_bits, scatter_dimension=1, tiled=True)
     early = jnp.concatenate([moe_gain_part[None], centroid_part], axis=0)
     everyone = (*users, "zh", "zl")
     early = jnp.swapaxes(early.reshape(experts + 1, lax.axis_size(everyone), -1), 0, 1)
     early = jnp.sum(lax.all_to_all(early, everyone, 0, 0, tiled=True), axis=0)
-    grad_att[2], early = tie(grad_att[2], early)
+    grad_att[2], early, up_part = tie(grad_att[2], early, up_part)
     grad_att[3] = flip(grad_att[2], "c")
+    up_rest = lax.psum_scatter(up_part, high_bits, scatter_dimension=1, tiled=True)
     down_rest, mixed_two, grad_att[3] = tie(down_rest, mixed_two, grad_att[3])
     down_home = send_home(down_rest, 1)
     away_output = lax.ppermute(mixed_two, ("c", "zh"), [(1, 2), (2, 1)])
@@ -872,7 +928,6 @@
         back_ranges, start, ranks, grad_att, normed_one, saved, qkv_used, proj_used
     )
     grad_one[3], away_output, *down_home = tie(grad_one[3], away_output, *down_home)
-    block_output = jnp.where(home, mixed_two, away_output)[None]
     one_far = far_rows(grad_one)
     one_near = near_rows(grad_one)
 
@@ -883,29 +938,33 @@
         return (grad_mixed + grad).astype(jnp.bfloat16)
 
     going = flip_some(one_far, False)
-    going, one_far, *up_home = tie(going, one_far, *send_home(up_rest, 1))
+    weights_part = lax.psum_scatter(weights_part, high_bits, scatter_dimension=1, tiled=True)
+    going, one_far, weights_part, *up_home = tie(
+        going, one_far, weights_part, *send_home(up_rest, 1)
+    )
+    going, one_far, weights_part, away_output, *homes = tie(
+        finish(going), one_far, weights_part, away_output, *down_home, *up_home
+    )
+    down_home, up_home = homes[:3], homes[3:]
+    block_output = jnp.where(home, mixed_two, away_output)[None]
+    going = lax.ppermute(going, ("c", "zh"), [(1, 2), (2, 1)])
     kept_far = flip_some(one_far, True)
-    weights_part = halve(weights_part, high_bits[0], 1)
-    going, weights_part = tie(finish(going), weights_part)
-    going = lax.ppermute(going, ("c", "zh"), [(1, 2), (2, 1)])
     input_grad = jnp.where(home, finish(kept_far), going)[None]
     down_summed = jnp.swapaxes(sum_home(*down_home), 1, 2)
     up_summed = sum_home(*up_home)
-    for bit in high_bits[1:]:
-        weights_part = halve(weights_part, bit, 1)
     weights_part = sum_home(*send_home(weights_part, 1))
     qkv_summed, proj_summed = weights_part[:3], weights_part[3].T
     gain_two_sum, centroid_sum = early[0], early[1:]
+    entries = gain_two_sum.shape[0]
+    own_entries = lax.axis_index(everyone) * entries
     slice_rows = qkv_summed.shape[1]
     own_rows = lax.dynamic_slice_in_dim(
         qkv_weight, lax.axis_index(users) * slice_rows, slice_rows, 1
     )
     gain_one = jnp.sum(own_rows.astype(jnp.float32) * qkv_summed, axis=(0, 2))
     for bit in ("zh", "zl"):
-        gain_one = halve(gain_one, bit, 0)
-    entries = gain_one.shape[0]
-    own_gain = lax.axis_index((*users, "zh", "zl")) * entries
-    gain_one_sum = gain_one / lax.dynamic_slice_in_dim(attention_gain, own_gain, entries, 0)
+        gain_one = halve(*send_half(gain_one, bit, 0))
+    gain_one_sum = gain_one / lax.dynamic_slice_in_dim(attention_gain, own_entries, entries, 0)
     return (
         block_output,
         input_grad,

time: 604 us -> 578 us (0.957)
  blocking collectives: 29.1 us -> 0 us
  Pallas kernels: 208 us -> 200 us
  other arithmetic: 64.8 us -> 72.4 us
    ppermute x3, waiting for transfers between devices: 49.8 us -> 13.8 us  [send_home(): turned = lax.ppermute(turned, ('c', 'zh'), [(0, 2), (1, 0), (2, 3), (3, 1)])]
    all_to_all x1 -> x0, blocking collectives: 29.1 us -> none  [body(): early = jnp.sum(lax.all_to_all(early, everyone, 0, 0, tiled=True), axis=0)]
    ppermute x30 -> x28, waiting for transfers between devices: 80.5 us -> 109 us  [flip(): return lax.ppermute(value, axis, [(0, 1), (1, 0)])]
    reduce_scatter x0 -> x1, waiting for transfers between devices: none -> 12.3 us  [body(): lax.psum_scatter(weights_part, high_bits, scatter_dimension=1, tiled=True)]
    ppermute x4, waiting for transfers between devices: 20.9 us -> 12.9 us  [flip_some(): return lax.ppermute(value, ('c', 'zh', 'zl'), moves)]
    pallas_call x4, Pallas kernels: 92.8 us -> 85.5 us  [moe_call(): pl.pallas_call(kernel, grid_spec=pltpu.PrefetchScalarGridSpec(num_scalar_...]
    ppermute x30 -> x28, starting transfers between devices: 36.3 us -> 33.8 us  [flip(): return lax.ppermute(value, axis, [(0, 1), (1, 0)])]
    unnamed x138 -> x136, local copies, waits for them, and re-layouts: 11.7 us -> 12.7 us
where the time goes in v4:
time: 578 us; the launch traced here: 569 us
  Pallas kernels  200 us (35%)
  waiting for transfers between devices  160 us (28%)
  other arithmetic  72.4 us (13%)
  starting transfers between devices  63.8 us (11%)
  local copies, waits for them, and re-layouts  42.8 us (7%)
  between operations  15.5 us (3%)
  matrix products  13.9 us (2%)
    ppermute x28, waiting for transfers between devices, flip(): return lax.ppermute(value, axis, [(0, 1), (1, 0)])  109 us
    pallas_call x4, Pallas kernels, moe_call(): pl.pallas_call(kernel, grid_spec=pltpu.PrefetchScalarGridSpec(num_scalar_...  85.5 us
    pallas_call x1, Pallas kernels, attention_backward(): pl.pallas_call(backward_kernel, grid_spec=pltpu.PrefetchScalarGridSpec(nu...  71.5 us
    pallas_call x1, Pallas kernels, attention_forward(): pl.pallas_call(forward_kernel, grid_spec=pltpu.PrefetchScalarGridSpec(num...  43.4 us
    ppermute x28, starting transfers between devices, flip(): return lax.ppermute(value, axis, [(0, 1), (1, 0)])  33.8 us
    ppermute x3, waiting for transfers between devices, send_home(): turned = lax.ppermute(turned, ('c', 'zh'), [(0, 2), (1, 0), (2, 3), (3, 1)])  13.8 us
    ppermute x4, waiting for transfers between devices, flip_some(): return lax.ppermute(value, ('c', 'zh', 'zl'), moves)  12.9 us
    unnamed x136, local copies, waits for them, and re-layouts  12.7 us
  transfers between devices with their start and end apart: 49, of which 21 were waited for; matrix products, arithmetic and copies ran while one was open for 17% of the time, Pallas kernels for 32%

profile of v4, /device:TPU:0, one launch (start us, length us, event | category | flops | bytes accessed | tf_op | source)
XLA Modules:
  0.0 568.5 jit_solution(8400471794926129123)
XLA Ops:
  12.1 3.6 collective-permute-start.1
  17.9 3.5 collective-permute-start.2
  35.5 12.9 %collective-permute-done.2 = bf16[768,768]{1,0:T(8,128)(2,1)} collective-permute-done((bf16[768,768]{1,0:T(8,128)(2,1)}, bf16[768,768]{1,0:T(8,128)(2,1)}, u32[]{:S(2)}, u32[]{:S(2)}) %collective-permute-start.2) | collective-permute-done | bytes 1179680 | tf_op jit(solution)/shard_map/ppermute | solution.py:724
  49.4 3.2 convert_reduce_fusion.1
  52.6 2.0 broadcast_select_fusion.4
  60.3 3.3 collective-permute-start.4
  63.7 2.4 broadcast_select_fusion.3.x2
  66.1 10.6 %collective-permute-start.6 = (bf16[768,768]{1,0:T(8,128)(2,1)}, bf16[768,768]{1,0:T(8,128)(2,1)}, u32[]{:S(2)}, u32[]{:S(2)}) collective-permute-start(bf16[768,768]{1,0:T(8,128)(2,1)} %broadcast_select_fusion.3.x2), channel_id=1, source_target_pairs={{0,4},{4,0},{1,5},{5,1},{2,6},{6,2},{3,7},{7,3},{8,12},{12,8},{9,1... | collective-permute-start | bytes 3538952 | tf_op jit(solution)/shard_map/ppermute | solution.py:719
  77.3 3.4 collective-permute-start.7
  80.7 6.0 %all-gather.4.cloned.1.call-done = bf16[3072,192]{1,0:T(8,128)(2,1)} async-done(((bf16[384,192]{1,0:T(8,128)(2,1)}), bf16[3072,192]{1,0:T(8,128)(2,1)}) %all-gather.4.cloned.1.call-update) | async-done | bytes 1179664 | tf_op jit(solution)/shard_map/all_gather | solution.py:783
  89.3 43.4 %attention_forward.1 = (bf16[768,768]{1,0:T(8,128)(2,1)}, bf16[768,768]{1,0:T(8,128)(2,1)}, bf16[768,768]{1,0:T(8,128)(2,1)}, bf16[768,768]{1,0:T(8,128)(2,1)}, ...) custom-call(s32[5,6]{1,0:T(8,128)} %stack.33.ranges, ...), custom_call_target="tpu_custom_call" | custom-call | flops 28991029248 | bytes 41943040 | tf_op jit(solution)/shard_map/attention_forward/pallas_call | solution.py:194
  155.1 2.6 convert_reduce_fusion
  158.9 24.3 %collective-permute-done.10 = bf16[768,768]{1,0:T(8,128)(2,1)S(1)} collective-permute-done((bf16[768,768]{1,0:T(8,128)(2,1)S(1)}, bf16[768,768]{1,0:T(8,128)(2,1)S(1)}, u32[]{:S(2)}, u32[]{:S(2)}) %collective-permute-start.10) | collective-permute-done | bytes 1179680 | tf_op jit(solution)/shard_map/ppermute | solution.py:719
  184.2 4.0 fusion.58
  188.9 2.2 fusion.27
  194.1 2.3 convolution_convert_fusion.d0.a0
  196.4 23.5 %collective-permute-done.12.x2.a2 = bf16[768,768]{1,0:T(8,128)(2,1)S(1)} collective-permute-done((bf16[768,768]{1,0:T(8,128)(2,1)S(1)}, bf16[768,768]{1,0:T(8,128)(2,1)S(1)}, u32[]{:S(2)}, u32[]{:S(2)}) %collective-permute-start.12) | collective-permute-done | bytes 1179680 | tf_op jit(solution)/shard_map/ppermute | solution.py:719
  222.9 28.5 %moe_forward.1 = (bf16[768,768]{1,0:T(8,128)(2,1)}, bf16[768,768]{1,0:T(8,128)(2,1)}, bf16[768,768]{1,0:T(8,128)(2,1)}, bf16[768,768]{1,0:T(8,128)(2,1)}, bf16[4...) custom-call(s32[33]{0:T(128)} %concatenate.15.table, bf16[768,768]{1,0:T(8,128)(2,1)} %copy-done.60, ...), custom_call_target="tpu_custom_call" | custom-call | flops 9059696640 | bytes 41943040 | tf_op jit(solution)/shard_map/moe_forward/pallas_call | solution.py:646
  252.1 2.5 collective-permute-done.18
  259.0 24.4 %moe_backward.1 = (bf16[768,768]{1,0:T(8,128)(2,1)}, bf16[768,768]{1,0:T(8,128)(2,1)}, bf16[768,768]{1,0:T(8,128)(2,1)}, bf16[768,768]{1,0:T(8,128)(2,1)}, bf16[4,1024,768]{2,1,0:T(8,128)(2,1)}) custom-call(s32[33]{0:T(128)} %concatenate.15.table, bf16[768,768]{1,0:T(8,128)(2,1)} %convolution_convert_fusion.d0.a0, bf16[768,768]{1,0:T(8,128)(2,1)} %copy-done.65, ...), custom_call_target="tpu_custom_call" | custom-call | flops 9059696640 | bytes 41943040 | tf_op jit(solution)/shard_map/moe_backward/pallas_call | solution.py:646
  284.3 3.1 collective-permute-done.21
  287.4 2.7 add_convert_fusion.4
  290.0 16.3 %moe_weights.2 = (bf16[4,768,768]{2,1,0:T(8,128)(2,1)}, bf16[16,128]{1,0:T(8,128)(2,1)}) custom-call(s32[33]{0:T(128)} %concatenate.15.table, bf16[768,768]{1,0:T(8,128)(2,1)} %convolution_convert_fusion.d0.a0, bf16[768,768]{1,0:T(8,128)(2,1)} %copy-done.65, bf16[768,768]{1,0:T(8,128)(2,1)} %collective-permute-done.15.d2.a2, bf16[768,768]{1,0:T(8,128)(2,1)} %copy-done.64, ...), custom_call_target="tpu_custom_call" | custom-call | flops 4529848320 | bytes 41943040 | tf_op jit(solution)/shard_map/moe_weights/pallas_call | solution.py:646
  307.0 2.4 collective-permute-done.22
  309.5 3.7 fusion.30
  313.2 21.8 %collective-permute-done.24 = bf16[768,768]{1,0:T(8,128)(2,1)S(1)} collective-permute-done((bf16[768,768]{1,0:T(8,128)(2,1)}, bf16[768,768]{1,0:T(8,128)(2,1)S(1)}, u32[]{:S(2)}, u32[]{:S(2)}) %collective-permute-start.24) | collective-permute-done | bytes 1179680 | tf_op jit(solution)/shard_map/ppermute | solution.py:719
  335.1 2.6 multiply_reduce_fusion
  337.7 3.3 convert_add_fusion
  342.7 2.0 fusion.28
  348.4 5.0 all-to-all-start
  353.4 16.2 %moe_weights.3 = (bf16[4,768,768]{2,1,0:T(8,128)(2,1)}, bf16[16,128]{1,0:T(8,128)(2,1)}) custom-call(s32[33]{0:T(128)} %concatenate.15.table, bf16[768,768]{1,0:T(8,128)(2,1)} %copy-done.60, bf16[768,768]{1,0:T(8,128)(2,1)} %copy-done.62, bf16[768,768]{1,0:T(8,128)(2,1)} %copy-done.61, bf16[768,768]{1,0:T(8,128)(2,1)} %collective-permute-done.17.x3.a3, ...), custom_call_target="tpu_custom_call" | custom-call | flops 4529848320 | bytes 41943040 | tf_op jit(solution)/shard_map/moe_weights/pallas_call | solution.py:646
  369.6 4.9 all-to-all-done
  376.7 2.7 collective-permute-done.26.g3
  384.2 71.5 %attention_backward.1 = (bf16[768,768]{1,0:T(8,128)(2,1)}, bf16[768,768]{1,0:T(8,128)(2,1)}, bf16[768,768]{1,0:T(8,128)(2,1)}, bf16[768,768]{1,0:T(8,128)(2,1)}, bf16[4,768,192]{2,1,0:T(8,128)(2,1)}) custom-call(s32[5,12]{1,0:T(8,128)} %stack.39.ranges, s32[4]{0:T(128)} %pad_add_fusion.1.ranks, bf16[768,768]{1,0:T(8,128)(2,1)} %convert_element_type.215.g0, ...), custom_call_target="tpu_custom_call" | custom-call | flops 65229815808 | bytes 41943040 | tf_op jit(solution)/shard_map/attention_backward/pallas_call | solution.py:363
  456.9 3.6 collective-permute-start.32
  460.5 2.8 collective-permute-done.32
  463.3 2.9 add_convert_fusion
  468.6 2.3 constant_dynamic-slice_fusion.2
  472.4 5.1 collective-permute-start.35
  480.1 12.3 %reduce-scatter.6.cloned.1.call-done = bf16[4,192,192]{2,1,0:T(8,128)(2,1)} async-done(((bf16[4,768,192]{2,1,0:T(8,128)(2,1)}), bf16[4,192,192]{2,1,0:T(8,128)(2,1)}) %reduce-scatter.6.cloned.1.call-update) | async-done | bytes 294928 | tf_op jit(solution)/shard_map/reduce_scatter | solution.py:941
  492.4 12.2 %collective-permute-done.35 = bf16[4,96,768]{2,1,0:T(8,128)(2,1)} collective-permute-done((bf16[4,96,768]{2,1,0:T(8,128)(2,1)}, bf16[4,96,768]{2,1,0:T(8,128)(2,1)}, u32[]{:S(2)}, u32[]{:S(2)}) %collective-permute-start.35) | collective-permute-done | bytes 589856 | tf_op jit(solution)/shard_map/ppermute | solution.py:767
  504.6 3.2 fusion.39
  507.9 3.6 fusion.14
  519.4 2.4 convert_add_fusion.3
  527.0 21.5 %collective-permute-done.40 = f32[48]{0:T(128)S(1)} collective-permute-done((f32[48]{0:T(128)S(1)}, f32[48]{0:T(128)S(1)}, u32[]{:S(2)}, u32[]{:S(2)}) %collective-permute-start.40) | collective-permute-done | bytes 224 | tf_op jit(solution)/shard_map/ppermute | solution.py:719
  550.7 2.0 collective-permute-done.41
  554.0 3.2 fusion.40
  557.3 3.9 fusion.36
  (307 shorter events, 105.2 us)
Async XLA Ops:
  7.2 79.5 %all-gather.4.cloned.1.call-start = ((), (), s32[]{:S(2)}) async-start(), calls=%async_computation.4 | async-start | bytes 1769472 | tf_op jit(solution)/shard_map/all_gather | solution.py:783
  8.7 14.6 %collective-permute-start.3 = (s32[3,3072]{1,0:T(4,128)}, s32[3,3072]{1,0:T(4,128)}, u32[]{:S(2)}, u32[]{:S(2)}) collective-permute-start(s32[3,3072]{1,0:T(4,128)} %pad_add_fusion), channel_id=1, source_target_pairs={{0,4},{4,0},{1,5},{5,1},{2,6},{6,2},{3,7},{7,3},{8,12},{12,8},{9,1... | collective-permute-start | bytes 110600 | tf_op jit(solution)/shard_map/ppermute | solution.py:719
  12.1 23.5 %collective-permute-start.1 = (bf16[384,192]{1,0:T(8,128)(2,1)}, bf16[384,192]{1,0:T(8,128)(2,1)}, u32[]{:S(2)}, u32[]{:S(2)}) collective-permute-start(bf16[384,192]{1,0:T(8,128)(2,1)} %constant_dynamic-slice_fusion.18), channel_id=1, source_target_pairs={{0,2},{2,0},{1,3},{3,1},{4,6},{6,4},{5,7},{7,5},{8,10},{10,8},{9,1... | collective-permute-start | bytes 442376 | tf_op jit(solution)/shard_map/ppermute | solution.py:719
  17.9 30.5 %collective-permute-start.2 = (bf16[768,768]{1,0:T(8,128)(2,1)}, bf16[768,768]{1,0:T(8,128)(2,1)}, u32[]{:S(2)}, u32[]{:S(2)}) collective-permute-start(bf16[768,768]{1,0:T(8,128)(2,1)} %fusion.26), channel_id=1, source_target_pairs={{0,1},{1,0},{6,7},{7,6},{8,9},{9,8},{14,15},{15,14},{16,17},{17,16... | collective-permute-start | bytes 3538952 | tf_op jit(solution)/shard_map/ppermute | solution.py:724
  21.4 27.0 %collective-permute-start = (bf16[768,768]{1,0:T(8,128)(2,1)S(1)}, bf16[768,768]{1,0:T(8,128)(2,1)S(1)}, u32[]{:S(2)}, u32[]{:S(2)}) collective-permute-start(bf16[768,768]{1,0:T(8,128)(2,1)S(1)} %bitcast.86), channel_id=1, source_target_pairs={{2,4},{4,2},{3,5},{5,3},{10,12},{12,10},{11,13},{13,11},{18,20},{2... | collective-permute-start | bytes 3538952 | tf_op jit(solution)/shard_map/ppermute | solution.py:822
  54.6 9.0 %collective-permute-start.5 = (bf16[768,768]{1,0:T(8,128)(2,1)}, bf16[768,768]{1,0:T(8,128)(2,1)}, u32[]{:S(2)}, u32[]{:S(2)}) collective-permute-start(bf16[768,768]{1,0:T(8,128)(2,1)} %get-tuple-element.254), channel_id=1, source_target_pairs={{2,3},{3,2},{4,5},{5,4},{10,11},{11,10},{12,13},{13,12},{18,19},{1... | collective-permute-start | bytes 3538952 | tf_op jit(solution)/shard_map/ppermute | solution.py:724
  56.3 166.5 %all-gather.6.cloned.1.call-start = ((), (), s32[]{:S(2)}) async-start(), calls=%async_computation.5 | async-start | bytes 5308416 | tf_op jit(solution)/shard_map/all_gather | solution.py:783
  60.3 29.0 %collective-permute-start.4 = (bf16[768,768]{1,0:T(8,128)(2,1)}, bf16[768,768]{1,0:T(8,128)(2,1)}, u32[]{:S(2)}, u32[]{:S(2)}) collective-permute-start(bf16[768,768]{1,0:T(8,128)(2,1)} %get-tuple-element.253.x0), channel_id=1, source_target_pairs={{0,4},{4,0},{1,5},{5,1},{2,6},{6,2},{3,7},{7,3},{8,12},{12,8},{9,1... | collective-permute-start | bytes 3538952 | tf_op jit(solution)/shard_map/ppermute | solution.py:719
  66.1 23.3 %collective-permute-start.6 = (bf16[768,768]{1,0:T(8,128)(2,1)}, bf16[768,768]{1,0:T(8,128)(2,1)}, u32[]{:S(2)}, u32[]{:S(2)}) collective-permute-start(bf16[768,768]{1,0:T(8,128)(2,1)} %broadcast_select_fusion.3.x2), channel_id=1, source_target_pairs={{0,4},{4,0},{1,5},{5,1},{2,6},{6,2},{3,7},{7,3},{8,12},{12,8},{9,1... | collective-permute-start | bytes 3538952 | tf_op jit(solution)/shard_map/ppermute | solution.py:719
  77.3 55.4 %collective-permute-start.7 = (bf16[384,768]{1,0:T(8,128)(2,1)}, bf16[384,768]{1,0:T(8,128)(2,1)S(1)}, u32[]{:S(2)}, u32[]{:S(2)}) collective-permute-start(bf16[384,768]{1,0:T(8,128)(2,1)} %constant_dynamic-slice_fusion.17), channel_id=1, source_target_pairs={{0,2},{2,0},{1,3},{3,1},{4,6},{6,4},{5,7},{7,5},{8,10},{10,8},{9,1... | collective-permute-start | bytes 1769480 | tf_op jit(solution)/shard_map/ppermute | solution.py:719
  80.7 52.2 %collective-permute-start.8 = (bf16[384,768]{1,0:T(8,128)(2,1)}, bf16[384,768]{1,0:T(8,128)(2,1)}, u32[]{:S(2)}, u32[]{:S(2)}) collective-permute-start(bf16[384,768]{1,0:T(8,128)(2,1)} %constant_dynamic-slice_fusion.16), channel_id=1, source_target_pairs={{0,2},{2,0},{1,3},{3,1},{4,6},{6,4},{5,7},{7,5},{8,10},{10,8},{9,1... | collective-permute-start | bytes 1769480 | tf_op jit(solution)/shard_map/ppermute | solution.py:719
  133.6 89.3 %all-gather.8.cloned.1.call-start = ((), (), s32[]{:S(2)}) async-start(), calls=%async_computation.6 | async-start | bytes 5308416 | tf_op jit(solution)/shard_map/all_gather | solution.py:783
  134.3 245.1 %reduce-scatter.4.cloned.1.call-start = ((), (), s32[]{:S(2)}) async-start(), calls=%async_computation.7 | async-start | bytes 5898240 | tf_op jit(solution)/shard_map/reduce_scatter | solution.py:903
  134.5 6.0 %collective-permute-start.9 = (bf16[768,768]{1,0:T(8,128)(2,1)}, bf16[768,768]{1,0:T(8,128)(2,1)S(1)}, u32[]{:S(2)}, u32[]{:S(2)}) collective-permute-start(bf16[768,768]{1,0:T(8,128)(2,1)} %get-tuple-element.110), channel_id=1, source_target_pairs={{0,4},{4,0},{1,5},{5,1},{2,6},{6,2},{3,7},{7,3},{8,12},{12,8},{9,1... | collective-permute-start | bytes 3538952 | tf_op jit(solution)/shard_map/ppermute | solution.py:719
  137.2 45.9 %collective-permute-start.11 = (bf16[768,768]{1,0:T(8,128)(2,1)}, bf16[768,768]{1,0:T(8,128)(2,1)}, u32[]{:S(2)}, u32[]{:S(2)}) collective-permute-start(bf16[768,768]{1,0:T(8,128)(2,1)} %get-tuple-element.116), channel_id=1, source_target_pairs={{0,4},{4,0},{1,5},{5,1},{2,6},{6,2},{3,7},{7,3},{8,12},{12,8},{9,1... | collective-permute-start | bytes 3538952 | tf_op jit(solution)/shard_map/ppermute | solution.py:719
  142.1 41.1 %collective-permute-start.10 = (bf16[768,768]{1,0:T(8,128)(2,1)S(1)}, bf16[768,768]{1,0:T(8,128)(2,1)S(1)}, u32[]{:S(2)}, u32[]{:S(2)}) collective-permute-start(bf16[768,768]{1,0:T(8,128)(2,1)S(1)} %add_convert_fusion.6), channel_id=1, source_target_pairs={{0,1},{1,0},{2,3},{3,2},{4,5},{5,4},{6,7},{7,6},{8,9},{9,8},{10,11... | collective-permute-start | bytes 3538952 | tf_op jit(solution)/shard_map/ppermute | solution.py:719
  145.6 46.7 %collective-permute-start.13 = (bf16[768,768]{1,0:T(8,128)(2,1)}, bf16[768,768]{1,0:T(8,128)(2,1)}, u32[]{:S(2)}, u32[]{:S(2)}) collective-permute-start(bf16[768,768]{1,0:T(8,128)(2,1)} %bitcast.89), channel_id=1, source_target_pairs={{2,4},{4,2},{3,5},{5,3},{10,12},{12,10},{11,13},{13,11},{18,20},{2... | collective-permute-start | bytes 3538952 | tf_op jit(solution)/shard_map/ppermute | solution.py:859
  192.3 27.6 %collective-permute-start.12 = (bf16[768,768]{1,0:T(8,128)(2,1)S(1)}, bf16[768,768]{1,0:T(8,128)(2,1)S(1)}, u32[]{:S(2)}, u32[]{:S(2)}) collective-permute-start(bf16[768,768]{1,0:T(8,128)(2,1)S(1)} %convolution_convert_fusion.1.x0.a0), channel_id=1, source_target_pairs={{0,1},{1,0},{2,3},{3,2},{4,5},{5,4},{6,7},{7,6},{8,9},{9,8},{10,11... | collective-permute-start | bytes 3538952 | tf_op jit(solution)/shard_map/ppermute | solution.py:719
  193.1 27.1 %collective-permute-start.16 = (bf16[768,768]{1,0:T(8,128)(2,1)S(1)}, bf16[768,768]{1,0:T(8,128)(2,1)S(1)}, u32[]{:S(2)}, u32[]{:S(2)}) collective-permute-start(bf16[768,768]{1,0:T(8,128)(2,1)S(1)} %convolution_convert_fusion.1.x0.a0), channel_id=1, source_target_pairs={{0,4},{4,0},{1,5},{5,1},{2,6},{6,2},{3,7},{7,3},{8,12},{12,8},{9,1... | collective-permute-start | bytes 3538952 | tf_op jit(solution)/shard_map/ppermute | solution.py:719
  219.9 31.5 %collective-permute-start.15 = (bf16[768,768]{1,0:T(8,128)(2,1)}, bf16[768,768]{1,0:T(8,128)(2,1)}, u32[]{:S(2)}, u32[]{:S(2)}) collective-permute-start(bf16[768,768]{1,0:T(8,128)(2,1)} %convolution_convert_fusion.d0.a0), channel_id=1, source_target_pairs={{0,1},{1,0},{2,3},{3,2},{4,5},{5,4},{6,7},{7,6},{8,9},{9,8},{10,11... | collective-permute-start | bytes 3538952 | tf_op jit(solution)/shard_map/ppermute | solution.py:719
  251.4 3.1 collective-permute-start.18
  251.5 4.7 collective-permute-start.19
  252.0 5.9 %collective-permute-start.14 = (bf16[768,768]{1,0:T(8,128)(2,1)}, bf16[768,768]{1,0:T(8,128)(2,1)S(1)}, u32[]{:S(2)}, u32[]{:S(2)}) collective-permute-start(bf16[768,768]{1,0:T(8,128)(2,1)} %convolution_convert_fusion.d0.a0), channel_id=1, source_target_pairs={{0,4},{4,0},{1,5},{5,1},{2,6},{6,2},{3,7},{7,3},{8,12},{12,8},{9,1... | collective-permute-start | bytes 3538952 | tf_op jit(solution)/shard_map/ppermute | solution.py:719
  256.3 28.0 %collective-permute-start.20 = (bf16[768,768]{1,0:T(8,128)(2,1)S(1)}, bf16[768,768]{1,0:T(8,128)(2,1)S(1)}, u32[]{:S(2)}, u32[]{:S(2)}) collective-permute-start(bf16[768,768]{1,0:T(8,128)(2,1)S(1)} %add_convert_fusion.5), channel_id=1, source_target_pairs={{0,1},{1,0},{2,3},{3,2},{4,5},{5,4},{6,7},{7,6},{8,9},{9,8},{10,11... | collective-permute-start | bytes 3538952 | tf_op jit(solution)/shard_map/ppermute | solution.py:719
  284.3 3.1 collective-permute-start.21
  306.3 3.1 collective-permute-start.22
  306.6 28.4 %collective-permute-start.24 = (bf16[768,768]{1,0:T(8,128)(2,1)}, bf16[768,768]{1,0:T(8,128)(2,1)S(1)}, u32[]{:S(2)}, u32[]{:S(2)}) collective-permute-start(bf16[768,768]{1,0:T(8,128)(2,1)} %add_convert_fusion.4), channel_id=1, source_target_pairs={{0,1},{1,0},{2,3},{3,2},{4,5},{5,4},{6,7},{7,6},{8,9},{9,8},{10,11... | collective-permute-start | bytes 3538952 | tf_op jit(solution)/shard_map/ppermute | solution.py:719
  306.9 28.1 %collective-permute-start.23 = (bf16[768,768]{1,0:T(8,128)(2,1)}, bf16[768,768]{1,0:T(8,128)(2,1)S(1)}, u32[]{:S(2)}, u32[]{:S(2)}) collective-permute-start(bf16[768,768]{1,0:T(8,128)(2,1)} %get-tuple-element.144), channel_id=1, source_target_pairs={{0,4},{4,0},{1,5},{5,1},{2,6},{6,2},{3,7},{7,3},{8,12},{12,8},{9,1... | collective-permute-start | bytes 3538952 | tf_op jit(solution)/shard_map/ppermute | solution.py:719
  342.1 34.0 %collective-permute-start.25 = (bf16[768,768]{1,0:T(8,128)(2,1)}, bf16[768,768]{1,0:T(8,128)(2,1)}, u32[]{:S(2)}, u32[]{:S(2)}) collective-permute-start(bf16[768,768]{1,0:T(8,128)(2,1)} %convert_element_type.215.g0), channel_id=1, source_target_pairs={{0,1},{1,0},{2,3},{3,2},{4,5},{5,4},{6,7},{7,6},{8,9},{9,8},{10,11... | collective-permute-start | bytes 3538952 | tf_op jit(solution)/shard_map/ppermute | solution.py:719
  348.4 26.2 %all-to-all-start = ((f32[32,5,24]{2,1,0:T(8,128)}), f32[32,5,24]{2,1,0:T(8,128)}, u32[]{:S(2)}, u32[]{:S(2)}) async-start(f32[32,5,24]{2,1,0:T(8,128)} %copy.60), calls=%async_computation.1 | async-start | bytes 262144 | tf_op jit(solution)/shard_map/all_to_all | solution.py:920
  353.4 115.3 %reduce-scatter.8.cloned.1.call-start = ((), (), s32[]{:S(2)}) async-start(), calls=%async_computation.9 | async-start | bytes 5898240 | tf_op jit(solution)/shard_map/reduce_scatter | solution.py:923
  376.1 116.2 %reduce-scatter.6.cloned.1.call-start = ((), (), s32[]{:S(2)}) async-start(), calls=%async_computation.8 | async-start | bytes 1966080 | tf_op jit(solution)/shard_map/reduce_scatter | solution.py:941
  376.2 3.3 collective-permute-start.26
  376.2 8.0 %collective-permute-start.27 = (bf16[768,768]{1,0:T(8,128)(2,1)}, bf16[768,768]{1,0:T(8,128)(2,1)}, u32[]{:S(2)}, u32[]{:S(2)}) collective-permute-start(bf16[768,768]{1,0:T(8,128)(2,1)} %convert_element_type.215.g0), channel_id=1, source_target_pairs={{0,4},{4,0},{1,5},{5,1},{2,6},{6,2},{3,7},{7,3},{8,12},{12,8},{9,1... | collective-permute-start | bytes 3538952 | tf_op jit(solution)/shard_map/ppermute | solution.py:719
  380.8 74.8 %collective-permute-start.30 = (bf16[4,96,768]{2,1,0:T(8,128)(2,1)S(1)}, bf16[4,96,768]{2,1,0:T(8,128)(2,1)S(1)}, u32[]{:S(2)}, u32[]{:S(2)}) collective-permute-start(bf16[4,96,768]{2,1,0:T(8,128)(2,1)S(1)} %get-tuple-element.190), channel_id=1, source_target_pairs={{2,4},{4,2},{3,5},{5,3},{10,12},{12,10},{11,13},{13,11},{18,20},{2... | collective-permute-start | bytes 1769480 | tf_op jit(solution)/shard_map/ppermute | solution.py:768
  381.6 74.1 %collective-permute-start.31 = (bf16[4,96,768]{2,1,0:T(8,128)(2,1)S(1)}, bf16[4,96,768]{2,1,0:T(8,128)(2,1)S(1)}, u32[]{:S(2)}, u32[]{:S(2)}) collective-permute-start(bf16[4,96,768]{2,1,0:T(8,128)(2,1)S(1)} %get-tuple-element.260), channel_id=1, source_target_pairs={{0,4},{2,0},{4,6},{6,2},{1,5},{3,1},{5,7},{7,3},{8,12},{10,8},{12,... | collective-permute-start | bytes 1769480 | tf_op jit(solution)/shard_map/ppermute | solution.py:767
  383.5 72.3 %collective-permute-start.29 = (bf16[768,768]{1,0:T(8,128)(2,1)S(1)}, bf16[768,768]{1,0:T(8,128)(2,1)S(1)}, u32[]{:S(2)}, u32[]{:S(2)}) collective-permute-start(bf16[768,768]{1,0:T(8,128)(2,1)S(1)} %copy-done.9), channel_id=1, source_target_pairs={{2,4},{4,2},{3,5},{5,3},{10,12},{12,10},{11,13},{13,11},{18,20},{2... | collective-permute-start | bytes 3538952 | tf_op jit(solution)/shard_map/ppermute | solution.py:926
  456.9 6.4 %collective-permute-start.32 = (bf16[768,768]{1,0:T(8,128)(2,1)}, bf16[768,768]{1,0:T(8,128)(2,1)}, u32[]{:S(2)}, u32[]{:S(2)}) collective-permute-start(bf16[768,768]{1,0:T(8,128)(2,1)} %get-tuple-element.168), channel_id=1, source_target_pairs={{0,4},{4,0},{1,5},{5,1},{2,6},{6,2},{3,7},{7,3},{8,12},{12,8},{9,1... | collective-permute-start | bytes 3538952 | tf_op jit(solution)/shard_map/ppermute | solution.py:719
  466.3 38.3 %collective-permute-start.33 = (bf16[768,768]{1,0:T(8,128)(2,1)}, bf16[768,768]{1,0:T(8,128)(2,1)}, u32[]{:S(2)}, u32[]{:S(2)}) collective-permute-start(bf16[768,768]{1,0:T(8,128)(2,1)} %add_convert_fusion), channel_id=1, source_target_pairs={{2,3},{3,2},{4,5},{5,4},{10,11},{11,10},{12,13},{13,12},{18,19},{1... | collective-permute-start | bytes 3538952 | tf_op jit(solution)/shard_map/ppermute | solution.py:724
  468.0 36.6 %collective-permute-start.28 = (bf16[768,768]{1,0:T(8,128)(2,1)}, bf16[768,768]{1,0:T(8,128)(2,1)}, u32[]{:S(2)}, u32[]{:S(2)}) collective-permute-start(bf16[768,768]{1,0:T(8,128)(2,1)} %get-tuple-element.165), channel_id=1, source_target_pairs={{0,4},{4,0},{1,5},{5,1},{2,6},{6,2},{3,7},{7,3},{8,12},{12,8},{9,1... | collective-permute-start | bytes 3538952 | tf_op jit(solution)/shard_map/ppermute | solution.py:719
  470.9 21.4 %collective-permute-start.34 = (bf16[4,96,768]{2,1,0:T(8,128)(2,1)}, bf16[4,96,768]{2,1,0:T(8,128)(2,1)}, u32[]{:S(2)}, u32[]{:S(2)}) collective-permute-start(bf16[4,96,768]{2,1,0:T(8,128)(2,1)} %get-tuple-element.187), channel_id=1, source_target_pairs={{2,4},{4,2},{3,5},{5,3},{10,12},{12,10},{11,13},{13,11},{18,20},{2... | collective-permute-start | bytes 1769480 | tf_op jit(solution)/shard_map/ppermute | solution.py:768
  472.4 32.1 %collective-permute-start.35 = (bf16[4,96,768]{2,1,0:T(8,128)(2,1)}, bf16[4,96,768]{2,1,0:T(8,128)(2,1)}, u32[]{:S(2)}, u32[]{:S(2)}) collective-permute-start(bf16[4,96,768]{2,1,0:T(8,128)(2,1)} %get-tuple-element.258), channel_id=1, source_target_pairs={{0,4},{2,0},{4,6},{6,2},{1,5},{3,1},{5,7},{7,3},{8,12},{10,8},{12,... | collective-permute-start | bytes 1769480 | tf_op jit(solution)/shard_map/ppermute | solution.py:767
  511.6 10.2 %collective-permute-start.38 = (bf16[4,96,192]{2,1,0:T(8,128)(2,1)S(1)}, bf16[4,96,192]{2,1,0:T(8,128)(2,1)S(1)}, u32[]{:S(2)}, u32[]{:S(2)}) collective-permute-start(bf16[4,96,192]{2,1,0:T(8,128)(2,1)S(1)} %get-tuple-element.263), channel_id=1, source_target_pairs={{2,4},{4,2},{3,5},{5,3},{10,12},{12,10},{11,13},{13,11},{18,20},{2... | collective-permute-start | bytes 442376 | tf_op jit(solution)/shard_map/ppermute | solution.py:768
  512.4 11.0 %collective-permute-start.39 = (bf16[4,96,192]{2,1,0:T(8,128)(2,1)S(1)}, bf16[4,96,192]{2,1,0:T(8,128)(2,1)S(1)}, u32[]{:S(2)}, u32[]{:S(2)}) collective-permute-start(bf16[4,96,192]{2,1,0:T(8,128)(2,1)S(1)} %get-tuple-element.264), channel_id=1, source_target_pairs={{0,4},{2,0},{4,6},{6,2},{1,5},{3,1},{5,7},{7,3},{8,12},{10,8},{12,... | collective-permute-start | bytes 442376 | tf_op jit(solution)/shard_map/ppermute | solution.py:767
  513.4 40.6 %collective-permute-start.36 = (bf16[768,768]{1,0:T(8,128)(2,1)}, bf16[768,768]{1,0:T(8,128)(2,1)}, u32[]{:S(2)}, u32[]{:S(2)}) collective-permute-start(bf16[768,768]{1,0:T(8,128)(2,1)} %add_convert_fusion), channel_id=1, source_target_pairs={{0,1},{1,0},{6,7},{7,6},{8,9},{9,8},{14,15},{15,14},{16,17},{17,16... | collective-permute-start | bytes 3538952 | tf_op jit(solution)/shard_map/ppermute | solution.py:724
  515.3 42.0 %collective-permute-start.37 = (bf16[768,768]{1,0:T(8,128)(2,1)}, bf16[768,768]{1,0:T(8,128)(2,1)}, u32[]{:S(2)}, u32[]{:S(2)}) collective-permute-start(bf16[768,768]{1,0:T(8,128)(2,1)} %fusion.14), channel_id=1, source_target_pairs={{2,4},{4,2},{3,5},{5,3},{10,12},{12,10},{11,13},{13,11},{18,20},{2... | collective-permute-start | bytes 3538952 | tf_op jit(solution)/shard_map/ppermute | solution.py:950
  525.4 23.1 %collective-permute-start.40 = (f32[48]{0:T(128)S(1)}, f32[48]{0:T(128)S(1)}, u32[]{:S(2)}, u32[]{:S(2)}) collective-permute-start(f32[48]{0:T(128)S(1)} %dynamic_slice.97), channel_id=1, source_target_pairs={{0,2},{2,0},{1,3},{3,1},{4,6},{6,4},{5,7},{7,5},{8,10},{10,8},{9,1... | collective-permute-start | bytes 584 | tf_op jit(solution)/shard_map/ppermute | solution.py:719
  549.1 3.6 collective-permute-start.41
  (68 other events, 1207.7 us)
Sparse Core Ops, SparseCore 0:
  56.5 30.2 all-gather.3
  133.7 41.1 all-gather.5
  176.8 38.9 all-gather.7
  306.5 58.0 reduce-scatter.3
  376.2 55.4 reduce-scatter.7
  460.7 31.6 reduce-scatter.5

commit v5 on v4

--- a/solution.py
+++ b/solution.py
@@ -7,8 +7,8 @@
 from jax.sharding import PartitionSpec as P
 
 HEAD_DIM = 64
-QUERY_BLOCK = 512
-BLOCK = 256
+FORWARD_BLOCKS = (512, 512)
+BACKWARD_BLOCKS = (512, 256)
 LOG2E = 1.4426950408889634
 NEGATIVE = -1e30
 TILE = 256
@@ -39,17 +39,18 @@
     return lax.dot_general(a, b, (dims, ((), ())), preferred_element_type=jnp.float32)
 
 
-def key_ranges(segment, block):
+def key_ranges(segment, blocks):
+    block, fine = blocks
     token_count = segment.shape[0]
     numbers = jnp.arange(1, CONTINUATIONS + 1, dtype=jnp.int32)[:, None]
     earlier = jnp.sum((segment[None, :] < numbers).astype(jnp.int32), axis=1, keepdims=True)
     prompt = earlier[0, 0]
     start = jnp.sum(jnp.where(segment[None, :] == numbers, earlier, 0), axis=0)
     first = jnp.arange(token_count // block, dtype=jnp.int32) * block
-    whole = jnp.minimum(prompt, first) // block
-    shared = (jnp.minimum(prompt, first + block) + block - 1) // block
-    own = jnp.maximum(shared, start.reshape(-1, block)[:, 0] // block)
-    last = first // block + 1
+    whole = jnp.minimum(prompt, first) // fine
+    shared = (jnp.minimum(prompt, first + block) + fine - 1) // fine
+    own = jnp.maximum(shared, start.reshape(-1, block)[:, 0] // fine)
+    last = (first + block) // fine
     return (jnp.stack([whole, shared, own, last, jnp.full_like(whole, prompt)]), start[None, :])
 
 
@@ -89,6 +90,25 @@
                     pltpu.make_async_copy(source, target, semaphores.at[b]).start()
 
 
+def take_ranks(ref, sources, ranks, semaphores, edge, block, first):
+    count = sources[0].shape[0]
+
+    @pl.when(first)
+    def _():
+        for b, source in enumerate(sources):
+            target = rank_rows(ref, ranks[b], source)
+            pltpu.make_async_copy(source, target, semaphores.at[b]).start()
+
+    for b, source in enumerate(sources):
+        begin = ranks[b] * count
+        before = jnp.where(first, 0, edge)
+
+        @pl.when((begin >= before) & (begin < edge + block))
+        def _(b=b, source=source):
+            target = rank_rows(ref, ranks[b], source)
+            pltpu.make_async_copy(source, target, semaphores.at[b]).wait()
+
+
 def await_ranks(ref, targets, ranks, semaphores):
     for b, target in enumerate(targets):
         pltpu.make_async_copy(rank_rows(ref, ranks[b], target), target, semaphores.at[b]).wait()
@@ -96,46 +116,47 @@
 
 def forward_kernel(
     ranges, ranks, x0, x1, x2, x3, w_ref, proj_ref, start_ref,
-    p0, p1, p2, p3, q_ref, qt_ref, k_ref, kt_ref, v_ref, ctx_ref, lse_ref,
+    p0, p1, p2, p3, qt_ref, k_ref, kt_ref, v_ref, ctx_ref, lse_ref,
     x_ref, part_ref, vt_ref, score_ref, top_ref, sum_ref, arrived, left,
 ):
     step = pl.program_id(0)
-    heads = q_ref.shape[0]
-    block = q_ref.shape[1]
+    heads = qt_ref.shape[0]
+    block = qt_ref.shape[2]
+    fine = vt_ref.shape[3]
+    step_keys = kt_ref.shape[3]
     rows = pl.ds(pl.multiple_of(step * block, block), block)
 
-    @pl.when(step == 0)
-    def _():
-        copies(
-            [(x, rank_rows(x_ref, ranks[b], x)) for b, x in enumerate((x0, x1, x2, x3))], arrived
-        )
-
+    take_ranks(x_ref, (x0, x1, x2, x3), ranks, arrived, step * block, block, step == 0)
     x = x_ref[rows, :]
-    kinds = []
     for kind in range(3):
-        made = matmul(x, w_ref[kind])
-        kinds.append((made.astype(jnp.bfloat16), made.T.astype(jnp.bfloat16)))
-    for head in range(heads):
-        part = slice(head * HEAD_DIM, (head + 1) * HEAD_DIM)
-        q_ref[head] = kinds[0][0][:, part]
-        k_ref[head, rows, :] = kinds[1][0][:, part]
-        v_ref[head, rows, :] = kinds[2][0][:, part]
-        qt_ref[head] = kinds[0][1][part]
-        for piece in range(kt_ref.shape[0]):
-            columns = slice(piece * kt_ref.shape[3], (piece + 1) * kt_ref.shape[3])
-            kt_ref[piece, head] = kinds[1][1][part, columns]
-        vt_ref[step, head, :HEAD_DIM] = kinds[2][1][part]
-        vt_ref[step, head, HEAD_DIM:] = jnp.ones((16, block), jnp.bfloat16)
+        made = matmul(x, w_ref[kind]).astype(jnp.bfloat16)
+        turned = made.T
+        for head in range(heads):
+            part = slice(head * HEAD_DIM, (head + 1) * HEAD_DIM)
+            if kind == 0:
+                qt_ref[head] = turned[part]
+            if kind == 1:
+                k_ref[head, rows, :] = made[:, part]
+            if kind == 2:
+                v_ref[head, rows, :] = made[:, part]
+            for piece in range(block // step_keys if kind == 1 else 0):
+                columns = slice(piece * step_keys, (piece + 1) * step_keys)
+                kt_ref[piece, head] = turned[part, columns]
+            for piece in range(block // fine if kind == 2 else 0):
+                columns = slice(piece * fine, (piece + 1) * fine)
+                at = step * (block // fine) + piece
+                vt_ref[at, head, :HEAD_DIM] = turned[part, columns]
+                vt_ref[at, head, HEAD_DIM:] = jnp.ones((16, fine), jnp.bfloat16)
     top_ref[...] = jnp.full_like(top_ref, NEGATIVE)
     sum_ref[...] = jnp.zeros_like(sum_ref)
     prompt = ranges[4, step]
     scale = LOG2E * HEAD_DIM ** (-0.5)
 
     def visit(key, masked):
-        place = pl.ds(pl.multiple_of(key * block, block), block)
+        place = pl.ds(pl.multiple_of(key * fine, fine), fine)
         if masked:
-            key_at = key * block + lax.broadcasted_iota(jnp.int32, (block, block), 0)
-            query_at = step * block + lax.broadcasted_iota(jnp.int32, (block, block), 1)
+            key_at = key * fine + lax.broadcasted_iota(jnp.int32, (fine, block), 0)
+            query_at = step * block + lax.broadcasted_iota(jnp.int32, (fine, block), 1)
             seen = (key_at <= query_at) & ((key_at < prompt) | (key_at >= start_ref[...]))
         for head in range(heads):
             scores = matmul(k_ref[head, place, :], qt_ref[head])
@@ -143,7 +164,7 @@
                 scores = jnp.where(seen, scores, NEGATIVE)
             score_ref[key, head] = scores
             top_ref[head] = jnp.maximum(
-                top_ref[head], jnp.max(scores.reshape(block // 8, 8, block), axis=0)
+                top_ref[head], jnp.max(scores.reshape(fine // 8, 8, block), axis=0)
             )
 
     def plain(key, carry):
@@ -185,8 +206,8 @@
     tokens, width = start.shape[1], x[0].shape[1]
     local = w.shape[2]
     heads = local // HEAD_DIM
-    block = QUERY_BLOCK
-    fine = BLOCK
+    block, fine = FORWARD_BLOCKS
+    step_keys = BACKWARD_BLOCKS[1]
     count = tokens // block
     low = jnp.bfloat16
     head_rows = pl.BlockSpec((heads, tokens, HEAD_DIM), lambda i, r, n: (0, 0, 0))
@@ -204,10 +225,11 @@
             ],
             out_specs=[
                 *[HBM] * 4,
-                pl.BlockSpec((heads, block, HEAD_DIM), lambda i, r, n: (0, i, 0)),
                 pl.BlockSpec((heads, HEAD_DIM, block), lambda i, r, n: (0, 0, i)),
                 head_rows,
-                pl.BlockSpec((block // fine, heads, HEAD_DIM, fine), lambda i, r, n: (i, 0, 0, 0)),
+                pl.BlockSpec(
+                    (block // step_keys, heads, HEAD_DIM, step_keys), lambda i, r, n: (i, 0, 0, 0)
+                ),
                 head_rows,
                 pl.BlockSpec((local, block), lambda i, r, n: (0, i)),
                 pl.BlockSpec((heads, 1, block), lambda i, r, n: (0, 0, i)),
@@ -215,8 +237,8 @@
             scratch_shapes=[
                 pltpu.VMEM((tokens, width), low),
                 pltpu.VMEM((tokens, width), low),
-                pltpu.VMEM((count, heads, HEAD_DIM + 16, block), low),
-                pltpu.VMEM((count, heads, block, block), jnp.float32),
+                pltpu.VMEM((tokens // fine, heads, HEAD_DIM + 16, fine), low),
+                pltpu.VMEM((tokens // fine, heads, fine, block), jnp.float32),
                 pltpu.VMEM((heads, 8, block), jnp.float32),
                 pltpu.VMEM((heads, HEAD_DIM + 16, block), jnp.float32),
                 pltpu.SemaphoreType.DMA((4,)),
@@ -225,10 +247,9 @@
         ),
         out_shape=[
             *[jax.ShapeDtypeStruct(x[0].shape, low)] * 4,
-            jax.ShapeDtypeStruct((heads, tokens, HEAD_DIM), low),
             jax.ShapeDtypeStruct((heads, HEAD_DIM, tokens), low),
             jax.ShapeDtypeStruct((heads, tokens, HEAD_DIM), low),
-            jax.ShapeDtypeStruct((tokens // fine, heads, HEAD_DIM, fine), low),
+            jax.ShapeDtypeStruct((tokens // step_keys, heads, HEAD_DIM, step_keys), low),
             jax.ShapeDtypeStruct((heads, tokens, HEAD_DIM), low),
             jax.ShapeDtypeStruct((local, tokens), low),
             jax.ShapeDtypeStruct((heads, 1, tokens), jnp.float32),
@@ -243,115 +264,121 @@
 
 def backward_kernel(
     ranges, ranks, g0, g1, g2, g3, x0, x1, x2, x3,
-    ctx_ref, lse_ref, q_ref, qt_ref, start_ref, k_ref, kt_ref, v_ref, w_ref, proj_ref,
+    ctx_ref, lse_ref, qt_ref, start_ref, k_ref, kt_ref, v_ref, w_ref, proj_ref,
     p0, p1, p2, p3, weights_ref,
     g_ref, x_ref, part_ref, wgrad_ref, pgrad_ref,
-    dk_ref, dv_ref, dqt_ref, out_ref, outt_ref, inner_ref, arrived, left,
+    dk_ref, dv_ref, dq_ref, outer_ref, inner_ref, grad_ref, prob_ref, dscore_ref, arrived, left,
 ):
     number = pl.program_id(0)
     step = pl.num_programs(0) - 1 - number
-    heads = q_ref.shape[0]
-    block = q_ref.shape[1]
+    heads = qt_ref.shape[0]
+    block = qt_ref.shape[2]
+    fine = kt_ref.shape[3]
+    local = heads * HEAD_DIM
     rows = pl.ds(pl.multiple_of(step * block, block), block)
 
     @pl.when(number == 0)
     def _():
-        copies(
-            [(g, rank_rows(g_ref, ranks[b], g)) for b, g in enumerate((g0, g1, g2, g3))]
-            + [(x, rank_rows(x_ref, ranks[b], x)) for b, x in enumerate((x0, x1, x2, x3))],
-            arrived,
-        )
+        for place, (ref, sources) in enumerate(((g_ref, (g0, g1, g2, g3)), (x_ref, (x0, x1, x2, x3)))):
+            for b, source in enumerate(sources):
+                target = rank_rows(ref, ranks[b], source)
+                pltpu.make_async_copy(source, target, arrived.at[place, b]).start()
         dk_ref[...] = jnp.zeros_like(dk_ref)
         dv_ref[...] = jnp.zeros_like(dv_ref)
         wgrad_ref[...] = jnp.zeros_like(wgrad_ref)
         pgrad_ref[...] = jnp.zeros_like(pgrad_ref)
+        await_copies(g_ref, (g0, g1, g2, g3), ranks, arrived.at[0])
 
     upstream = g_ref[rows, :]
-    outer = matmul(upstream, proj_ref[...], ((1,), (1,)))
-    low = outer.astype(jnp.bfloat16)
-    turned = outer.T.astype(jnp.bfloat16)
+    outer = matmul(upstream, proj_ref[...], ((1,), (1,))).astype(jnp.bfloat16).T
     for head in range(heads):
         part = slice(head * HEAD_DIM, (head + 1) * HEAD_DIM)
-        out_ref[head] = low[:, part]
-        outt_ref[head] = turned[part]
+        outer_ref[head] = outer[part]
         inner_ref[head] = jnp.sum(
-            turned[part].astype(jnp.float32) * ctx_ref[part].astype(jnp.float32),
+            outer[part].astype(jnp.float32) * ctx_ref[part].astype(jnp.float32),
             axis=0,
             keepdims=True,
         )
     pgrad_ref[...] += matmul(ctx_ref[...], upstream)
-    dqt_ref[...] = jnp.zeros_like(dqt_ref)
+    dq_ref[...] = jnp.zeros_like(dq_ref)
     prompt = ranges[4, step]
     scale = LOG2E * HEAD_DIM ** (-0.5)
 
-    def visit(key, masked):
-        place = pl.ds(pl.multiple_of(key * block, block), block)
+    def add(key, head):
+        prob, dscore = prob_ref[head], dscore_ref[head]
+        dv_ref[key, head] += matmul(outer_ref[head], prob, ((1,), (1,)))
+        dk_ref[key, head] += matmul(qt_ref[head], dscore, ((1,), (1,)))
+        dq_ref[head] += matmul(kt_ref[key, head], dscore)
+
+    def visit(number, before, masked):
+        key = jnp.where(number < ranges[1, step], number, number - ranges[1, step] + ranges[2, step])
+        place = pl.ds(pl.multiple_of(key * fine, fine), fine)
         if masked:
-            key_at = key * block + lax.broadcasted_iota(jnp.int32, (block, block), 0)
-            query_at = step * block + lax.broadcasted_iota(jnp.int32, (block, block), 1)
+            key_at = key * fine + lax.broadcasted_iota(jnp.int32, (fine, block), 0)
+            query_at = step * block + lax.broadcasted_iota(jnp.int32, (fine, block), 1)
             seen = (key_at <= query_at) & ((key_at < prompt) | (key_at >= start_ref[...]))
-        made = [
-            (
-                matmul(k_ref[head, place, :], qt_ref[head]),
-                matmul(v_ref[head, place, :], outt_ref[head]),
-            )
-            for head in range(heads)
-        ]
         for head in range(heads):
-            scores, dprob = made[head]
-            scores = scores * scale
+            scores = matmul(k_ref[head, place, :], qt_ref[head]) * scale
+            dprob = matmul(v_ref[head, place, :], outer_ref[head])
+            if before is not None:
+                add(before, head)
             if masked:
                 scores = jnp.where(seen, scores, NEGATIVE)
             prob = jnp.exp2(scores - lse_ref[head])
-            dscore = (prob * (dprob - inner_ref[head])).astype(jnp.bfloat16)
-            made[head] = prob.astype(jnp.bfloat16), dscore
-        for head in range(heads):
-            prob, dscore = made[head]
-            dv_ref[head, place, :] += matmul(prob, out_ref[head])
-            dk_ref[head, place, :] += matmul(dscore, q_ref[head])
-            dqt_ref[head] += matmul(kt_ref[key, head], dscore)
-
-    def plain(key, carry):
-        visit(key, False)
-        return carry
-
-    def edge(key, carry):
-        visit(key, True)
-        return carry
-
-    lax.fori_loop(0, ranges[0, step], plain, 0)
-    lax.fori_loop(ranges[0, step], ranges[1, step], edge, 0)
-    lax.fori_loop(ranges[2, step], ranges[3, step], edge, 0)
+            prob_ref[head] = prob.astype(jnp.bfloat16)
+            dscore_ref[head] = (prob * (dprob - inner_ref[head])).astype(jnp.bfloat16)
+        return key
+
+    visits = ranges[1, step] + ranges[3, step] - ranges[2, step]
+    plain = jnp.maximum(ranges[0, step], 1)
+    key = visit(0, None, True)
+    key = lax.fori_loop(1, plain, lambda number, before: visit(number, before, False), key)
+    key = lax.fori_loop(plain, visits, lambda number, before: visit(number, before, True), key)
+    for head in range(heads):
+        add(key, head)
     small = HEAD_DIM ** (-0.5)
+
+    @pl.when(number == 0)
+    def _():
+        await_copies(x_ref, (x0, x1, x2, x3), ranks, arrived.at[1])
+
+    for head in range(heads):
+        part = slice(head * HEAD_DIM, (head + 1) * HEAD_DIM)
+        grad_ref[0, part] = (dq_ref[head] * small).astype(jnp.bfloat16)
+        for piece in range(block // fine):
+            at = step * (block // fine) + piece
+            columns = slice(piece * fine, (piece + 1) * fine)
+            grad_ref[1, part, columns] = (dk_ref[at, head] * small).astype(jnp.bfloat16)
+            grad_ref[2, part, columns] = dv_ref[at, head].astype(jnp.bfloat16)
     x = x_ref[rows, :]
     total = None
     for kind in range(3):
-        if kind == 0:
-            grad = jnp.concatenate([dqt_ref[head] for head in range(heads)], axis=0).T * small
-        elif kind == 1:
-            grad = jnp.concatenate([dk_ref[head, rows, :] for head in range(heads)], axis=1) * small
-        else:
-            grad = jnp.concatenate([dv_ref[head, rows, :] for head in range(heads)], axis=1)
-        grad = grad.astype(jnp.bfloat16)
-        wgrad_ref[kind] += matmul(x, grad, ((0,), (0,)))
-        term = matmul(grad, w_ref[kind], ((1,), (1,)))
+        wgrad_ref[kind] += matmul(grad_ref[kind], x)
+        term = matmul(grad_ref[kind].T, w_ref[kind], ((1,), (1,)))
         total = term if total is None else total + term
     part_ref[rows, :] = total.astype(jnp.bfloat16)
     send_ranks(part_ref, (p0, p1, p2, p3), ranks, left, step * block, block, True)
 
     @pl.when(step == 0)
     def _():
-        weights_ref[:3] = wgrad_ref[...].astype(jnp.bfloat16)
+        for kind in range(3):
+            weights_ref[kind] = wgrad_ref[kind].T.astype(jnp.bfloat16)
         weights_ref[3] = pgrad_ref[...].T.astype(jnp.bfloat16)
         await_ranks(part_ref, (p0, p1, p2, p3), ranks, left)
 
 
+def await_copies(ref, sources, ranks, semaphores):
+    for b, source in enumerate(sources):
+        target = rank_rows(ref, ranks[b], source)
+        pltpu.make_async_copy(source, target, semaphores.at[b]).wait()
+
+
 def attention_backward(ranges, start, ranks, upstream, x, saved, w, proj):
-    q, qt, k, kt, v, ctx, lse = saved
+    qt, k, kt, v, ctx, lse = saved
     tokens, width = start.shape[1], x[0].shape[1]
     local = w.shape[2]
     heads = local // HEAD_DIM
-    block = BLOCK
+    block, fine = BACKWARD_BLOCKS
     count = tokens // block
     low = jnp.bfloat16
 
@@ -369,11 +396,10 @@
                 *[HBM] * 8,
                 pl.BlockSpec((local, block), lambda i, r, n: (0, at(i))),
                 pl.BlockSpec((heads, 1, block), lambda i, r, n: (0, 0, at(i))),
-                pl.BlockSpec((heads, block, HEAD_DIM), lambda i, r, n: (0, at(i), 0)),
                 pl.BlockSpec((heads, HEAD_DIM, block), lambda i, r, n: (0, 0, at(i))),
                 pl.BlockSpec((1, block), lambda i, r, n: (0, at(i))),
                 head_rows,
-                pl.BlockSpec((count, heads, HEAD_DIM, block), lambda i, r, n: (0, 0, 0, 0)),
+                pl.BlockSpec((tokens // fine, heads, HEAD_DIM, fine), lambda i, r, n: (0, 0, 0, 0)),
                 head_rows,
                 pl.BlockSpec((3, width, local), lambda i, r, n: (0, 0, 0)),
                 pl.BlockSpec((local, width), lambda i, r, n: (0, 0)),
@@ -386,15 +412,17 @@
                 pltpu.VMEM((tokens, width), low),
                 pltpu.VMEM((tokens, width), low),
                 pltpu.VMEM((tokens, width), low),
-                pltpu.VMEM((3, width, local), jnp.float32),
+                pltpu.VMEM((3, local, width), jnp.float32),
                 pltpu.VMEM((local, width), jnp.float32),
-                pltpu.VMEM((heads, tokens, HEAD_DIM), jnp.float32),
-                pltpu.VMEM((heads, tokens, HEAD_DIM), jnp.float32),
+                pltpu.VMEM((tokens // fine, heads, HEAD_DIM, fine), jnp.float32),
+                pltpu.VMEM((tokens // fine, heads, HEAD_DIM, fine), jnp.float32),
                 pltpu.VMEM((heads, HEAD_DIM, block), jnp.float32),
-                pltpu.VMEM((heads, block, HEAD_DIM), low),
                 pltpu.VMEM((heads, HEAD_DIM, block), low),
                 pltpu.VMEM((heads, 1, block), jnp.float32),
-                pltpu.SemaphoreType.DMA((8,)),
+                pltpu.VMEM((3, local, block), low),
+                pltpu.VMEM((heads, fine, block), low),
+                pltpu.VMEM((heads, fine, block), low),
+                pltpu.SemaphoreType.DMA((2, 4)),
                 pltpu.SemaphoreType.DMA((4,)),
             ],
         ),
@@ -407,7 +435,7 @@
             flops=4 * flops, transcendentals=tokens * tokens * heads // 2, bytes_accessed=40 << 20
         ),
         name="attention_backward",
-    )(ranges, ranks, *upstream, *x, ctx, lse, q, qt, start, k, kt, v, w, proj)
+    )(ranges, ranks, *upstream, *x, ctx, lse, qt, start, k, kt, v, w, proj)
 
 
 def route_rows(route, priority, experts, capacity, row_count, ranks):
@@ -831,7 +859,7 @@
     indices = jnp.stack([routes[0, :, 0], priority[0], segments[0]])
     indices = jnp.where(home, indices, flip(indices, "c"))
     segment = indices[2]
-    ranges, start = key_ranges(segment, QUERY_BLOCK)
+    ranges, start = key_ranges(segment, FORWARD_BLOCKS)
     coming, small_piece, home_across, ranges, start = tie(
         coming, small_piece, home_across, ranges, start
     )
@@ -849,16 +877,16 @@
     unit_one, inverse_one = normalize_plain(inputs)
     small = jnp.where(home, small, small_other)
     qkv_used, proj_used = small[:3], small[3].reshape(local_width, model_width)
-    *attended, q, qt, k, kt, v, ctx, lse = attention_forward(
+    *attended, qt, k, kt, v, ctx, lse = attention_forward(
         ranges, start, ranks, normed_one, qkv_used, proj_used
     )
-    saved = (q, qt, k, kt, v, ctx, lse)
+    saved = (qt, k, kt, v, ctx, lse)
     attended[3], up_piece, down_piece, indices, upstream = tie(
         attended[3], up_piece, down_piece, indices, out_grad[0]
     )
     away_upstream = lax.ppermute(upstream, ("c", "zh"), [(1, 2), (2, 1)])
     new_experts = [share(piece, users, expert_up.shape) for piece in (up_piece, down_piece)]
-    back_ranges = key_ranges(indices[2], BLOCK)[0]
+    back_ranges = key_ranges(indices[2], BACKWARD_BLOCKS)[0]
     kept_rows, order, table, hot_rows = route_rows(
         indices[0], indices[1], experts, capacity, row_count, ranks
     )

time: 578 us -> 569 us (0.984)
  Pallas kernels: 200 us -> 190 us
    pallas_call x1, Pallas kernels: 71.5 us -> 62.8 us  [attention_backward(): pl.pallas_call(backward_kernel, grid_spec=pltpu.PrefetchScalarGridSpec(nu...]
  transfers between devices with their start and end apart: 49 -> 49, of which waited for: 21 -> 21; matrix products, arithmetic and copies ran while one was open for 17% -> 18% of each run, Pallas kernels for 32% -> 31%
where the time goes in v5:
time: 569 us; the launch traced here: 558 us
  Pallas kernels  190 us (33%)
  waiting for transfers between devices  162 us (28%)
  other arithmetic  72.8 us (13%)
  starting transfers between devices  61.5 us (11%)
  local copies, waits for them, and re-layouts  42.3 us (7%)
  between operations  15.5 us (3%)
  matrix products  13.9 us (2%)
    ppermute x28, waiting for transfers between devices, flip(): return lax.ppermute(value, axis, [(0, 1), (1, 0)])  110 us
    pallas_call x4, Pallas kernels, moe_call(): pl.pallas_call(kernel, grid_spec=pltpu.PrefetchScalarGridSpec(num_scalar_...  85.4 us
    pallas_call x1, Pallas kernels, attention_backward(): pl.pallas_call(backward_kernel, grid_spec=pltpu.PrefetchScalarGridSpec(nu...  62.8 us
    pallas_call x1, Pallas kernels, attention_forward(): pl.pallas_call(forward_kernel, grid_spec=pltpu.PrefetchScalarGridSpec(num...  42 us
    ppermute x28, starting transfers between devices, flip(): return lax.ppermute(value, axis, [(0, 1), (1, 0)])  34.6 us
    reduce_scatter x1, waiting for transfers between devices, body(): lax.psum_scatter(weights_part, high_bits, scatter_dimension=1, tiled=True)  14.2 us
    ppermute x4, waiting for transfers between devices, flip_some(): return lax.ppermute(value, ('c', 'zh', 'zl'), moves)  13 us
    ppermute x3, waiting for transfers between devices, send_home(): turned = lax.ppermute(turned, ('c', 'zh'), [(0, 2), (1, 0), (2, 3), (3, 1)])  12.6 us
  transfers between devices with their start and end apart: 49, of which 21 were waited for; matrix products, arithmetic and copies ran while one was open for 18% of the time, Pallas kernels for 31%

profile of v5, /device:TPU:0, one launch (start us, length us, event | category | flops | bytes accessed | tf_op | source)
XLA Modules:
  0.0 558.4 jit_solution(10081333563100371802)
XLA Ops:
  12.1 3.6 collective-permute-start.1
  17.9 3.5 collective-permute-start.2
  35.4 13.0 %collective-permute-done.2 = bf16[768,768]{1,0:T(8,128)(2,1)} collective-permute-done((bf16[768,768]{1,0:T(8,128)(2,1)}, bf16[768,768]{1,0:T(8,128)(2,1)}, u32[]{:S(2)}, u32[]{:S(2)}) %collective-permute-start.2) | collective-permute-done | bytes 1179680 | tf_op jit(solution)/shard_map/ppermute | solution.py:752
  49.5 3.2 convert_reduce_fusion.1
  52.7 2.0 broadcast_select_fusion.4
  60.3 3.3 collective-permute-start.4
  63.7 2.4 broadcast_select_fusion.3.x2
  66.1 10.6 %collective-permute-start.6 = (bf16[768,768]{1,0:T(8,128)(2,1)}, bf16[768,768]{1,0:T(8,128)(2,1)}, u32[]{:S(2)}, u32[]{:S(2)}) collective-permute-start(bf16[768,768]{1,0:T(8,128)(2,1)} %broadcast_select_fusion.3.x2), channel_id=1, source_target_pairs={{0,4},{4,0},{1,5},{5,1},{2,6},{6,2},{3,7},{7,3},{8,12},{12,8},{9,1... | collective-permute-start | bytes 3538952 | tf_op jit(solution)/shard_map/ppermute | solution.py:747
  77.3 3.4 collective-permute-start.7
  80.7 6.0 %all-gather.4.cloned.1.call-done = bf16[3072,192]{1,0:T(8,128)(2,1)} async-done(((bf16[384,192]{1,0:T(8,128)(2,1)}), bf16[3072,192]{1,0:T(8,128)(2,1)}) %all-gather.4.cloned.1.call-update) | async-done | bytes 1179664 | tf_op jit(solution)/shard_map/all_gather | solution.py:811
  89.3 42.0 %attention_forward.1 = (bf16[768,768]{1,0:T(8,128)(2,1)}, bf16[768,768]{1,0:T(8,128)(2,1)}, bf16[768,768]{1,0:T(8,128)(2,1)}, bf16[768,768]{1,0:T(8,128)(2,1)}, ...) custom-call(s32[5,6]{1,0:T(8,128)} %stack.33.ranges, ...), custom_call_target="tpu_custom_call" | custom-call | flops 28991029248 | bytes 41943040 | tf_op jit(solution)/shard_map/attention_forward/pallas_call | solution.py:215
  141.8 2.3 collective-permute-start.10
  155.6 2.6 convert_reduce_fusion
  159.4 24.0 %collective-permute-done.10 = bf16[768,768]{1,0:T(8,128)(2,1)S(1)} collective-permute-done((bf16[768,768]{1,0:T(8,128)(2,1)S(1)}, bf16[768,768]{1,0:T(8,128)(2,1)S(1)}, u32[]{:S(2)}, u32[]{:S(2)}) %collective-permute-start.10) | collective-permute-done | bytes 1179680 | tf_op jit(solution)/shard_map/ppermute | solution.py:747
  184.4 3.9 fusion.57
  188.9 2.3 fusion.27
  194.6 2.2 convolution_convert_fusion.d0.a0
  196.9 23.5 %collective-permute-done.12.x2.a2 = bf16[768,768]{1,0:T(8,128)(2,1)S(1)} collective-permute-done((bf16[768,768]{1,0:T(8,128)(2,1)S(1)}, bf16[768,768]{1,0:T(8,128)(2,1)S(1)}, u32[]{:S(2)}, u32[]{:S(2)}) %collective-permute-start.12) | collective-permute-done | bytes 1179680 | tf_op jit(solution)/shard_map/ppermute | solution.py:747
  223.3 28.6 %moe_forward.1 = (bf16[768,768]{1,0:T(8,128)(2,1)}, bf16[768,768]{1,0:T(8,128)(2,1)}, bf16[768,768]{1,0:T(8,128)(2,1)}, bf16[768,768]{1,0:T(8,128)(2,1)}, bf16[4...) custom-call(s32[33]{0:T(128)} %concatenate.15.table, bf16[768,768]{1,0:T(8,128)(2,1)} %copy-done.60, ...), custom_call_target="tpu_custom_call" | custom-call | flops 9059696640 | bytes 41943040 | tf_op jit(solution)/shard_map/moe_forward/pallas_call | solution.py:674
  252.6 2.5 collective-permute-done.18
  259.5 24.4 %moe_backward.1 = (bf16[768,768]{1,0:T(8,128)(2,1)}, bf16[768,768]{1,0:T(8,128)(2,1)}, bf16[768,768]{1,0:T(8,128)(2,1)}, bf16[768,768]{1,0:T(8,128)(2,1)}, bf16[4,1024,768]{2,1,0:T(8,128)(2,1)}) custom-call(s32[33]{0:T(128)} %concatenate.15.table, bf16[768,768]{1,0:T(8,128)(2,1)} %convolution_convert_fusion.d0.a0, bf16[768,768]{1,0:T(8,128)(2,1)} %copy-done.65, ...), custom_call_target="tpu_custom_call" | custom-call | flops 9059696640 | bytes 41943040 | tf_op jit(solution)/shard_map/moe_backward/pallas_call | solution.py:674
  284.8 3.1 collective-permute-done.21
  287.8 2.7 add_convert_fusion.4
  290.5 16.3 %moe_weights.2 = (bf16[4,768,768]{2,1,0:T(8,128)(2,1)}, bf16[16,128]{1,0:T(8,128)(2,1)}) custom-call(s32[33]{0:T(128)} %concatenate.15.table, bf16[768,768]{1,0:T(8,128)(2,1)} %convolution_convert_fusion.d0.a0, bf16[768,768]{1,0:T(8,128)(2,1)} %copy-done.65, bf16[768,768]{1,0:T(8,128)(2,1)} %collective-permute-done.15.d2.a2, bf16[768,768]{1,0:T(8,128)(2,1)} %copy-done.64, ...), custom_call_target="tpu_custom_call" | custom-call | flops 4529848320 | bytes 41943040 | tf_op jit(solution)/shard_map/moe_weights/pallas_call | solution.py:674
  307.5 2.4 collective-permute-done.22
  309.9 3.7 fusion.30
  313.6 21.8 %collective-permute-done.24 = bf16[768,768]{1,0:T(8,128)(2,1)S(1)} collective-permute-done((bf16[768,768]{1,0:T(8,128)(2,1)}, bf16[768,768]{1,0:T(8,128)(2,1)S(1)}, u32[]{:S(2)}, u32[]{:S(2)}) %collective-permute-start.24) | collective-permute-done | bytes 1179680 | tf_op jit(solution)/shard_map/ppermute | solution.py:747
  335.6 2.6 multiply_reduce_fusion
  338.1 3.3 convert_add_fusion
  343.2 2.0 fusion.28
  348.9 4.5 all-to-all-start
  353.5 16.2 %moe_weights.3 = (bf16[4,768,768]{2,1,0:T(8,128)(2,1)}, bf16[16,128]{1,0:T(8,128)(2,1)}) custom-call(s32[33]{0:T(128)} %concatenate.15.table, bf16[768,768]{1,0:T(8,128)(2,1)} %copy-done.60, bf16[768,768]{1,0:T(8,128)(2,1)} %copy-done.62, bf16[768,768]{1,0:T(8,128)(2,1)} %copy-done.61, bf16[768,768]{1,0:T(8,128)(2,1)} %collective-permute-done.17.x3.a3, ...), custom_call_target="tpu_custom_call" | custom-call | flops 4529848320 | bytes 41943040 | tf_op jit(solution)/shard_map/moe_weights/pallas_call | solution.py:674
  369.7 5.1 all-to-all-done
  377.0 2.7 collective-permute-done.26.g3
  384.2 62.8 %attention_backward.1 = (bf16[768,768]{1,0:T(8,128)(2,1)}, bf16[768,768]{1,0:T(8,128)(2,1)}, bf16[768,768]{1,0:T(8,128)(2,1)}, bf16[768,768]{1,0:T(8,128)(2,1)}, bf16[4,768,192]{2,1,0:T(8,128)(2,1)}) custom-call(s32[5,6]{1,0:T(8,128)} %stack.39.ranges, s32[4]{0:T(128)} %pad_add_fusion.1.ranks, bf16[768,768]{1,0:T(8,128)(2,1)} %convert_element_type.215.g0, ...), custom_call_target="tpu_custom_call" | custom-call | flops 65229815808 | bytes 41943040 | tf_op jit(solution)/shard_map/attention_backward/pallas_call | solution.py:390
  448.3 4.1 collective-permute-start.32
  452.5 2.8 collective-permute-done.32
  455.3 2.9 add_convert_fusion
  460.6 2.3 constant_dynamic-slice_fusion.2
  464.4 2.7 collective-permute-start.35
  469.6 14.2 %reduce-scatter.6.cloned.1.call-done = bf16[4,192,192]{2,1,0:T(8,128)(2,1)} async-done(((bf16[4,768,192]{2,1,0:T(8,128)(2,1)}), bf16[4,192,192]{2,1,0:T(8,128)(2,1)}) %reduce-scatter.6.cloned.1.call-update) | async-done | bytes 294928 | tf_op jit(solution)/shard_map/reduce_scatter | solution.py:969
  483.9 10.7 %collective-permute-done.35 = bf16[4,96,768]{2,1,0:T(8,128)(2,1)} collective-permute-done((bf16[4,96,768]{2,1,0:T(8,128)(2,1)}, bf16[4,96,768]{2,1,0:T(8,128)(2,1)}, u32[]{:S(2)}, u32[]{:S(2)}) %collective-permute-start.35) | collective-permute-done | bytes 589856 | tf_op jit(solution)/shard_map/ppermute | solution.py:795
  494.6 3.2 fusion.39
  497.9 3.6 fusion.14
  509.3 2.4 convert_add_fusion.3
  516.9 21.5 %collective-permute-done.40 = f32[48]{0:T(128)S(1)} collective-permute-done((f32[48]{0:T(128)S(1)}, f32[48]{0:T(128)S(1)}, u32[]{:S(2)}, u32[]{:S(2)}) %collective-permute-start.40) | collective-permute-done | bytes 224 | tf_op jit(solution)/shard_map/ppermute | solution.py:747
  543.9 3.2 fusion.40
  547.2 3.9 fusion.36
  (308 shorter events, 106.8 us)
Async XLA Ops:
  7.2 79.5 %all-gather.4.cloned.1.call-start = ((), (), s32[]{:S(2)}) async-start(), calls=%async_computation.4 | async-start | bytes 1769472 | tf_op jit(solution)/shard_map/all_gather | solution.py:811
  8.7 14.5 %collective-permute-start.3 = (s32[3,3072]{1,0:T(4,128)}, s32[3,3072]{1,0:T(4,128)}, u32[]{:S(2)}, u32[]{:S(2)}) collective-permute-start(s32[3,3072]{1,0:T(4,128)} %pad_add_fusion), channel_id=1, source_target_pairs={{0,4},{4,0},{1,5},{5,1},{2,6},{6,2},{3,7},{7,3},{8,12},{12,8},{9,1... | collective-permute-start | bytes 110600 | tf_op jit(solution)/shard_map/ppermute | solution.py:747
  12.1 23.3 %collective-permute-start.1 = (bf16[384,192]{1,0:T(8,128)(2,1)}, bf16[384,192]{1,0:T(8,128)(2,1)}, u32[]{:S(2)}, u32[]{:S(2)}) collective-permute-start(bf16[384,192]{1,0:T(8,128)(2,1)} %constant_dynamic-slice_fusion.18), channel_id=1, source_target_pairs={{0,2},{2,0},{1,3},{3,1},{4,6},{6,4},{5,7},{7,5},{8,10},{10,8},{9,1... | collective-permute-start | bytes 442376 | tf_op jit(solution)/shard_map/ppermute | solution.py:747
  17.9 30.5 %collective-permute-start.2 = (bf16[768,768]{1,0:T(8,128)(2,1)}, bf16[768,768]{1,0:T(8,128)(2,1)}, u32[]{:S(2)}, u32[]{:S(2)}) collective-permute-start(bf16[768,768]{1,0:T(8,128)(2,1)} %fusion.26), channel_id=1, source_target_pairs={{0,1},{1,0},{6,7},{7,6},{8,9},{9,8},{14,15},{15,14},{16,17},{17,16... | collective-permute-start | bytes 3538952 | tf_op jit(solution)/shard_map/ppermute | solution.py:752
  21.4 27.1 %collective-permute-start = (bf16[768,768]{1,0:T(8,128)(2,1)S(1)}, bf16[768,768]{1,0:T(8,128)(2,1)S(1)}, u32[]{:S(2)}, u32[]{:S(2)}) collective-permute-start(bf16[768,768]{1,0:T(8,128)(2,1)S(1)} %bitcast.86), channel_id=1, source_target_pairs={{2,4},{4,2},{3,5},{5,3},{10,12},{12,10},{11,13},{13,11},{18,20},{2... | collective-permute-start | bytes 3538952 | tf_op jit(solution)/shard_map/ppermute | solution.py:850
  54.7 9.0 %collective-permute-start.5 = (bf16[768,768]{1,0:T(8,128)(2,1)}, bf16[768,768]{1,0:T(8,128)(2,1)}, u32[]{:S(2)}, u32[]{:S(2)}) collective-permute-start(bf16[768,768]{1,0:T(8,128)(2,1)} %get-tuple-element.252), channel_id=1, source_target_pairs={{2,3},{3,2},{4,5},{5,4},{10,11},{11,10},{12,13},{13,12},{18,19},{1... | collective-permute-start | bytes 3538952 | tf_op jit(solution)/shard_map/ppermute | solution.py:752
  56.3 167.0 %all-gather.6.cloned.1.call-start = ((), (), s32[]{:S(2)}) async-start(), calls=%async_computation.5 | async-start | bytes 5308416 | tf_op jit(solution)/shard_map/all_gather | solution.py:811
  60.3 29.0 %collective-permute-start.4 = (bf16[768,768]{1,0:T(8,128)(2,1)}, bf16[768,768]{1,0:T(8,128)(2,1)}, u32[]{:S(2)}, u32[]{:S(2)}) collective-permute-start(bf16[768,768]{1,0:T(8,128)(2,1)} %get-tuple-element.251.x0), channel_id=1, source_target_pairs={{0,4},{4,0},{1,5},{5,1},{2,6},{6,2},{3,7},{7,3},{8,12},{12,8},{9,1... | collective-permute-start | bytes 3538952 | tf_op jit(solution)/shard_map/ppermute | solution.py:747
  66.1 23.3 %collective-permute-start.6 = (bf16[768,768]{1,0:T(8,128)(2,1)}, bf16[768,768]{1,0:T(8,128)(2,1)}, u32[]{:S(2)}, u32[]{:S(2)}) collective-permute-start(bf16[768,768]{1,0:T(8,128)(2,1)} %broadcast_select_fusion.3.x2), channel_id=1, source_target_pairs={{0,4},{4,0},{1,5},{5,1},{2,6},{6,2},{3,7},{7,3},{8,12},{12,8},{9,1... | collective-permute-start | bytes 3538952 | tf_op jit(solution)/shard_map/ppermute | solution.py:747
  77.3 54.0 %collective-permute-start.7 = (bf16[384,768]{1,0:T(8,128)(2,1)}, bf16[384,768]{1,0:T(8,128)(2,1)S(1)}, u32[]{:S(2)}, u32[]{:S(2)}) collective-permute-start(bf16[384,768]{1,0:T(8,128)(2,1)} %constant_dynamic-slice_fusion.17), channel_id=1, source_target_pairs={{0,2},{2,0},{1,3},{3,1},{4,6},{6,4},{5,7},{7,5},{8,10},{10,8},{9,1... | collective-permute-start | bytes 1769480 | tf_op jit(solution)/shard_map/ppermute | solution.py:747
  80.7 52.2 %collective-permute-start.8 = (bf16[384,768]{1,0:T(8,128)(2,1)}, bf16[384,768]{1,0:T(8,128)(2,1)}, u32[]{:S(2)}, u32[]{:S(2)}) collective-permute-start(bf16[384,768]{1,0:T(8,128)(2,1)} %constant_dynamic-slice_fusion.16), channel_id=1, source_target_pairs={{0,2},{2,0},{1,3},{3,1},{4,6},{6,4},{5,7},{7,5},{8,10},{10,8},{9,1... | collective-permute-start | bytes 1769480 | tf_op jit(solution)/shard_map/ppermute | solution.py:747
  133.0 90.4 %all-gather.8.cloned.1.call-start = ((), (), s32[]{:S(2)}) async-start(), calls=%async_computation.6 | async-start | bytes 5308416 | tf_op jit(solution)/shard_map/all_gather | solution.py:811
  133.7 245.9 %reduce-scatter.4.cloned.1.call-start = ((), (), s32[]{:S(2)}) async-start(), calls=%async_computation.7 | async-start | bytes 5898240 | tf_op jit(solution)/shard_map/reduce_scatter | solution.py:931
  133.9 6.2 %collective-permute-start.9 = (bf16[768,768]{1,0:T(8,128)(2,1)}, bf16[768,768]{1,0:T(8,128)(2,1)S(1)}, u32[]{:S(2)}, u32[]{:S(2)}) collective-permute-start(bf16[768,768]{1,0:T(8,128)(2,1)} %get-tuple-element.109), channel_id=1, source_target_pairs={{0,4},{4,0},{1,5},{5,1},{2,6},{6,2},{3,7},{7,3},{8,12},{12,8},{9,1... | collective-permute-start | bytes 3538952 | tf_op jit(solution)/shard_map/ppermute | solution.py:747
  136.3 47.1 %collective-permute-start.11 = (bf16[768,768]{1,0:T(8,128)(2,1)}, bf16[768,768]{1,0:T(8,128)(2,1)}, u32[]{:S(2)}, u32[]{:S(2)}) collective-permute-start(bf16[768,768]{1,0:T(8,128)(2,1)} %get-tuple-element.115), channel_id=1, source_target_pairs={{0,4},{4,0},{1,5},{5,1},{2,6},{6,2},{3,7},{7,3},{8,12},{12,8},{9,1... | collective-permute-start | bytes 3538952 | tf_op jit(solution)/shard_map/ppermute | solution.py:747
  141.8 41.6 %collective-permute-start.10 = (bf16[768,768]{1,0:T(8,128)(2,1)S(1)}, bf16[768,768]{1,0:T(8,128)(2,1)S(1)}, u32[]{:S(2)}, u32[]{:S(2)}) collective-permute-start(bf16[768,768]{1,0:T(8,128)(2,1)S(1)} %add_convert_fusion.6), channel_id=1, source_target_pairs={{0,1},{1,0},{2,3},{3,2},{4,5},{5,4},{6,7},{7,6},{8,9},{9,8},{10,11... | collective-permute-start | bytes 3538952 | tf_op jit(solution)/shard_map/ppermute | solution.py:747
  146.0 46.5 %collective-permute-start.13 = (bf16[768,768]{1,0:T(8,128)(2,1)}, bf16[768,768]{1,0:T(8,128)(2,1)}, u32[]{:S(2)}, u32[]{:S(2)}) collective-permute-start(bf16[768,768]{1,0:T(8,128)(2,1)} %bitcast.89), channel_id=1, source_target_pairs={{2,4},{4,2},{3,5},{5,3},{10,12},{12,10},{11,13},{13,11},{18,20},{2... | collective-permute-start | bytes 3538952 | tf_op jit(solution)/shard_map/ppermute | solution.py:887
  192.4 28.0 %collective-permute-start.12 = (bf16[768,768]{1,0:T(8,128)(2,1)S(1)}, bf16[768,768]{1,0:T(8,128)(2,1)S(1)}, u32[]{:S(2)}, u32[]{:S(2)}) collective-permute-start(bf16[768,768]{1,0:T(8,128)(2,1)S(1)} %convolution_convert_fusion.1.x0.a0), channel_id=1, source_target_pairs={{0,1},{1,0},{2,3},{3,2},{4,5},{5,4},{6,7},{7,6},{8,9},{9,8},{10,11... | collective-permute-start | bytes 3538952 | tf_op jit(solution)/shard_map/ppermute | solution.py:747
  193.2 27.5 %collective-permute-start.16 = (bf16[768,768]{1,0:T(8,128)(2,1)S(1)}, bf16[768,768]{1,0:T(8,128)(2,1)S(1)}, u32[]{:S(2)}, u32[]{:S(2)}) collective-permute-start(bf16[768,768]{1,0:T(8,128)(2,1)S(1)} %convolution_convert_fusion.1.x0.a0), channel_id=1, source_target_pairs={{0,4},{4,0},{1,5},{5,1},{2,6},{6,2},{3,7},{7,3},{8,12},{12,8},{9,1... | collective-permute-start | bytes 3538952 | tf_op jit(solution)/shard_map/ppermute | solution.py:747
  220.4 31.6 %collective-permute-start.15 = (bf16[768,768]{1,0:T(8,128)(2,1)}, bf16[768,768]{1,0:T(8,128)(2,1)}, u32[]{:S(2)}, u32[]{:S(2)}) collective-permute-start(bf16[768,768]{1,0:T(8,128)(2,1)} %convolution_convert_fusion.d0.a0), channel_id=1, source_target_pairs={{0,1},{1,0},{2,3},{3,2},{4,5},{5,4},{6,7},{7,6},{8,9},{9,8},{10,11... | collective-permute-start | bytes 3538952 | tf_op jit(solution)/shard_map/ppermute | solution.py:747
  251.9 3.1 collective-permute-start.18
  252.0 4.7 collective-permute-start.19
  252.5 5.9 %collective-permute-start.14 = (bf16[768,768]{1,0:T(8,128)(2,1)}, bf16[768,768]{1,0:T(8,128)(2,1)S(1)}, u32[]{:S(2)}, u32[]{:S(2)}) collective-permute-start(bf16[768,768]{1,0:T(8,128)(2,1)} %convolution_convert_fusion.d0.a0), channel_id=1, source_target_pairs={{0,4},{4,0},{1,5},{5,1},{2,6},{6,2},{3,7},{7,3},{8,12},{12,8},{9,1... | collective-permute-start | bytes 3538952 | tf_op jit(solution)/shard_map/ppermute | solution.py:747
  256.7 28.0 %collective-permute-start.20 = (bf16[768,768]{1,0:T(8,128)(2,1)S(1)}, bf16[768,768]{1,0:T(8,128)(2,1)S(1)}, u32[]{:S(2)}, u32[]{:S(2)}) collective-permute-start(bf16[768,768]{1,0:T(8,128)(2,1)S(1)} %add_convert_fusion.5), channel_id=1, source_target_pairs={{0,1},{1,0},{2,3},{3,2},{4,5},{5,4},{6,7},{7,6},{8,9},{9,8},{10,11... | collective-permute-start | bytes 3538952 | tf_op jit(solution)/shard_map/ppermute | solution.py:747
  284.8 3.1 collective-permute-start.21
  306.8 3.1 collective-permute-start.22
  307.0 28.4 %collective-permute-start.24 = (bf16[768,768]{1,0:T(8,128)(2,1)}, bf16[768,768]{1,0:T(8,128)(2,1)S(1)}, u32[]{:S(2)}, u32[]{:S(2)}) collective-permute-start(bf16[768,768]{1,0:T(8,128)(2,1)} %add_convert_fusion.4), channel_id=1, source_target_pairs={{0,1},{1,0},{2,3},{3,2},{4,5},{5,4},{6,7},{7,6},{8,9},{9,8},{10,11... | collective-permute-start | bytes 3538952 | tf_op jit(solution)/shard_map/ppermute | solution.py:747
  307.4 28.1 %collective-permute-start.23 = (bf16[768,768]{1,0:T(8,128)(2,1)}, bf16[768,768]{1,0:T(8,128)(2,1)S(1)}, u32[]{:S(2)}, u32[]{:S(2)}) collective-permute-start(bf16[768,768]{1,0:T(8,128)(2,1)} %get-tuple-element.143), channel_id=1, source_target_pairs={{0,4},{4,0},{1,5},{5,1},{2,6},{6,2},{3,7},{7,3},{8,12},{12,8},{9,1... | collective-permute-start | bytes 3538952 | tf_op jit(solution)/shard_map/ppermute | solution.py:747
  342.6 33.7 %collective-permute-start.25 = (bf16[768,768]{1,0:T(8,128)(2,1)}, bf16[768,768]{1,0:T(8,128)(2,1)}, u32[]{:S(2)}, u32[]{:S(2)}) collective-permute-start(bf16[768,768]{1,0:T(8,128)(2,1)} %convert_element_type.215.g0), channel_id=1, source_target_pairs={{0,1},{1,0},{2,3},{3,2},{4,5},{5,4},{6,7},{7,6},{8,9},{9,8},{10,11... | collective-permute-start | bytes 3538952 | tf_op jit(solution)/shard_map/ppermute | solution.py:747
  348.9 25.9 %all-to-all-start = ((f32[32,5,24]{2,1,0:T(8,128)}), f32[32,5,24]{2,1,0:T(8,128)}, u32[]{:S(2)}, u32[]{:S(2)}) async-start(f32[32,5,24]{2,1,0:T(8,128)} %copy.60), calls=%async_computation.1 | async-start | bytes 262144 | tf_op jit(solution)/shard_map/all_to_all | solution.py:948
  353.4 107.2 %reduce-scatter.8.cloned.1.call-start = ((), (), s32[]{:S(2)}) async-start(), calls=%async_computation.9 | async-start | bytes 5898240 | tf_op jit(solution)/shard_map/reduce_scatter | solution.py:951
  376.4 107.5 %reduce-scatter.6.cloned.1.call-start = ((), (), s32[]{:S(2)}) async-start(), calls=%async_computation.8 | async-start | bytes 1966080 | tf_op jit(solution)/shard_map/reduce_scatter | solution.py:969
  376.4 3.3 collective-permute-start.26
  376.5 7.7 %collective-permute-start.27 = (bf16[768,768]{1,0:T(8,128)(2,1)}, bf16[768,768]{1,0:T(8,128)(2,1)}, u32[]{:S(2)}, u32[]{:S(2)}) collective-permute-start(bf16[768,768]{1,0:T(8,128)(2,1)} %convert_element_type.215.g0), channel_id=1, source_target_pairs={{0,4},{4,0},{1,5},{5,1},{2,6},{6,2},{3,7},{7,3},{8,12},{12,8},{9,1... | collective-permute-start | bytes 3538952 | tf_op jit(solution)/shard_map/ppermute | solution.py:747
  381.1 66.0 %collective-permute-start.30 = (bf16[4,96,768]{2,1,0:T(8,128)(2,1)S(1)}, bf16[4,96,768]{2,1,0:T(8,128)(2,1)S(1)}, u32[]{:S(2)}, u32[]{:S(2)}) collective-permute-start(bf16[4,96,768]{2,1,0:T(8,128)(2,1)S(1)} %get-tuple-element.188), channel_id=1, source_target_pairs={{2,4},{4,2},{3,5},{5,3},{10,12},{12,10},{11,13},{13,11},{18,20},{2... | collective-permute-start | bytes 1769480 | tf_op jit(solution)/shard_map/ppermute | solution.py:796
  381.8 65.3 %collective-permute-start.31 = (bf16[4,96,768]{2,1,0:T(8,128)(2,1)S(1)}, bf16[4,96,768]{2,1,0:T(8,128)(2,1)S(1)}, u32[]{:S(2)}, u32[]{:S(2)}) collective-permute-start(bf16[4,96,768]{2,1,0:T(8,128)(2,1)S(1)} %get-tuple-element.258), channel_id=1, source_target_pairs={{0,4},{2,0},{4,6},{6,2},{1,5},{3,1},{5,7},{7,3},{8,12},{10,8},{12,... | collective-permute-start | bytes 1769480 | tf_op jit(solution)/shard_map/ppermute | solution.py:795
  383.5 63.7 %collective-permute-start.29 = (bf16[768,768]{1,0:T(8,128)(2,1)S(1)}, bf16[768,768]{1,0:T(8,128)(2,1)S(1)}, u32[]{:S(2)}, u32[]{:S(2)}) collective-permute-start(bf16[768,768]{1,0:T(8,128)(2,1)S(1)} %copy-done.9), channel_id=1, source_target_pairs={{2,4},{4,2},{3,5},{5,3},{10,12},{12,10},{11,13},{13,11},{18,20},{2... | collective-permute-start | bytes 3538952 | tf_op jit(solution)/shard_map/ppermute | solution.py:954
  448.3 6.9 %collective-permute-start.32 = (bf16[768,768]{1,0:T(8,128)(2,1)}, bf16[768,768]{1,0:T(8,128)(2,1)}, u32[]{:S(2)}, u32[]{:S(2)}) collective-permute-start(bf16[768,768]{1,0:T(8,128)(2,1)} %get-tuple-element.166), channel_id=1, source_target_pairs={{0,4},{4,0},{1,5},{5,1},{2,6},{6,2},{3,7},{7,3},{8,12},{12,8},{9,1... | collective-permute-start | bytes 3538952 | tf_op jit(solution)/shard_map/ppermute | solution.py:747
  458.2 36.3 %collective-permute-start.33 = (bf16[768,768]{1,0:T(8,128)(2,1)}, bf16[768,768]{1,0:T(8,128)(2,1)}, u32[]{:S(2)}, u32[]{:S(2)}) collective-permute-start(bf16[768,768]{1,0:T(8,128)(2,1)} %add_convert_fusion), channel_id=1, source_target_pairs={{2,3},{3,2},{4,5},{5,4},{10,11},{11,10},{12,13},{13,12},{18,19},{1... | collective-permute-start | bytes 3538952 | tf_op jit(solution)/shard_map/ppermute | solution.py:752
  459.9 34.6 %collective-permute-start.28 = (bf16[768,768]{1,0:T(8,128)(2,1)}, bf16[768,768]{1,0:T(8,128)(2,1)}, u32[]{:S(2)}, u32[]{:S(2)}) collective-permute-start(bf16[768,768]{1,0:T(8,128)(2,1)} %get-tuple-element.163), channel_id=1, source_target_pairs={{0,4},{4,0},{1,5},{5,1},{2,6},{6,2},{3,7},{7,3},{8,12},{12,8},{9,1... | collective-permute-start | bytes 3538952 | tf_op jit(solution)/shard_map/ppermute | solution.py:747
  462.9 21.0 %collective-permute-start.34 = (bf16[4,96,768]{2,1,0:T(8,128)(2,1)}, bf16[4,96,768]{2,1,0:T(8,128)(2,1)}, u32[]{:S(2)}, u32[]{:S(2)}) collective-permute-start(bf16[4,96,768]{2,1,0:T(8,128)(2,1)} %get-tuple-element.185), channel_id=1, source_target_pairs={{2,4},{4,2},{3,5},{5,3},{10,12},{12,10},{11,13},{13,11},{18,20},{2... | collective-permute-start | bytes 1769480 | tf_op jit(solution)/shard_map/ppermute | solution.py:796
  464.4 30.2 %collective-permute-start.35 = (bf16[4,96,768]{2,1,0:T(8,128)(2,1)}, bf16[4,96,768]{2,1,0:T(8,128)(2,1)}, u32[]{:S(2)}, u32[]{:S(2)}) collective-permute-start(bf16[4,96,768]{2,1,0:T(8,128)(2,1)} %get-tuple-element.256), channel_id=1, source_target_pairs={{0,4},{2,0},{4,6},{6,2},{1,5},{3,1},{5,7},{7,3},{8,12},{10,8},{12,... | collective-permute-start | bytes 1769480 | tf_op jit(solution)/shard_map/ppermute | solution.py:795
  501.6 10.2 %collective-permute-start.38 = (bf16[4,96,192]{2,1,0:T(8,128)(2,1)S(1)}, bf16[4,96,192]{2,1,0:T(8,128)(2,1)S(1)}, u32[]{:S(2)}, u32[]{:S(2)}) collective-permute-start(bf16[4,96,192]{2,1,0:T(8,128)(2,1)S(1)} %get-tuple-element.261), channel_id=1, source_target_pairs={{2,4},{4,2},{3,5},{5,3},{10,12},{12,10},{11,13},{13,11},{18,20},{2... | collective-permute-start | bytes 442376 | tf_op jit(solution)/shard_map/ppermute | solution.py:796
  502.4 11.4 %collective-permute-start.39 = (bf16[4,96,192]{2,1,0:T(8,128)(2,1)S(1)}, bf16[4,96,192]{2,1,0:T(8,128)(2,1)S(1)}, u32[]{:S(2)}, u32[]{:S(2)}) collective-permute-start(bf16[4,96,192]{2,1,0:T(8,128)(2,1)S(1)} %get-tuple-element.262), channel_id=1, source_target_pairs={{0,4},{2,0},{4,6},{6,2},{1,5},{3,1},{5,7},{7,3},{8,12},{10,8},{12,... | collective-permute-start | bytes 442376 | tf_op jit(solution)/shard_map/ppermute | solution.py:795
  503.4 40.6 %collective-permute-start.36 = (bf16[768,768]{1,0:T(8,128)(2,1)}, bf16[768,768]{1,0:T(8,128)(2,1)}, u32[]{:S(2)}, u32[]{:S(2)}) collective-permute-start(bf16[768,768]{1,0:T(8,128)(2,1)} %add_convert_fusion), channel_id=1, source_target_pairs={{0,1},{1,0},{6,7},{7,6},{8,9},{9,8},{14,15},{15,14},{16,17},{17,16... | collective-permute-start | bytes 3538952 | tf_op jit(solution)/shard_map/ppermute | solution.py:752
  505.3 41.9 %collective-permute-start.37 = (bf16[768,768]{1,0:T(8,128)(2,1)}, bf16[768,768]{1,0:T(8,128)(2,1)}, u32[]{:S(2)}, u32[]{:S(2)}) collective-permute-start(bf16[768,768]{1,0:T(8,128)(2,1)} %fusion.14), channel_id=1, source_target_pairs={{2,4},{4,2},{3,5},{5,3},{10,12},{12,10},{11,13},{13,11},{18,20},{2... | collective-permute-start | bytes 3538952 | tf_op jit(solution)/shard_map/ppermute | solution.py:978
  515.7 22.7 %collective-permute-start.40 = (f32[48]{0:T(128)S(1)}, f32[48]{0:T(128)S(1)}, u32[]{:S(2)}, u32[]{:S(2)}) collective-permute-start(f32[48]{0:T(128)S(1)} %dynamic_slice.97), channel_id=1, source_target_pairs={{0,2},{2,0},{1,3},{3,1},{4,6},{6,4},{5,7},{7,5},{8,10},{10,8},{9,1... | collective-permute-start | bytes 584 | tf_op jit(solution)/shard_map/ppermute | solution.py:747
  539.1 3.6 collective-permute-start.41
  (68 other events, 1196.5 us)
Sparse Core Ops, SparseCore 0:
  56.5 30.2 all-gather.3
  133.1 41.1 all-gather.5
  176.2 38.9 all-gather.7
  306.9 57.5 reduce-scatter.3
  376.5 55.4 reduce-scatter.7
  452.6 31.2 reduce-scatter.5

commit v6 on v5

--- a/solution.py
+++ b/solution.py
@@ -115,7 +115,7 @@
 
 
 def forward_kernel(
-    ranges, ranks, x0, x1, x2, x3, w_ref, proj_ref, start_ref,
+    ranges, ranks, x0, x1, x2, x3, w_ref, start_ref,
     p0, p1, p2, p3, qt_ref, k_ref, kt_ref, v_ref, ctx_ref, lse_ref,
     x_ref, part_ref, vt_ref, score_ref, top_ref, sum_ref, arrived, left,
 ):
@@ -194,7 +194,7 @@
         context = sum_ref[head, :HEAD_DIM] / total
         ctx_ref[head * HEAD_DIM : (head + 1) * HEAD_DIM] = context.astype(jnp.bfloat16)
         lse_ref[head] = top_ref[head, :1] + jnp.log(total) * LOG2E
-    part_ref[rows, :] = matmul(ctx_ref[...], proj_ref[...], ((0,), (0,))).astype(jnp.bfloat16)
+    part_ref[rows, :] = matmul(ctx_ref[...].T, w_ref[3], ((1,), (1,))).astype(jnp.bfloat16)
     send_ranks(part_ref, (p0, p1, p2, p3), ranks, left, (step + 1) * block, block, False)
 
     @pl.when(step == pl.num_programs(0) - 1)
@@ -202,7 +202,7 @@
         await_ranks(part_ref, (p0, p1, p2, p3), ranks, left)
 
 
-def attention_forward(ranges, start, ranks, x, w, proj):
+def attention_forward(ranges, start, ranks, x, w):
     tokens, width = start.shape[1], x[0].shape[1]
     local = w.shape[2]
     heads = local // HEAD_DIM
@@ -219,8 +219,7 @@
             grid=(count,),
             in_specs=[
                 *[HBM] * 4,
-                pl.BlockSpec((3, width, local), lambda i, r, n: (0, 0, 0)),
-                pl.BlockSpec((local, width), lambda i, r, n: (0, 0)),
+                pl.BlockSpec((4, width, local), lambda i, r, n: (0, 0, 0)),
                 pl.BlockSpec((1, block), lambda i, r, n: (0, i)),
             ],
             out_specs=[
@@ -259,12 +258,12 @@
             flops=4 * flops, transcendentals=tokens * tokens * heads // 2, bytes_accessed=40 << 20
         ),
         name="attention_forward",
-    )(ranges, ranks, *x, w, proj, start)
+    )(ranges, ranks, *x, w, start)
 
 
 def backward_kernel(
     ranges, ranks, g0, g1, g2, g3, x0, x1, x2, x3,
-    ctx_ref, lse_ref, qt_ref, start_ref, k_ref, kt_ref, v_ref, w_ref, proj_ref,
+    ctx_ref, lse_ref, qt_ref, start_ref, k_ref, kt_ref, v_ref, w_ref,
     p0, p1, p2, p3, weights_ref,
     g_ref, x_ref, part_ref, wgrad_ref, pgrad_ref,
     dk_ref, dv_ref, dq_ref, outer_ref, inner_ref, grad_ref, prob_ref, dscore_ref, arrived, left,
@@ -290,7 +289,7 @@
         await_copies(g_ref, (g0, g1, g2, g3), ranks, arrived.at[0])
 
     upstream = g_ref[rows, :]
-    outer = matmul(upstream, proj_ref[...], ((1,), (1,))).astype(jnp.bfloat16).T
+    outer = matmul(upstream, w_ref[3]).astype(jnp.bfloat16).T
     for head in range(heads):
         part = slice(head * HEAD_DIM, (head + 1) * HEAD_DIM)
         outer_ref[head] = outer[part]
@@ -373,7 +372,7 @@
         pltpu.make_async_copy(source, target, semaphores.at[b]).wait()
 
 
-def attention_backward(ranges, start, ranks, upstream, x, saved, w, proj):
+def attention_backward(ranges, start, ranks, upstream, x, saved, w):
     qt, k, kt, v, ctx, lse = saved
     tokens, width = start.shape[1], x[0].shape[1]
     local = w.shape[2]
@@ -401,8 +400,7 @@
                 head_rows,
                 pl.BlockSpec((tokens // fine, heads, HEAD_DIM, fine), lambda i, r, n: (0, 0, 0, 0)),
                 head_rows,
-                pl.BlockSpec((3, width, local), lambda i, r, n: (0, 0, 0)),
-                pl.BlockSpec((local, width), lambda i, r, n: (0, 0)),
+                pl.BlockSpec((4, width, local), lambda i, r, n: (0, 0, 0)),
             ],
             out_specs=[
                 *[HBM] * 4,
@@ -435,7 +433,7 @@
             flops=4 * flops, transcendentals=tokens * tokens * heads // 2, bytes_accessed=40 << 20
         ),
         name="attention_backward",
-    )(ranges, ranks, *upstream, *x, ctx, lse, qt, start, k, kt, v, w, proj)
+    )(ranges, ranks, *upstream, *x, ctx, lse, qt, start, k, kt, v, w)
 
 
 def route_rows(route, priority, experts, capacity, row_count, ranks):
@@ -839,7 +837,6 @@
     experts = expert_up.shape[0]
     token_count = segments.shape[1]
     capacity = 9 * token_count // (8 * experts)
-    local_width = qkv_weight.shape[2]
     users = (*high_bits, "c")
     core, near = lax.axis_index("c"), lax.axis_index("zl")
     ranks = jnp.stack(
@@ -848,7 +845,7 @@
     home = at_home()
     staying = block_input[0]
     coming = lax.ppermute(staying, ("c", "zh"), [(1, 2), (2, 1)])
-    small = jnp.concatenate([qkv_weight, proj_weight.reshape(1, model_width, local_width)], axis=0)
+    small = jnp.concatenate([qkv_weight, proj_weight.T[None]], axis=0)
     small_piece = flip(piece_of(small, users), "zh")
 
     def normed(rows):
@@ -876,24 +873,23 @@
     inputs = jnp.where(home, staying, coming).astype(jnp.float32)
     unit_one, inverse_one = normalize_plain(inputs)
     small = jnp.where(home, small, small_other)
-    qkv_used, proj_used = small[:3], small[3].reshape(local_width, model_width)
     *attended, qt, k, kt, v, ctx, lse = attention_forward(
-        ranges, start, ranks, normed_one, qkv_used, proj_used
+        ranges, start, ranks, normed_one, small
     )
     saved = (qt, k, kt, v, ctx, lse)
-    attended[3], up_piece, down_piece, indices, upstream = tie(
-        attended[3], up_piece, down_piece, indices, out_grad[0]
-    )
-    away_upstream = lax.ppermute(upstream, ("c", "zh"), [(1, 2), (2, 1)])
+    attended[3], up_piece, down_piece, indices = tie(
+        attended[3], up_piece, down_piece, indices
+    )
     new_experts = [share(piece, users, expert_up.shape) for piece in (up_piece, down_piece)]
     back_ranges = key_ranges(indices[2], BACKWARD_BLOCKS)[0]
     kept_rows, order, table, hot_rows = route_rows(
         indices[0], indices[1], experts, capacity, row_count, ranks
     )
     own_experts = (expert_up, expert_down)
-    far, back_ranges, order, table, kept_rows = tie(
-        flip(far_rows(attended), "zl"), back_ranges, order, table, kept_rows
-    )
+    far, back_ranges, order, table, kept_rows, upstream = tie(
+        flip(far_rows(attended), "zl"), back_ranges, order, table, kept_rows, out_grad[0]
+    )
+    away_upstream = lax.ppermute(upstream, ("c", "zh"), [(1, 2), (2, 1)])
     upstream = jnp.where(home, upstream, away_upstream).astype(jnp.float32)
     attended = near_rows(attended) + far.astype(jnp.float32)
     mixed_one = inputs + attended
@@ -953,7 +949,7 @@
     down_home = send_home(down_rest, 1)
     away_output = lax.ppermute(mixed_two, ("c", "zh"), [(1, 2), (2, 1)])
     *grad_one, weights_part = attention_backward(
-        back_ranges, start, ranks, grad_att, normed_one, saved, qkv_used, proj_used
+        back_ranges, start, ranks, grad_att, normed_one, saved, small
     )
     grad_one[3], away_output, *down_home = tie(grad_one[3], away_output, *down_home)
     one_far = far_rows(grad_one)

time: 569 us -> 568 us (level)
    unnamed x136 -> x137, local copies, waits for them, and re-layouts: 12.1 us -> 10.1 us
  transfers between devices with their start and end apart: 49 -> 49, of which waited for: 21 -> 21; matrix products, arithmetic and copies ran while one was open for 18% -> 18% of each run, Pallas kernels for 31% -> 32%
where the time goes in v6:
time: 568 us; the launch traced here: 559 us
  Pallas kernels  193 us (34%)
  waiting for transfers between devices  161 us (28%)
  other arithmetic  74 us (13%)
  starting transfers between devices  64.1 us (11%)
  local copies, waits for them, and re-layouts  37.7 us (7%)
  between operations  15.6 us (3%)
  matrix products  13.9 us (2%)
    ppermute x28, waiting for transfers between devices, flip(): return lax.ppermute(value, axis, [(0, 1), (1, 0)])  109 us
    pallas_call x4, Pallas kernels, moe_call(): pl.pallas_call(kernel, grid_spec=pltpu.PrefetchScalarGridSpec(num_scalar_...  85.5 us
    pallas_call x1, Pallas kernels, attention_backward(): pl.pallas_call(backward_kernel, grid_spec=pltpu.PrefetchScalarGridSpec(nu...  64.4 us
    pallas_call x1, Pallas kernels, attention_forward(): pl.pallas_call(forward_kernel, grid_spec=pltpu.PrefetchScalarGridSpec(num...  42.9 us
    ppermute x28, starting transfers between devices, flip(): return lax.ppermute(value, axis, [(0, 1), (1, 0)])  38.1 us
    ppermute x3, waiting for transfers between devices, send_home(): turned = lax.ppermute(turned, ('c', 'zh'), [(0, 2), (1, 0), (2, 3), (3, 1)])  15.4 us
    ppermute x4, waiting for transfers between devices, flip_some(): return lax.ppermute(value, ('c', 'zh', 'zl'), moves)  13.3 us
    reduce_scatter x1, waiting for transfers between devices, body(): lax.psum_scatter(weights_part, high_bits, scatter_dimension=1, tiled=True)  11.5 us
  transfers between devices with their start and end apart: 49, of which 21 were waited for; matrix products, arithmetic and copies ran while one was open for 18% of the time, Pallas kernels for 32%

profile of v6, /device:TPU:0, one launch (start us, length us, event | category | flops | bytes accessed | tf_op | source)
XLA Modules:
  0.0 558.8 jit_solution(7192854310392728947)
XLA Ops:
  11.9 3.6 collective-permute-start.1
  17.7 3.5 collective-permute-start.2
  35.2 13.2 %collective-permute-done.2 = bf16[768,768]{1,0:T(8,128)(2,1)} collective-permute-done((bf16[768,768]{1,0:T(8,128)(2,1)}, bf16[768,768]{1,0:T(8,128)(2,1)}, u32[]{:S(2)}, u32[]{:S(2)}) %collective-permute-start.2) | collective-permute-done | bytes 1179680 | tf_op jit(solution)/shard_map/ppermute | solution.py:750
  49.5 3.2 convert_reduce_fusion.1
  60.3 3.1 collective-permute-start.4
  63.4 2.4 broadcast_select_fusion.3.x2
  65.8 10.7 %collective-permute-start.6 = (bf16[768,768]{1,0:T(8,128)(2,1)}, bf16[768,768]{1,0:T(8,128)(2,1)}, u32[]{:S(2)}, u32[]{:S(2)}) collective-permute-start(bf16[768,768]{1,0:T(8,128)(2,1)} %broadcast_select_fusion.3.x2), channel_id=1, source_target_pairs={{0,4},{4,0},{1,5},{5,1},{2,6},{6,2},{3,7},{7,3},{8,12},{12,8},{9,1... | collective-permute-start | bytes 3538952 | tf_op jit(solution)/shard_map/ppermute | solution.py:745
  77.1 3.4 collective-permute-start.7
  80.5 6.0 %all-gather.4.cloned.1.call-done = bf16[3072,192]{1,0:T(8,128)(2,1)} async-done(((bf16[384,192]{1,0:T(8,128)(2,1)}), bf16[3072,192]{1,0:T(8,128)(2,1)}) %all-gather.4.cloned.1.call-update) | async-done | bytes 1179664 | tf_op jit(solution)/shard_map/all_gather | solution.py:809
  88.1 42.9 %attention_forward.1 = (bf16[768,768]{1,0:T(8,128)(2,1)}, bf16[768,768]{1,0:T(8,128)(2,1)}, bf16[768,768]{1,0:T(8,128)(2,1)}, bf16[768,768]{1,0:T(8,128)(2,1)}, ...) custom-call(s32[5,6]{1,0:T(8,128)} %stack.33.ranges, ...), custom_call_target="tpu_custom_call" | custom-call | flops 28991029248 | bytes 41943040 | tf_op jit(solution)/shard_map/attention_forward/pallas_call | solution.py:215
  141.5 2.2 collective-permute-start.10
  153.4 2.6 convert_reduce_fusion
  157.1 13.2 %collective-permute-done.10 = bf16[768,768]{1,0:T(8,128)(2,1)S(1)} collective-permute-done((bf16[768,768]{1,0:T(8,128)(2,1)S(1)}, bf16[768,768]{1,0:T(8,128)(2,1)S(1)}, u32[]{:S(2)}, u32[]{:S(2)}) %collective-permute-start.10) | collective-permute-done | bytes 1179680 | tf_op jit(solution)/shard_map/ppermute | solution.py:745
  171.3 3.9 fusion.57
  175.9 2.3 fusion.27
  181.1 2.5 collective-permute-start.16
  183.8 2.3 convolution_convert_fusion.d0.a0
  186.1 32.7 %collective-permute-done.12.x2.a2 = bf16[768,768]{1,0:T(8,128)(2,1)S(1)} collective-permute-done((bf16[768,768]{1,0:T(8,128)(2,1)S(1)}, bf16[768,768]{1,0:T(8,128)(2,1)S(1)}, u32[]{:S(2)}, u32[]{:S(2)}) %collective-permute-start.12) | collective-permute-done | bytes 1179680 | tf_op jit(solution)/shard_map/ppermute | solution.py:745
  222.2 28.8 %moe_forward.1 = (bf16[768,768]{1,0:T(8,128)(2,1)}, bf16[768,768]{1,0:T(8,128)(2,1)}, bf16[768,768]{1,0:T(8,128)(2,1)}, bf16[768,768]{1,0:T(8,128)(2,1)}, bf16[4...) custom-call(s32[33]{0:T(128)} %concatenate.15.table, bf16[768,768]{1,0:T(8,128)(2,1)} %copy-done.60, ...), custom_call_target="tpu_custom_call" | custom-call | flops 9059696640 | bytes 41943040 | tf_op jit(solution)/shard_map/moe_forward/pallas_call | solution.py:672
  251.6 2.5 collective-permute-done.18
  258.5 24.4 %moe_backward.1 = (bf16[768,768]{1,0:T(8,128)(2,1)}, bf16[768,768]{1,0:T(8,128)(2,1)}, bf16[768,768]{1,0:T(8,128)(2,1)}, bf16[768,768]{1,0:T(8,128)(2,1)}, bf16[4,1024,768]{2,1,0:T(8,128)(2,1)}) custom-call(s32[33]{0:T(128)} %concatenate.15.table, bf16[768,768]{1,0:T(8,128)(2,1)} %convolution_convert_fusion.d0.a0, bf16[768,768]{1,0:T(8,128)(2,1)} %copy-done.65, ...), custom_call_target="tpu_custom_call" | custom-call | flops 9059696640 | bytes 41943040 | tf_op jit(solution)/shard_map/moe_backward/pallas_call | solution.py:672
  283.8 3.1 collective-permute-done.21
  286.9 2.7 add_convert_fusion.4
  289.5 16.1 %moe_weights.2 = (bf16[4,768,768]{2,1,0:T(8,128)(2,1)}, bf16[16,128]{1,0:T(8,128)(2,1)}) custom-call(s32[33]{0:T(128)} %concatenate.15.table, bf16[768,768]{1,0:T(8,128)(2,1)} %convolution_convert_fusion.d0.a0, bf16[768,768]{1,0:T(8,128)(2,1)} %copy-done.65, bf16[768,768]{1,0:T(8,128)(2,1)} %collective-permute-done.15.d2.a2, bf16[768,768]{1,0:T(8,128)(2,1)} %copy-done.64, ...), custom_call_target="tpu_custom_call" | custom-call | flops 4529848320 | bytes 41943040 | tf_op jit(solution)/shard_map/moe_weights/pallas_call | solution.py:672
  306.6 2.2 collective-permute-done.22
  308.8 3.7 fusion.30
  312.5 21.8 %collective-permute-done.24 = bf16[768,768]{1,0:T(8,128)(2,1)S(1)} collective-permute-done((bf16[768,768]{1,0:T(8,128)(2,1)}, bf16[768,768]{1,0:T(8,128)(2,1)S(1)}, u32[]{:S(2)}, u32[]{:S(2)}) %collective-permute-start.24) | collective-permute-done | bytes 1179680 | tf_op jit(solution)/shard_map/ppermute | solution.py:745
  334.4 2.6 multiply_reduce_fusion
  337.0 3.3 convert_add_fusion
  342.1 2.0 fusion.28
  347.8 4.2 all-to-all-start
  352.0 16.2 %moe_weights.3 = (bf16[4,768,768]{2,1,0:T(8,128)(2,1)}, bf16[16,128]{1,0:T(8,128)(2,1)}) custom-call(s32[33]{0:T(128)} %concatenate.15.table, bf16[768,768]{1,0:T(8,128)(2,1)} %copy-done.60, bf16[768,768]{1,0:T(8,128)(2,1)} %copy-done.62, bf16[768,768]{1,0:T(8,128)(2,1)} %copy-done.61, bf16[768,768]{1,0:T(8,128)(2,1)} %collective-permute-done.17.x3.a3, ...), custom_call_target="tpu_custom_call" | custom-call | flops 4529848320 | bytes 41943040 | tf_op jit(solution)/shard_map/moe_weights/pallas_call | solution.py:672
  368.2 5.0 all-to-all-done
  375.5 2.7 collective-permute-done.26.g3
  383.0 64.4 %attention_backward.1 = (bf16[768,768]{1,0:T(8,128)(2,1)}, bf16[768,768]{1,0:T(8,128)(2,1)}, bf16[768,768]{1,0:T(8,128)(2,1)}, bf16[768,768]{1,0:T(8,128)(2,1)}, bf16[4,768,192]{2,1,0:T(8,128)(2,1)}) custom-call(s32[5,6]{1,0:T(8,128)} %stack.39.ranges, s32[4]{0:T(128)} %pad_add_fusion.1.ranks, bf16[768,768]{1,0:T(8,128)(2,1)} %convert_element_type.215.g0, ...), custom_call_target="tpu_custom_call" | custom-call | flops 65229815808 | bytes 41943040 | tf_op jit(solution)/shard_map/attention_backward/pallas_call | solution.py:389
  448.6 4.0 collective-permute-start.32
  452.7 2.8 collective-permute-done.32
  455.5 3.0 add_convert_fusion
  460.9 2.4 constant_dynamic-slice_fusion.2
  464.8 2.7 collective-permute-start.35
  469.9 11.5 %reduce-scatter.6.cloned.1.call-done = bf16[4,192,192]{2,1,0:T(8,128)(2,1)} async-done(((bf16[4,768,192]{2,1,0:T(8,128)(2,1)}), bf16[4,192,192]{2,1,0:T(8,128)(2,1)}) %reduce-scatter.6.cloned.1.call-update) | async-done | bytes 294928 | tf_op jit(solution)/shard_map/reduce_scatter | solution.py:965
  481.4 13.4 %collective-permute-done.35 = bf16[4,96,768]{2,1,0:T(8,128)(2,1)} collective-permute-done((bf16[4,96,768]{2,1,0:T(8,128)(2,1)}, bf16[4,96,768]{2,1,0:T(8,128)(2,1)}, u32[]{:S(2)}, u32[]{:S(2)}) %collective-permute-start.35) | collective-permute-done | bytes 589856 | tf_op jit(solution)/shard_map/ppermute | solution.py:793
  494.9 3.2 fusion.39
  498.2 3.6 fusion.14
  509.9 2.4 convert_add_fusion.3
  517.5 21.2 %collective-permute-done.40 = f32[48]{0:T(128)S(1)} collective-permute-done((f32[48]{0:T(128)S(1)}, f32[48]{0:T(128)S(1)}, u32[]{:S(2)}, u32[]{:S(2)}) %collective-permute-start.40) | collective-permute-done | bytes 224 | tf_op jit(solution)/shard_map/ppermute | solution.py:745
  544.2 3.2 fusion.40
  547.5 3.9 fusion.36
  (305 shorter events, 106.6 us)
Async XLA Ops:
  7.2 79.3 %all-gather.4.cloned.1.call-start = ((), (), s32[]{:S(2)}) async-start(), calls=%async_computation.4 | async-start | bytes 1769472 | tf_op jit(solution)/shard_map/all_gather | solution.py:809
  8.7 14.2 %collective-permute-start.3 = (s32[3,3072]{1,0:T(4,128)}, s32[3,3072]{1,0:T(4,128)}, u32[]{:S(2)}, u32[]{:S(2)}) collective-permute-start(s32[3,3072]{1,0:T(4,128)} %pad_add_fusion), channel_id=1, source_target_pairs={{0,4},{4,0},{1,5},{5,1},{2,6},{6,2},{3,7},{7,3},{8,12},{12,8},{9,1... | collective-permute-start | bytes 110600 | tf_op jit(solution)/shard_map/ppermute | solution.py:745
  11.9 23.3 %collective-permute-start.1 = (bf16[384,192]{1,0:T(8,128)(2,1)}, bf16[384,192]{1,0:T(8,128)(2,1)}, u32[]{:S(2)}, u32[]{:S(2)}) collective-permute-start(bf16[384,192]{1,0:T(8,128)(2,1)} %constant_dynamic-slice_fusion.18), channel_id=1, source_target_pairs={{0,2},{2,0},{1,3},{3,1},{4,6},{6,4},{5,7},{7,5},{8,10},{10,8},{9,1... | collective-permute-start | bytes 442376 | tf_op jit(solution)/shard_map/ppermute | solution.py:745
  17.7 30.8 %collective-permute-start.2 = (bf16[768,768]{1,0:T(8,128)(2,1)}, bf16[768,768]{1,0:T(8,128)(2,1)}, u32[]{:S(2)}, u32[]{:S(2)}) collective-permute-start(bf16[768,768]{1,0:T(8,128)(2,1)} %fusion.26), channel_id=1, source_target_pairs={{0,1},{1,0},{6,7},{7,6},{8,9},{9,8},{14,15},{15,14},{16,17},{17,16... | collective-permute-start | bytes 3538952 | tf_op jit(solution)/shard_map/ppermute | solution.py:750
  21.2 27.3 %collective-permute-start = (bf16[768,768]{1,0:T(8,128)(2,1)S(1)}, bf16[768,768]{1,0:T(8,128)(2,1)S(1)}, u32[]{:S(2)}, u32[]{:S(2)}) collective-permute-start(bf16[768,768]{1,0:T(8,128)(2,1)S(1)} %bitcast.89), channel_id=1, source_target_pairs={{2,4},{4,2},{3,5},{5,3},{10,12},{12,10},{11,13},{13,11},{18,20},{2... | collective-permute-start | bytes 3538952 | tf_op jit(solution)/shard_map/ppermute | solution.py:847
  54.6 8.8 %collective-permute-start.5 = (bf16[768,768]{1,0:T(8,128)(2,1)}, bf16[768,768]{1,0:T(8,128)(2,1)}, u32[]{:S(2)}, u32[]{:S(2)}) collective-permute-start(bf16[768,768]{1,0:T(8,128)(2,1)} %get-tuple-element.252), channel_id=1, source_target_pairs={{2,3},{3,2},{4,5},{5,4},{10,11},{11,10},{12,13},{13,12},{18,19},{1... | collective-permute-start | bytes 3538952 | tf_op jit(solution)/shard_map/ppermute | solution.py:750
  56.3 165.9 %all-gather.6.cloned.1.call-start = ((), (), s32[]{:S(2)}) async-start(), calls=%async_computation.5 | async-start | bytes 5308416 | tf_op jit(solution)/shard_map/all_gather | solution.py:809
  60.3 27.8 %collective-permute-start.4 = (bf16[768,768]{1,0:T(8,128)(2,1)}, bf16[768,768]{1,0:T(8,128)(2,1)}, u32[]{:S(2)}, u32[]{:S(2)}) collective-permute-start(bf16[768,768]{1,0:T(8,128)(2,1)} %get-tuple-element.251.x0), channel_id=1, source_target_pairs={{0,4},{4,0},{1,5},{5,1},{2,6},{6,2},{3,7},{7,3},{8,12},{12,8},{9,1... | collective-permute-start | bytes 3538952 | tf_op jit(solution)/shard_map/ppermute | solution.py:745
  65.8 22.2 %collective-permute-start.6 = (bf16[768,768]{1,0:T(8,128)(2,1)}, bf16[768,768]{1,0:T(8,128)(2,1)}, u32[]{:S(2)}, u32[]{:S(2)}) collective-permute-start(bf16[768,768]{1,0:T(8,128)(2,1)} %broadcast_select_fusion.3.x2), channel_id=1, source_target_pairs={{0,4},{4,0},{1,5},{5,1},{2,6},{6,2},{3,7},{7,3},{8,12},{12,8},{9,1... | collective-permute-start | bytes 3538952 | tf_op jit(solution)/shard_map/ppermute | solution.py:745
  77.1 53.8 %collective-permute-start.7 = (bf16[384,768]{1,0:T(8,128)(2,1)}, bf16[384,768]{1,0:T(8,128)(2,1)S(1)}, u32[]{:S(2)}, u32[]{:S(2)}) collective-permute-start(bf16[384,768]{1,0:T(8,128)(2,1)} %constant_dynamic-slice_fusion.17), channel_id=1, source_target_pairs={{0,2},{2,0},{1,3},{3,1},{4,6},{6,4},{5,7},{7,5},{8,10},{10,8},{9,1... | collective-permute-start | bytes 1769480 | tf_op jit(solution)/shard_map/ppermute | solution.py:745
  80.5 52.2 %collective-permute-start.8 = (bf16[384,768]{1,0:T(8,128)(2,1)}, bf16[384,768]{1,0:T(8,128)(2,1)}, u32[]{:S(2)}, u32[]{:S(2)}) collective-permute-start(bf16[384,768]{1,0:T(8,128)(2,1)} %constant_dynamic-slice_fusion.16), channel_id=1, source_target_pairs={{0,2},{2,0},{1,3},{3,1},{4,6},{6,4},{5,7},{7,5},{8,10},{10,8},{9,1... | collective-permute-start | bytes 1769480 | tf_op jit(solution)/shard_map/ppermute | solution.py:745
  132.7 89.5 %all-gather.8.cloned.1.call-start = ((), (), s32[]{:S(2)}) async-start(), calls=%async_computation.6 | async-start | bytes 5308416 | tf_op jit(solution)/shard_map/all_gather | solution.py:809
  133.5 244.7 %reduce-scatter.4.cloned.1.call-start = ((), (), s32[]{:S(2)}) async-start(), calls=%async_computation.7 | async-start | bytes 5898240 | tf_op jit(solution)/shard_map/reduce_scatter | solution.py:927
  133.7 6.1 %collective-permute-start.9 = (bf16[768,768]{1,0:T(8,128)(2,1)}, bf16[768,768]{1,0:T(8,128)(2,1)S(1)}, u32[]{:S(2)}, u32[]{:S(2)}) collective-permute-start(bf16[768,768]{1,0:T(8,128)(2,1)} %get-tuple-element.109), channel_id=1, source_target_pairs={{0,4},{4,0},{1,5},{5,1},{2,6},{6,2},{3,7},{7,3},{8,12},{12,8},{9,1... | collective-permute-start | bytes 3538952 | tf_op jit(solution)/shard_map/ppermute | solution.py:745
  135.9 35.1 %collective-permute-start.11 = (bf16[768,768]{1,0:T(8,128)(2,1)}, bf16[768,768]{1,0:T(8,128)(2,1)}, u32[]{:S(2)}, u32[]{:S(2)}) collective-permute-start(bf16[768,768]{1,0:T(8,128)(2,1)} %get-tuple-element.115), channel_id=1, source_target_pairs={{0,4},{4,0},{1,5},{5,1},{2,6},{6,2},{3,7},{7,3},{8,12},{12,8},{9,1... | collective-permute-start | bytes 3538952 | tf_op jit(solution)/shard_map/ppermute | solution.py:745
  141.5 28.8 %collective-permute-start.10 = (bf16[768,768]{1,0:T(8,128)(2,1)S(1)}, bf16[768,768]{1,0:T(8,128)(2,1)S(1)}, u32[]{:S(2)}, u32[]{:S(2)}) collective-permute-start(bf16[768,768]{1,0:T(8,128)(2,1)S(1)} %add_convert_fusion.6), channel_id=1, source_target_pairs={{0,1},{1,0},{2,3},{3,2},{4,5},{5,4},{6,7},{7,6},{8,9},{9,8},{10,11... | collective-permute-start | bytes 3538952 | tf_op jit(solution)/shard_map/ppermute | solution.py:745
  170.3 13.3 %collective-permute-start.13 = (bf16[768,768]{1,0:T(8,128)(2,1)}, bf16[768,768]{1,0:T(8,128)(2,1)S(1)}, u32[]{:S(2)}, u32[]{:S(2)}) collective-permute-start(bf16[768,768]{1,0:T(8,128)(2,1)} %bitcast.94), channel_id=1, source_target_pairs={{2,4},{4,2},{3,5},{5,3},{10,12},{12,10},{11,13},{13,11},{18,20},{2... | collective-permute-start | bytes 3538952 | tf_op jit(solution)/shard_map/ppermute | solution.py:892
  179.3 39.5 %collective-permute-start.12 = (bf16[768,768]{1,0:T(8,128)(2,1)S(1)}, bf16[768,768]{1,0:T(8,128)(2,1)S(1)}, u32[]{:S(2)}, u32[]{:S(2)}) collective-permute-start(bf16[768,768]{1,0:T(8,128)(2,1)S(1)} %convolution_convert_fusion.1.x0.a0), channel_id=1, source_target_pairs={{0,1},{1,0},{2,3},{3,2},{4,5},{5,4},{6,7},{7,6},{8,9},{9,8},{10,11... | collective-permute-start | bytes 3538952 | tf_op jit(solution)/shard_map/ppermute | solution.py:745
  181.1 38.5 %collective-permute-start.16 = (bf16[768,768]{1,0:T(8,128)(2,1)S(1)}, bf16[768,768]{1,0:T(8,128)(2,1)S(1)}, u32[]{:S(2)}, u32[]{:S(2)}) collective-permute-start(bf16[768,768]{1,0:T(8,128)(2,1)S(1)} %convolution_convert_fusion.1.x0.a0), channel_id=1, source_target_pairs={{0,4},{4,0},{1,5},{5,1},{2,6},{6,2},{3,7},{7,3},{8,12},{12,8},{9,1... | collective-permute-start | bytes 3538952 | tf_op jit(solution)/shard_map/ppermute | solution.py:745
  218.8 3.4 collective-permute-start.17
  219.6 31.4 %collective-permute-start.15 = (bf16[768,768]{1,0:T(8,128)(2,1)}, bf16[768,768]{1,0:T(8,128)(2,1)}, u32[]{:S(2)}, u32[]{:S(2)}) collective-permute-start(bf16[768,768]{1,0:T(8,128)(2,1)} %convolution_convert_fusion.d0.a0), channel_id=1, source_target_pairs={{0,1},{1,0},{2,3},{3,2},{4,5},{5,4},{6,7},{7,6},{8,9},{9,8},{10,11... | collective-permute-start | bytes 3538952 | tf_op jit(solution)/shard_map/ppermute | solution.py:745
  251.0 3.1 collective-permute-start.18
  251.1 4.7 collective-permute-start.19
  251.6 5.9 %collective-permute-start.14 = (bf16[768,768]{1,0:T(8,128)(2,1)}, bf16[768,768]{1,0:T(8,128)(2,1)S(1)}, u32[]{:S(2)}, u32[]{:S(2)}) collective-permute-start(bf16[768,768]{1,0:T(8,128)(2,1)} %convolution_convert_fusion.d0.a0), channel_id=1, source_target_pairs={{0,4},{4,0},{1,5},{5,1},{2,6},{6,2},{3,7},{7,3},{8,12},{12,8},{9,1... | collective-permute-start | bytes 3538952 | tf_op jit(solution)/shard_map/ppermute | solution.py:745
  255.8 28.0 %collective-permute-start.20 = (bf16[768,768]{1,0:T(8,128)(2,1)S(1)}, bf16[768,768]{1,0:T(8,128)(2,1)S(1)}, u32[]{:S(2)}, u32[]{:S(2)}) collective-permute-start(bf16[768,768]{1,0:T(8,128)(2,1)S(1)} %add_convert_fusion.5), channel_id=1, source_target_pairs={{0,1},{1,0},{2,3},{3,2},{4,5},{5,4},{6,7},{7,6},{8,9},{9,8},{10,11... | collective-permute-start | bytes 3538952 | tf_op jit(solution)/shard_map/ppermute | solution.py:745
  305.7 3.1 collective-permute-start.22
  305.9 28.4 %collective-permute-start.24 = (bf16[768,768]{1,0:T(8,128)(2,1)}, bf16[768,768]{1,0:T(8,128)(2,1)S(1)}, u32[]{:S(2)}, u32[]{:S(2)}) collective-permute-start(bf16[768,768]{1,0:T(8,128)(2,1)} %add_convert_fusion.4), channel_id=1, source_target_pairs={{0,1},{1,0},{2,3},{3,2},{4,5},{5,4},{6,7},{7,6},{8,9},{9,8},{10,11... | collective-permute-start | bytes 3538952 | tf_op jit(solution)/shard_map/ppermute | solution.py:745
  306.4 27.9 %collective-permute-start.23 = (bf16[768,768]{1,0:T(8,128)(2,1)}, bf16[768,768]{1,0:T(8,128)(2,1)S(1)}, u32[]{:S(2)}, u32[]{:S(2)}) collective-permute-start(bf16[768,768]{1,0:T(8,128)(2,1)} %get-tuple-element.143), channel_id=1, source_target_pairs={{0,4},{4,0},{1,5},{5,1},{2,6},{6,2},{3,7},{7,3},{8,12},{12,8},{9,1... | collective-permute-start | bytes 3538952 | tf_op jit(solution)/shard_map/ppermute | solution.py:745
  341.5 33.3 %collective-permute-start.25 = (bf16[768,768]{1,0:T(8,128)(2,1)}, bf16[768,768]{1,0:T(8,128)(2,1)}, u32[]{:S(2)}, u32[]{:S(2)}) collective-permute-start(bf16[768,768]{1,0:T(8,128)(2,1)} %convert_element_type.215.g0), channel_id=1, source_target_pairs={{0,1},{1,0},{2,3},{3,2},{4,5},{5,4},{6,7},{7,6},{8,9},{9,8},{10,11... | collective-permute-start | bytes 3538952 | tf_op jit(solution)/shard_map/ppermute | solution.py:745
  347.8 25.5 %all-to-all-start = ((f32[32,5,24]{2,1,0:T(8,128)}), f32[32,5,24]{2,1,0:T(8,128)}, u32[]{:S(2)}, u32[]{:S(2)}) async-start(f32[32,5,24]{2,1,0:T(8,128)} %copy.65), calls=%async_computation.1 | async-start | bytes 262144 | tf_op jit(solution)/shard_map/all_to_all | solution.py:944
  352.0 108.9 %reduce-scatter.8.cloned.1.call-start = ((), (), s32[]{:S(2)}) async-start(), calls=%async_computation.9 | async-start | bytes 5898240 | tf_op jit(solution)/shard_map/reduce_scatter | solution.py:947
  374.8 106.6 %reduce-scatter.6.cloned.1.call-start = ((), (), s32[]{:S(2)}) async-start(), calls=%async_computation.8 | async-start | bytes 1966080 | tf_op jit(solution)/shard_map/reduce_scatter | solution.py:965
  374.9 3.3 collective-permute-start.26
  375.0 8.0 %collective-permute-start.27 = (bf16[768,768]{1,0:T(8,128)(2,1)}, bf16[768,768]{1,0:T(8,128)(2,1)}, u32[]{:S(2)}, u32[]{:S(2)}) collective-permute-start(bf16[768,768]{1,0:T(8,128)(2,1)} %convert_element_type.215.g0), channel_id=1, source_target_pairs={{0,4},{4,0},{1,5},{5,1},{2,6},{6,2},{3,7},{7,3},{8,12},{12,8},{9,1... | collective-permute-start | bytes 3538952 | tf_op jit(solution)/shard_map/ppermute | solution.py:745
  379.6 67.8 %collective-permute-start.30 = (bf16[4,96,768]{2,1,0:T(8,128)(2,1)S(1)}, bf16[4,96,768]{2,1,0:T(8,128)(2,1)S(1)}, u32[]{:S(2)}, u32[]{:S(2)}) collective-permute-start(bf16[4,96,768]{2,1,0:T(8,128)(2,1)S(1)} %get-tuple-element.188), channel_id=1, source_target_pairs={{2,4},{4,2},{3,5},{5,3},{10,12},{12,10},{11,13},{13,11},{18,20},{2... | collective-permute-start | bytes 1769480 | tf_op jit(solution)/shard_map/ppermute | solution.py:794
  380.3 67.1 %collective-permute-start.31 = (bf16[4,96,768]{2,1,0:T(8,128)(2,1)S(1)}, bf16[4,96,768]{2,1,0:T(8,128)(2,1)S(1)}, u32[]{:S(2)}, u32[]{:S(2)}) collective-permute-start(bf16[4,96,768]{2,1,0:T(8,128)(2,1)S(1)} %get-tuple-element.258), channel_id=1, source_target_pairs={{0,4},{2,0},{4,6},{6,2},{1,5},{3,1},{5,7},{7,3},{8,12},{10,8},{12,... | collective-permute-start | bytes 1769480 | tf_op jit(solution)/shard_map/ppermute | solution.py:793
  382.0 65.5 %collective-permute-start.29 = (bf16[768,768]{1,0:T(8,128)(2,1)S(1)}, bf16[768,768]{1,0:T(8,128)(2,1)S(1)}, u32[]{:S(2)}, u32[]{:S(2)}) collective-permute-start(bf16[768,768]{1,0:T(8,128)(2,1)S(1)} %copy-done.9), channel_id=1, source_target_pairs={{2,4},{4,2},{3,5},{5,3},{10,12},{12,10},{11,13},{13,11},{18,20},{2... | collective-permute-start | bytes 3538952 | tf_op jit(solution)/shard_map/ppermute | solution.py:950
  448.6 6.8 %collective-permute-start.32 = (bf16[768,768]{1,0:T(8,128)(2,1)}, bf16[768,768]{1,0:T(8,128)(2,1)}, u32[]{:S(2)}, u32[]{:S(2)}) collective-permute-start(bf16[768,768]{1,0:T(8,128)(2,1)} %get-tuple-element.166), channel_id=1, source_target_pairs={{0,4},{4,0},{1,5},{5,1},{2,6},{6,2},{3,7},{7,3},{8,12},{12,8},{9,1... | collective-permute-start | bytes 3538952 | tf_op jit(solution)/shard_map/ppermute | solution.py:745
  458.5 36.4 %collective-permute-start.33 = (bf16[768,768]{1,0:T(8,128)(2,1)}, bf16[768,768]{1,0:T(8,128)(2,1)}, u32[]{:S(2)}, u32[]{:S(2)}) collective-permute-start(bf16[768,768]{1,0:T(8,128)(2,1)} %add_convert_fusion), channel_id=1, source_target_pairs={{2,3},{3,2},{4,5},{5,4},{10,11},{11,10},{12,13},{13,12},{18,19},{1... | collective-permute-start | bytes 3538952 | tf_op jit(solution)/shard_map/ppermute | solution.py:750
  460.1 34.7 %collective-permute-start.28 = (bf16[768,768]{1,0:T(8,128)(2,1)}, bf16[768,768]{1,0:T(8,128)(2,1)}, u32[]{:S(2)}, u32[]{:S(2)}) collective-permute-start(bf16[768,768]{1,0:T(8,128)(2,1)} %get-tuple-element.163), channel_id=1, source_target_pairs={{0,4},{4,0},{1,5},{5,1},{2,6},{6,2},{3,7},{7,3},{8,12},{12,8},{9,1... | collective-permute-start | bytes 3538952 | tf_op jit(solution)/shard_map/ppermute | solution.py:745
  463.3 18.2 %collective-permute-start.34 = (bf16[4,96,768]{2,1,0:T(8,128)(2,1)}, bf16[4,96,768]{2,1,0:T(8,128)(2,1)}, u32[]{:S(2)}, u32[]{:S(2)}) collective-permute-start(bf16[4,96,768]{2,1,0:T(8,128)(2,1)} %get-tuple-element.185), channel_id=1, source_target_pairs={{2,4},{4,2},{3,5},{5,3},{10,12},{12,10},{11,13},{13,11},{18,20},{2... | collective-permute-start | bytes 1769480 | tf_op jit(solution)/shard_map/ppermute | solution.py:794
  464.8 30.1 %collective-permute-start.35 = (bf16[4,96,768]{2,1,0:T(8,128)(2,1)}, bf16[4,96,768]{2,1,0:T(8,128)(2,1)}, u32[]{:S(2)}, u32[]{:S(2)}) collective-permute-start(bf16[4,96,768]{2,1,0:T(8,128)(2,1)} %get-tuple-element.256), channel_id=1, source_target_pairs={{0,4},{2,0},{4,6},{6,2},{1,5},{3,1},{5,7},{7,3},{8,12},{10,8},{12,... | collective-permute-start | bytes 1769480 | tf_op jit(solution)/shard_map/ppermute | solution.py:793
  501.9 10.5 %collective-permute-start.38 = (bf16[4,96,192]{2,1,0:T(8,128)(2,1)S(1)}, bf16[4,96,192]{2,1,0:T(8,128)(2,1)S(1)}, u32[]{:S(2)}, u32[]{:S(2)}) collective-permute-start(bf16[4,96,192]{2,1,0:T(8,128)(2,1)S(1)} %get-tuple-element.261), channel_id=1, source_target_pairs={{2,4},{4,2},{3,5},{5,3},{10,12},{12,10},{11,13},{13,11},{18,20},{2... | collective-permute-start | bytes 442376 | tf_op jit(solution)/shard_map/ppermute | solution.py:794
  502.7 11.7 %collective-permute-start.39 = (bf16[4,96,192]{2,1,0:T(8,128)(2,1)S(1)}, bf16[4,96,192]{2,1,0:T(8,128)(2,1)S(1)}, u32[]{:S(2)}, u32[]{:S(2)}) collective-permute-start(bf16[4,96,192]{2,1,0:T(8,128)(2,1)S(1)} %get-tuple-element.262), channel_id=1, source_target_pairs={{0,4},{2,0},{4,6},{6,2},{1,5},{3,1},{5,7},{7,3},{8,12},{10,8},{12,... | collective-permute-start | bytes 442376 | tf_op jit(solution)/shard_map/ppermute | solution.py:793
  503.7 40.6 %collective-permute-start.36 = (bf16[768,768]{1,0:T(8,128)(2,1)}, bf16[768,768]{1,0:T(8,128)(2,1)}, u32[]{:S(2)}, u32[]{:S(2)}) collective-permute-start(bf16[768,768]{1,0:T(8,128)(2,1)} %add_convert_fusion), channel_id=1, source_target_pairs={{0,1},{1,0},{6,7},{7,6},{8,9},{9,8},{14,15},{15,14},{16,17},{17,16... | collective-permute-start | bytes 3538952 | tf_op jit(solution)/shard_map/ppermute | solution.py:750
  505.6 41.9 %collective-permute-start.37 = (bf16[768,768]{1,0:T(8,128)(2,1)}, bf16[768,768]{1,0:T(8,128)(2,1)}, u32[]{:S(2)}, u32[]{:S(2)}) collective-permute-start(bf16[768,768]{1,0:T(8,128)(2,1)} %fusion.14), channel_id=1, source_target_pairs={{2,4},{4,2},{3,5},{5,3},{10,12},{12,10},{11,13},{13,11},{18,20},{2... | collective-permute-start | bytes 3538952 | tf_op jit(solution)/shard_map/ppermute | solution.py:974
  516.3 22.4 %collective-permute-start.40 = (f32[48]{0:T(128)S(1)}, f32[48]{0:T(128)S(1)}, u32[]{:S(2)}, u32[]{:S(2)}) collective-permute-start(f32[48]{0:T(128)S(1)} %dynamic_slice.97), channel_id=1, source_target_pairs={{0,2},{2,0},{1,3},{3,1},{4,6},{6,4},{5,7},{7,5},{8,10},{10,8},{9,1... | collective-permute-start | bytes 584 | tf_op jit(solution)/shard_map/ppermute | solution.py:745
  539.4 3.6 collective-permute-start.41
  (68 other events, 1188.8 us)
Sparse Core Ops, SparseCore 0:
  56.5 30.0 all-gather.3
  132.9 40.0 all-gather.5
  174.9 38.9 all-gather.7
  305.8 57.2 reduce-scatter.3
  375.0 55.5 reduce-scatter.7
  452.8 28.5 reduce-scatter.5

commit v7 on v6

--- a/solution.py
+++ b/solution.py
@@ -963,8 +963,9 @@
 
     going = flip_some(one_far, False)
     weights_part = lax.psum_scatter(weights_part, high_bits, scatter_dimension=1, tiled=True)
-    going, one_far, weights_part, *up_home = tie(
-        going, one_far, weights_part, *send_home(up_rest, 1)
+    up_home = send_home(up_rest, 1)
+    going, one_far, weights_part, up_home[0], up_home[1] = tie(
+        going, one_far, weights_part, up_home[0], up_home[1]
     )
     going, one_far, weights_part, away_output, *homes = tie(
         finish(going), one_far, weights_part, away_output, *down_home, *up_home

time: 568 us -> 561 us (0.988)
  transfers between devices with their start and end apart: 49 -> 49, of which waited for: 21 -> 21; matrix products, arithmetic and copies ran while one was open for 18% -> 19% of each run, Pallas kernels for 32% -> 32%
where the time goes in v7:
time: 561 us; the launch traced here: 552 us
  Pallas kernels  193 us (34%)
  waiting for transfers between devices  157 us (28%)
  other arithmetic  73.9 us (13%)
  starting transfers between devices  61.1 us (11%)
  local copies, waits for them, and re-layouts  38.4 us (7%)
  between operations  15.6 us (3%)
  matrix products  13.9 us (2%)
    ppermute x28, waiting for transfers between devices, flip(): return lax.ppermute(value, axis, [(0, 1), (1, 0)])  107 us
    pallas_call x4, Pallas kernels, moe_call(): pl.pallas_call(kernel, grid_spec=pltpu.PrefetchScalarGridSpec(num_scalar_...  85.4 us
    pallas_call x1, Pallas kernels, attention_backward(): pl.pallas_call(backward_kernel, grid_spec=pltpu.PrefetchScalarGridSpec(nu...  64.4 us
    pallas_call x1, Pallas kernels, attention_forward(): pl.pallas_call(forward_kernel, grid_spec=pltpu.PrefetchScalarGridSpec(num...  42.9 us
    ppermute x28, starting transfers between devices, flip(): return lax.ppermute(value, axis, [(0, 1), (1, 0)])  35.7 us
    reduce_scatter x1, waiting for transfers between devices, body(): lax.psum_scatter(weights_part, high_bits, scatter_dimension=1, tiled=True)  13.5 us
    ppermute x4, waiting for transfers between devices, flip_some(): return lax.ppermute(value, ('c', 'zh', 'zl'), moves)  13.3 us
  transfers between devices with their start and end apart: 49, of which 21 were waited for; matrix products, arithmetic and copies ran while one was open for 19% of the time, Pallas kernels for 32%

profile of v7, /device:TPU:0, one launch (start us, length us, event | category | flops | bytes accessed | tf_op | source)
XLA Modules:
  0.0 552.3 jit_solution(10591736613798699242)
XLA Ops:
  11.9 3.6 collective-permute-start.1
  17.7 3.5 collective-permute-start.2
  35.2 13.2 %collective-permute-done.2 = bf16[768,768]{1,0:T(8,128)(2,1)} collective-permute-done((bf16[768,768]{1,0:T(8,128)(2,1)}, bf16[768,768]{1,0:T(8,128)(2,1)}, u32[]{:S(2)}, u32[]{:S(2)}) %collective-permute-start.2) | collective-permute-done | bytes 1179680 | tf_op jit(solution)/shard_map/ppermute | solution.py:750
  49.5 3.2 convert_reduce_fusion.1
  52.6 2.0 broadcast_select_fusion.4
  60.3 3.1 collective-permute-start.4
  63.4 2.4 broadcast_select_fusion.3.x2
  65.8 10.7 %collective-permute-start.6 = (bf16[768,768]{1,0:T(8,128)(2,1)}, bf16[768,768]{1,0:T(8,128)(2,1)}, u32[]{:S(2)}, u32[]{:S(2)}) collective-permute-start(bf16[768,768]{1,0:T(8,128)(2,1)} %broadcast_select_fusion.3.x2), channel_id=1, source_target_pairs={{0,4},{4,0},{1,5},{5,1},{2,6},{6,2},{3,7},{7,3},{8,12},{12,8},{9,1... | collective-permute-start | bytes 3538952 | tf_op jit(solution)/shard_map/ppermute | solution.py:745
  77.1 3.4 collective-permute-start.7
  80.5 6.0 %all-gather.4.cloned.1.call-done = bf16[3072,192]{1,0:T(8,128)(2,1)} async-done(((bf16[384,192]{1,0:T(8,128)(2,1)}), bf16[3072,192]{1,0:T(8,128)(2,1)}) %all-gather.4.cloned.1.call-update) | async-done | bytes 1179664 | tf_op jit(solution)/shard_map/all_gather | solution.py:809
  88.1 42.9 %attention_forward.1 = (bf16[768,768]{1,0:T(8,128)(2,1)}, bf16[768,768]{1,0:T(8,128)(2,1)}, bf16[768,768]{1,0:T(8,128)(2,1)}, bf16[768,768]{1,0:T(8,128)(2,1)}, ...) custom-call(s32[5,6]{1,0:T(8,128)} %stack.33.ranges, ...), custom_call_target="tpu_custom_call" | custom-call | flops 28991029248 | bytes 41943040 | tf_op jit(solution)/shard_map/attention_forward/pallas_call | solution.py:215
  141.5 2.2 collective-permute-start.10
  153.4 2.6 convert_reduce_fusion
  157.1 13.2 %collective-permute-done.10 = bf16[768,768]{1,0:T(8,128)(2,1)S(1)} collective-permute-done((bf16[768,768]{1,0:T(8,128)(2,1)S(1)}, bf16[768,768]{1,0:T(8,128)(2,1)S(1)}, u32[]{:S(2)}, u32[]{:S(2)}) %collective-permute-start.10) | collective-permute-done | bytes 1179680 | tf_op jit(solution)/shard_map/ppermute | solution.py:745
  171.3 3.9 fusion.57
  175.9 2.3 fusion.27
  182.9 2.3 convolution_convert_fusion.d0.a0
  185.2 33.7 %collective-permute-done.12.x2.a2 = bf16[768,768]{1,0:T(8,128)(2,1)S(1)} collective-permute-done((bf16[768,768]{1,0:T(8,128)(2,1)S(1)}, bf16[768,768]{1,0:T(8,128)(2,1)S(1)}, u32[]{:S(2)}, u32[]{:S(2)}) %collective-permute-start.12) | collective-permute-done | bytes 1179680 | tf_op jit(solution)/shard_map/ppermute | solution.py:745
  221.9 28.8 %moe_forward.1 = (bf16[768,768]{1,0:T(8,128)(2,1)}, bf16[768,768]{1,0:T(8,128)(2,1)}, bf16[768,768]{1,0:T(8,128)(2,1)}, bf16[768,768]{1,0:T(8,128)(2,1)}, bf16[4...) custom-call(s32[33]{0:T(128)} %concatenate.15.table, bf16[768,768]{1,0:T(8,128)(2,1)} %copy-done.60, ...), custom_call_target="tpu_custom_call" | custom-call | flops 9059696640 | bytes 41943040 | tf_op jit(solution)/shard_map/moe_forward/pallas_call | solution.py:672
  251.3 2.5 collective-permute-done.18
  258.2 24.4 %moe_backward.1 = (bf16[768,768]{1,0:T(8,128)(2,1)}, bf16[768,768]{1,0:T(8,128)(2,1)}, bf16[768,768]{1,0:T(8,128)(2,1)}, bf16[768,768]{1,0:T(8,128)(2,1)}, bf16[4,1024,768]{2,1,0:T(8,128)(2,1)}) custom-call(s32[33]{0:T(128)} %concatenate.15.table, bf16[768,768]{1,0:T(8,128)(2,1)} %convolution_convert_fusion.d0.a0, bf16[768,768]{1,0:T(8,128)(2,1)} %copy-done.65, ...), custom_call_target="tpu_custom_call" | custom-call | flops 9059696640 | bytes 41943040 | tf_op jit(solution)/shard_map/moe_backward/pallas_call | solution.py:672
  283.5 3.1 collective-permute-done.21
  286.6 2.7 add_convert_fusion.4
  289.2 16.1 %moe_weights.2 = (bf16[4,768,768]{2,1,0:T(8,128)(2,1)}, bf16[16,128]{1,0:T(8,128)(2,1)}) custom-call(s32[33]{0:T(128)} %concatenate.15.table, bf16[768,768]{1,0:T(8,128)(2,1)} %convolution_convert_fusion.d0.a0, bf16[768,768]{1,0:T(8,128)(2,1)} %copy-done.65, bf16[768,768]{1,0:T(8,128)(2,1)} %collective-permute-done.15.d2.a2, bf16[768,768]{1,0:T(8,128)(2,1)} %copy-done.64, ...), custom_call_target="tpu_custom_call" | custom-call | flops 4529848320 | bytes 41943040 | tf_op jit(solution)/shard_map/moe_weights/pallas_call | solution.py:672
  306.2 2.3 collective-permute-done.22
  308.5 3.7 fusion.30
  312.2 21.8 %collective-permute-done.24 = bf16[768,768]{1,0:T(8,128)(2,1)S(1)} collective-permute-done((bf16[768,768]{1,0:T(8,128)(2,1)}, bf16[768,768]{1,0:T(8,128)(2,1)S(1)}, u32[]{:S(2)}, u32[]{:S(2)}) %collective-permute-start.24) | collective-permute-done | bytes 1179680 | tf_op jit(solution)/shard_map/ppermute | solution.py:745
  334.1 2.6 multiply_reduce_fusion
  336.7 3.3 convert_add_fusion
  341.7 2.0 fusion.28
  347.5 4.6 all-to-all-start
  352.1 16.2 %moe_weights.3 = (bf16[4,768,768]{2,1,0:T(8,128)(2,1)}, bf16[16,128]{1,0:T(8,128)(2,1)}) custom-call(s32[33]{0:T(128)} %concatenate.15.table, bf16[768,768]{1,0:T(8,128)(2,1)} %copy-done.60, bf16[768,768]{1,0:T(8,128)(2,1)} %copy-done.62, bf16[768,768]{1,0:T(8,128)(2,1)} %copy-done.61, bf16[768,768]{1,0:T(8,128)(2,1)} %collective-permute-done.17.x3.a3, ...), custom_call_target="tpu_custom_call" | custom-call | flops 4529848320 | bytes 41943040 | tf_op jit(solution)/shard_map/moe_weights/pallas_call | solution.py:672
  368.3 5.0 all-to-all-done
  375.5 2.7 collective-permute-done.26.g3
  383.0 64.4 %attention_backward.1 = (bf16[768,768]{1,0:T(8,128)(2,1)}, bf16[768,768]{1,0:T(8,128)(2,1)}, bf16[768,768]{1,0:T(8,128)(2,1)}, bf16[768,768]{1,0:T(8,128)(2,1)}, bf16[4,768,192]{2,1,0:T(8,128)(2,1)}) custom-call(s32[5,6]{1,0:T(8,128)} %stack.39.ranges, s32[4]{0:T(128)} %pad_add_fusion.1.ranks, bf16[768,768]{1,0:T(8,128)(2,1)} %convert_element_type.215.g0, ...), custom_call_target="tpu_custom_call" | custom-call | flops 65229815808 | bytes 41943040 | tf_op jit(solution)/shard_map/attention_backward/pallas_call | solution.py:389
  448.7 4.0 collective-permute-start.32
  452.7 2.8 collective-permute-done.32
  455.5 2.9 add_convert_fusion
  460.9 2.4 constant_dynamic-slice_fusion.2
  468.1 13.5 %reduce-scatter.6.cloned.1.call-done = bf16[4,192,192]{2,1,0:T(8,128)(2,1)} async-done(((bf16[4,768,192]{2,1,0:T(8,128)(2,1)}), bf16[4,192,192]{2,1,0:T(8,128)(2,1)}) %reduce-scatter.6.cloned.1.call-update) | async-done | bytes 294928 | tf_op jit(solution)/shard_map/reduce_scatter | solution.py:965
  481.7 3.2 fusion.39
  485.0 3.6 fusion.14
  488.6 6.3 %collective-permute-done.35 = bf16[4,96,768]{2,1,0:T(8,128)(2,1)} collective-permute-done((bf16[4,96,768]{2,1,0:T(8,128)(2,1)}, bf16[4,96,768]{2,1,0:T(8,128)(2,1)}, u32[]{:S(2)}, u32[]{:S(2)}) %collective-permute-start.35) | collective-permute-done | bytes 589856 | tf_op jit(solution)/shard_map/ppermute | solution.py:793
  503.8 2.4 convert_add_fusion.3
  506.2 4.4 collective-permute-done.39
  513.2 19.0 %collective-permute-done.40 = f32[48]{0:T(128)S(1)} collective-permute-done((f32[48]{0:T(128)S(1)}, f32[48]{0:T(128)S(1)}, u32[]{:S(2)}, u32[]{:S(2)}) %collective-permute-start.40) | collective-permute-done | bytes 224 | tf_op jit(solution)/shard_map/ppermute | solution.py:745
  537.7 3.2 fusion.40
  541.0 3.9 fusion.36
  (305 shorter events, 104.9 us)
Async XLA Ops:
  7.2 79.3 %all-gather.4.cloned.1.call-start = ((), (), s32[]{:S(2)}) async-start(), calls=%async_computation.4 | async-start | bytes 1769472 | tf_op jit(solution)/shard_map/all_gather | solution.py:809
  8.7 14.2 %collective-permute-start.3 = (s32[3,3072]{1,0:T(4,128)}, s32[3,3072]{1,0:T(4,128)}, u32[]{:S(2)}, u32[]{:S(2)}) collective-permute-start(s32[3,3072]{1,0:T(4,128)} %pad_add_fusion), channel_id=1, source_target_pairs={{0,4},{4,0},{1,5},{5,1},{2,6},{6,2},{3,7},{7,3},{8,12},{12,8},{9,1... | collective-permute-start | bytes 110600 | tf_op jit(solution)/shard_map/ppermute | solution.py:745
  11.9 23.3 %collective-permute-start.1 = (bf16[384,192]{1,0:T(8,128)(2,1)}, bf16[384,192]{1,0:T(8,128)(2,1)}, u32[]{:S(2)}, u32[]{:S(2)}) collective-permute-start(bf16[384,192]{1,0:T(8,128)(2,1)} %constant_dynamic-slice_fusion.18), channel_id=1, source_target_pairs={{0,2},{2,0},{1,3},{3,1},{4,6},{6,4},{5,7},{7,5},{8,10},{10,8},{9,1... | collective-permute-start | bytes 442376 | tf_op jit(solution)/shard_map/ppermute | solution.py:745
  17.7 30.8 %collective-permute-start.2 = (bf16[768,768]{1,0:T(8,128)(2,1)}, bf16[768,768]{1,0:T(8,128)(2,1)}, u32[]{:S(2)}, u32[]{:S(2)}) collective-permute-start(bf16[768,768]{1,0:T(8,128)(2,1)} %fusion.26), channel_id=1, source_target_pairs={{0,1},{1,0},{6,7},{7,6},{8,9},{9,8},{14,15},{15,14},{16,17},{17,16... | collective-permute-start | bytes 3538952 | tf_op jit(solution)/shard_map/ppermute | solution.py:750
  21.2 27.3 %collective-permute-start = (bf16[768,768]{1,0:T(8,128)(2,1)S(1)}, bf16[768,768]{1,0:T(8,128)(2,1)S(1)}, u32[]{:S(2)}, u32[]{:S(2)}) collective-permute-start(bf16[768,768]{1,0:T(8,128)(2,1)S(1)} %bitcast.89), channel_id=1, source_target_pairs={{2,4},{4,2},{3,5},{5,3},{10,12},{12,10},{11,13},{13,11},{18,20},{2... | collective-permute-start | bytes 3538952 | tf_op jit(solution)/shard_map/ppermute | solution.py:847
  54.6 8.8 %collective-permute-start.5 = (bf16[768,768]{1,0:T(8,128)(2,1)}, bf16[768,768]{1,0:T(8,128)(2,1)}, u32[]{:S(2)}, u32[]{:S(2)}) collective-permute-start(bf16[768,768]{1,0:T(8,128)(2,1)} %get-tuple-element.250), channel_id=1, source_target_pairs={{2,3},{3,2},{4,5},{5,4},{10,11},{11,10},{12,13},{13,12},{18,19},{1... | collective-permute-start | bytes 3538952 | tf_op jit(solution)/shard_map/ppermute | solution.py:750
  56.3 165.5 %all-gather.6.cloned.1.call-start = ((), (), s32[]{:S(2)}) async-start(), calls=%async_computation.5 | async-start | bytes 5308416 | tf_op jit(solution)/shard_map/all_gather | solution.py:809
  60.3 27.8 %collective-permute-start.4 = (bf16[768,768]{1,0:T(8,128)(2,1)}, bf16[768,768]{1,0:T(8,128)(2,1)}, u32[]{:S(2)}, u32[]{:S(2)}) collective-permute-start(bf16[768,768]{1,0:T(8,128)(2,1)} %get-tuple-element.249.x0), channel_id=1, source_target_pairs={{0,4},{4,0},{1,5},{5,1},{2,6},{6,2},{3,7},{7,3},{8,12},{12,8},{9,1... | collective-permute-start | bytes 3538952 | tf_op jit(solution)/shard_map/ppermute | solution.py:745
  65.8 22.2 %collective-permute-start.6 = (bf16[768,768]{1,0:T(8,128)(2,1)}, bf16[768,768]{1,0:T(8,128)(2,1)}, u32[]{:S(2)}, u32[]{:S(2)}) collective-permute-start(bf16[768,768]{1,0:T(8,128)(2,1)} %broadcast_select_fusion.3.x2), channel_id=1, source_target_pairs={{0,4},{4,0},{1,5},{5,1},{2,6},{6,2},{3,7},{7,3},{8,12},{12,8},{9,1... | collective-permute-start | bytes 3538952 | tf_op jit(solution)/shard_map/ppermute | solution.py:745
  77.1 53.8 %collective-permute-start.7 = (bf16[384,768]{1,0:T(8,128)(2,1)}, bf16[384,768]{1,0:T(8,128)(2,1)S(1)}, u32[]{:S(2)}, u32[]{:S(2)}) collective-permute-start(bf16[384,768]{1,0:T(8,128)(2,1)} %constant_dynamic-slice_fusion.17), channel_id=1, source_target_pairs={{0,2},{2,0},{1,3},{3,1},{4,6},{6,4},{5,7},{7,5},{8,10},{10,8},{9,1... | collective-permute-start | bytes 1769480 | tf_op jit(solution)/shard_map/ppermute | solution.py:745
  80.5 52.2 %collective-permute-start.8 = (bf16[384,768]{1,0:T(8,128)(2,1)}, bf16[384,768]{1,0:T(8,128)(2,1)}, u32[]{:S(2)}, u32[]{:S(2)}) collective-permute-start(bf16[384,768]{1,0:T(8,128)(2,1)} %constant_dynamic-slice_fusion.16), channel_id=1, source_target_pairs={{0,2},{2,0},{1,3},{3,1},{4,6},{6,4},{5,7},{7,5},{8,10},{10,8},{9,1... | collective-permute-start | bytes 1769480 | tf_op jit(solution)/shard_map/ppermute | solution.py:745
  132.7 89.1 %all-gather.8.cloned.1.call-start = ((), (), s32[]{:S(2)}) async-start(), calls=%async_computation.6 | async-start | bytes 5308416 | tf_op jit(solution)/shard_map/all_gather | solution.py:809
  133.5 244.7 %reduce-scatter.4.cloned.1.call-start = ((), (), s32[]{:S(2)}) async-start(), calls=%async_computation.7 | async-start | bytes 5898240 | tf_op jit(solution)/shard_map/reduce_scatter | solution.py:927
  133.7 6.1 %collective-permute-start.9 = (bf16[768,768]{1,0:T(8,128)(2,1)}, bf16[768,768]{1,0:T(8,128)(2,1)S(1)}, u32[]{:S(2)}, u32[]{:S(2)}) collective-permute-start(bf16[768,768]{1,0:T(8,128)(2,1)} %get-tuple-element.108), channel_id=1, source_target_pairs={{0,4},{4,0},{1,5},{5,1},{2,6},{6,2},{3,7},{7,3},{8,12},{12,8},{9,1... | collective-permute-start | bytes 3538952 | tf_op jit(solution)/shard_map/ppermute | solution.py:745
  135.9 35.1 %collective-permute-start.11 = (bf16[768,768]{1,0:T(8,128)(2,1)}, bf16[768,768]{1,0:T(8,128)(2,1)}, u32[]{:S(2)}, u32[]{:S(2)}) collective-permute-start(bf16[768,768]{1,0:T(8,128)(2,1)} %get-tuple-element.114), channel_id=1, source_target_pairs={{0,4},{4,0},{1,5},{5,1},{2,6},{6,2},{3,7},{7,3},{8,12},{12,8},{9,1... | collective-permute-start | bytes 3538952 | tf_op jit(solution)/shard_map/ppermute | solution.py:745
  141.5 28.8 %collective-permute-start.10 = (bf16[768,768]{1,0:T(8,128)(2,1)S(1)}, bf16[768,768]{1,0:T(8,128)(2,1)S(1)}, u32[]{:S(2)}, u32[]{:S(2)}) collective-permute-start(bf16[768,768]{1,0:T(8,128)(2,1)S(1)} %add_convert_fusion.6), channel_id=1, source_target_pairs={{0,1},{1,0},{2,3},{3,2},{4,5},{5,4},{6,7},{7,6},{8,9},{9,8},{10,11... | collective-permute-start | bytes 3538952 | tf_op jit(solution)/shard_map/ppermute | solution.py:745
  170.3 12.4 %collective-permute-start.13 = (bf16[768,768]{1,0:T(8,128)(2,1)}, bf16[768,768]{1,0:T(8,128)(2,1)S(1)}, u32[]{:S(2)}, u32[]{:S(2)}) collective-permute-start(bf16[768,768]{1,0:T(8,128)(2,1)} %bitcast.94), channel_id=1, source_target_pairs={{2,4},{4,2},{3,5},{5,3},{10,12},{12,10},{11,13},{13,11},{18,20},{2... | collective-permute-start | bytes 3538952 | tf_op jit(solution)/shard_map/ppermute | solution.py:892
  179.3 39.6 %collective-permute-start.12 = (bf16[768,768]{1,0:T(8,128)(2,1)S(1)}, bf16[768,768]{1,0:T(8,128)(2,1)S(1)}, u32[]{:S(2)}, u32[]{:S(2)}) collective-permute-start(bf16[768,768]{1,0:T(8,128)(2,1)S(1)} %convolution_convert_fusion.1.x0.a0), channel_id=1, source_target_pairs={{0,1},{1,0},{2,3},{3,2},{4,5},{5,4},{6,7},{7,6},{8,9},{9,8},{10,11... | collective-permute-start | bytes 3538952 | tf_op jit(solution)/shard_map/ppermute | solution.py:745
  181.1 38.1 %collective-permute-start.16 = (bf16[768,768]{1,0:T(8,128)(2,1)S(1)}, bf16[768,768]{1,0:T(8,128)(2,1)S(1)}, u32[]{:S(2)}, u32[]{:S(2)}) collective-permute-start(bf16[768,768]{1,0:T(8,128)(2,1)S(1)} %convolution_convert_fusion.1.x0.a0), channel_id=1, source_target_pairs={{0,4},{4,0},{1,5},{5,1},{2,6},{6,2},{3,7},{7,3},{8,12},{12,8},{9,1... | collective-permute-start | bytes 3538952 | tf_op jit(solution)/shard_map/ppermute | solution.py:745
  219.2 31.5 %collective-permute-start.15 = (bf16[768,768]{1,0:T(8,128)(2,1)}, bf16[768,768]{1,0:T(8,128)(2,1)}, u32[]{:S(2)}, u32[]{:S(2)}) collective-permute-start(bf16[768,768]{1,0:T(8,128)(2,1)} %convolution_convert_fusion.d0.a0), channel_id=1, source_target_pairs={{0,1},{1,0},{2,3},{3,2},{4,5},{5,4},{6,7},{7,6},{8,9},{9,8},{10,11... | collective-permute-start | bytes 3538952 | tf_op jit(solution)/shard_map/ppermute | solution.py:745
  250.7 3.1 collective-permute-start.18
  250.8 4.7 collective-permute-start.19
  251.3 5.9 %collective-permute-start.14 = (bf16[768,768]{1,0:T(8,128)(2,1)}, bf16[768,768]{1,0:T(8,128)(2,1)S(1)}, u32[]{:S(2)}, u32[]{:S(2)}) collective-permute-start(bf16[768,768]{1,0:T(8,128)(2,1)} %convolution_convert_fusion.d0.a0), channel_id=1, source_target_pairs={{0,4},{4,0},{1,5},{5,1},{2,6},{6,2},{3,7},{7,3},{8,12},{12,8},{9,1... | collective-permute-start | bytes 3538952 | tf_op jit(solution)/shard_map/ppermute | solution.py:745
  255.5 28.0 %collective-permute-start.20 = (bf16[768,768]{1,0:T(8,128)(2,1)S(1)}, bf16[768,768]{1,0:T(8,128)(2,1)S(1)}, u32[]{:S(2)}, u32[]{:S(2)}) collective-permute-start(bf16[768,768]{1,0:T(8,128)(2,1)S(1)} %add_convert_fusion.5), channel_id=1, source_target_pairs={{0,1},{1,0},{2,3},{3,2},{4,5},{5,4},{6,7},{7,6},{8,9},{9,8},{10,11... | collective-permute-start | bytes 3538952 | tf_op jit(solution)/shard_map/ppermute | solution.py:745
  283.5 3.1 collective-permute-start.21
  305.4 3.1 collective-permute-start.22
  305.6 28.4 %collective-permute-start.24 = (bf16[768,768]{1,0:T(8,128)(2,1)}, bf16[768,768]{1,0:T(8,128)(2,1)S(1)}, u32[]{:S(2)}, u32[]{:S(2)}) collective-permute-start(bf16[768,768]{1,0:T(8,128)(2,1)} %add_convert_fusion.4), channel_id=1, source_target_pairs={{0,1},{1,0},{2,3},{3,2},{4,5},{5,4},{6,7},{7,6},{8,9},{9,8},{10,11... | collective-permute-start | bytes 3538952 | tf_op jit(solution)/shard_map/ppermute | solution.py:745
  306.0 28.0 %collective-permute-start.23 = (bf16[768,768]{1,0:T(8,128)(2,1)}, bf16[768,768]{1,0:T(8,128)(2,1)S(1)}, u32[]{:S(2)}, u32[]{:S(2)}) collective-permute-start(bf16[768,768]{1,0:T(8,128)(2,1)} %get-tuple-element.142), channel_id=1, source_target_pairs={{0,4},{4,0},{1,5},{5,1},{2,6},{6,2},{3,7},{7,3},{8,12},{12,8},{9,1... | collective-permute-start | bytes 3538952 | tf_op jit(solution)/shard_map/ppermute | solution.py:745
  341.2 33.7 %collective-permute-start.25 = (bf16[768,768]{1,0:T(8,128)(2,1)}, bf16[768,768]{1,0:T(8,128)(2,1)}, u32[]{:S(2)}, u32[]{:S(2)}) collective-permute-start(bf16[768,768]{1,0:T(8,128)(2,1)} %convert_element_type.215.g0), channel_id=1, source_target_pairs={{0,1},{1,0},{2,3},{3,2},{4,5},{5,4},{6,7},{7,6},{8,9},{9,8},{10,11... | collective-permute-start | bytes 3538952 | tf_op jit(solution)/shard_map/ppermute | solution.py:745
  347.5 25.9 %all-to-all-start = ((f32[32,5,24]{2,1,0:T(8,128)}), f32[32,5,24]{2,1,0:T(8,128)}, u32[]{:S(2)}, u32[]{:S(2)}) async-start(f32[32,5,24]{2,1,0:T(8,128)} %copy.65), calls=%async_computation.1 | async-start | bytes 262144 | tf_op jit(solution)/shard_map/all_to_all | solution.py:944
  352.0 108.8 %reduce-scatter.8.cloned.1.call-start = ((), (), s32[]{:S(2)}) async-start(), calls=%async_computation.9 | async-start | bytes 5898240 | tf_op jit(solution)/shard_map/reduce_scatter | solution.py:947
  374.9 106.7 %reduce-scatter.6.cloned.1.call-start = ((), (), s32[]{:S(2)}) async-start(), calls=%async_computation.8 | async-start | bytes 1966080 | tf_op jit(solution)/shard_map/reduce_scatter | solution.py:965
  374.9 3.3 collective-permute-start.26
  375.0 8.0 %collective-permute-start.27 = (bf16[768,768]{1,0:T(8,128)(2,1)}, bf16[768,768]{1,0:T(8,128)(2,1)}, u32[]{:S(2)}, u32[]{:S(2)}) collective-permute-start(bf16[768,768]{1,0:T(8,128)(2,1)} %convert_element_type.215.g0), channel_id=1, source_target_pairs={{0,4},{4,0},{1,5},{5,1},{2,6},{6,2},{3,7},{7,3},{8,12},{12,8},{9,1... | collective-permute-start | bytes 3538952 | tf_op jit(solution)/shard_map/ppermute | solution.py:745
  379.6 67.9 %collective-permute-start.30 = (bf16[4,96,768]{2,1,0:T(8,128)(2,1)S(1)}, bf16[4,96,768]{2,1,0:T(8,128)(2,1)S(1)}, u32[]{:S(2)}, u32[]{:S(2)}) collective-permute-start(bf16[4,96,768]{2,1,0:T(8,128)(2,1)S(1)} %get-tuple-element.186), channel_id=1, source_target_pairs={{2,4},{4,2},{3,5},{5,3},{10,12},{12,10},{11,13},{13,11},{18,20},{2... | collective-permute-start | bytes 1769480 | tf_op jit(solution)/shard_map/ppermute | solution.py:794
  380.3 67.2 %collective-permute-start.31 = (bf16[4,96,768]{2,1,0:T(8,128)(2,1)S(1)}, bf16[4,96,768]{2,1,0:T(8,128)(2,1)S(1)}, u32[]{:S(2)}, u32[]{:S(2)}) collective-permute-start(bf16[4,96,768]{2,1,0:T(8,128)(2,1)S(1)} %get-tuple-element.256), channel_id=1, source_target_pairs={{0,4},{2,0},{4,6},{6,2},{1,5},{3,1},{5,7},{7,3},{8,12},{10,8},{12,... | collective-permute-start | bytes 1769480 | tf_op jit(solution)/shard_map/ppermute | solution.py:793
  382.1 65.5 %collective-permute-start.29 = (bf16[768,768]{1,0:T(8,128)(2,1)S(1)}, bf16[768,768]{1,0:T(8,128)(2,1)S(1)}, u32[]{:S(2)}, u32[]{:S(2)}) collective-permute-start(bf16[768,768]{1,0:T(8,128)(2,1)S(1)} %copy-done.9), channel_id=1, source_target_pairs={{2,4},{4,2},{3,5},{5,3},{10,12},{12,10},{11,13},{13,11},{18,20},{2... | collective-permute-start | bytes 3538952 | tf_op jit(solution)/shard_map/ppermute | solution.py:950
  448.7 6.8 %collective-permute-start.32 = (bf16[768,768]{1,0:T(8,128)(2,1)}, bf16[768,768]{1,0:T(8,128)(2,1)}, u32[]{:S(2)}, u32[]{:S(2)}) collective-permute-start(bf16[768,768]{1,0:T(8,128)(2,1)} %get-tuple-element.165), channel_id=1, source_target_pairs={{0,4},{4,0},{1,5},{5,1},{2,6},{6,2},{3,7},{7,3},{8,12},{12,8},{9,1... | collective-permute-start | bytes 3538952 | tf_op jit(solution)/shard_map/ppermute | solution.py:745
  458.5 23.1 %collective-permute-start.33 = (bf16[768,768]{1,0:T(8,128)(2,1)}, bf16[768,768]{1,0:T(8,128)(2,1)}, u32[]{:S(2)}, u32[]{:S(2)}) collective-permute-start(bf16[768,768]{1,0:T(8,128)(2,1)} %add_convert_fusion), channel_id=1, source_target_pairs={{2,3},{3,2},{4,5},{5,4},{10,11},{11,10},{12,13},{13,12},{18,19},{1... | collective-permute-start | bytes 3538952 | tf_op jit(solution)/shard_map/ppermute | solution.py:750
  460.1 21.5 %collective-permute-start.28 = (bf16[768,768]{1,0:T(8,128)(2,1)}, bf16[768,768]{1,0:T(8,128)(2,1)}, u32[]{:S(2)}, u32[]{:S(2)}) collective-permute-start(bf16[768,768]{1,0:T(8,128)(2,1)} %get-tuple-element.162), channel_id=1, source_target_pairs={{0,4},{4,0},{1,5},{5,1},{2,6},{6,2},{3,7},{7,3},{8,12},{12,8},{9,1... | collective-permute-start | bytes 3538952 | tf_op jit(solution)/shard_map/ppermute | solution.py:745
  463.2 18.4 %collective-permute-start.34 = (bf16[4,96,768]{2,1,0:T(8,128)(2,1)}, bf16[4,96,768]{2,1,0:T(8,128)(2,1)}, u32[]{:S(2)}, u32[]{:S(2)}) collective-permute-start(bf16[4,96,768]{2,1,0:T(8,128)(2,1)} %get-tuple-element.183), channel_id=1, source_target_pairs={{2,4},{4,2},{3,5},{5,3},{10,12},{12,10},{11,13},{13,11},{18,20},{2... | collective-permute-start | bytes 1769480 | tf_op jit(solution)/shard_map/ppermute | solution.py:794
  467.2 27.7 %collective-permute-start.35 = (bf16[4,96,768]{2,1,0:T(8,128)(2,1)}, bf16[4,96,768]{2,1,0:T(8,128)(2,1)}, u32[]{:S(2)}, u32[]{:S(2)}) collective-permute-start(bf16[4,96,768]{2,1,0:T(8,128)(2,1)} %get-tuple-element.253), channel_id=1, source_target_pairs={{0,4},{2,0},{4,6},{6,2},{1,5},{3,1},{5,7},{7,3},{8,12},{10,8},{12,... | collective-permute-start | bytes 1769480 | tf_op jit(solution)/shard_map/ppermute | solution.py:793
  494.9 11.3 %collective-permute-start.38 = (bf16[4,96,192]{2,1,0:T(8,128)(2,1)S(1)}, bf16[4,96,192]{2,1,0:T(8,128)(2,1)S(1)}, u32[]{:S(2)}, u32[]{:S(2)}) collective-permute-start(bf16[4,96,192]{2,1,0:T(8,128)(2,1)S(1)} %get-tuple-element.259), channel_id=1, source_target_pairs={{2,4},{4,2},{3,5},{5,3},{10,12},{12,10},{11,13},{13,11},{18,20},{2... | collective-permute-start | bytes 442376 | tf_op jit(solution)/shard_map/ppermute | solution.py:794
  495.6 15.0 %collective-permute-start.39 = (bf16[4,96,192]{2,1,0:T(8,128)(2,1)S(1)}, bf16[4,96,192]{2,1,0:T(8,128)(2,1)S(1)}, u32[]{:S(2)}, u32[]{:S(2)}) collective-permute-start(bf16[4,96,192]{2,1,0:T(8,128)(2,1)S(1)} %get-tuple-element.260), channel_id=1, source_target_pairs={{0,4},{2,0},{4,6},{6,2},{1,5},{3,1},{5,7},{7,3},{8,12},{10,8},{12,... | collective-permute-start | bytes 442376 | tf_op jit(solution)/shard_map/ppermute | solution.py:793
  497.5 40.2 %collective-permute-start.36 = (bf16[768,768]{1,0:T(8,128)(2,1)}, bf16[768,768]{1,0:T(8,128)(2,1)}, u32[]{:S(2)}, u32[]{:S(2)}) collective-permute-start(bf16[768,768]{1,0:T(8,128)(2,1)} %add_convert_fusion), channel_id=1, source_target_pairs={{0,1},{1,0},{6,7},{7,6},{8,9},{9,8},{14,15},{15,14},{16,17},{17,16... | collective-permute-start | bytes 3538952 | tf_op jit(solution)/shard_map/ppermute | solution.py:750
  499.4 41.5 %collective-permute-start.37 = (bf16[768,768]{1,0:T(8,128)(2,1)}, bf16[768,768]{1,0:T(8,128)(2,1)}, u32[]{:S(2)}, u32[]{:S(2)}) collective-permute-start(bf16[768,768]{1,0:T(8,128)(2,1)} %fusion.14), channel_id=1, source_target_pairs={{2,4},{4,2},{3,5},{5,3},{10,12},{12,10},{11,13},{13,11},{18,20},{2... | collective-permute-start | bytes 3538952 | tf_op jit(solution)/shard_map/ppermute | solution.py:975
  512.5 19.6 %collective-permute-start.40 = (f32[48]{0:T(128)S(1)}, f32[48]{0:T(128)S(1)}, u32[]{:S(2)}, u32[]{:S(2)}) collective-permute-start(f32[48]{0:T(128)S(1)} %dynamic_slice.97), channel_id=1, source_target_pairs={{0,2},{2,0},{1,3},{3,1},{4,6},{6,4},{5,7},{7,5},{8,10},{10,8},{9,1... | collective-permute-start | bytes 584 | tf_op jit(solution)/shard_map/ppermute | solution.py:745
  532.8 3.6 collective-permute-start.41
  (68 other events, 1206.5 us)
Sparse Core Ops, SparseCore 0:
  56.5 30.0 all-gather.3
  132.9 40.0 all-gather.5
  174.9 38.9 all-gather.7
  305.5 57.5 reduce-scatter.3
  375.0 55.4 reduce-scatter.7
  452.9 28.7 reduce-scatter.5

commit v8 on v7

--- a/solution.py
+++ b/solution.py
@@ -974,7 +974,6 @@
     block_output = jnp.where(home, mixed_two, away_output)[None]
     going = lax.ppermute(going, ("c", "zh"), [(1, 2), (2, 1)])
     kept_far = flip_some(one_far, True)
-    input_grad = jnp.where(home, finish(kept_far), going)[None]
     down_summed = jnp.swapaxes(sum_home(*down_home), 1, 2)
     up_summed = sum_home(*up_home)
     weights_part = sum_home(*send_home(weights_part, 1))
@@ -987,6 +986,8 @@
         qkv_weight, lax.axis_index(users) * slice_rows, slice_rows, 1
     )
     gain_one = jnp.sum(own_rows.astype(jnp.float32) * qkv_summed, axis=(0, 2))
+    gain_one, kept_rows = tie(gain_one, finish(kept_far))
+    input_grad = jnp.where(home, kept_rows, going)[None]
     for bit in ("zh", "zl"):
         gain_one = halve(*send_half(gain_one, bit, 0))
     gain_one_sum = gain_one / lax.dynamic_slice_in_dim(attention_gain, own_entries, entries, 0)

time: 561 us -> 556 us (level)
  waiting for transfers between devices: 157 us -> 149 us
  starting transfers between devices: 61.1 us -> 68.8 us
    ppermute x28, waiting for transfers between devices: 107 us -> 88.5 us  [flip(): return lax.ppermute(value, axis, [(0, 1), (1, 0)])]
    ppermute x4, waiting for transfers between devices: 13.3 us -> 28.8 us  [flip_some(): return lax.ppermute(value, ('c', 'zh', 'zl'), moves)]
  transfers between devices with their start and end apart: 49 -> 49, of which waited for: 21 -> 21; matrix products, arithmetic and copies ran while one was open for 19% -> 20% of each run, Pallas kernels for 32% -> 32%
where the time goes in v8:
time: 556 us; the launch traced here: 547 us
  Pallas kernels  190 us (34%)
  waiting for transfers between devices  149 us (27%)
  other arithmetic  74.6 us (13%)
  starting transfers between devices  68.8 us (12%)
  local copies, waits for them, and re-layouts  35.3 us (6%)
  between operations  15.6 us (3%)
  matrix products  13.9 us (2%)
    ppermute x28, waiting for transfers between devices, flip(): return lax.ppermute(value, axis, [(0, 1), (1, 0)])  88.5 us
    pallas_call x4, Pallas kernels, moe_call(): pl.pallas_call(kernel, grid_spec=pltpu.PrefetchScalarGridSpec(num_scalar_...  85.5 us
    pallas_call x1, Pallas kernels, attention_backward(): pl.pallas_call(backward_kernel, grid_spec=pltpu.PrefetchScalarGridSpec(nu...  62.5 us
    pallas_call x1, Pallas kernels, attention_forward(): pl.pallas_call(forward_kernel, grid_spec=pltpu.PrefetchScalarGridSpec(num...  42 us
    ppermute x28, starting transfers between devices, flip(): return lax.ppermute(value, axis, [(0, 1), (1, 0)])  40.6 us
    ppermute x4, waiting for transfers between devices, flip_some(): return lax.ppermute(value, ('c', 'zh', 'zl'), moves)  28.8 us
    reduce_scatter x1, waiting for transfers between devices, body(): lax.psum_scatter(weights_part, high_bits, scatter_dimension=1, tiled=True)  12.4 us
  transfers between devices with their start and end apart: 49, of which 21 were waited for; matrix products, arithmetic and copies ran while one was open for 20% of the time, Pallas kernels for 32%

profile of v8, /device:TPU:0, one launch (start us, length us, event | category | flops | bytes accessed | tf_op | source)
XLA Modules:
  0.0 546.9 jit_solution(4516282471691521694)
XLA Ops:
  11.9 3.6 collective-permute-start.1
  17.7 3.5 collective-permute-start.2
  35.2 13.2 %collective-permute-done.2 = bf16[768,768]{1,0:T(8,128)(2,1)} collective-permute-done((bf16[768,768]{1,0:T(8,128)(2,1)}, bf16[768,768]{1,0:T(8,128)(2,1)}, u32[]{:S(2)}, u32[]{:S(2)}) %collective-permute-start.2) | collective-permute-done | bytes 1179680 | tf_op jit(solution)/shard_map/ppermute | solution.py:750
  49.5 3.2 convert_reduce_fusion.1
  60.3 3.1 collective-permute-start.4
  63.4 2.4 broadcast_select_fusion.3.x2
  65.8 10.7 %collective-permute-start.6 = (bf16[768,768]{1,0:T(8,128)(2,1)}, bf16[768,768]{1,0:T(8,128)(2,1)}, u32[]{:S(2)}, u32[]{:S(2)}) collective-permute-start(bf16[768,768]{1,0:T(8,128)(2,1)} %broadcast_select_fusion.3.x2), channel_id=1, source_target_pairs={{0,4},{4,0},{1,5},{5,1},{2,6},{6,2},{3,7},{7,3},{8,12},{12,8},{9,1... | collective-permute-start | bytes 3538952 | tf_op jit(solution)/shard_map/ppermute | solution.py:745
  77.1 3.4 collective-permute-start.7
  80.5 6.0 %all-gather.4.cloned.1.call-done = bf16[3072,192]{1,0:T(8,128)(2,1)} async-done(((bf16[384,192]{1,0:T(8,128)(2,1)}), bf16[3072,192]{1,0:T(8,128)(2,1)}) %all-gather.4.cloned.1.call-update) | async-done | bytes 1179664 | tf_op jit(solution)/shard_map/all_gather | solution.py:809
  88.1 42.0 %attention_forward.1 = (bf16[768,768]{1,0:T(8,128)(2,1)}, bf16[768,768]{1,0:T(8,128)(2,1)}, bf16[768,768]{1,0:T(8,128)(2,1)}, bf16[768,768]{1,0:T(8,128)(2,1)}, ...) custom-call(s32[5,6]{1,0:T(8,128)} %stack.33.ranges, ...), custom_call_target="tpu_custom_call" | custom-call | flops 28991029248 | bytes 41943040 | tf_op jit(solution)/shard_map/attention_forward/pallas_call | solution.py:215
  130.1 2.6 collective-permute-done.8
  152.5 2.6 convert_reduce_fusion
  156.2 13.2 %collective-permute-done.10 = bf16[768,768]{1,0:T(8,128)(2,1)S(1)} collective-permute-done((bf16[768,768]{1,0:T(8,128)(2,1)S(1)}, bf16[768,768]{1,0:T(8,128)(2,1)S(1)}, u32[]{:S(2)}, u32[]{:S(2)}) %collective-permute-start.10) | collective-permute-done | bytes 1179680 | tf_op jit(solution)/shard_map/ppermute | solution.py:745
  170.5 3.8 fusion.55
  175.0 2.3 fusion.27
  180.3 3.3 collective-permute-start.16
  183.8 2.3 convolution_convert_fusion.d0.a0
  186.1 30.7 %collective-permute-done.12.x2.a2 = bf16[768,768]{1,0:T(8,128)(2,1)S(1)} collective-permute-done((bf16[768,768]{1,0:T(8,128)(2,1)S(1)}, bf16[768,768]{1,0:T(8,128)(2,1)S(1)}, u32[]{:S(2)}, u32[]{:S(2)}) %collective-permute-start.12) | collective-permute-done | bytes 1179680 | tf_op jit(solution)/shard_map/ppermute | solution.py:745
  221.1 28.8 %moe_forward.1 = (bf16[768,768]{1,0:T(8,128)(2,1)}, bf16[768,768]{1,0:T(8,128)(2,1)}, bf16[768,768]{1,0:T(8,128)(2,1)}, bf16[768,768]{1,0:T(8,128)(2,1)}, bf16[4...) custom-call(s32[33]{0:T(128)} %concatenate.15.table, bf16[768,768]{1,0:T(8,128)(2,1)} %copy-done.60, ...), custom_call_target="tpu_custom_call" | custom-call | flops 9059696640 | bytes 41943040 | tf_op jit(solution)/shard_map/moe_forward/pallas_call | solution.py:672
  250.5 2.5 collective-permute-done.18
  257.4 24.4 %moe_backward.1 = (bf16[768,768]{1,0:T(8,128)(2,1)}, bf16[768,768]{1,0:T(8,128)(2,1)}, bf16[768,768]{1,0:T(8,128)(2,1)}, bf16[768,768]{1,0:T(8,128)(2,1)}, bf16[4,1024,768]{2,1,0:T(8,128)(2,1)}) custom-call(s32[33]{0:T(128)} %concatenate.15.table, bf16[768,768]{1,0:T(8,128)(2,1)} %convolution_convert_fusion.d0.a0, bf16[768,768]{1,0:T(8,128)(2,1)} %copy-done.65, ...), custom_call_target="tpu_custom_call" | custom-call | flops 9059696640 | bytes 41943040 | tf_op jit(solution)/shard_map/moe_backward/pallas_call | solution.py:672
  282.7 3.1 collective-permute-done.21
  285.8 2.7 add_convert_fusion.4
  288.4 16.1 %moe_weights.2 = (bf16[4,768,768]{2,1,0:T(8,128)(2,1)}, bf16[16,128]{1,0:T(8,128)(2,1)}) custom-call(s32[33]{0:T(128)} %concatenate.15.table, bf16[768,768]{1,0:T(8,128)(2,1)} %convolution_convert_fusion.d0.a0, bf16[768,768]{1,0:T(8,128)(2,1)} %copy-done.65, bf16[768,768]{1,0:T(8,128)(2,1)} %collective-permute-done.15.d2.a2, bf16[768,768]{1,0:T(8,128)(2,1)} %copy-done.64, ...), custom_call_target="tpu_custom_call" | custom-call | flops 4529848320 | bytes 41943040 | tf_op jit(solution)/shard_map/moe_weights/pallas_call | solution.py:672
  307.7 3.7 fusion.30
  311.4 21.8 %collective-permute-done.24 = bf16[768,768]{1,0:T(8,128)(2,1)S(1)} collective-permute-done((bf16[768,768]{1,0:T(8,128)(2,1)}, bf16[768,768]{1,0:T(8,128)(2,1)S(1)}, u32[]{:S(2)}, u32[]{:S(2)}) %collective-permute-start.24) | collective-permute-done | bytes 1179680 | tf_op jit(solution)/shard_map/ppermute | solution.py:745
  333.4 2.6 multiply_reduce_fusion
  335.9 3.3 convert_add_fusion
  346.6 5.4 all-to-all-start
  352.1 16.2 %moe_weights.3 = (bf16[4,768,768]{2,1,0:T(8,128)(2,1)}, bf16[16,128]{1,0:T(8,128)(2,1)}) custom-call(s32[33]{0:T(128)} %concatenate.15.table, bf16[768,768]{1,0:T(8,128)(2,1)} %copy-done.60, bf16[768,768]{1,0:T(8,128)(2,1)} %copy-done.62, bf16[768,768]{1,0:T(8,128)(2,1)} %copy-done.61, bf16[768,768]{1,0:T(8,128)(2,1)} %collective-permute-done.17.x3.a3, ...), custom_call_target="tpu_custom_call" | custom-call | flops 4529848320 | bytes 41943040 | tf_op jit(solution)/shard_map/moe_weights/pallas_call | solution.py:672
  368.3 5.1 all-to-all-done
  375.6 2.7 collective-permute-done.26.g3
  383.1 62.5 %attention_backward.1 = (bf16[768,768]{1,0:T(8,128)(2,1)}, bf16[768,768]{1,0:T(8,128)(2,1)}, bf16[768,768]{1,0:T(8,128)(2,1)}, bf16[768,768]{1,0:T(8,128)(2,1)}, bf16[4,768,192]{2,1,0:T(8,128)(2,1)}) custom-call(s32[5,6]{1,0:T(8,128)} %stack.39.ranges, s32[4]{0:T(128)} %pad_add_fusion.1.ranks, bf16[768,768]{1,0:T(8,128)(2,1)} %convert_element_type.215.g0, ...), custom_call_target="tpu_custom_call" | custom-call | flops 65229815808 | bytes 41943040 | tf_op jit(solution)/shard_map/attention_backward/pallas_call | solution.py:389
  446.9 4.1 collective-permute-start.32
  451.0 2.8 collective-permute-done.32
  453.8 2.9 add_convert_fusion
  459.1 2.3 constant_dynamic-slice_fusion.2
  465.4 4.7 collective-permute-start.35
  470.0 12.4 %reduce-scatter.6.cloned.1.call-done = bf16[4,192,192]{2,1,0:T(8,128)(2,1)} async-done(((bf16[4,768,192]{2,1,0:T(8,128)(2,1)}), bf16[4,192,192]{2,1,0:T(8,128)(2,1)}) %reduce-scatter.6.cloned.1.call-update) | async-done | bytes 294928 | tf_op jit(solution)/shard_map/reduce_scatter | solution.py:965
  482.5 3.2 fusion.37
  485.8 3.6 fusion.14
  489.4 5.2 collective-permute-done.35
  501.7 2.4 convert_add_fusion.3
  507.8 15.6 %collective-permute-done.38 = bf16[768,768]{1,0:T(8,128)(2,1)S(1)} collective-permute-done((bf16[768,768]{1,0:T(8,128)(2,1)}, bf16[768,768]{1,0:T(8,128)(2,1)S(1)}, u32[]{:S(2)}, u32[]{:S(2)}) %collective-permute-start.38) | collective-permute-done | bytes 1179680 | tf_op jit(solution)/shard_map/ppermute | solution.py:750
  523.4 2.4 fusion.38
  525.9 3.3 fusion.19
  530.1 3.7 collective-permute-done.40
  536.6 2.4 select_bitcast_fusion
  (306 shorter events, 107.6 us)
Async XLA Ops:
  7.2 79.3 %all-gather.4.cloned.1.call-start = ((), (), s32[]{:S(2)}) async-start(), calls=%async_computation.4 | async-start | bytes 1769472 | tf_op jit(solution)/shard_map/all_gather | solution.py:809
  8.7 14.2 %collective-permute-start.3 = (s32[3,3072]{1,0:T(4,128)}, s32[3,3072]{1,0:T(4,128)}, u32[]{:S(2)}, u32[]{:S(2)}) collective-permute-start(s32[3,3072]{1,0:T(4,128)} %pad_add_fusion), channel_id=1, source_target_pairs={{0,4},{4,0},{1,5},{5,1},{2,6},{6,2},{3,7},{7,3},{8,12},{12,8},{9,1... | collective-permute-start | bytes 110600 | tf_op jit(solution)/shard_map/ppermute | solution.py:745
  11.9 23.3 %collective-permute-start.1 = (bf16[384,192]{1,0:T(8,128)(2,1)}, bf16[384,192]{1,0:T(8,128)(2,1)}, u32[]{:S(2)}, u32[]{:S(2)}) collective-permute-start(bf16[384,192]{1,0:T(8,128)(2,1)} %constant_dynamic-slice_fusion.18), channel_id=1, source_target_pairs={{0,2},{2,0},{1,3},{3,1},{4,6},{6,4},{5,7},{7,5},{8,10},{10,8},{9,1... | collective-permute-start | bytes 442376 | tf_op jit(solution)/shard_map/ppermute | solution.py:745
  17.7 30.8 %collective-permute-start.2 = (bf16[768,768]{1,0:T(8,128)(2,1)}, bf16[768,768]{1,0:T(8,128)(2,1)}, u32[]{:S(2)}, u32[]{:S(2)}) collective-permute-start(bf16[768,768]{1,0:T(8,128)(2,1)} %fusion.26), channel_id=1, source_target_pairs={{0,1},{1,0},{6,7},{7,6},{8,9},{9,8},{14,15},{15,14},{16,17},{17,16... | collective-permute-start | bytes 3538952 | tf_op jit(solution)/shard_map/ppermute | solution.py:750
  21.2 27.3 %collective-permute-start = (bf16[768,768]{1,0:T(8,128)(2,1)S(1)}, bf16[768,768]{1,0:T(8,128)(2,1)S(1)}, u32[]{:S(2)}, u32[]{:S(2)}) collective-permute-start(bf16[768,768]{1,0:T(8,128)(2,1)S(1)} %bitcast.89), channel_id=1, source_target_pairs={{2,4},{4,2},{3,5},{5,3},{10,12},{12,10},{11,13},{13,11},{18,20},{2... | collective-permute-start | bytes 3538952 | tf_op jit(solution)/shard_map/ppermute | solution.py:847
  54.6 8.8 %collective-permute-start.5 = (bf16[768,768]{1,0:T(8,128)(2,1)}, bf16[768,768]{1,0:T(8,128)(2,1)}, u32[]{:S(2)}, u32[]{:S(2)}) collective-permute-start(bf16[768,768]{1,0:T(8,128)(2,1)} %get-tuple-element.254), channel_id=1, source_target_pairs={{2,3},{3,2},{4,5},{5,4},{10,11},{11,10},{12,13},{13,12},{18,19},{1... | collective-permute-start | bytes 3538952 | tf_op jit(solution)/shard_map/ppermute | solution.py:750
  56.3 164.7 %all-gather.6.cloned.1.call-start = ((), (), s32[]{:S(2)}) async-start(), calls=%async_computation.5 | async-start | bytes 5308416 | tf_op jit(solution)/shard_map/all_gather | solution.py:809
  60.3 27.8 %collective-permute-start.4 = (bf16[768,768]{1,0:T(8,128)(2,1)}, bf16[768,768]{1,0:T(8,128)(2,1)}, u32[]{:S(2)}, u32[]{:S(2)}) collective-permute-start(bf16[768,768]{1,0:T(8,128)(2,1)} %get-tuple-element.253.x0), channel_id=1, source_target_pairs={{0,4},{4,0},{1,5},{5,1},{2,6},{6,2},{3,7},{7,3},{8,12},{12,8},{9,1... | collective-permute-start | bytes 3538952 | tf_op jit(solution)/shard_map/ppermute | solution.py:745
  65.8 22.2 %collective-permute-start.6 = (bf16[768,768]{1,0:T(8,128)(2,1)}, bf16[768,768]{1,0:T(8,128)(2,1)}, u32[]{:S(2)}, u32[]{:S(2)}) collective-permute-start(bf16[768,768]{1,0:T(8,128)(2,1)} %broadcast_select_fusion.3.x2), channel_id=1, source_target_pairs={{0,4},{4,0},{1,5},{5,1},{2,6},{6,2},{3,7},{7,3},{8,12},{12,8},{9,1... | collective-permute-start | bytes 3538952 | tf_op jit(solution)/shard_map/ppermute | solution.py:745
  77.1 53.0 %collective-permute-start.7 = (bf16[384,768]{1,0:T(8,128)(2,1)}, bf16[384,768]{1,0:T(8,128)(2,1)S(1)}, u32[]{:S(2)}, u32[]{:S(2)}) collective-permute-start(bf16[384,768]{1,0:T(8,128)(2,1)} %constant_dynamic-slice_fusion.17), channel_id=1, source_target_pairs={{0,2},{2,0},{1,3},{3,1},{4,6},{6,4},{5,7},{7,5},{8,10},{10,8},{9,1... | collective-permute-start | bytes 1769480 | tf_op jit(solution)/shard_map/ppermute | solution.py:745
  80.5 52.2 %collective-permute-start.8 = (bf16[384,768]{1,0:T(8,128)(2,1)}, bf16[384,768]{1,0:T(8,128)(2,1)}, u32[]{:S(2)}, u32[]{:S(2)}) collective-permute-start(bf16[384,768]{1,0:T(8,128)(2,1)} %constant_dynamic-slice_fusion.16), channel_id=1, source_target_pairs={{0,2},{2,0},{1,3},{3,1},{4,6},{6,4},{5,7},{7,5},{8,10},{10,8},{9,1... | collective-permute-start | bytes 1769480 | tf_op jit(solution)/shard_map/ppermute | solution.py:745
  132.7 88.3 %all-gather.8.cloned.1.call-start = ((), (), s32[]{:S(2)}) async-start(), calls=%async_computation.6 | async-start | bytes 5308416 | tf_op jit(solution)/shard_map/all_gather | solution.py:809
  133.5 244.8 %reduce-scatter.4.cloned.1.call-start = ((), (), s32[]{:S(2)}) async-start(), calls=%async_computation.7 | async-start | bytes 5898240 | tf_op jit(solution)/shard_map/reduce_scatter | solution.py:927
  133.7 5.4 collective-permute-start.9
  135.1 35.1 %collective-permute-start.11 = (bf16[768,768]{1,0:T(8,128)(2,1)}, bf16[768,768]{1,0:T(8,128)(2,1)}, u32[]{:S(2)}, u32[]{:S(2)}) collective-permute-start(bf16[768,768]{1,0:T(8,128)(2,1)} %get-tuple-element.116), channel_id=1, source_target_pairs={{0,4},{4,0},{1,5},{5,1},{2,6},{6,2},{3,7},{7,3},{8,12},{12,8},{9,1... | collective-permute-start | bytes 3538952 | tf_op jit(solution)/shard_map/ppermute | solution.py:745
  140.7 28.7 %collective-permute-start.10 = (bf16[768,768]{1,0:T(8,128)(2,1)S(1)}, bf16[768,768]{1,0:T(8,128)(2,1)S(1)}, u32[]{:S(2)}, u32[]{:S(2)}) collective-permute-start(bf16[768,768]{1,0:T(8,128)(2,1)S(1)} %add_convert_fusion.6), channel_id=1, source_target_pairs={{0,1},{1,0},{2,3},{3,2},{4,5},{5,4},{6,7},{7,6},{8,9},{9,8},{10,11... | collective-permute-start | bytes 3538952 | tf_op jit(solution)/shard_map/ppermute | solution.py:745
  169.4 14.2 %collective-permute-start.13 = (bf16[768,768]{1,0:T(8,128)(2,1)}, bf16[768,768]{1,0:T(8,128)(2,1)S(1)}, u32[]{:S(2)}, u32[]{:S(2)}) collective-permute-start(bf16[768,768]{1,0:T(8,128)(2,1)} %bitcast.94), channel_id=1, source_target_pairs={{2,4},{4,2},{3,5},{5,3},{10,12},{12,10},{11,13},{13,11},{18,20},{2... | collective-permute-start | bytes 3538952 | tf_op jit(solution)/shard_map/ppermute | solution.py:892
  178.4 38.4 %collective-permute-start.12 = (bf16[768,768]{1,0:T(8,128)(2,1)S(1)}, bf16[768,768]{1,0:T(8,128)(2,1)S(1)}, u32[]{:S(2)}, u32[]{:S(2)}) collective-permute-start(bf16[768,768]{1,0:T(8,128)(2,1)S(1)} %convolution_convert_fusion.1.x0.a0), channel_id=1, source_target_pairs={{0,1},{1,0},{2,3},{3,2},{4,5},{5,4},{6,7},{7,6},{8,9},{9,8},{10,11... | collective-permute-start | bytes 3538952 | tf_op jit(solution)/shard_map/ppermute | solution.py:745
  180.3 38.2 %collective-permute-start.16 = (bf16[768,768]{1,0:T(8,128)(2,1)S(1)}, bf16[768,768]{1,0:T(8,128)(2,1)S(1)}, u32[]{:S(2)}, u32[]{:S(2)}) collective-permute-start(bf16[768,768]{1,0:T(8,128)(2,1)S(1)} %convolution_convert_fusion.1.x0.a0), channel_id=1, source_target_pairs={{0,4},{4,0},{1,5},{5,1},{2,6},{6,2},{3,7},{7,3},{8,12},{12,8},{9,1... | collective-permute-start | bytes 3538952 | tf_op jit(solution)/shard_map/ppermute | solution.py:745
  216.8 4.3 collective-permute-start.17
  218.5 31.4 %collective-permute-start.15 = (bf16[768,768]{1,0:T(8,128)(2,1)}, bf16[768,768]{1,0:T(8,128)(2,1)}, u32[]{:S(2)}, u32[]{:S(2)}) collective-permute-start(bf16[768,768]{1,0:T(8,128)(2,1)} %convolution_convert_fusion.d0.a0), channel_id=1, source_target_pairs={{0,1},{1,0},{2,3},{3,2},{4,5},{5,4},{6,7},{7,6},{8,9},{9,8},{10,11... | collective-permute-start | bytes 3538952 | tf_op jit(solution)/shard_map/ppermute | solution.py:745
  249.9 3.1 collective-permute-start.18
  250.0 4.7 collective-permute-start.19
  250.4 5.9 %collective-permute-start.14 = (bf16[768,768]{1,0:T(8,128)(2,1)}, bf16[768,768]{1,0:T(8,128)(2,1)S(1)}, u32[]{:S(2)}, u32[]{:S(2)}) collective-permute-start(bf16[768,768]{1,0:T(8,128)(2,1)} %convolution_convert_fusion.d0.a0), channel_id=1, source_target_pairs={{0,4},{4,0},{1,5},{5,1},{2,6},{6,2},{3,7},{7,3},{8,12},{12,8},{9,1... | collective-permute-start | bytes 3538952 | tf_op jit(solution)/shard_map/ppermute | solution.py:745
  254.7 28.0 %collective-permute-start.20 = (bf16[768,768]{1,0:T(8,128)(2,1)S(1)}, bf16[768,768]{1,0:T(8,128)(2,1)S(1)}, u32[]{:S(2)}, u32[]{:S(2)}) collective-permute-start(bf16[768,768]{1,0:T(8,128)(2,1)S(1)} %add_convert_fusion.5), channel_id=1, source_target_pairs={{0,1},{1,0},{2,3},{3,2},{4,5},{5,4},{6,7},{7,6},{8,9},{9,8},{10,11... | collective-permute-start | bytes 3538952 | tf_op jit(solution)/shard_map/ppermute | solution.py:745
  304.6 3.1 collective-permute-start.22
  304.8 28.5 %collective-permute-start.24 = (bf16[768,768]{1,0:T(8,128)(2,1)}, bf16[768,768]{1,0:T(8,128)(2,1)S(1)}, u32[]{:S(2)}, u32[]{:S(2)}) collective-permute-start(bf16[768,768]{1,0:T(8,128)(2,1)} %add_convert_fusion.4), channel_id=1, source_target_pairs={{0,1},{1,0},{2,3},{3,2},{4,5},{5,4},{6,7},{7,6},{8,9},{9,8},{10,11... | collective-permute-start | bytes 3538952 | tf_op jit(solution)/shard_map/ppermute | solution.py:745
  305.3 27.9 %collective-permute-start.23 = (bf16[768,768]{1,0:T(8,128)(2,1)}, bf16[768,768]{1,0:T(8,128)(2,1)S(1)}, u32[]{:S(2)}, u32[]{:S(2)}) collective-permute-start(bf16[768,768]{1,0:T(8,128)(2,1)} %get-tuple-element.144), channel_id=1, source_target_pairs={{0,4},{4,0},{1,5},{5,1},{2,6},{6,2},{3,7},{7,3},{8,12},{12,8},{9,1... | collective-permute-start | bytes 3538952 | tf_op jit(solution)/shard_map/ppermute | solution.py:745
  340.4 34.6 %collective-permute-start.25 = (bf16[768,768]{1,0:T(8,128)(2,1)}, bf16[768,768]{1,0:T(8,128)(2,1)}, u32[]{:S(2)}, u32[]{:S(2)}) collective-permute-start(bf16[768,768]{1,0:T(8,128)(2,1)} %convert_element_type.215.g0), channel_id=1, source_target_pairs={{0,1},{1,0},{2,3},{3,2},{4,5},{5,4},{6,7},{7,6},{8,9},{9,8},{10,11... | collective-permute-start | bytes 3538952 | tf_op jit(solution)/shard_map/ppermute | solution.py:745
  346.6 26.8 %all-to-all-start = ((f32[32,5,24]{2,1,0:T(8,128)}), f32[32,5,24]{2,1,0:T(8,128)}, u32[]{:S(2)}, u32[]{:S(2)}) async-start(f32[32,5,24]{2,1,0:T(8,128)} %copy.65), calls=%async_computation.1 | async-start | bytes 262144 | tf_op jit(solution)/shard_map/all_to_all | solution.py:944
  352.1 107.0 %reduce-scatter.8.cloned.1.call-start = ((), (), s32[]{:S(2)}) async-start(), calls=%async_computation.9 | async-start | bytes 5898240 | tf_op jit(solution)/shard_map/reduce_scatter | solution.py:947
  375.0 107.5 %reduce-scatter.6.cloned.1.call-start = ((), (), s32[]{:S(2)}) async-start(), calls=%async_computation.8 | async-start | bytes 1966080 | tf_op jit(solution)/shard_map/reduce_scatter | solution.py:965
  375.0 3.3 collective-permute-start.26
  375.1 8.0 %collective-permute-start.27 = (bf16[768,768]{1,0:T(8,128)(2,1)}, bf16[768,768]{1,0:T(8,128)(2,1)}, u32[]{:S(2)}, u32[]{:S(2)}) collective-permute-start(bf16[768,768]{1,0:T(8,128)(2,1)} %convert_element_type.215.g0), channel_id=1, source_target_pairs={{0,4},{4,0},{1,5},{5,1},{2,6},{6,2},{3,7},{7,3},{8,12},{12,8},{9,1... | collective-permute-start | bytes 3538952 | tf_op jit(solution)/shard_map/ppermute | solution.py:745
  379.7 66.0 %collective-permute-start.30 = (bf16[4,96,768]{2,1,0:T(8,128)(2,1)S(1)}, bf16[4,96,768]{2,1,0:T(8,128)(2,1)S(1)}, u32[]{:S(2)}, u32[]{:S(2)}) collective-permute-start(bf16[4,96,768]{2,1,0:T(8,128)(2,1)S(1)} %get-tuple-element.190), channel_id=1, source_target_pairs={{2,4},{4,2},{3,5},{5,3},{10,12},{12,10},{11,13},{13,11},{18,20},{2... | collective-permute-start | bytes 1769480 | tf_op jit(solution)/shard_map/ppermute | solution.py:794
  380.4 65.3 %collective-permute-start.31 = (bf16[4,96,768]{2,1,0:T(8,128)(2,1)S(1)}, bf16[4,96,768]{2,1,0:T(8,128)(2,1)S(1)}, u32[]{:S(2)}, u32[]{:S(2)}) collective-permute-start(bf16[4,96,768]{2,1,0:T(8,128)(2,1)S(1)} %get-tuple-element.260), channel_id=1, source_target_pairs={{0,4},{2,0},{4,6},{6,2},{1,5},{3,1},{5,7},{7,3},{8,12},{10,8},{12,... | collective-permute-start | bytes 1769480 | tf_op jit(solution)/shard_map/ppermute | solution.py:793
  382.1 63.6 %collective-permute-start.29 = (bf16[768,768]{1,0:T(8,128)(2,1)S(1)}, bf16[768,768]{1,0:T(8,128)(2,1)S(1)}, u32[]{:S(2)}, u32[]{:S(2)}) collective-permute-start(bf16[768,768]{1,0:T(8,128)(2,1)S(1)} %copy-done.8), channel_id=1, source_target_pairs={{2,4},{4,2},{3,5},{5,3},{10,12},{12,10},{11,13},{13,11},{18,20},{2... | collective-permute-start | bytes 3538952 | tf_op jit(solution)/shard_map/ppermute | solution.py:950
  446.9 6.9 %collective-permute-start.32 = (bf16[768,768]{1,0:T(8,128)(2,1)}, bf16[768,768]{1,0:T(8,128)(2,1)}, u32[]{:S(2)}, u32[]{:S(2)}) collective-permute-start(bf16[768,768]{1,0:T(8,128)(2,1)} %get-tuple-element.167), channel_id=1, source_target_pairs={{0,4},{4,0},{1,5},{5,1},{2,6},{6,2},{3,7},{7,3},{8,12},{12,8},{9,1... | collective-permute-start | bytes 3538952 | tf_op jit(solution)/shard_map/ppermute | solution.py:745
  456.7 25.7 %collective-permute-start.33 = (bf16[768,768]{1,0:T(8,128)(2,1)}, bf16[768,768]{1,0:T(8,128)(2,1)}, u32[]{:S(2)}, u32[]{:S(2)}) collective-permute-start(bf16[768,768]{1,0:T(8,128)(2,1)} %add_convert_fusion), channel_id=1, source_target_pairs={{2,3},{3,2},{4,5},{5,4},{10,11},{11,10},{12,13},{13,12},{18,19},{1... | collective-permute-start | bytes 3538952 | tf_op jit(solution)/shard_map/ppermute | solution.py:750
  458.4 24.0 %collective-permute-start.28 = (bf16[768,768]{1,0:T(8,128)(2,1)}, bf16[768,768]{1,0:T(8,128)(2,1)}, u32[]{:S(2)}, u32[]{:S(2)}) collective-permute-start(bf16[768,768]{1,0:T(8,128)(2,1)} %get-tuple-element.164), channel_id=1, source_target_pairs={{0,4},{4,0},{1,5},{5,1},{2,6},{6,2},{3,7},{7,3},{8,12},{12,8},{9,1... | collective-permute-start | bytes 3538952 | tf_op jit(solution)/shard_map/ppermute | solution.py:745
  461.4 21.0 %collective-permute-start.34 = (bf16[4,96,768]{2,1,0:T(8,128)(2,1)}, bf16[4,96,768]{2,1,0:T(8,128)(2,1)}, u32[]{:S(2)}, u32[]{:S(2)}) collective-permute-start(bf16[4,96,768]{2,1,0:T(8,128)(2,1)} %get-tuple-element.187), channel_id=1, source_target_pairs={{2,4},{4,2},{3,5},{5,3},{10,12},{12,10},{11,13},{13,11},{18,20},{2... | collective-permute-start | bytes 1769480 | tf_op jit(solution)/shard_map/ppermute | solution.py:794
  465.4 29.2 %collective-permute-start.35 = (bf16[4,96,768]{2,1,0:T(8,128)(2,1)}, bf16[4,96,768]{2,1,0:T(8,128)(2,1)}, u32[]{:S(2)}, u32[]{:S(2)}) collective-permute-start(bf16[4,96,768]{2,1,0:T(8,128)(2,1)} %get-tuple-element.257), channel_id=1, source_target_pairs={{0,4},{2,0},{4,6},{6,2},{1,5},{3,1},{5,7},{7,3},{8,12},{10,8},{12,... | collective-permute-start | bytes 1769480 | tf_op jit(solution)/shard_map/ppermute | solution.py:793
  494.6 28.8 %collective-permute-start.38 = (bf16[768,768]{1,0:T(8,128)(2,1)}, bf16[768,768]{1,0:T(8,128)(2,1)S(1)}, u32[]{:S(2)}, u32[]{:S(2)}) collective-permute-start(bf16[768,768]{1,0:T(8,128)(2,1)} %add_convert_fusion), channel_id=1, source_target_pairs={{0,1},{1,0},{6,7},{7,6},{8,9},{9,8},{14,15},{15,14},{16,17},{17,16... | collective-permute-start | bytes 3538952 | tf_op jit(solution)/shard_map/ppermute | solution.py:750
  496.5 7.6 %collective-permute-start.36 = (bf16[4,96,192]{2,1,0:T(8,128)(2,1)S(1)}, bf16[4,96,192]{2,1,0:T(8,128)(2,1)S(1)}, u32[]{:S(2)}, u32[]{:S(2)}) collective-permute-start(bf16[4,96,192]{2,1,0:T(8,128)(2,1)S(1)} %get-tuple-element.263), channel_id=1, source_target_pairs={{2,4},{4,2},{3,5},{5,3},{10,12},{12,10},{11,13},{13,11},{18,20},{2... | collective-permute-start | bytes 442376 | tf_op jit(solution)/shard_map/ppermute | solution.py:794
  497.2 8.7 %collective-permute-start.37 = (bf16[4,96,192]{2,1,0:T(8,128)(2,1)S(1)}, bf16[4,96,192]{2,1,0:T(8,128)(2,1)S(1)}, u32[]{:S(2)}, u32[]{:S(2)}) collective-permute-start(bf16[4,96,192]{2,1,0:T(8,128)(2,1)S(1)} %get-tuple-element.264), channel_id=1, source_target_pairs={{0,4},{2,0},{4,6},{6,2},{1,5},{3,1},{5,7},{7,3},{8,12},{10,8},{12,... | collective-permute-start | bytes 442376 | tf_op jit(solution)/shard_map/ppermute | solution.py:793
  497.3 39.3 %collective-permute-start.39 = (bf16[768,768]{1,0:T(8,128)(2,1)}, bf16[768,768]{1,0:T(8,128)(2,1)}, u32[]{:S(2)}, u32[]{:S(2)}) collective-permute-start(bf16[768,768]{1,0:T(8,128)(2,1)} %fusion.14), channel_id=1, source_target_pairs={{2,4},{4,2},{3,5},{5,3},{10,12},{12,10},{11,13},{13,11},{18,20},{2... | collective-permute-start | bytes 3538952 | tf_op jit(solution)/shard_map/ppermute | solution.py:975
  529.3 4.4 collective-permute-start.40
  534.6 4.4 collective-permute-start.41
  (68 other events, 1218.3 us)
Sparse Core Ops, SparseCore 0:
  56.5 30.0 all-gather.3
  132.9 40.1 all-gather.5
  174.9 38.9 all-gather.7
  304.7 58.3 reduce-scatter.3
  375.1 55.4 reduce-scatter.7
  451.1 31.2 reduce-scatter.5
